TPU v7x, 512 devices: a whole 4x8x8 slice. The times are simulated.
512 devices in a mesh: role: 2 (over z_lo), seq: 64 (over y, x, core), head: 4 (over z_hi).
Axes of the slice: x: 4, y: 8, z: 8 (z_hi: 4, z_lo: 2; z = z_hi * 2 + z_lo), core: 2. Of those that a mesh axis runs over, the one named last changes fastest.
Arguments:
- query_heads: bfloat16 [8192, 16, 128], P('seq', ('role', 'head')), may hold values from -16 to 16
- key_heads: bfloat16 [8192, 8, 128], P('seq', ('role', 'head')), may hold values from -16 to 16
- value_heads: bfloat16 [8192, 8, 128], P('seq', ('role', 'head')), may hold values from -6 to 6
- distill_proj: bfloat16 [16, 128, 1024], P(('role', 'head')), may hold values from -6 to 6
- conv_input: bfloat16 [1024, 8192], P(('role', 'head'), 'seq'), may hold values from -6 to 6
- gate_input: bfloat16 [1024, 8192], P(('role', 'head'), 'seq'), may hold values from -6 to 6
- filter_taps: float32 [1024, 8192], P(('role', 'head'), 'seq'), may hold values from -0.0625 to 0.0625
- skip_gain: float32 [1024], P(('role', 'head')), may hold values from -4 to 4
Outputs:
- grad_input: float32 [1024, 8192], P(('role', 'head'), 'seq')
- filter_step: float32 [1024, 8192], P(('role', 'head'), 'seq')
All inputs are finite; a program needn't handle non-finite values.
Results may differ from a plain program's by a relative error of at most 0.005.
Values may be sent and summed in bfloat16 or wider, within the bound.
No kernel may reach another device: no remote copies, remote signals or barrier semaphores. Data moves between devices by JAX's collectives and lax.ppermute only.
A program may use at most 64 MiB of HBM per device.

v0:
```python
import math

import jax
import jax.numpy as jnp
from jax import lax
from jax.sharding import PartitionSpec as P

WINDOW = 4096


highest = lax.Precision.HIGHEST


def shifted(value, axis, steps):
    count = lax.axis_size(axis)
    leading, last = (max(0, -steps), min(count, count - steps))
    return lax.ppermute(value, axis, [(source, source + steps) for source in range(leading, last)])


def angle_table(row_ids, col_ids, length):
    product = row_ids[:, None] * col_ids[None, :] % length
    quarter = length // 4
    eighth = length // 8
    quadrant = product // quarter
    within = product % quarter
    flipped = within > eighth
    reduced = jnp.where(flipped, quarter - within, within)
    angles = reduced.astype(jnp.float32) * (2.0 * math.pi / length)
    base_cos = jnp.cos(angles)
    base_sin = jnp.sin(angles)
    first_cos = jnp.where(flipped, base_sin, base_cos)
    first_sin = jnp.where(flipped, base_cos, base_sin)
    cosine = jnp.where(
        quadrant == 0,
        first_cos,
        jnp.where(quadrant == 1, -first_sin, jnp.where(quadrant == 2, -first_cos, first_sin)),
    )
    sine_part = jnp.where(
        quadrant == 0,
        first_sin,
        jnp.where(quadrant == 1, first_cos, jnp.where(quadrant == 2, -first_sin, -first_cos)),
    )
    return (cosine, sine_part)


def spread_rows(stacked):
    pieces = stacked.shape[2]
    cosine, sine_part = angle_table(
        jnp.arange(2 * pieces, dtype=jnp.int32), jnp.arange(pieces, dtype=jnp.int32), 2 * pieces
    )
    real_part = jnp.einsum("kd,ncdr->nckr", cosine, stacked, precision=highest)
    imag_part = -jnp.einsum("kd,ncdr->nckr", sine_part, stacked, precision=highest)
    return (real_part, imag_part)


def twist(real_part, imag_part, freq_ids, time_ids, length, turning):
    cosine, sine_part = angle_table(freq_ids, time_ids, length)
    return (
        real_part * cosine - turning * imag_part * sine_part,
        imag_part * cosine + turning * real_part * sine_part,
    )


def along_block(real_part, imag_part, turning):
    length = real_part.shape[-1]
    cosine, sine_part = angle_table(
        jnp.arange(length, dtype=jnp.int32), jnp.arange(length, dtype=jnp.int32), length
    )
    out_real = jnp.einsum(
        "nckb,bj->nckj", real_part, cosine, precision=highest
    ) - turning * jnp.einsum("nckb,bj->nckj", imag_part, sine_part, precision=highest)
    out_imag = jnp.einsum(
        "nckb,bj->nckj", imag_part, cosine, precision=highest
    ) + turning * jnp.einsum("nckb,bj->nckj", real_part, sine_part, precision=highest)
    return (out_real, out_imag)


def gather_rows(real_part, imag_part, length):
    doubled = real_part.shape[2]
    cosine, sine_part = angle_table(
        jnp.arange(doubled // 2, dtype=jnp.int32), jnp.arange(doubled, dtype=jnp.int32), doubled
    )
    signal = jnp.einsum("dk,nckr->ncdr", cosine, real_part, precision=highest) - jnp.einsum(
        "dk,nckr->ncdr", sine_part, imag_part, precision=highest
    )
    return signal / length


def student(signal, gate_part, taps, target, skip_part, forward, inverse, seq_total):
    spec_real, spec_imag = forward(jnp.stack([signal, taps]))
    input_re, taps_re = (spec_real[0], spec_real[1])
    input_im, taps_im = (spec_imag[0], spec_imag[1])
    conv_re = input_re * taps_re - input_im * taps_im
    conv_im = input_re * taps_im + input_im * taps_re
    convolved = inverse(conv_re[None], conv_im[None])[0]
    output = gate_part * (convolved + skip_part[:, None] * signal)
    backed = gate_part * (output - target)
    back_real, back_imag = forward(backed[None])
    back_re, back_im = (back_real[0], back_imag[0])
    left_re = taps_re * back_re + taps_im * back_im
    left_im = taps_re * back_im - taps_im * back_re
    right_re = input_re * back_re + input_im * back_im
    right_im = input_re * back_im - input_im * back_re
    corrected = inverse(jnp.stack([left_re, right_re]), jnp.stack([left_im, right_im]))
    grad_input = skip_part[:, None] * backed + corrected[0]
    filter_step = corrected[1] * seq_total ** (-0.5)
    return (grad_input, filter_step)


def body(
    query_heads,
    key_heads,
    value_heads,
    distill_proj,
    conv_input,
    gate_input,
    filter_taps,
    skip_gain,
):
    shard_len = query_heads.shape[0]
    kv_local = key_heads.shape[1]
    per_group = query_heads.shape[1] // kv_local
    head_dim = query_heads.shape[2]
    devices = lax.axis_size("seq")
    seq_rank = lax.axis_index("seq")
    shards = min((WINDOW + shard_len - 1) // shard_len, devices - 1)
    per_step = max(1, 512 // shard_len)
    total_shards = -(-(shards + 1) // per_step) * per_step
    own_block = jnp.stack([key_heads, value_heads])
    buffer = jnp.concatenate(
        [jnp.zeros((total_shards - 1,) + own_block.shape, jnp.bfloat16), own_block[None]], axis=0
    )

    def fetch(step_id, carried):
        current, stored = carried
        current = shifted(current, "seq", 1)
        stored = lax.dynamic_update_index_in_dim(stored, current, total_shards - 1 - step_id, 0)
        return (current, stored)

    buffer = lax.fori_loop(1, shards + 1, fetch, (own_block, buffer))[1]
    key_span = per_step * shard_len
    blocks = total_shards // per_step
    keys_all = buffer[:, 0].reshape(blocks, key_span, kv_local, head_dim)
    values_all = buffer[:, 1].reshape(blocks, key_span, kv_local, head_dim)
    first_key = (seq_rank + 1 - total_shards) * shard_len
    query_pos = seq_rank * shard_len + jnp.arange(shard_len, dtype=jnp.int32)
    queries = query_heads.reshape(shard_len, kv_local, per_group, head_dim)
    score_scale = head_dim ** (-0.5)
    block_ids = jnp.arange(blocks, dtype=jnp.int32)

    def online_step(carried, element):
        row_max, row_sum, weighted = carried
        block_id, key_block, value_block = element
        scores = (
            jnp.einsum("qgae,kge->gaqk", queries, key_block, preferred_element_type=jnp.float32)
            * score_scale
        )
        key_pos = first_key + block_id * key_span + jnp.arange(key_span, dtype=jnp.int32)
        in_window = (
            (key_pos[None, :] <= query_pos[:, None])
            & (key_pos[None, :] > query_pos[:, None] - WINDOW)
            & (key_pos[None, :] >= 0)
        )
        new_max = jnp.maximum(row_max, jnp.max(jnp.where(in_window, scores, -jnp.inf), axis=-1))
        safe_max = jnp.where(new_max == -jnp.inf, 0.0, new_max)
        rescale = jnp.exp(row_max - safe_max)
        weight = jnp.where(in_window, jnp.exp(scores - safe_max[..., None]), 0.0)
        row_sum = row_sum * rescale + jnp.sum(weight, axis=-1)
        weighted = weighted * jnp.transpose(rescale, (2, 0, 1))[..., None] + jnp.einsum(
            "gaqk,kge->qgae",
            weight.astype(jnp.bfloat16),
            value_block,
            preferred_element_type=jnp.float32,
        )
        return ((new_max, row_sum, weighted), None)

    start_state = (
        jnp.full((kv_local, per_group, shard_len), -jnp.inf, jnp.float32),
        jnp.zeros((kv_local, per_group, shard_len), jnp.float32),
        jnp.zeros((shard_len, kv_local, per_group, head_dim), jnp.float32),
    )
    final_state = lax.scan(online_step, start_state, (block_ids, keys_all, values_all))[0]
    row_sum, weighted = (final_state[1], final_state[2])
    attended = (
        (weighted / jnp.transpose(row_sum, (2, 0, 1))[..., None])
        .reshape(shard_len, kv_local * per_group, head_dim)
        .astype(jnp.bfloat16)
    )
    target = lax.psum_scatter(
        jnp.einsum("the,hec->ct", attended, distill_proj, preferred_element_type=jnp.float32),
        ("role", "head"),
        scatter_dimension=0,
        tiled=True,
    )
    signal = conv_input.astype(jnp.float32)
    gate_part = gate_input.astype(jnp.float32)
    full_len = 2 * devices * shard_len
    seq_total = devices * shard_len
    freq_all = jnp.arange(2 * devices, dtype=jnp.int32)
    time_all = jnp.arange(shard_len, dtype=jnp.int32)
    part_len = shard_len // devices
    freq_mine = 2 * seq_rank + jnp.arange(2, dtype=jnp.int32)
    time_mine = seq_rank * part_len + jnp.arange(part_len, dtype=jnp.int32)

    def to_rows(stacked):
        return lax.all_to_all(stacked, "seq", split_axis=3, concat_axis=2, tiled=True)

    def to_cols(stacked):
        return lax.all_to_all(stacked, "seq", split_axis=2, concat_axis=3, tiled=True)

    def forward(stacked):
        pieces = stacked.shape[0]
        arrived = to_rows(stacked[:, :, None, :])
        real_part, imag_part = spread_rows(arrived)
        real_part, imag_part = twist(real_part, imag_part, freq_all, time_mine, full_len, -1.0)
        joined = to_cols(jnp.concatenate([real_part, imag_part], axis=0))
        return along_block(joined[:pieces], joined[pieces:], -1.0)

    def inverse(real_part, imag_part):
        pieces = real_part.shape[0]
        real_part, imag_part = along_block(real_part, imag_part, 1.0)
        real_part, imag_part = twist(real_part, imag_part, freq_mine, time_all, full_len, 1.0)
        arrived = to_rows(jnp.concatenate([real_part, imag_part], axis=0))
        rebuilt = gather_rows(arrived[:pieces], arrived[pieces:], full_len)
        return to_cols(rebuilt)[:, :, 0, :]

    grad_input, filter_step = student(
        signal, gate_part, filter_taps, target, skip_gain, forward, inverse, seq_total
    )
    return (grad_input, filter_step)


def solution(mesh):
    in_specs = (
        P("seq", ("role", "head"), None),
        P("seq", ("role", "head"), None),
        P("seq", ("role", "head"), None),
        P(("role", "head"), None, None),
        P(("role", "head"), "seq"),
        P(("role", "head"), "seq"),
        P(("role", "head"), "seq"),
        P(("role", "head")),
    )
    out_specs = (P(("role", "head"), "seq"), P(("role", "head"), "seq"))
    return jax.shard_map(body, mesh=mesh, in_specs=in_specs, out_specs=out_specs, check_vma=False)
```

profile of v0, /device:TPU:1, one launch (start us, length us, event | category | flops | bytes accessed | tf_op | source)
XLA Modules:
  0.0 527.7 jit_solution(3453285585860932308)
XLA Ops:
  9.8 11.6 %all-to-all-start = ((f32[2,128,1,128]{1,0,2,3:T(2,128)}), f32[2,128,1,128]{1,0,2,3:T(2,128)S(1)}, u32[]{:S(2)}, u32[]{:S(2)}) async-start(f32[2,128,1,128]{1,0,2,3:T(2,128)} %copy.120), calls=%async_computation | async-start | bytes 262144 | tf_op jit(solution)/shard_map/all_to_all | solution.py:206
  23.0 9.6 %all-to-all-done = f32[2,128,1,128]{1,0,2,3:T(2,128)S(1)} async-done(((f32[2,128,1,128]{1,0,2,3:T(2,128)}), f32[2,128,1,128]{1,0,2,3:T(2,128)S(1)}, u32[]{:S(2)}, u32[]{:S(2)}) %all-to-all-start) | async-done | bytes 131104 | tf_op jit(solution)/shard_map/all_to_all | solution.py:206
  42.1 227.0 %while.32 = (s32[]{:T(128)}, bf16[2,128,1,128]{3,1,0,2:T(8,128)(2,1)S(1)}, bf16[36,2,128,1,128]{4,2,1,3,0:T(8,128)(2,1)S(1)}, s32[]{:T(128)}, s32[]{:T(128)}, /*index=5*/s32[]{:T(128)}, s32[]{:T(128)}) while((s32[]{:T(128)}, bf16[2,128,1,128]{3,1,0,2:T(8,128)(2,1)S(1)}, bf16[36,2,128,1,128]{4,2,1,3,0:T(8,128)(2,1)S(1)}, s32[]{:T(128)}, ...), condition=%wide.region_1.2_spmd, body=%wide.region_0.1_spmd.sunk | while | flops 6 | bytes 524455 | solution.py:140
  99.1 6.4 %collective-permute-start = (bf16[2,128,1,128]{3,1,0,2:T(8,128)(2,1)S(1)}, bf16[2,128,1,128]{3,1,0,2:T(8,128)(2,1)S(1)}, u32[]{:S(2)}, u32[]{:S(2)}) collective-permute-start(bf16[2,128,1,128]{3,1,0,2:T(8,128)(2,1)S(1)} %get-tuple-element.440), channel_id=1, source_target_pairs={{0,4},{4,8},{8,12},{12,16},{16,20},{20,24},{24,28},{28,32},{32,36}... | collective-permute-start | bytes 196616 | tf_op jit(solution)/shard_map/while/body/eval_jaxpr/ppermute | solution.py:17
  106.8 6.4 %collective-permute-start = (bf16[2,128,1,128]{3,1,0,2:T(8,128)(2,1)S(1)}, bf16[2,128,1,128]{3,1,0,2:T(8,128)(2,1)S(1)}, u32[]{:S(2)}, u32[]{:S(2)}) collective-permute-start(bf16[2,128,1,128]{3,1,0,2:T(8,128)(2,1)S(1)} %get-tuple-element.440), channel_id=1, source_target_pairs={{0,4},{4,8},{8,12},{12,16},{16,20},{20,24},{24,28},{28,32},{32,36}... | collective-permute-start | bytes 196616 | tf_op jit(solution)/shard_map/while/body/eval_jaxpr/ppermute | solution.py:17
  114.6 6.4 %collective-permute-start = (bf16[2,128,1,128]{3,1,0,2:T(8,128)(2,1)S(1)}, bf16[2,128,1,128]{3,1,0,2:T(8,128)(2,1)S(1)}, u32[]{:S(2)}, u32[]{:S(2)}) collective-permute-start(bf16[2,128,1,128]{3,1,0,2:T(8,128)(2,1)S(1)} %get-tuple-element.440), channel_id=1, source_target_pairs={{0,4},{4,8},{8,12},{12,16},{16,20},{20,24},{24,28},{28,32},{32,36}... | collective-permute-start | bytes 196616 | tf_op jit(solution)/shard_map/while/body/eval_jaxpr/ppermute | solution.py:17
  122.3 6.4 %collective-permute-start = (bf16[2,128,1,128]{3,1,0,2:T(8,128)(2,1)S(1)}, bf16[2,128,1,128]{3,1,0,2:T(8,128)(2,1)S(1)}, u32[]{:S(2)}, u32[]{:S(2)}) collective-permute-start(bf16[2,128,1,128]{3,1,0,2:T(8,128)(2,1)S(1)} %get-tuple-element.440), channel_id=1, source_target_pairs={{0,4},{4,8},{8,12},{12,16},{16,20},{20,24},{24,28},{28,32},{32,36}... | collective-permute-start | bytes 196616 | tf_op jit(solution)/shard_map/while/body/eval_jaxpr/ppermute | solution.py:17
  130.0 6.4 %collective-permute-start = (bf16[2,128,1,128]{3,1,0,2:T(8,128)(2,1)S(1)}, bf16[2,128,1,128]{3,1,0,2:T(8,128)(2,1)S(1)}, u32[]{:S(2)}, u32[]{:S(2)}) collective-permute-start(bf16[2,128,1,128]{3,1,0,2:T(8,128)(2,1)S(1)} %get-tuple-element.440), channel_id=1, source_target_pairs={{0,4},{4,8},{8,12},{12,16},{16,20},{20,24},{24,28},{28,32},{32,36}... | collective-permute-start | bytes 196616 | tf_op jit(solution)/shard_map/while/body/eval_jaxpr/ppermute | solution.py:17
  137.7 6.4 %collective-permute-start = (bf16[2,128,1,128]{3,1,0,2:T(8,128)(2,1)S(1)}, bf16[2,128,1,128]{3,1,0,2:T(8,128)(2,1)S(1)}, u32[]{:S(2)}, u32[]{:S(2)}) collective-permute-start(bf16[2,128,1,128]{3,1,0,2:T(8,128)(2,1)S(1)} %get-tuple-element.440), channel_id=1, source_target_pairs={{0,4},{4,8},{8,12},{12,16},{16,20},{20,24},{24,28},{28,32},{32,36}... | collective-permute-start | bytes 196616 | tf_op jit(solution)/shard_map/while/body/eval_jaxpr/ppermute | solution.py:17
  145.5 6.4 %collective-permute-start = (bf16[2,128,1,128]{3,1,0,2:T(8,128)(2,1)S(1)}, bf16[2,128,1,128]{3,1,0,2:T(8,128)(2,1)S(1)}, u32[]{:S(2)}, u32[]{:S(2)}) collective-permute-start(bf16[2,128,1,128]{3,1,0,2:T(8,128)(2,1)S(1)} %get-tuple-element.440), channel_id=1, source_target_pairs={{0,4},{4,8},{8,12},{12,16},{16,20},{20,24},{24,28},{28,32},{32,36}... | collective-permute-start | bytes 196616 | tf_op jit(solution)/shard_map/while/body/eval_jaxpr/ppermute | solution.py:17
  153.2 6.4 %collective-permute-start = (bf16[2,128,1,128]{3,1,0,2:T(8,128)(2,1)S(1)}, bf16[2,128,1,128]{3,1,0,2:T(8,128)(2,1)S(1)}, u32[]{:S(2)}, u32[]{:S(2)}) collective-permute-start(bf16[2,128,1,128]{3,1,0,2:T(8,128)(2,1)S(1)} %get-tuple-element.440), channel_id=1, source_target_pairs={{0,4},{4,8},{8,12},{12,16},{16,20},{20,24},{24,28},{28,32},{32,36}... | collective-permute-start | bytes 196616 | tf_op jit(solution)/shard_map/while/body/eval_jaxpr/ppermute | solution.py:17
  160.9 6.4 %collective-permute-start = (bf16[2,128,1,128]{3,1,0,2:T(8,128)(2,1)S(1)}, bf16[2,128,1,128]{3,1,0,2:T(8,128)(2,1)S(1)}, u32[]{:S(2)}, u32[]{:S(2)}) collective-permute-start(bf16[2,128,1,128]{3,1,0,2:T(8,128)(2,1)S(1)} %get-tuple-element.440), channel_id=1, source_target_pairs={{0,4},{4,8},{8,12},{12,16},{16,20},{20,24},{24,28},{28,32},{32,36}... | collective-permute-start | bytes 196616 | tf_op jit(solution)/shard_map/while/body/eval_jaxpr/ppermute | solution.py:17
  168.6 6.4 %collective-permute-start = (bf16[2,128,1,128]{3,1,0,2:T(8,128)(2,1)S(1)}, bf16[2,128,1,128]{3,1,0,2:T(8,128)(2,1)S(1)}, u32[]{:S(2)}, u32[]{:S(2)}) collective-permute-start(bf16[2,128,1,128]{3,1,0,2:T(8,128)(2,1)S(1)} %get-tuple-element.440), channel_id=1, source_target_pairs={{0,4},{4,8},{8,12},{12,16},{16,20},{20,24},{24,28},{28,32},{32,36}... | collective-permute-start | bytes 196616 | tf_op jit(solution)/shard_map/while/body/eval_jaxpr/ppermute | solution.py:17
  176.4 6.4 %collective-permute-start = (bf16[2,128,1,128]{3,1,0,2:T(8,128)(2,1)S(1)}, bf16[2,128,1,128]{3,1,0,2:T(8,128)(2,1)S(1)}, u32[]{:S(2)}, u32[]{:S(2)}) collective-permute-start(bf16[2,128,1,128]{3,1,0,2:T(8,128)(2,1)S(1)} %get-tuple-element.440), channel_id=1, source_target_pairs={{0,4},{4,8},{8,12},{12,16},{16,20},{20,24},{24,28},{28,32},{32,36}... | collective-permute-start | bytes 196616 | tf_op jit(solution)/shard_map/while/body/eval_jaxpr/ppermute | solution.py:17
  184.1 6.4 %collective-permute-start = (bf16[2,128,1,128]{3,1,0,2:T(8,128)(2,1)S(1)}, bf16[2,128,1,128]{3,1,0,2:T(8,128)(2,1)S(1)}, u32[]{:S(2)}, u32[]{:S(2)}) collective-permute-start(bf16[2,128,1,128]{3,1,0,2:T(8,128)(2,1)S(1)} %get-tuple-element.440), channel_id=1, source_target_pairs={{0,4},{4,8},{8,12},{12,16},{16,20},{20,24},{24,28},{28,32},{32,36}... | collective-permute-start | bytes 196616 | tf_op jit(solution)/shard_map/while/body/eval_jaxpr/ppermute | solution.py:17
  191.8 6.4 %collective-permute-start = (bf16[2,128,1,128]{3,1,0,2:T(8,128)(2,1)S(1)}, bf16[2,128,1,128]{3,1,0,2:T(8,128)(2,1)S(1)}, u32[]{:S(2)}, u32[]{:S(2)}) collective-permute-start(bf16[2,128,1,128]{3,1,0,2:T(8,128)(2,1)S(1)} %get-tuple-element.440), channel_id=1, source_target_pairs={{0,4},{4,8},{8,12},{12,16},{16,20},{20,24},{24,28},{28,32},{32,36}... | collective-permute-start | bytes 196616 | tf_op jit(solution)/shard_map/while/body/eval_jaxpr/ppermute | solution.py:17
  280.3 73.3 %all-to-all-start.2 = ((f32[2,128,2,128]{1,2,0,3:T(2,128)}), f32[2,128,2,128]{1,2,0,3:T(2,128)S(1)}, u32[]{:S(2)}, u32[]{:S(2)}) async-start(f32[2,128,2,128]{1,2,0,3:T(2,128)} %copy.132), calls=%async_computation.2 | async-start | bytes 524288 | tf_op jit(solution)/shard_map/all_to_all | solution.py:206
  353.7 29.1 %while.33 = (s32[]{:T(128)}, f32[1,2,128]{2,1,0:T(2,128)S(1)}, f32[1,2,128]{2,1,0:T(2,128)S(1)}, f32[128,1,2,128]{0,3,2,1:T(8,128)S(1)}, s32[9]{0:T(128)S(1)}, /...) while((s32[]{:T(128)}, f32[1,2,128]{2,1,0:T(2,128)S(1)}, ...), condition=%wide.region_5.6_spmd.clone, body=%wide.region_2.5_spmd.clone.sunk | while | flops 68653824 | bytes 2450633 | solution.py:182
  385.7 10.3 %all-to-all-start.3 = ((f32[1,128,64,2]{1,3,0,2:T(2,128)}), f32[1,128,64,2]{1,3,0,2:T(2,128)S(1)}, u32[]{:S(2)}, u32[]{:S(2)}) async-start(f32[1,128,64,2]{1,3,0,2:T(2,128)} %copy.138), calls=%async_computation.3 | async-start | bytes 131072 | tf_op jit(solution)/shard_map/all_to_all | solution.py:209
  396.1 32.8 %reduce-scatter.2.cloned.1.call-done = f32[128,128]{0,1:T(8,128)} async-done(((f32[1024,128]{0,1:T(8,128)}), f32[128,128]{0,1:T(8,128)}) %reduce-scatter.2.cloned.1.call-update) | async-done | bytes 65552 | tf_op jit(solution)/shard_map/reduce_scatter | solution.py:189
  429.8 24.7 %all_to_all.99 = f32[1,128,1,128]{1,2,0,3:T(1,128)S(1)} all-to-all(f32[1,128,1,128]{1,2,0,3:T(1,128)S(1)} %bitcast.259), channel_id=1, replica_groups=mesh['role'=2,'seq'=64,'head'=4] {'seq'}, dimensions={3} | all-to-all | bytes 131072 | tf_op jit(solution)/shard_map/all_to_all | solution.py:206
  455.6 16.9 %all_to_all.100 = f32[2,128,128,2]{1,3,0,2:T(2,128)S(1)} all-to-all(f32[2,128,128,2]{1,3,0,2:T(2,128)S(1)} %copy.147), channel_id=1, replica_groups=mesh['role'=2,'seq'=64,'head'=4] {'seq'}, dimensions={2} | all-to-all | bytes 524288 | tf_op jit(solution)/shard_map/all_to_all | solution.py:209
  478.8 22.2 %all_to_all.101 = f32[4,128,2,128]{1,2,0,3:T(2,128)S(1)} all-to-all(f32[4,128,2,128]{1,2,0,3:T(2,128)S(1)} %copy.155), channel_id=1, replica_groups=mesh['role'=2,'seq'=64,'head'=4] {'seq'}, dimensions={3} | all-to-all | bytes 1048576 | tf_op jit(solution)/shard_map/all_to_all | solution.py:206
  502.7 16.6 %all_to_all.102 = f32[2,128,64,2]{1,3,0,2:T(2,128)S(1)} all-to-all(f32[2,128,64,2]{1,3,0,2:T(2,128)S(1)} %copy.161), channel_id=1, replica_groups=mesh['role'=2,'seq'=64,'head'=4] {'seq'}, dimensions={2} | all-to-all | bytes 262144 | tf_op jit(solution)/shard_map/all_to_all | solution.py:209
  (315 shorter events, 204.4 us)
Async XLA Ops:
  9.8 22.7 %all-to-all-start = ((f32[2,128,1,128]{1,0,2,3:T(2,128)}), f32[2,128,1,128]{1,0,2,3:T(2,128)S(1)}, u32[]{:S(2)}, u32[]{:S(2)}) async-start(f32[2,128,1,128]{1,0,2,3:T(2,128)} %copy.120), calls=%async_computation | async-start | bytes 262144 | tf_op jit(solution)/shard_map/all_to_all | solution.py:206
  36.9 235.0 %all-to-all-start.1 = ((f32[4,128,128,2]{1,3,0,2:T(2,128)}), f32[4,128,128,2]{1,3,0,2:T(2,128)}, u32[]{:S(2)}, u32[]{:S(2)}) async-start(f32[4,128,128,2]{1,3,0,2:T(2,128)} %copy.124), calls=%async_computation.1 | async-start | bytes 1048576 | tf_op jit(solution)/shard_map/all_to_all | solution.py:209
  99.1 7.7 %collective-permute-start = (bf16[2,128,1,128]{3,1,0,2:T(8,128)(2,1)S(1)}, bf16[2,128,1,128]{3,1,0,2:T(8,128)(2,1)S(1)}, u32[]{:S(2)}, u32[]{:S(2)}) collective-permute-start(bf16[2,128,1,128]{3,1,0,2:T(8,128)(2,1)S(1)} %get-tuple-element.440), channel_id=1, source_target_pairs={{0,4},{4,8},{8,12},{12,16},{16,20},{20,24},{24,28},{28,32},{32,36}... | collective-permute-start | bytes 196616 | tf_op jit(solution)/shard_map/while/body/eval_jaxpr/ppermute | solution.py:17
  106.8 7.7 %collective-permute-start = (bf16[2,128,1,128]{3,1,0,2:T(8,128)(2,1)S(1)}, bf16[2,128,1,128]{3,1,0,2:T(8,128)(2,1)S(1)}, u32[]{:S(2)}, u32[]{:S(2)}) collective-permute-start(bf16[2,128,1,128]{3,1,0,2:T(8,128)(2,1)S(1)} %get-tuple-element.440), channel_id=1, source_target_pairs={{0,4},{4,8},{8,12},{12,16},{16,20},{20,24},{24,28},{28,32},{32,36}... | collective-permute-start | bytes 196616 | tf_op jit(solution)/shard_map/while/body/eval_jaxpr/ppermute | solution.py:17
  114.6 7.7 %collective-permute-start = (bf16[2,128,1,128]{3,1,0,2:T(8,128)(2,1)S(1)}, bf16[2,128,1,128]{3,1,0,2:T(8,128)(2,1)S(1)}, u32[]{:S(2)}, u32[]{:S(2)}) collective-permute-start(bf16[2,128,1,128]{3,1,0,2:T(8,128)(2,1)S(1)} %get-tuple-element.440), channel_id=1, source_target_pairs={{0,4},{4,8},{8,12},{12,16},{16,20},{20,24},{24,28},{28,32},{32,36}... | collective-permute-start | bytes 196616 | tf_op jit(solution)/shard_map/while/body/eval_jaxpr/ppermute | solution.py:17
  122.3 7.7 %collective-permute-start = (bf16[2,128,1,128]{3,1,0,2:T(8,128)(2,1)S(1)}, bf16[2,128,1,128]{3,1,0,2:T(8,128)(2,1)S(1)}, u32[]{:S(2)}, u32[]{:S(2)}) collective-permute-start(bf16[2,128,1,128]{3,1,0,2:T(8,128)(2,1)S(1)} %get-tuple-element.440), channel_id=1, source_target_pairs={{0,4},{4,8},{8,12},{12,16},{16,20},{20,24},{24,28},{28,32},{32,36}... | collective-permute-start | bytes 196616 | tf_op jit(solution)/shard_map/while/body/eval_jaxpr/ppermute | solution.py:17
  130.0 7.7 %collective-permute-start = (bf16[2,128,1,128]{3,1,0,2:T(8,128)(2,1)S(1)}, bf16[2,128,1,128]{3,1,0,2:T(8,128)(2,1)S(1)}, u32[]{:S(2)}, u32[]{:S(2)}) collective-permute-start(bf16[2,128,1,128]{3,1,0,2:T(8,128)(2,1)S(1)} %get-tuple-element.440), channel_id=1, source_target_pairs={{0,4},{4,8},{8,12},{12,16},{16,20},{20,24},{24,28},{28,32},{32,36}... | collective-permute-start | bytes 196616 | tf_op jit(solution)/shard_map/while/body/eval_jaxpr/ppermute | solution.py:17
  145.5 7.7 %collective-permute-start = (bf16[2,128,1,128]{3,1,0,2:T(8,128)(2,1)S(1)}, bf16[2,128,1,128]{3,1,0,2:T(8,128)(2,1)S(1)}, u32[]{:S(2)}, u32[]{:S(2)}) collective-permute-start(bf16[2,128,1,128]{3,1,0,2:T(8,128)(2,1)S(1)} %get-tuple-element.440), channel_id=1, source_target_pairs={{0,4},{4,8},{8,12},{12,16},{16,20},{20,24},{24,28},{28,32},{32,36}... | collective-permute-start | bytes 196616 | tf_op jit(solution)/shard_map/while/body/eval_jaxpr/ppermute | solution.py:17
  153.2 7.7 %collective-permute-start = (bf16[2,128,1,128]{3,1,0,2:T(8,128)(2,1)S(1)}, bf16[2,128,1,128]{3,1,0,2:T(8,128)(2,1)S(1)}, u32[]{:S(2)}, u32[]{:S(2)}) collective-permute-start(bf16[2,128,1,128]{3,1,0,2:T(8,128)(2,1)S(1)} %get-tuple-element.440), channel_id=1, source_target_pairs={{0,4},{4,8},{8,12},{12,16},{16,20},{20,24},{24,28},{28,32},{32,36}... | collective-permute-start | bytes 196616 | tf_op jit(solution)/shard_map/while/body/eval_jaxpr/ppermute | solution.py:17
  160.9 7.7 %collective-permute-start = (bf16[2,128,1,128]{3,1,0,2:T(8,128)(2,1)S(1)}, bf16[2,128,1,128]{3,1,0,2:T(8,128)(2,1)S(1)}, u32[]{:S(2)}, u32[]{:S(2)}) collective-permute-start(bf16[2,128,1,128]{3,1,0,2:T(8,128)(2,1)S(1)} %get-tuple-element.440), channel_id=1, source_target_pairs={{0,4},{4,8},{8,12},{12,16},{16,20},{20,24},{24,28},{28,32},{32,36}... | collective-permute-start | bytes 196616 | tf_op jit(solution)/shard_map/while/body/eval_jaxpr/ppermute | solution.py:17
  168.6 7.7 %collective-permute-start = (bf16[2,128,1,128]{3,1,0,2:T(8,128)(2,1)S(1)}, bf16[2,128,1,128]{3,1,0,2:T(8,128)(2,1)S(1)}, u32[]{:S(2)}, u32[]{:S(2)}) collective-permute-start(bf16[2,128,1,128]{3,1,0,2:T(8,128)(2,1)S(1)} %get-tuple-element.440), channel_id=1, source_target_pairs={{0,4},{4,8},{8,12},{12,16},{16,20},{20,24},{24,28},{28,32},{32,36}... | collective-permute-start | bytes 196616 | tf_op jit(solution)/shard_map/while/body/eval_jaxpr/ppermute | solution.py:17
  176.4 7.7 %collective-permute-start = (bf16[2,128,1,128]{3,1,0,2:T(8,128)(2,1)S(1)}, bf16[2,128,1,128]{3,1,0,2:T(8,128)(2,1)S(1)}, u32[]{:S(2)}, u32[]{:S(2)}) collective-permute-start(bf16[2,128,1,128]{3,1,0,2:T(8,128)(2,1)S(1)} %get-tuple-element.440), channel_id=1, source_target_pairs={{0,4},{4,8},{8,12},{12,16},{16,20},{20,24},{24,28},{28,32},{32,36}... | collective-permute-start | bytes 196616 | tf_op jit(solution)/shard_map/while/body/eval_jaxpr/ppermute | solution.py:17
  191.8 7.7 %collective-permute-start = (bf16[2,128,1,128]{3,1,0,2:T(8,128)(2,1)S(1)}, bf16[2,128,1,128]{3,1,0,2:T(8,128)(2,1)S(1)}, u32[]{:S(2)}, u32[]{:S(2)}) collective-permute-start(bf16[2,128,1,128]{3,1,0,2:T(8,128)(2,1)S(1)} %get-tuple-element.440), channel_id=1, source_target_pairs={{0,4},{4,8},{8,12},{12,16},{16,20},{20,24},{24,28},{28,32},{32,36}... | collective-permute-start | bytes 196616 | tf_op jit(solution)/shard_map/while/body/eval_jaxpr/ppermute | solution.py:17
  199.5 7.7 %collective-permute-start = (bf16[2,128,1,128]{3,1,0,2:T(8,128)(2,1)S(1)}, bf16[2,128,1,128]{3,1,0,2:T(8,128)(2,1)S(1)}, u32[]{:S(2)}, u32[]{:S(2)}) collective-permute-start(bf16[2,128,1,128]{3,1,0,2:T(8,128)(2,1)S(1)} %get-tuple-element.440), channel_id=1, source_target_pairs={{0,4},{4,8},{8,12},{12,16},{16,20},{20,24},{24,28},{28,32},{32,36}... | collective-permute-start | bytes 196616 | tf_op jit(solution)/shard_map/while/body/eval_jaxpr/ppermute | solution.py:17
  207.3 7.7 %collective-permute-start = (bf16[2,128,1,128]{3,1,0,2:T(8,128)(2,1)S(1)}, bf16[2,128,1,128]{3,1,0,2:T(8,128)(2,1)S(1)}, u32[]{:S(2)}, u32[]{:S(2)}) collective-permute-start(bf16[2,128,1,128]{3,1,0,2:T(8,128)(2,1)S(1)} %get-tuple-element.440), channel_id=1, source_target_pairs={{0,4},{4,8},{8,12},{12,16},{16,20},{20,24},{24,28},{28,32},{32,36}... | collective-permute-start | bytes 196616 | tf_op jit(solution)/shard_map/while/body/eval_jaxpr/ppermute | solution.py:17
  215.0 7.7 %collective-permute-start = (bf16[2,128,1,128]{3,1,0,2:T(8,128)(2,1)S(1)}, bf16[2,128,1,128]{3,1,0,2:T(8,128)(2,1)S(1)}, u32[]{:S(2)}, u32[]{:S(2)}) collective-permute-start(bf16[2,128,1,128]{3,1,0,2:T(8,128)(2,1)S(1)} %get-tuple-element.440), channel_id=1, source_target_pairs={{0,4},{4,8},{8,12},{12,16},{16,20},{20,24},{24,28},{28,32},{32,36}... | collective-permute-start | bytes 196616 | tf_op jit(solution)/shard_map/while/body/eval_jaxpr/ppermute | solution.py:17
  222.7 7.7 %collective-permute-start = (bf16[2,128,1,128]{3,1,0,2:T(8,128)(2,1)S(1)}, bf16[2,128,1,128]{3,1,0,2:T(8,128)(2,1)S(1)}, u32[]{:S(2)}, u32[]{:S(2)}) collective-permute-start(bf16[2,128,1,128]{3,1,0,2:T(8,128)(2,1)S(1)} %get-tuple-element.440), channel_id=1, source_target_pairs={{0,4},{4,8},{8,12},{12,16},{16,20},{20,24},{24,28},{28,32},{32,36}... | collective-permute-start | bytes 196616 | tf_op jit(solution)/shard_map/while/body/eval_jaxpr/ppermute | solution.py:17
  238.2 7.7 %collective-permute-start = (bf16[2,128,1,128]{3,1,0,2:T(8,128)(2,1)S(1)}, bf16[2,128,1,128]{3,1,0,2:T(8,128)(2,1)S(1)}, u32[]{:S(2)}, u32[]{:S(2)}) collective-permute-start(bf16[2,128,1,128]{3,1,0,2:T(8,128)(2,1)S(1)} %get-tuple-element.440), channel_id=1, source_target_pairs={{0,4},{4,8},{8,12},{12,16},{16,20},{20,24},{24,28},{28,32},{32,36}... | collective-permute-start | bytes 196616 | tf_op jit(solution)/shard_map/while/body/eval_jaxpr/ppermute | solution.py:17
  245.9 7.7 %collective-permute-start = (bf16[2,128,1,128]{3,1,0,2:T(8,128)(2,1)S(1)}, bf16[2,128,1,128]{3,1,0,2:T(8,128)(2,1)S(1)}, u32[]{:S(2)}, u32[]{:S(2)}) collective-permute-start(bf16[2,128,1,128]{3,1,0,2:T(8,128)(2,1)S(1)} %get-tuple-element.440), channel_id=1, source_target_pairs={{0,4},{4,8},{8,12},{12,16},{16,20},{20,24},{24,28},{28,32},{32,36}... | collective-permute-start | bytes 196616 | tf_op jit(solution)/shard_map/while/body/eval_jaxpr/ppermute | solution.py:17
  253.6 7.7 %collective-permute-start = (bf16[2,128,1,128]{3,1,0,2:T(8,128)(2,1)S(1)}, bf16[2,128,1,128]{3,1,0,2:T(8,128)(2,1)S(1)}, u32[]{:S(2)}, u32[]{:S(2)}) collective-permute-start(bf16[2,128,1,128]{3,1,0,2:T(8,128)(2,1)S(1)} %get-tuple-element.440), channel_id=1, source_target_pairs={{0,4},{4,8},{8,12},{12,16},{16,20},{20,24},{24,28},{28,32},{32,36}... | collective-permute-start | bytes 196616 | tf_op jit(solution)/shard_map/while/body/eval_jaxpr/ppermute | solution.py:17
  261.3 7.7 %collective-permute-start = (bf16[2,128,1,128]{3,1,0,2:T(8,128)(2,1)S(1)}, bf16[2,128,1,128]{3,1,0,2:T(8,128)(2,1)S(1)}, u32[]{:S(2)}, u32[]{:S(2)}) collective-permute-start(bf16[2,128,1,128]{3,1,0,2:T(8,128)(2,1)S(1)} %get-tuple-element.440), channel_id=1, source_target_pairs={{0,4},{4,8},{8,12},{12,16},{16,20},{20,24},{24,28},{28,32},{32,36}... | collective-permute-start | bytes 196616 | tf_op jit(solution)/shard_map/while/body/eval_jaxpr/ppermute | solution.py:17
  280.3 103.6 %all-to-all-start.2 = ((f32[2,128,2,128]{1,2,0,3:T(2,128)}), f32[2,128,2,128]{1,2,0,3:T(2,128)S(1)}, u32[]{:S(2)}, u32[]{:S(2)}) async-start(f32[2,128,2,128]{1,2,0,3:T(2,128)} %copy.132), calls=%async_computation.2 | async-start | bytes 524288 | tf_op jit(solution)/shard_map/all_to_all | solution.py:206
  353.6 75.3 %reduce-scatter.2.cloned.1.call-start = ((), (), s32[]{:S(2)}) async-start(), calls=%async_computation.9 | async-start | bytes 589824 | tf_op jit(solution)/shard_map/reduce_scatter | solution.py:189
  385.7 43.2 %all-to-all-start.3 = ((f32[1,128,64,2]{1,3,0,2:T(2,128)}), f32[1,128,64,2]{1,3,0,2:T(2,128)S(1)}, u32[]{:S(2)}, u32[]{:S(2)}) async-start(f32[1,128,64,2]{1,3,0,2:T(2,128)} %copy.138), calls=%async_computation.3 | async-start | bytes 131072 | tf_op jit(solution)/shard_map/all_to_all | solution.py:209
  (18 other events, 592.5 us)
Sparse Core Ops, SparseCore 0:
  384.1 44.7 reduce-scatter.1
where the time goes:
time: 530 us; the launch traced here: 528 us
  starting transfers between devices  283 us (53%)
  waiting for transfers between devices  85.3 us (16%)
  blocking collectives  80.4 us (15%)
  matrix products  29.4 us (6%)
  local copies, waits for them, and re-layouts  20.8 us (4%)
  between operations  14.6 us (3%)
  loops' own time  7.8 us (1%)
  other arithmetic  6.36 us (1%)
    ppermute x32, starting transfers between devices, shifted(): lax.ppermute(value, axis, [(source, source + steps) for source in range(l...  183 us
    all_to_all x2, starting transfers between devices, to_rows(): lax.all_to_all(stacked, 'seq', split_axis=3, concat_axis=2, tiled=True)  84.9 us
    all_to_all x2, blocking collectives, to_rows(): lax.all_to_all(stacked, 'seq', split_axis=3, concat_axis=2, tiled=True)  46.9 us
    ppermute x32, waiting for transfers between devices, shifted(): lax.ppermute(value, axis, [(source, source + steps) for source in range(l...  42.9 us
    all_to_all x2, blocking collectives, to_cols(): lax.all_to_all(stacked, 'seq', split_axis=2, concat_axis=3, tiled=True)  33.5 us
    reduce_scatter x1, waiting for transfers between devices, body(): lax.psum_scatter(jnp.einsum('the,hec->ct', attended, distill_proj, prefer...  32.8 us
    all_to_all x2, starting transfers between devices, to_cols(): lax.all_to_all(stacked, 'seq', split_axis=2, concat_axis=3, tiled=True)  15.5 us
  transfers between devices with their start and end apart: 37, of which 34 were waited for; matrix products, arithmetic and copies ran while one was open for 6% of the time, Pallas kernels for 0%

commit v1 on v0

v1 whole, which is shorter than its diff:
```python
import math

import jax
import jax.numpy as jnp
import numpy as np
from jax import lax
from jax.experimental import pallas as pl
from jax.experimental.pallas import tpu as pltpu
from jax.sharding import PartitionSpec as P

WINDOW = 4096
SHARD = 128
ROW = 8
BACK = WINDOW // (ROW * SHARD)
SHARDS = 64
HALF = 72
NEG = -1e30
highest = lax.Precision.HIGHEST


def transform_tables():
    length = 2 * SHARDS * SHARD
    k1 = np.arange(HALF)[:, None]
    live = (k1 <= SHARDS).astype(np.float64)
    a = np.arange(SHARDS)[None, :]
    angle = 2.0 * np.pi * ((k1 * a) % 128) / 128
    first = np.concatenate([live * np.cos(angle), -live * np.sin(angle)], 0)
    weight = live * np.where((k1 == 0) | (k1 == SHARDS), 1.0, 2.0) / length
    last = np.concatenate([weight * np.cos(angle), -weight * np.sin(angle)], 0).T
    b = np.arange(128)[None, :]
    turn = 2.0 * np.pi * (k1 * b) / length
    b2 = np.arange(128)[:, None]
    grid = 2.0 * np.pi * ((b2 * b) % 128) / 128
    cosine, sine = np.cos(grid), np.sin(grid)
    forward = np.block([[cosine, -sine], [sine, cosine]])
    backward = np.block([[cosine, sine], [-sine, cosine]])
    return [np.asarray(t, np.float32) for t in (first, last, np.cos(turn), np.sin(turn), forward, backward)]


def mul(a, b):
    return jnp.dot(a, b, precision=highest, preferred_element_type=jnp.float32)


def to_spectra(signals, first, turn_cos, turn_sin, forward):
    stacked = mul(first, jnp.concatenate(signals, 1))
    rows = []
    for n in range(len(signals)):
        re = stacked[:HALF, n * 128 : (n + 1) * 128]
        im = stacked[HALF:, n * 128 : (n + 1) * 128]
        rows.append(jnp.concatenate([re * turn_cos + im * turn_sin, im * turn_cos - re * turn_sin], 1))
    spectra = mul(jnp.concatenate(rows, 0), forward)
    return [spectra[n * HALF : (n + 1) * HALF] for n in range(len(signals))]


def to_signals(spectra, last, turn_cos, turn_sin, backward):
    rows = mul(jnp.concatenate(spectra, 0), backward)
    columns = []
    for n in range(len(spectra)):
        re = rows[n * HALF : (n + 1) * HALF, :128]
        im = rows[n * HALF : (n + 1) * HALF, 128:]
        columns.append(jnp.concatenate([re * turn_cos - im * turn_sin, re * turn_sin + im * turn_cos], 0))
    return mul(last, jnp.concatenate(columns, 1))


def product(a, b):
    ar, ai, br, bi = a[:, :128], a[:, 128:], b[:, :128], b[:, 128:]
    return jnp.concatenate([ar * br - ai * bi, ar * bi + ai * br], 1)


def product_conj(a, b):
    ar, ai, br, bi = a[:, :128], a[:, 128:], b[:, :128], b[:, 128:]
    return jnp.concatenate([ar * br + ai * bi, ar * bi - ai * br], 1)


def before_kernel(skip_ref, in_ref, first, last, tc, ts, fwd, bwd, spec_ref, pre_ref, gate_ref):
    x = [in_ref[:, c, :] for c in (0, 1)]
    gate = [in_ref[:, c, :] for c in (2, 3)]
    taps = [in_ref[:, c, :] for c in (4, 5)]
    spectra = to_spectra(x + taps, first[...], tc[...], ts[...], fwd[...])
    for n in range(4):
        spec_ref[n] = spectra[n]
    conv = to_signals(
        [product(spectra[c], spectra[2 + c]) for c in (0, 1)], last[...], tc[...], ts[...], bwd[...]
    )
    for c in (0, 1):
        pre_ref[c] = gate[c] * (conv[:, c * 128 : (c + 1) * 128] + skip_ref[c] * x[c])
        gate_ref[c] = gate[c]


def after_kernel(skip_ref, target_ref, spec_ref, pre_ref, gate_ref, first, last, tc, ts, fwd, bwd, out_ref):
    back = [gate_ref[c] * (pre_ref[c] - target_ref[:, c, :]) for c in (0, 1)]
    spectra = to_spectra(back, first[...], tc[...], ts[...], fwd[...])
    mixed = [product_conj(spec_ref[2 + c], spectra[c]) for c in (0, 1)]
    mixed += [product_conj(spec_ref[c], spectra[c]) for c in (0, 1)]
    signals = to_signals(mixed, last[...], tc[...], ts[...], bwd[...])
    scale = (SHARDS * SHARD) ** -0.5
    for c in (0, 1):
        out_ref[:, c, :] = skip_ref[c] * back[c] + signals[:, c * 128 : (c + 1) * 128]
        out_ref[:, 2 + c, :] = scale * signals[:, (2 + c) * 128 : (3 + c) * 128]


def attend_kernel(place_ref, q_ref, kv0, kv1, kv2, kv3, kv4, out_ref):
    row, mine = place_ref[0], place_ref[1]
    theirs = pl.program_id(0)
    scale = 128 ** -0.5
    q = q_ref[0].reshape(2 * SHARD, 128)

    def scores(ref):
        return lax.dot_general(ref[0], q, (((1,), (1,)), ((), ())), preferred_element_type=jnp.float32)

    def gathered(ref, weight):
        return lax.dot_general(ref[1], weight, (((0,), (0,)), ((), ())), preferred_element_type=jnp.float32)

    key = lax.broadcasted_iota(jnp.int32, (SHARD, 2 * SHARD), 0)
    query = lax.broadcasted_iota(jnp.int32, (SHARD, 2 * SHARD), 1) % SHARD
    newest = (theirs - mine) * SHARD + query - key >= 0
    oldest = jnp.where(row >= BACK, scores(kv0), NEG)
    blocks = [jnp.where(newest, scores(kv4), oldest)]
    for r, ref in ((1, kv1), (2, kv2), (3, kv3)):
        blocks.append(jnp.where(row >= BACK - r, scores(ref), NEG))
    top = jnp.maximum(jnp.maximum(blocks[0], blocks[1]), jnp.maximum(blocks[2], blocks[3]))
    top = jnp.maximum(jnp.max(top, axis=0, keepdims=True), 0.5 * NEG)
    weights = [jnp.exp((b - top) * scale) for b in blocks]
    total = jnp.sum(weights[0] + weights[1] + weights[2] + weights[3], axis=0, keepdims=True)
    zero = jnp.zeros_like(weights[0])
    out = gathered(kv4, jnp.where(newest, weights[0], zero).astype(jnp.bfloat16))
    out += gathered(kv0, jnp.where(newest, zero, weights[0]).astype(jnp.bfloat16))
    for ref, w in zip((kv1, kv2, kv3), weights[1:]):
        out += gathered(ref, w.astype(jnp.bfloat16))
    out = out / jnp.maximum(total, 1e-30)
    log_sum = jnp.where(total > 0.0, top * scale + jnp.log(jnp.maximum(total, 1e-30)), NEG)
    high = log_sum.astype(jnp.bfloat16).astype(jnp.float32)
    rest = log_sum - high
    middle = rest.astype(jnp.bfloat16).astype(jnp.float32)
    low = rest - middle
    stats = []
    for h in (0, 1):
        out_ref[0, h * 128 : (h + 1) * 128, :] = out[:, h * 128 : (h + 1) * 128].astype(jnp.bfloat16)
        stats += [part[:, h * 128 : (h + 1) * 128] for part in (high, middle, low)]
    stats.append(jnp.zeros((10, 128), jnp.float32))
    out_ref[0, 256:272, :] = jnp.concatenate(stats, 0).astype(jnp.bfloat16)


def merge_kernel(parts_ref, proj_ref, out_ref):
    heads = []
    for h in (0, 1):
        sums = []
        for p in range(ROW):
            stats = parts_ref[p, 256:272, :].astype(jnp.float32)
            sums.append(stats[3 * h : 3 * h + 1] + stats[3 * h + 1 : 3 * h + 2] + stats[3 * h + 2 : 3 * h + 3])
        top = sums[0]
        for p in range(1, ROW):
            top = jnp.maximum(top, sums[p])
        shares = [jnp.exp(s - top) for s in sums]
        total = shares[0]
        merged = shares[0] * parts_ref[0, h * 128 : (h + 1) * 128, :].astype(jnp.float32)
        for p in range(1, ROW):
            total += shares[p]
            merged += shares[p] * parts_ref[p, h * 128 : (h + 1) * 128, :].astype(jnp.float32)
        heads.append((merged / total).astype(jnp.bfloat16))
    target = jnp.dot(proj_ref[...], jnp.concatenate(heads, 0), preferred_element_type=jnp.float32)
    out_ref[...] = target.reshape(8, 128, 128).astype(jnp.bfloat16)


VMEM = pl.BlockSpec(memory_space=pltpu.VMEM)
SMEM = pl.BlockSpec(memory_space=pltpu.SMEM)


def call_before(skip, packed, tables):
    return pl.pallas_call(
        before_kernel,
        out_shape=(
            jax.ShapeDtypeStruct((4, HALF, 256), jnp.float32),
            jax.ShapeDtypeStruct((2, SHARDS, 128), jnp.float32),
            jax.ShapeDtypeStruct((2, SHARDS, 128), jnp.float32),
        ),
        in_specs=[SMEM] + [VMEM] * 7,
        out_specs=(VMEM,) * 3,
    )(skip, packed, *tables)


def call_after(skip, target, spectra, pre, gate, tables):
    return pl.pallas_call(
        after_kernel,
        out_shape=jax.ShapeDtypeStruct((SHARDS, 4, 128), jnp.float32),
        in_specs=[SMEM] + [VMEM] * 10,
        out_specs=VMEM,
    )(skip, target, spectra, pre, gate, *tables)


def call_attend(place, queries, blocks):
    fixed = pl.BlockSpec((2, SHARD, 128), lambda p: (0, 0, 0))
    return pl.pallas_call(
        attend_kernel,
        out_shape=jax.ShapeDtypeStruct((ROW, 272, 128), jnp.bfloat16),
        grid=(ROW,),
        in_specs=[SMEM, pl.BlockSpec((1, 2, SHARD, 128), lambda p: (p, 0, 0, 0))] + [fixed] * 5,
        out_specs=pl.BlockSpec((1, 272, 128), lambda p: (p, 0, 0)),
    )(place, queries, *blocks)


def call_merge(parts, proj):
    return pl.pallas_call(
        merge_kernel,
        out_shape=jax.ShapeDtypeStruct((8, 128, 128), jnp.bfloat16),
        in_specs=[VMEM] * 2,
        out_specs=VMEM,
    )(parts, proj)


def body(
    query_heads,
    key_heads,
    value_heads,
    distill_proj,
    conv_input,
    gate_input,
    filter_taps,
    skip_gain,
):
    tables = [jnp.asarray(t) for t in transform_tables()]
    rank = lax.axis_index("seq")
    rows = [[y * ROW + p for p in range(ROW)] for y in range(SHARDS // ROW)]
    place = jnp.stack([rank // ROW, rank % ROW]).astype(jnp.int32)

    own = jnp.stack([key_heads[:, 0], value_heads[:, 0]])
    blocks = [
        lax.ppermute(own, "seq", [(i, i + ROW * k) for i in range(SHARDS - ROW * k)])
        for k in range(BACK, 0, -1)
    ] + [own]
    queries = lax.all_gather(jnp.transpose(query_heads, (1, 0, 2)), "seq", axis_index_groups=rows)

    packed = jnp.concatenate(
        [
            part.astype(jnp.float32).reshape(SHARDS, 2, 128)
            for part in (conv_input, gate_input, filter_taps)
        ],
        axis=1,
    )
    packed = lax.all_to_all(packed, "seq", 0, 0)
    skip = lax.dynamic_slice(skip_gain, (2 * rank,), (2,))
    spectra, pre, gate = call_before(skip, packed, tables)

    proj = distill_proj.reshape(256, 1024).T
    parts = call_attend(place, queries, blocks)
    parts = lax.all_to_all(parts, "seq", 0, 0, axis_index_groups=rows)
    target = call_merge(parts, proj)
    target = lax.all_to_all(target, ("role", "head"), 0, 0)
    target = jnp.sum(target.astype(jnp.float32), axis=0).reshape(SHARDS, 2, 128)
    target = lax.all_to_all(target, "seq", 0, 0)
    out = call_after(skip, target, spectra, pre, gate, tables)
    out = lax.all_to_all(out, "seq", 0, 0)
    return out[:, :2].reshape(128, 128), out[:, 2:].reshape(128, 128)


def solution(mesh):
    in_specs = (
        P("seq", ("role", "head"), None),
        P("seq", ("role", "head"), None),
        P("seq", ("role", "head"), None),
        P(("role", "head"), None, None),
        P(("role", "head"), "seq"),
        P(("role", "head"), "seq"),
        P(("role", "head"), "seq"),
        P(("role", "head")),
    )
    out_specs = (P(("role", "head"), "seq"), P(("role", "head"), "seq"))
    return jax.shard_map(body, mesh=mesh, in_specs=in_specs, out_specs=out_specs, check_vma=False)
```

time: 530 us -> 134 us (0.25)
  starting transfers between devices: 283 us -> 40.7 us
  waiting for transfers between devices: 85.3 us -> 32.8 us
  blocking collectives: 80.4 us -> 32 us
  matrix products: 29.4 us -> 0 us
  Pallas kernels: 0 us -> 17.1 us
  local copies, waits for them, and re-layouts: 20.8 us -> 5.95 us
  between operations: 14.6 us -> 0.83 us
  loops' own time: 7.8 us -> 0 us
    ppermute x32 -> x4, starting transfers between devices: 183 us -> 14.9 us  [body(): lax.ppermute(own, 'seq', [(i, i + ROW * k) for i in range(SHARDS - ROW *...]
    all_to_all x4, starting transfers between devices: 100 us -> 25.7 us  [the longest x1 10.2 us: body(): target = lax.all_to_all(target, ('role', 'head'), 0, 0)]
    all_to_all x4 -> x1, blocking collectives: 80.4 us -> 16.1 us  [body(): out = lax.all_to_all(out, 'seq', 0, 0)]
    ppermute x32 -> x4, waiting for transfers between devices: 42.9 us -> 0.01 us  [body(): lax.ppermute(own, 'seq', [(i, i + ROW * k) for i in range(SHARDS - ROW *...]
    reduce_scatter x1 -> x0, waiting for transfers between devices: 32.8 us -> none  [body(): lax.psum_scatter(jnp.einsum('the,hec->ct', attended, distill_proj, prefer...]
    dot_general x43 -> x0, matrix products: 29.4 us -> none  [the longest x9 10.5 us: online_step(): jnp.einsum('qgae,kge->gaqk', queries, key_block, preferred_element_type=j...]
    all_to_all x4, waiting for transfers between devices: 9.58 us -> 32.8 us  [the longest x1 12.6 us: body(): packed = lax.all_to_all(packed, 'seq', 0, 0)]
    pallas_call x0 -> x4, Pallas kernels: none -> 17.1 us  [the longest x1 7.93 us: call_attend(): pl.pallas_call(attend_kernel, out_shape=jax.ShapeDtypeStruct((ROW, 272, 1...]
  transfers between devices with their start and end apart: 37 -> 8, of which waited for: 34 -> 4; matrix products, arithmetic and copies ran while one was open for 6% -> 3% of each run, Pallas kernels for 0% -> 3%
where the time goes in v1:
time: 134 us; the launch traced here: 132 us
  starting transfers between devices  40.7 us (30%)
  waiting for transfers between devices  32.8 us (24%)
  blocking collectives  32 us (24%)
  Pallas kernels  17.1 us (13%)
  local copies, waits for them, and re-layouts  5.95 us (4%)
  other arithmetic  2.93 us (2%)
    all_to_all x1, blocking collectives, body(): out = lax.all_to_all(out, 'seq', 0, 0)  16.1 us
    all_gather x1, blocking collectives, body(): lax.all_gather(jnp.transpose(query_heads, (1, 0, 2)), 'seq', axis_index_g...  15.9 us
    ppermute x4, starting transfers between devices, body(): lax.ppermute(own, 'seq', [(i, i + ROW * k) for i in range(SHARDS - ROW *...  14.9 us
    all_to_all x1, waiting for transfers between devices, body(): packed = lax.all_to_all(packed, 'seq', 0, 0)  12.6 us
    all_to_all x1, starting transfers between devices, body(): target = lax.all_to_all(target, ('role', 'head'), 0, 0)  10.2 us
    all_to_all x1, waiting for transfers between devices, body(): parts = lax.all_to_all(parts, 'seq', 0, 0, axis_index_groups=rows)  8.81 us
    pallas_call x1, Pallas kernels, call_attend(): pl.pallas_call(attend_kernel, out_shape=jax.ShapeDtypeStruct((ROW, 272, 1...  7.93 us
    all_to_all x1, starting transfers between devices, body(): packed = lax.all_to_all(packed, 'seq', 0, 0)  6.85 us
  transfers between devices with their start and end apart: 8, of which 4 were waited for; matrix products, arithmetic and copies ran while one was open for 3% of the time, Pallas kernels for 3%

profile of v1, /device:TPU:1, one launch (start us, length us, event | category | flops | bytes accessed | tf_op | source)
XLA Modules:
  0.0 132.3 jit_solution(3981158078315640129)
XLA Ops:
  0.6 0.8 pad_maximum_fusion.1.kv4
  1.5 8.3 %collective-permute-start = (bf16[2,128,128]{2,1,0:T(8,128)(2,1)S(1)}, bf16[2,128,128]{2,1,0:T(8,128)(2,1)S(1)}, u32[]{:S(2)}, u32[]{:S(2)}) collective-permute-start(bf16[2,128,128]{2,1,0:T(8,128)(2,1)S(1)} %pad_maximum_fusion.1.kv4), channel_id=1, source_target_pairs={{0,128},{4,132},{8,136},{12,140},{16,144},{20,148},{24,152},{28,15... | collective-permute-start | bytes 196616 | tf_op jit(solution)/shard_map/ppermute | solution.py:228
  9.7 2.5 %collective-permute-start.1 = (bf16[2,128,128]{2,1,0:T(8,128)(2,1)S(1)}, bf16[2,128,128]{2,1,0:T(8,128)(2,1)S(1)}, u32[]{:S(2)}, u32[]{:S(2)}) collective-permute-start(bf16[2,128,128]{2,1,0:T(8,128)(2,1)S(1)} %pad_maximum_fusion.1.kv4), channel_id=1, source_target_pairs={{0,96},{4,100},{8,104},{12,108},{16,112},{20,116},{24,120},{28,124... | collective-permute-start | bytes 196616 | tf_op jit(solution)/shard_map/ppermute | solution.py:228
  12.3 1.3 collective-permute-start.2
  13.6 2.8 %collective-permute-start.3 = (bf16[2,128,128]{2,1,0:T(8,128)(2,1)S(1)}, bf16[2,128,128]{2,1,0:T(8,128)(2,1)S(1)}, u32[]{:S(2)}, u32[]{:S(2)}) collective-permute-start(bf16[2,128,128]{2,1,0:T(8,128)(2,1)S(1)} %pad_maximum_fusion.1.kv4), channel_id=1, source_target_pairs={{0,32},{4,36},{8,40},{12,44},{16,48},{20,52},{24,56},{28,60},{32,6... | collective-permute-start | bytes 196616 | tf_op jit(solution)/shard_map/ppermute | solution.py:228
  16.5 15.9 %all-gather = bf16[16,128,128]{2,1,0:T(8,128)(2,1)} all-gather(bf16[2,128,128]{2,1,0:T(8,128)(2,1)S(1)} %bitcast.21), channel_id=2, replica_groups={{0,4,8,12,16,20,24,28},{32,36,40,44,48,52,56,60},{64,68,72,76,80,84,88,..., dimensions={0}, use_global_device_ids=true | all-gather | bytes 589824 | tf_op jit(solution)/shard_map/all_gather | solution.py:231
  33.7 7.9 %shard_map.149 = bf16[8,272,128]{2,1,0:T(8,128)(2,1)} custom-call(s32[2]{0:T(128)} %pad_add_fusion.place_ref, bf16[8,2,128,128]{3,2,1,0:T(8,128)(2,1)} %bitcast.18, bf16[2,128,128]{2,1,0:T(8,128)(2,1)} %copy-done.6, bf16[2,128,128]{2,1,0:T(8,128)(2,1)} %copy-done.7, bf16[2,128,128]{2,1,0:T(8,128)(2,1)} %copy-done.8, bf16[2,128,128]{2,1,0:T(8,128)(2,1)} %copy-done.9, ...), custom_call_target="tpu_custom_call" | custom-call | tf_op jit(solution)/shard_map/pallas_call | solution.py:193
  41.6 4.0 %all-to-all-start = ((bf16[8,272,128]{2,1,0:T(8,128)(2,1)}), bf16[8,272,128]{2,1,0:T(8,128)(2,1)S(1)}, u32[]{:S(2)}, u32[]{:S(2)}) async-start(bf16[8,272,128]{2,1,0:T(8,128)(2,1)} %shard_map.149), calls=%async_computation | async-start | bytes 1114112 | tf_op jit(solution)/shard_map/all_to_all | solution.py:246
  45.6 1.0 copy.20
  46.6 8.8 %all-to-all-done.parts_ref = bf16[8,272,128]{2,1,0:T(8,128)(2,1)S(1)} async-done(((bf16[8,272,128]{2,1,0:T(8,128)(2,1)}), bf16[8,272,128]{2,1,0:T(8,128)(2,1)S(1)}, u32[]{:S(2)}, u32[]{:S(2)}) %all-to-all-start) | async-done | bytes 557088 | tf_op jit(solution)/shard_map/all_to_all | solution.py:246
  55.4 0.8 copy-done
  56.2 2.3 %shard_map.150 = bf16[8,128,128]{2,1,0:T(8,128)(2,1)} custom-call(bf16[8,272,128]{2,1,0:T(8,128)(2,1)} %copy-done, bf16[1024,256]{1,0:T(8,128)(2,1)} %bitcast.19), custom_call_target="tpu_custom_call" | custom-call | tf_op jit(solution)/shard_map/pallas_call | solution.py:203
  58.5 10.2 %all-to-all-start.1 = ((bf16[8,128,128]{2,1,0:T(8,128)(2,1)}), bf16[8,128,128]{2,1,0:T(8,128)(2,1)S(1)}, u32[]{:S(2)}, u32[]{:S(2)}) async-start(bf16[8,128,128]{2,1,0:T(8,128)(2,1)} %shard_map.150), calls=%async_computation.1 | async-start | bytes 524288 | tf_op jit(solution)/shard_map/all_to_all | solution.py:248
  68.8 0.7 copy-done.12
  69.6 0.8 pad_maximum_fusion
  70.4 6.1 %all-to-all-done.1 = bf16[8,128,128]{2,1,0:T(8,128)(2,1)S(1)} async-done(((bf16[8,128,128]{2,1,0:T(8,128)(2,1)}), bf16[8,128,128]{2,1,0:T(8,128)(2,1)S(1)}, u32[]{:S(2)}, u32[]{:S(2)}) %all-to-all-start.1) | async-done | bytes 262176 | tf_op jit(solution)/shard_map/all_to_all | solution.py:248
  76.5 6.9 %all-to-all-start.3 = ((f32[64,6,128]{2,1,0:T(8,128)}), f32[64,6,128]{2,1,0:T(8,128)S(1)}, u32[]{:S(2)}, u32[]{:S(2)}) async-start(f32[64,6,128]{2,1,0:T(8,128)} %pad_maximum_fusion), calls=%async_computation.3 | async-start | bytes 524288 | tf_op jit(solution)/shard_map/all_to_all | solution.py:240
  84.0 12.6 %all-to-all-done.3.in_ref = f32[64,6,128]{2,1,0:T(8,128)S(1)} async-done(((f32[64,6,128]{2,1,0:T(8,128)}), f32[64,6,128]{2,1,0:T(8,128)S(1)}, u32[]{:S(2)}, u32[]{:S(2)}) %all-to-all-start.3) | async-done | bytes 196640 | tf_op jit(solution)/shard_map/all_to_all | solution.py:240
  96.6 4.7 %all-to-all-start.2 = ((f32[64,2,128]{2,1,0:T(2,128)}), f32[64,2,128]{2,1,0:T(2,128)S(1)}, u32[]{:S(2)}, u32[]{:S(2)}) async-start(f32[64,2,128]{2,1,0:T(2,128)} %bitcast.8), calls=%async_computation.2 | async-start | bytes 131072 | tf_op jit(solution)/shard_map/all_to_all | solution.py:250
  102.7 3.4 %shard_map.151 = (f32[4,72,256]{2,1,0:T(8,128)}, f32[2,64,128]{2,1,0:T(8,128)}, f32[2,64,128]{2,1,0:T(8,128)}) custom-call(f32[2]{0:T(128)} %dynamic_slice.3.skip_ref, f32[64,6,128]{2,1,0:T(8,128)} %copy-done.1, f32[144,64]{1,0:T(8,128)} %constant.51.clone.first, f32[64,144]{1,0:T(8,128)} %constant.52.clone.last, f32[72,128]{1,0:T(8,128)} %constant.53.clone.tc, ...), custom_call_target="tpu_custom_call" | custom-call | tf_op jit(solution)/shard_map/pallas_call | solution.py:170
  106.1 5.3 %all-to-all-done.2.target_ref = f32[64,2,128]{2,1,0:T(2,128)S(1)} async-done(((f32[64,2,128]{2,1,0:T(2,128)}), f32[64,2,128]{2,1,0:T(2,128)S(1)}, u32[]{:S(2)}, u32[]{:S(2)}) %all-to-all-start.2) | async-done | bytes 65568 | tf_op jit(solution)/shard_map/all_to_all | solution.py:250
  112.1 3.5 %shard_map.152 = f32[64,4,128]{2,1,0:T(4,128)} custom-call(f32[2]{0:T(128)} %dynamic_slice.3.skip_ref, f32[64,2,128]{2,1,0:T(2,128)} %copy-done.4, f32[4,72,256]{2,1,0:T(8,128)} %get-tuple-element.5.spec_ref, f32[2,64,128]{2,1,0:T(8,128)} %get-tuple-element.6.pre_ref, f32[2,64,128]{2,1,0:T(8,128)} %get-tuple-element.7.gate_ref, ...), custom_call_target="tpu_custom_call" | custom-call | tf_op jit(solution)/shard_map/pallas_call | solution.py:183
  115.5 16.1 %all_to_all.25 = f32[64,4,128]{2,1,0:T(4,128)S(1)} all-to-all(f32[64,4,128]{2,1,0:T(4,128)} %shard_map.152), channel_id=1, replica_groups=mesh['role'=2,'seq'=64,'head'=4] {'seq'}, dimensions={0} | all-to-all | bytes 262144 | tf_op jit(solution)/shard_map/all_to_all | solution.py:252
  131.6 0.7 fusion
  (36 shorter events, 4.0 us)
Async XLA Ops:
  0.6 15.8 %copy-start.10 = (bf16[128,2,128]{2,1,0:T(2,128)(2,1)S(1)}, bf16[128,2,128]{2,1,0:T(2,128)(2,1)}, u32[]{:S(2)}) copy-start(bf16[128,2,128]{2,1,0:T(2,128)(2,1)} %param.14) | copy-start | bytes 196612
  1.5 15.0 %copy-start.3 = (bf16[2,128,128]{2,1,0:T(8,128)(2,1)}, bf16[2,128,128]{2,1,0:T(8,128)(2,1)S(1)}, u32[]{:S(2)}) copy-start(bf16[2,128,128]{2,1,0:T(8,128)(2,1)S(1)} %pad_maximum_fusion.1.kv4) | copy-start | bytes 196612
  1.5 31.5 %collective-permute-start = (bf16[2,128,128]{2,1,0:T(8,128)(2,1)S(1)}, bf16[2,128,128]{2,1,0:T(8,128)(2,1)S(1)}, u32[]{:S(2)}, u32[]{:S(2)}) collective-permute-start(bf16[2,128,128]{2,1,0:T(8,128)(2,1)S(1)} %pad_maximum_fusion.1.kv4), channel_id=1, source_target_pairs={{0,128},{4,132},{8,136},{12,140},{16,144},{20,148},{24,152},{28,15... | collective-permute-start | bytes 196616 | tf_op jit(solution)/shard_map/ppermute | solution.py:228
  9.7 23.2 %collective-permute-start.1 = (bf16[2,128,128]{2,1,0:T(8,128)(2,1)S(1)}, bf16[2,128,128]{2,1,0:T(8,128)(2,1)S(1)}, u32[]{:S(2)}, u32[]{:S(2)}) collective-permute-start(bf16[2,128,128]{2,1,0:T(8,128)(2,1)S(1)} %pad_maximum_fusion.1.kv4), channel_id=1, source_target_pairs={{0,96},{4,100},{8,104},{12,108},{16,112},{20,116},{24,120},{28,124... | collective-permute-start | bytes 196616 | tf_op jit(solution)/shard_map/ppermute | solution.py:228
  12.3 20.7 %collective-permute-start.2 = (bf16[2,128,128]{2,1,0:T(8,128)(2,1)S(1)}, bf16[2,128,128]{2,1,0:T(8,128)(2,1)S(1)}, u32[]{:S(2)}, u32[]{:S(2)}) collective-permute-start(bf16[2,128,128]{2,1,0:T(8,128)(2,1)S(1)} %pad_maximum_fusion.1.kv4), channel_id=1, source_target_pairs={{0,64},{4,68},{8,72},{12,76},{16,80},{20,84},{24,88},{28,92},{32,9... | collective-permute-start | bytes 196616 | tf_op jit(solution)/shard_map/ppermute | solution.py:228
  13.6 19.4 %collective-permute-start.3 = (bf16[2,128,128]{2,1,0:T(8,128)(2,1)S(1)}, bf16[2,128,128]{2,1,0:T(8,128)(2,1)S(1)}, u32[]{:S(2)}, u32[]{:S(2)}) collective-permute-start(bf16[2,128,128]{2,1,0:T(8,128)(2,1)S(1)} %pad_maximum_fusion.1.kv4), channel_id=1, source_target_pairs={{0,32},{4,36},{8,40},{12,44},{16,48},{20,52},{24,56},{28,60},{32,6... | collective-permute-start | bytes 196616 | tf_op jit(solution)/shard_map/ppermute | solution.py:228
  33.0 0.6 copy-start.6
  33.0 0.6 copy-start.7
  33.0 0.6 copy-start.8
  33.0 0.6 copy-start.9
  41.6 4.0 %copy-start.2 = (bf16[2,128,1024]{2,1,0:T(8,128)(2,1)S(1)}, bf16[2,128,1024]{2,1,0:T(8,128)(2,1)}, u32[]{:S(2)}) copy-start(bf16[2,128,1024]{2,1,0:T(8,128)(2,1)} %param.17) | copy-start | bytes 1572868
  41.6 13.8 %all-to-all-start = ((bf16[8,272,128]{2,1,0:T(8,128)(2,1)}), bf16[8,272,128]{2,1,0:T(8,128)(2,1)S(1)}, u32[]{:S(2)}, u32[]{:S(2)}) async-start(bf16[8,272,128]{2,1,0:T(8,128)(2,1)} %shard_map.149), calls=%async_computation | async-start | bytes 1114112 | tf_op jit(solution)/shard_map/all_to_all | solution.py:246
  55.4 0.8 copy-start
  58.5 10.2 %copy-start.11 = (bf16[128,128]{1,0:T(8,128)(2,1)S(1)}, bf16[128,128]{1,0:T(8,128)(2,1)}, u32[]{:S(2)}) copy-start(bf16[128,128]{1,0:T(8,128)(2,1)} %param.18) | copy-start | bytes 98308
  58.5 17.9 %all-to-all-start.1 = ((bf16[8,128,128]{2,1,0:T(8,128)(2,1)}), bf16[8,128,128]{2,1,0:T(8,128)(2,1)S(1)}, u32[]{:S(2)}, u32[]{:S(2)}) async-start(bf16[8,128,128]{2,1,0:T(8,128)(2,1)} %shard_map.150), calls=%async_computation.1 | async-start | bytes 524288 | tf_op jit(solution)/shard_map/all_to_all | solution.py:248
  68.7 0.8 copy-start.12
  68.7 0.8 copy-start.5
  76.5 20.1 %all-to-all-start.3 = ((f32[64,6,128]{2,1,0:T(8,128)}), f32[64,6,128]{2,1,0:T(8,128)S(1)}, u32[]{:S(2)}, u32[]{:S(2)}) async-start(f32[64,6,128]{2,1,0:T(8,128)} %pad_maximum_fusion), calls=%async_computation.3 | async-start | bytes 524288 | tf_op jit(solution)/shard_map/all_to_all | solution.py:240
  96.6 6.1 %copy-start.1 = (f32[64,6,128]{2,1,0:T(8,128)}, f32[64,6,128]{2,1,0:T(8,128)S(1)}, u32[]{:S(2)}) copy-start(f32[64,6,128]{2,1,0:T(8,128)S(1)} %all-to-all-done.3.in_ref) | copy-start | bytes 589828
  96.6 14.8 %all-to-all-start.2 = ((f32[64,2,128]{2,1,0:T(2,128)}), f32[64,2,128]{2,1,0:T(2,128)S(1)}, u32[]{:S(2)}, u32[]{:S(2)}) async-start(f32[64,2,128]{2,1,0:T(2,128)} %bitcast.8), calls=%async_computation.2 | async-start | bytes 131072 | tf_op jit(solution)/shard_map/all_to_all | solution.py:250
  101.3 0.7 copy-start.13
  111.4 0.6 copy-start.4

commit v2 on v1

v2 whole, which is shorter than its diff:
```python
import math

import jax
import jax.numpy as jnp
import numpy as np
from jax import lax
from jax.experimental import pallas as pl
from jax.experimental.pallas import tpu as pltpu
from jax.sharding import PartitionSpec as P

WINDOW = 4096
SHARD = 128
ROW = 8
BACK = WINDOW // (ROW * SHARD)
SHARDS = 64
HALF = 72
NEG = -1e30
highest = lax.Precision.HIGHEST


def transform_tables():
    length = 2 * SHARDS * SHARD
    k1 = np.arange(HALF)[:, None]
    live = (k1 <= SHARDS).astype(np.float64)
    a = np.arange(SHARDS)[None, :]
    angle = 2.0 * np.pi * ((k1 * a) % 128) / 128
    first = np.concatenate([live * np.cos(angle), -live * np.sin(angle)], 0)
    weight = live * np.where((k1 == 0) | (k1 == SHARDS), 1.0, 2.0) / length
    last = np.concatenate([weight * np.cos(angle), -weight * np.sin(angle)], 0).T
    b = np.arange(128)[None, :]
    turn = 2.0 * np.pi * (k1 * b) / length
    b2 = np.arange(128)[:, None]
    grid = 2.0 * np.pi * ((b2 * b) % 128) / 128
    cosine, sine = np.cos(grid), np.sin(grid)
    forward = np.block([[cosine, -sine], [sine, cosine]])
    backward = np.block([[cosine, sine], [-sine, cosine]])
    return [np.asarray(t, np.float32) for t in (first, last, np.cos(turn), np.sin(turn), forward, backward)]


def mul(a, b):
    return jnp.dot(a, b, precision=highest, preferred_element_type=jnp.float32)


def to_spectra(signals, first, turn_cos, turn_sin, forward):
    stacked = mul(first, jnp.concatenate(signals, 1))
    rows = []
    for n in range(len(signals)):
        re = stacked[:HALF, n * 128 : (n + 1) * 128]
        im = stacked[HALF:, n * 128 : (n + 1) * 128]
        rows.append(jnp.concatenate([re * turn_cos + im * turn_sin, im * turn_cos - re * turn_sin], 1))
    spectra = mul(jnp.concatenate(rows, 0), forward)
    return [spectra[n * HALF : (n + 1) * HALF] for n in range(len(signals))]


def to_signals(spectra, last, turn_cos, turn_sin, backward):
    rows = mul(jnp.concatenate(spectra, 0), backward)
    columns = []
    for n in range(len(spectra)):
        re = rows[n * HALF : (n + 1) * HALF, :128]
        im = rows[n * HALF : (n + 1) * HALF, 128:]
        columns.append(jnp.concatenate([re * turn_cos - im * turn_sin, re * turn_sin + im * turn_cos], 0))
    return mul(last, jnp.concatenate(columns, 1))


def product(a, b):
    ar, ai, br, bi = a[:, :128], a[:, 128:], b[:, :128], b[:, 128:]
    return jnp.concatenate([ar * br - ai * bi, ar * bi + ai * br], 1)


def product_conj(a, b):
    ar, ai, br, bi = a[:, :128], a[:, 128:], b[:, :128], b[:, 128:]
    return jnp.concatenate([ar * br + ai * bi, ar * bi - ai * br], 1)


def before_kernel(skip_ref, in_ref, first, last, tc, ts, fwd, bwd, spec_ref, pre_ref, gate_ref):
    first_channel = 2 * lax.axis_index("seq")
    x = [in_ref[:, c, :] for c in (0, 1)]
    gate = [in_ref[:, c, :] for c in (2, 3)]
    taps = [in_ref[:, c, :] for c in (4, 5)]
    spectra = to_spectra(x + taps, first[...], tc[...], ts[...], fwd[...])
    for n in range(4):
        spec_ref[n] = spectra[n]
    conv = to_signals(
        [product(spectra[c], spectra[2 + c]) for c in (0, 1)], last[...], tc[...], ts[...], bwd[...]
    )
    for c in (0, 1):
        pre_ref[c] = gate[c] * (conv[:, c * 128 : (c + 1) * 128] + skip_ref[first_channel + c] * x[c])
        gate_ref[c] = gate[c]


def after_kernel(skip_ref, target_ref, spec_ref, pre_ref, gate_ref, first, last, tc, ts, fwd, bwd, out_ref):
    first_channel = 2 * lax.axis_index("seq")
    back = [gate_ref[c] * (pre_ref[c] - target_ref[:, c, :]) for c in (0, 1)]
    spectra = to_spectra(back, first[...], tc[...], ts[...], fwd[...])
    mixed = [product_conj(spec_ref[2 + c], spectra[c]) for c in (0, 1)]
    mixed += [product_conj(spec_ref[c], spectra[c]) for c in (0, 1)]
    signals = to_signals(mixed, last[...], tc[...], ts[...], bwd[...])
    scale = (SHARDS * SHARD) ** -0.5
    for c in (0, 1):
        out_ref[:, c, :] = skip_ref[first_channel + c] * back[c] + signals[:, c * 128 : (c + 1) * 128]
        out_ref[:, 2 + c, :] = scale * signals[:, (2 + c) * 128 : (3 + c) * 128]


def attend_kernel(q_ref, kv0, kv1, kv2, kv3, kv4, out_ref):
    rank = lax.axis_index("seq")
    row, mine = rank // ROW, rank % ROW
    scale = 128 ** -0.5
    keys = jnp.concatenate([ref[0] for ref in (kv4, kv0, kv1, kv2, kv3)], 0)
    ones = jnp.ones((5 * SHARD, 128), jnp.bfloat16)
    values = jnp.concatenate([jnp.concatenate([ref[1] for ref in (kv4, kv0, kv1, kv2, kv3)], 0), ones], 1)
    lag = lax.broadcasted_iota(jnp.int32, (SHARD, SHARD), 0) - lax.broadcasted_iota(jnp.int32, (SHARD, SHARD), 1)
    diagonal = lag == 0
    zero = jnp.zeros((SHARD, SHARD), jnp.float32)
    for theirs in range(ROW):
        newest = lag >= (mine - theirs) * SHARD
        stats = []
        for h in (0, 1):
            scores = lax.dot_general(
                q_ref[theirs, h], keys, (((1,), (1,)), ((), ())), preferred_element_type=jnp.float32
            )
            parts = [scores[:, n * SHARD : (n + 1) * SHARD] for n in range(5)]
            blocks = [jnp.where(newest, parts[0], jnp.where(row >= BACK, parts[1], NEG))]
            blocks += [jnp.where(row >= BACK - r, parts[1 + r], NEG) for r in (1, 2, 3)]
            top = jnp.maximum(jnp.maximum(blocks[0], blocks[1]), jnp.maximum(blocks[2], blocks[3]))
            top = jnp.maximum(jnp.max(top, axis=1, keepdims=True), 0.5 * NEG)
            weights = [jnp.exp((b - top) * scale) for b in blocks]
            spread = [jnp.where(newest, weights[0], zero), jnp.where(newest, zero, weights[0])] + weights[1:]
            spread = jnp.concatenate([w.astype(jnp.bfloat16) for w in spread], 1)
            sums = jnp.dot(spread, values, preferred_element_type=jnp.float32)
            total = sums[:, 128:]
            safe = jnp.maximum(total, 1e-30)
            out_ref[theirs, h * 128 : (h + 1) * 128, :] = (sums[:, :128] / safe).astype(jnp.bfloat16)
            log_sum = jnp.where(total > 0.0, top * scale + jnp.log(safe), NEG)
            log_sum = jnp.sum(jnp.where(diagonal, log_sum, 0.0), axis=0, keepdims=True)
            high = log_sum.astype(jnp.bfloat16).astype(jnp.float32)
            rest = log_sum - high
            middle = rest.astype(jnp.bfloat16).astype(jnp.float32)
            stats += [high, middle, rest - middle]
        stats.append(jnp.zeros((10, 128), jnp.float32))
        out_ref[theirs, 256:272, :] = jnp.concatenate(stats, 0).astype(jnp.bfloat16)


def merge_kernel(parts_ref, proj_ref, out_ref):
    shares = []
    for h in (0, 1):
        sums = []
        for p in range(ROW):
            stats = parts_ref[p, 256:272, :].astype(jnp.float32)
            sums.append(stats[3 * h : 3 * h + 1] + stats[3 * h + 1 : 3 * h + 2] + stats[3 * h + 2 : 3 * h + 3])
        sums = jnp.concatenate(sums, 0)
        share = jnp.exp(sums - jnp.max(sums, axis=0, keepdims=True))
        shares.append(share / jnp.sum(share, axis=0, keepdims=True))
    shares.append(jnp.zeros((112, 128), jnp.float32))
    shares = jnp.concatenate(shares, 0).T
    heads = []
    for h in (0, 1):
        merged = None
        for p in range(ROW):
            part = parts_ref[p, h * 128 : (h + 1) * 128, :].astype(jnp.float32)
            part = shares[:, h * ROW + p : h * ROW + p + 1] * part
            merged = part if merged is None else merged + part
        heads.append(merged.astype(jnp.bfloat16))
    attended = jnp.concatenate(heads, 1)
    target = lax.dot_general(
        proj_ref[...], attended, (((1,), (1,)), ((), ())), preferred_element_type=jnp.float32
    )
    out_ref[...] = target.reshape(8, 128, 128).astype(jnp.bfloat16)


VMEM = pl.BlockSpec(memory_space=pltpu.VMEM)
SMEM = pl.BlockSpec(memory_space=pltpu.SMEM)


def near(x):
    return pltpu.with_memory_space_constraint(x, pltpu.VMEM)


def call_before(skip, packed, tables):
    return pl.pallas_call(
        before_kernel,
        out_shape=(
            pltpu.VMEM((4, HALF, 256), jnp.float32),
            pltpu.VMEM((2, SHARDS, 128), jnp.float32),
            pltpu.VMEM((2, SHARDS, 128), jnp.float32),
        ),
        in_specs=[SMEM] + [VMEM] * 7,
        out_specs=(VMEM,) * 3,
    )(skip, near(packed), *tables)


def call_after(skip, target, spectra, pre, gate, tables):
    return pl.pallas_call(
        after_kernel,
        out_shape=pltpu.VMEM((SHARDS, 4, 128), jnp.float32),
        in_specs=[SMEM] + [VMEM] * 10,
        out_specs=VMEM,
    )(skip, near(target), near(spectra), near(pre), near(gate), *tables)


def call_attend(queries, blocks):
    return pl.pallas_call(
        attend_kernel,
        out_shape=pltpu.VMEM((ROW, 272, 128), jnp.bfloat16),
        in_specs=[VMEM] * 6,
        out_specs=VMEM,
    )(near(queries), *[near(b) for b in blocks])


def call_merge(parts, proj):
    return pl.pallas_call(
        merge_kernel,
        out_shape=pltpu.VMEM((8, 128, 128), jnp.bfloat16),
        in_specs=[VMEM] * 2,
        out_specs=VMEM,
    )(near(parts), near(proj))


def body(
    query_heads,
    key_heads,
    value_heads,
    distill_proj,
    conv_input,
    gate_input,
    filter_taps,
    skip_gain,
):
    tables = [near(jnp.asarray(t)) for t in transform_tables()]
    rows = [[y * ROW + p for p in range(ROW)] for y in range(SHARDS // ROW)]

    packed = jnp.concatenate(
        [
            part.astype(jnp.float32).reshape(SHARDS, 2, 128)
            for part in (conv_input, gate_input, filter_taps)
        ],
        axis=1,
    )
    packed = lax.all_to_all(packed, "seq", 0, 0)
    own = jnp.stack([key_heads[:, 0], value_heads[:, 0]])
    blocks = [
        lax.ppermute(own, "seq", [(i, i + ROW * k) for i in range(SHARDS - ROW * k)])
        for k in range(BACK, 0, -1)
    ] + [own]
    packed, queries = lax.optimization_barrier((packed, jnp.transpose(query_heads, (1, 0, 2))))
    queries = lax.all_gather(queries, "seq", axis_index_groups=rows)
    spectra, pre, gate = call_before(skip_gain, packed, tables)

    proj = distill_proj.reshape(256, 1024).T
    parts = call_attend(queries, blocks)
    parts = lax.all_to_all(parts, "seq", 0, 0, axis_index_groups=rows)
    target = call_merge(parts, proj)
    target = lax.all_to_all(target, ("role", "head"), 0, 0)
    target = jnp.sum(target.astype(jnp.float32), axis=0).reshape(SHARDS, 2, 128)
    target = lax.all_to_all(target, "seq", 0, 0)
    out = call_after(skip_gain, target, spectra, pre, gate, tables)
    out = lax.all_to_all(out, "seq", 0, 0)
    return out[:, :2].reshape(128, 128), out[:, 2:].reshape(128, 128)


def solution(mesh):
    in_specs = (
        P("seq", ("role", "head"), None),
        P("seq", ("role", "head"), None),
        P("seq", ("role", "head"), None),
        P(("role", "head"), None, None),
        P(("role", "head"), "seq"),
        P(("role", "head"), "seq"),
        P(("role", "head"), "seq"),
        P(("role", "head")),
    )
    out_specs = (P(("role", "head"), "seq"), P(("role", "head"), "seq"))
    return jax.shard_map(body, mesh=mesh, in_specs=in_specs, out_specs=out_specs, check_vma=False)
```

time: 134 us -> 115 us (0.86)
  waiting for transfers between devices: 32.8 us -> 17.9 us
  blocking collectives: 32 us -> 46.8 us
  Pallas kernels: 17.1 us -> 8.62 us
  starting transfers between devices: 40.7 us -> 36.5 us
  local copies, waits for them, and re-layouts: 5.95 us -> 1.76 us
    all_to_all x0 -> x1, blocking collectives: none -> 17.7 us  [body(): target = lax.all_to_all(target, ('role', 'head'), 0, 0)]
    all_to_all x1, waiting for transfers between devices: 12.6 us -> 0.43 us  [body(): packed = lax.all_to_all(packed, 'seq', 0, 0)]
    all_to_all x1 -> x0, starting transfers between devices: 10.2 us -> none  [body(): target = lax.all_to_all(target, ('role', 'head'), 0, 0)]
    pallas_call x4, Pallas kernels: 17.1 us -> 8.62 us  [the longest x1 3.32 us: call_attend(): pl.pallas_call(attend_kernel, out_shape=pltpu.VMEM((ROW, 272, 128), jnp.b...]
    all_to_all x1 -> x0, waiting for transfers between devices: 6.09 us -> none  [body(): target = lax.all_to_all(target, ('role', 'head'), 0, 0)]
    all_to_all x1, starting transfers between devices: 6.85 us -> 11.8 us  [body(): packed = lax.all_to_all(packed, 'seq', 0, 0)]
    unnamed x29 -> x25, local copies, waits for them, and re-layouts: 3.57 us -> 0.85 us
    all_to_all x1, waiting for transfers between devices: 5.33 us -> 7.83 us  [body(): target = lax.all_to_all(target, 'seq', 0, 0)]
  transfers between devices with their start and end apart: 8 -> 7, of which waited for: 4 -> 3; matrix products, arithmetic and copies ran while one was open for 3% -> 0% of each run, Pallas kernels for 3% -> 2%
where the time goes in v2:
time: 115 us
  blocking collectives  46.8 us (41%)
  starting transfers between devices  36.5 us (32%)
  waiting for transfers between devices  17.9 us (16%)
  Pallas kernels  8.62 us (7%)
  other arithmetic  2.27 us (2%)
  local copies, waits for them, and re-layouts  1.76 us (2%)
    all_to_all x1, blocking collectives, body(): target = lax.all_to_all(target, ('role', 'head'), 0, 0)  17.7 us
    all_to_all x1, blocking collectives, body(): out = lax.all_to_all(out, 'seq', 0, 0)  15 us
    all_gather x1, blocking collectives, body(): queries = lax.all_gather(queries, 'seq', axis_index_groups=rows)  14 us
    ppermute x4, starting transfers between devices, body(): lax.ppermute(own, 'seq', [(i, i + ROW * k) for i in range(SHARDS - ROW *...  13.8 us
    all_to_all x1, starting transfers between devices, body(): packed = lax.all_to_all(packed, 'seq', 0, 0)  11.8 us
    all_to_all x1, waiting for transfers between devices, body(): parts = lax.all_to_all(parts, 'seq', 0, 0, axis_index_groups=rows)  9.62 us
    all_to_all x1, waiting for transfers between devices, body(): target = lax.all_to_all(target, 'seq', 0, 0)  7.83 us
    all_to_all x1, starting transfers between devices, body(): target = lax.all_to_all(target, 'seq', 0, 0)  6.99 us
  transfers between devices with their start and end apart: 7, of which 3 were waited for; matrix products, arithmetic and copies ran while one was open for 0% of the time, Pallas kernels for 2%

profile of v2, /device:TPU:1, one launch (start us, length us, event | category | flops | bytes accessed | tf_op | source)
XLA Modules:
  0.0 114.6 jit_solution(11887248389305744753)
XLA Ops:
  0.6 0.8 convert.2
  1.5 0.8 copy-done.7
  2.3 0.8 pad_maximum_fusion
  3.1 11.8 %all-to-all-start = ((f32[64,6,128]{2,1,0:T(8,128)}), f32[64,6,128]{2,1,0:T(8,128)S(1)}, u32[]{:S(2)}, u32[]{:S(2)}) async-start(f32[64,6,128]{2,1,0:T(8,128)} %pad_maximum_fusion), calls=%async_computation | async-start | bytes 524288 | tf_op jit(solution)/shard_map/all_to_all | solution.py:238
  14.9 7.3 %collective-permute-start = (bf16[2,128,128]{2,1,0:T(8,128)(2,1)S(1)}, bf16[2,128,128]{2,1,0:T(8,128)(2,1)S(1)}, u32[]{:S(2)}, u32[]{:S(2)}) collective-permute-start(bf16[2,128,128]{2,1,0:T(8,128)(2,1)S(1)} %pad_maximum_fusion.1.kv4), channel_id=1, source_target_pairs={{0,128},{4,132},{8,136},{12,140},{16,144},{20,148},{24,152},{28,15... | collective-permute-start | bytes 196616 | tf_op jit(solution)/shard_map/ppermute | solution.py:241
  22.2 2.4 %collective-permute-start.1 = (bf16[2,128,128]{2,1,0:T(8,128)(2,1)S(1)}, bf16[2,128,128]{2,1,0:T(8,128)(2,1)S(1)}, u32[]{:S(2)}, u32[]{:S(2)}) collective-permute-start(bf16[2,128,128]{2,1,0:T(8,128)(2,1)S(1)} %pad_maximum_fusion.1.kv4), channel_id=1, source_target_pairs={{0,96},{4,100},{8,104},{12,108},{16,112},{20,116},{24,120},{28,124... | collective-permute-start | bytes 196616 | tf_op jit(solution)/shard_map/ppermute | solution.py:241
  24.5 1.3 %collective-permute-start.2 = (bf16[2,128,128]{2,1,0:T(8,128)(2,1)S(1)}, bf16[2,128,128]{2,1,0:T(8,128)(2,1)S(1)}, u32[]{:S(2)}, u32[]{:S(2)}) collective-permute-start(bf16[2,128,128]{2,1,0:T(8,128)(2,1)S(1)} %pad_maximum_fusion.1.kv4), channel_id=1, source_target_pairs={{0,64},{4,68},{8,72},{12,76},{16,80},{20,84},{24,88},{28,92},{32,9... | collective-permute-start | bytes 196616 | tf_op jit(solution)/shard_map/ppermute | solution.py:241
  25.8 2.8 %collective-permute-start.3 = (bf16[2,128,128]{2,1,0:T(8,128)(2,1)S(1)}, bf16[2,128,128]{2,1,0:T(8,128)(2,1)S(1)}, u32[]{:S(2)}, u32[]{:S(2)}) collective-permute-start(bf16[2,128,128]{2,1,0:T(8,128)(2,1)S(1)} %pad_maximum_fusion.1.kv4), channel_id=1, source_target_pairs={{0,32},{4,36},{8,40},{12,44},{16,48},{20,52},{24,56},{28,60},{32,6... | collective-permute-start | bytes 196616 | tf_op jit(solution)/shard_map/ppermute | solution.py:241
  28.7 0.4 all-to-all-done.in_ref
  29.1 14.0 %all-gather = bf16[16,128,128]{2,1,0:T(8,128)(2,1)S(1)} all-gather(bf16[2,128,128]{2,1,0:T(8,128)(2,1)S(1)} %bitcast.19), channel_id=2, replica_groups={{0,4,8,12,16,20,24,28},{32,36,40,44,48,52,56,60},{64,68,72,76,80,84,88,..., dimensions={0}, use_global_device_ids=true | all-gather | bytes 589824 | tf_op jit(solution)/shard_map/all_gather | solution.py:245
  43.2 3.3 %shard_map.149 = bf16[8,272,128]{2,1,0:T(8,128)(2,1)} custom-call(bf16[8,2,128,128]{3,2,1,0:T(8,128)(2,1)S(1)} %bitcast.16, bf16[2,128,128]{2,1,0:T(8,128)(2,1)S(1)} %collective-permute-done.kv0, bf16[2,128,128]{2,1,0:T(8,128)(2,1)S(1)} %collective-permute-done.1.kv1, bf16[2,128,128]{2,1,0:T(8,128)(2,1)S(1)} %collective-permute-done.2.kv2, ...), custom_call_target="tpu_custom_call" | custom-call | tf_op jit(solution)/shard_map/pallas_call | solution.py:201
  46.5 4.0 %all-to-all-start.1 = ((bf16[8,272,128]{2,1,0:T(8,128)(2,1)}), bf16[8,272,128]{2,1,0:T(8,128)(2,1)S(1)}, u32[]{:S(2)}, u32[]{:S(2)}) async-start(bf16[8,272,128]{2,1,0:T(8,128)(2,1)} %shard_map.149), calls=%async_computation.1 | async-start | bytes 1114112 | tf_op jit(solution)/shard_map/all_to_all | solution.py:250
  50.5 0.2 copy.20
  50.7 9.6 %all-to-all-done.1.parts_ref = bf16[8,272,128]{2,1,0:T(8,128)(2,1)S(1)} async-done(((bf16[8,272,128]{2,1,0:T(8,128)(2,1)}), bf16[8,272,128]{2,1,0:T(8,128)(2,1)S(1)}, u32[]{:S(2)}, u32[]{:S(2)}) %all-to-all-start.1) | async-done | bytes 557088 | tf_op jit(solution)/shard_map/all_to_all | solution.py:250
  60.3 0.9 shard_map.150
  61.2 0.0 copy-start.1
  61.2 17.7 %all_to_all.25 = bf16[8,128,128]{2,1,0:T(8,128)(2,1)S(1)} all-to-all(bf16[8,128,128]{2,1,0:T(8,128)(2,1)S(1)} %shard_map.150), channel_id=1, replica_groups=mesh['role'=2,'seq'=64,'head'=4] {'role','head'}, dimensions={0} | all-to-all | bytes 524288 | tf_op jit(solution)/shard_map/all_to_all | solution.py:252
  79.0 0.7 convert_reduce_fusion
  79.6 7.0 %all-to-all-start.3 = ((f32[64,2,128]{2,1,0:T(2,128)}), f32[64,2,128]{2,1,0:T(2,128)S(1)}, u32[]{:S(2)}, u32[]{:S(2)}) async-start(f32[64,2,128]{2,1,0:T(2,128)} %bitcast.9), calls=%async_computation.3 | async-start | bytes 131072 | tf_op jit(solution)/shard_map/all_to_all | solution.py:254
  86.7 2.2 %shard_map.151 = (f32[4,72,256]{2,1,0:T(8,128)S(1)}, f32[2,64,128]{2,1,0:T(8,128)S(1)}, f32[2,64,128]{2,1,0:T(8,128)S(1)}) custom-call(f32[128]{0:T(128)} %skip_ref.3, f32[64,6,128]{2,1,0:T(8,128)S(1)} %all-to-all-done.in_ref, f32[144,64]{1,0:T(8,128)S(1)} %copy-done.2, f32[64,144]{1,0:T(8,128)S(1)} %copy-done.3, f32[72,128]{1,0:T(8,128)S(1)} %copy-done.4, ...), custom_call_target="tpu_custom_call" | custom-call | tf_op jit(solution)/shard_map/pallas_call | solution.py:179
  88.9 7.8 %all-to-all-done.3.target_ref = f32[64,2,128]{2,1,0:T(2,128)S(1)} async-done(((f32[64,2,128]{2,1,0:T(2,128)}), f32[64,2,128]{2,1,0:T(2,128)S(1)}, u32[]{:S(2)}, u32[]{:S(2)}) %all-to-all-start.3) | async-done | bytes 65568 | tf_op jit(solution)/shard_map/all_to_all | solution.py:254
  96.8 2.2 %shard_map.152 = f32[64,4,128]{2,1,0:T(4,128)S(1)} custom-call(f32[128]{0:T(128)} %skip_ref.3, f32[64,2,128]{2,1,0:T(2,128)S(1)} %all-to-all-done.3.target_ref, f32[4,72,256]{2,1,0:T(8,128)S(1)} %get-tuple-element.9.spec_ref, f32[2,64,128]{2,1,0:T(8,128)S(1)} %get-tuple-element.10.pre_ref, f32[2,64,128]{2,1,0:T(8,128)S(1)} %get-tuple-element.11.gate_ref, ...), custom_call_target="tpu_custom_call" | custom-call | tf_op jit(solution)/shard_map/pallas_call | solution.py:192
  99.0 15.0 %all_to_all.26 = f32[64,4,128]{2,1,0:T(4,128)S(1)} all-to-all(f32[64,4,128]{2,1,0:T(4,128)S(1)} %shard_map.152), channel_id=1, replica_groups=mesh['role'=2,'seq'=64,'head'=4] {'seq'}, dimensions={0} | all-to-all | bytes 262144 | tf_op jit(solution)/shard_map/all_to_all | solution.py:256
  113.9 0.7 fusion
  (29 shorter events, 0.1 us)
Async XLA Ops:
  0.6 0.8 copy-start.9
  1.4 0.8 copy-start.7
  3.1 11.8 %copy-start.10 = (bf16[128,1,128]{2,0,1:T(8,128)(2,1)S(1)}, bf16[128,1,128]{2,0,1:T(8,128)(2,1)}, u32[]{:S(2)}) copy-start(bf16[128,1,128]{2,0,1:T(8,128)(2,1)} %param.16) | copy-start | bytes 98308
  3.1 11.8 %copy-start.11 = (bf16[128,1,128]{2,0,1:T(8,128)(2,1)S(1)}, bf16[128,1,128]{2,0,1:T(8,128)(2,1)}, u32[]{:S(2)}) copy-start(bf16[128,1,128]{2,0,1:T(8,128)(2,1)} %param.15) | copy-start | bytes 98308
  3.1 26.1 %all-to-all-start = ((f32[64,6,128]{2,1,0:T(8,128)}), f32[64,6,128]{2,1,0:T(8,128)S(1)}, u32[]{:S(2)}, u32[]{:S(2)}) async-start(f32[64,6,128]{2,1,0:T(8,128)} %pad_maximum_fusion), calls=%async_computation | async-start | bytes 524288 | tf_op jit(solution)/shard_map/all_to_all | solution.py:238
  14.8 13.8 %copy-start.8 = (bf16[128,2,128]{2,1,0:T(2,128)(2,1)S(1)}, bf16[128,2,128]{2,1,0:T(2,128)(2,1)}, u32[]{:S(2)}) copy-start(bf16[128,2,128]{2,1,0:T(2,128)(2,1)} %param.14) | copy-start | bytes 196612
  14.9 28.3 %collective-permute-start = (bf16[2,128,128]{2,1,0:T(8,128)(2,1)S(1)}, bf16[2,128,128]{2,1,0:T(8,128)(2,1)S(1)}, u32[]{:S(2)}, u32[]{:S(2)}) collective-permute-start(bf16[2,128,128]{2,1,0:T(8,128)(2,1)S(1)} %pad_maximum_fusion.1.kv4), channel_id=1, source_target_pairs={{0,128},{4,132},{8,136},{12,140},{16,144},{20,148},{24,152},{28,15... | collective-permute-start | bytes 196616 | tf_op jit(solution)/shard_map/ppermute | solution.py:241
  22.2 21.0 %collective-permute-start.1 = (bf16[2,128,128]{2,1,0:T(8,128)(2,1)S(1)}, bf16[2,128,128]{2,1,0:T(8,128)(2,1)S(1)}, u32[]{:S(2)}, u32[]{:S(2)}) collective-permute-start(bf16[2,128,128]{2,1,0:T(8,128)(2,1)S(1)} %pad_maximum_fusion.1.kv4), channel_id=1, source_target_pairs={{0,96},{4,100},{8,104},{12,108},{16,112},{20,116},{24,120},{28,124... | collective-permute-start | bytes 196616 | tf_op jit(solution)/shard_map/ppermute | solution.py:241
  24.5 18.6 %collective-permute-start.2 = (bf16[2,128,128]{2,1,0:T(8,128)(2,1)S(1)}, bf16[2,128,128]{2,1,0:T(8,128)(2,1)S(1)}, u32[]{:S(2)}, u32[]{:S(2)}) collective-permute-start(bf16[2,128,128]{2,1,0:T(8,128)(2,1)S(1)} %pad_maximum_fusion.1.kv4), channel_id=1, source_target_pairs={{0,64},{4,68},{8,72},{12,76},{16,80},{20,84},{24,88},{28,92},{32,9... | collective-permute-start | bytes 196616 | tf_op jit(solution)/shard_map/ppermute | solution.py:241
  25.8 17.3 %collective-permute-start.3 = (bf16[2,128,128]{2,1,0:T(8,128)(2,1)S(1)}, bf16[2,128,128]{2,1,0:T(8,128)(2,1)S(1)}, u32[]{:S(2)}, u32[]{:S(2)}) collective-permute-start(bf16[2,128,128]{2,1,0:T(8,128)(2,1)S(1)} %pad_maximum_fusion.1.kv4), channel_id=1, source_target_pairs={{0,32},{4,36},{8,40},{12,44},{16,48},{20,52},{24,56},{28,60},{32,6... | collective-permute-start | bytes 196616 | tf_op jit(solution)/shard_map/ppermute | solution.py:241
  46.5 4.0 %copy-start.6 = (bf16[2,128,1024]{2,1,0:T(8,128)(2,1)S(1)}, bf16[2,128,1024]{2,1,0:T(8,128)(2,1)}, u32[]{:S(2)}) copy-start(bf16[2,128,1024]{2,1,0:T(8,128)(2,1)} %param.17) | copy-start | bytes 1572868
  46.5 13.8 %all-to-all-start.1 = ((bf16[8,272,128]{2,1,0:T(8,128)(2,1)}), bf16[8,272,128]{2,1,0:T(8,128)(2,1)S(1)}, u32[]{:S(2)}, u32[]{:S(2)}) async-start(bf16[8,272,128]{2,1,0:T(8,128)(2,1)} %shard_map.149), calls=%async_computation.1 | async-start | bytes 1114112 | tf_op jit(solution)/shard_map/all_to_all | solution.py:250
  61.2 25.4 %copy-start.1 = (f32[256,256]{1,0:T(8,128)S(1)}, f32[256,256]{1,0:T(8,128)}, u32[]{:S(2)}) copy-start(f32[256,256]{1,0:T(8,128)} %constant.19.clone.bwd) | copy-start | bytes 786436
  61.2 25.4 %copy-start.5 = (f32[72,128]{1,0:T(8,128)S(1)}, f32[72,128]{1,0:T(8,128)}, u32[]{:S(2)}) copy-start(f32[72,128]{1,0:T(8,128)} %constant.17.clone.ts) | copy-start | bytes 110596
  79.0 7.7 %copy-start = (f32[256,256]{1,0:T(8,128)S(1)}, f32[256,256]{1,0:T(8,128)}, u32[]{:S(2)}) copy-start(f32[256,256]{1,0:T(8,128)} %constant.18.clone.fwd) | copy-start | bytes 786436
  79.0 7.7 %copy-start.3 = (f32[64,144]{1,0:T(8,128)S(1)}, f32[64,144]{1,0:T(8,128)}, u32[]{:S(2)}) copy-start(f32[64,144]{1,0:T(8,128)} %constant.15.clone.last) | copy-start | bytes 110596
  79.6 7.0 %copy-start.2 = (f32[144,64]{1,0:T(8,128)S(1)}, f32[144,64]{1,0:T(8,128)}, u32[]{:S(2)}) copy-start(f32[144,64]{1,0:T(8,128)} %constant.14.clone.first) | copy-start | bytes 110596
  79.6 7.0 %copy-start.4 = (f32[72,128]{1,0:T(8,128)S(1)}, f32[72,128]{1,0:T(8,128)}, u32[]{:S(2)}) copy-start(f32[72,128]{1,0:T(8,128)} %constant.16.clone.tc) | copy-start | bytes 110596
  79.6 17.1 %all-to-all-start.3 = ((f32[64,2,128]{2,1,0:T(2,128)}), f32[64,2,128]{2,1,0:T(2,128)S(1)}, u32[]{:S(2)}, u32[]{:S(2)}) async-start(f32[64,2,128]{2,1,0:T(2,128)} %bitcast.9), calls=%async_computation.3 | async-start | bytes 131072 | tf_op jit(solution)/shard_map/all_to_all | solution.py:254

commit v3 on v2

--- a/solution.py
+++ b/solution.py
@@ -1,7 +1,6 @@
-import math
-
 import jax
 import jax.numpy as jnp
+import ml_dtypes
 import numpy as np
 from jax import lax
 from jax.experimental import pallas as pl
@@ -15,7 +14,6 @@
 SHARDS = 64
 HALF = 72
 NEG = -1e30
-highest = lax.Precision.HIGHEST
 
 
 def transform_tables():
@@ -34,32 +32,51 @@
     cosine, sine = np.cos(grid), np.sin(grid)
     forward = np.block([[cosine, -sine], [sine, cosine]])
     backward = np.block([[cosine, sine], [-sine, cosine]])
-    return [np.asarray(t, np.float32) for t in (first, last, np.cos(turn), np.sin(turn), forward, backward)]
-
-
-def mul(a, b):
-    return jnp.dot(a, b, precision=highest, preferred_element_type=jnp.float32)
+    tables = [np.asarray(t, np.float32) for t in (np.cos(turn), np.sin(turn))]
+    for table in (first, last, forward, backward):
+        high = np.asarray(table, ml_dtypes.bfloat16)
+        tables += [high, np.asarray(table - high.astype(np.float64), ml_dtypes.bfloat16)]
+    return tables
+
+
+def halves(x):
+    high = x.astype(jnp.bfloat16)
+    return high, (x - high.astype(jnp.float32)).astype(jnp.bfloat16)
+
+
+def dot32(a, b):
+    return jnp.dot(a, b, preferred_element_type=jnp.float32)
+
+
+def table_times(table, x):
+    high, low = halves(x)
+    return dot32(table[0], high) + (dot32(table[0], low) + dot32(table[1], high))
+
+
+def times_table(x, table):
+    high, low = halves(x)
+    return dot32(high, table[0]) + (dot32(low, table[0]) + dot32(high, table[1]))
 
 
 def to_spectra(signals, first, turn_cos, turn_sin, forward):
-    stacked = mul(first, jnp.concatenate(signals, 1))
+    stacked = table_times(first, jnp.concatenate(signals, 1))
     rows = []
     for n in range(len(signals)):
         re = stacked[:HALF, n * 128 : (n + 1) * 128]
         im = stacked[HALF:, n * 128 : (n + 1) * 128]
         rows.append(jnp.concatenate([re * turn_cos + im * turn_sin, im * turn_cos - re * turn_sin], 1))
-    spectra = mul(jnp.concatenate(rows, 0), forward)
+    spectra = times_table(jnp.concatenate(rows, 0), forward)
     return [spectra[n * HALF : (n + 1) * HALF] for n in range(len(signals))]
 
 
 def to_signals(spectra, last, turn_cos, turn_sin, backward):
-    rows = mul(jnp.concatenate(spectra, 0), backward)
+    rows = times_table(jnp.concatenate(spectra, 0), backward)
     columns = []
     for n in range(len(spectra)):
         re = rows[n * HALF : (n + 1) * HALF, :128]
         im = rows[n * HALF : (n + 1) * HALF, 128:]
         columns.append(jnp.concatenate([re * turn_cos - im * turn_sin, re * turn_sin + im * turn_cos], 0))
-    return mul(last, jnp.concatenate(columns, 1))
+    return table_times(last, jnp.concatenate(columns, 1))
 
 
 def product(a, b):
@@ -72,33 +89,44 @@
     return jnp.concatenate([ar * br + ai * bi, ar * bi - ai * br], 1)
 
 
-def before_kernel(skip_ref, in_ref, first, last, tc, ts, fwd, bwd, spec_ref, pre_ref, gate_ref):
-    first_channel = 2 * lax.axis_index("seq")
-    x = [in_ref[:, c, :] for c in (0, 1)]
-    gate = [in_ref[:, c, :] for c in (2, 3)]
-    taps = [in_ref[:, c, :] for c in (4, 5)]
-    spectra = to_spectra(x + taps, first[...], tc[...], ts[...], fwd[...])
-    for n in range(4):
-        spec_ref[n] = spectra[n]
-    conv = to_signals(
-        [product(spectra[c], spectra[2 + c]) for c in (0, 1)], last[...], tc[...], ts[...], bwd[...]
-    )
+def pack_kernel(parts_ref, input_ref, gate_ref, taps_ref, out_ref):
+    target = parts_ref[0].astype(jnp.float32)
+    for n in range(1, 8):
+        target += parts_ref[n].astype(jnp.float32)
+    arrays = (target, input_ref[...], gate_ref[...], taps_ref[...])
+    for n, array in enumerate(arrays):
+        array = array.astype(jnp.float32)
+        out_ref[:, 2 * n, :] = array[:SHARDS]
+        out_ref[:, 2 * n + 1, :] = array[SHARDS:]
+
+
+def student_kernel(skip_ref, in_ref, tc, ts, f0, f1, l0, l1, w0, w1, b0, b1, out_ref):
+    rank = lax.axis_index("seq")
+    skip = [skip_ref[rank], skip_ref[rank + SHARDS]]
+    target, signal, gate, taps = [[in_ref[:, 2 * n + c, :] for c in (0, 1)] for n in range(4)]
+    turn = tc[...], ts[...]
+    ahead = (f0[...], f1[...]), *turn, (w0[...], w1[...])
+    behind = (l0[...], l1[...]), *turn, (b0[...], b1[...])
+    spectra = to_spectra(signal + taps, *ahead)
+    conv = to_signals([product(spectra[c], spectra[2 + c]) for c in (0, 1)], *behind)
+    back = []
     for c in (0, 1):
-        pre_ref[c] = gate[c] * (conv[:, c * 128 : (c + 1) * 128] + skip_ref[first_channel + c] * x[c])
-        gate_ref[c] = gate[c]
-
-
-def after_kernel(skip_ref, target_ref, spec_ref, pre_ref, gate_ref, first, last, tc, ts, fwd, bwd, out_ref):
-    first_channel = 2 * lax.axis_index("seq")
-    back = [gate_ref[c] * (pre_ref[c] - target_ref[:, c, :]) for c in (0, 1)]
-    spectra = to_spectra(back, first[...], tc[...], ts[...], fwd[...])
-    mixed = [product_conj(spec_ref[2 + c], spectra[c]) for c in (0, 1)]
-    mixed += [product_conj(spec_ref[c], spectra[c]) for c in (0, 1)]
-    signals = to_signals(mixed, last[...], tc[...], ts[...], bwd[...])
+        output = gate[c] * (conv[:, c * 128 : (c + 1) * 128] + skip[c] * signal[c])
+        back.append(gate[c] * (output - target[c]))
+    gradient = to_spectra(back, *ahead)
+    mixed = [product_conj(spectra[2 + c], gradient[c]) for c in (0, 1)]
+    mixed += [product_conj(spectra[c], gradient[c]) for c in (0, 1)]
+    signals = to_signals(mixed, *behind)
     scale = (SHARDS * SHARD) ** -0.5
     for c in (0, 1):
-        out_ref[:, c, :] = skip_ref[first_channel + c] * back[c] + signals[:, c * 128 : (c + 1) * 128]
+        out_ref[:, c, :] = skip[c] * back[c] + signals[:, c * 128 : (c + 1) * 128]
         out_ref[:, 2 + c, :] = scale * signals[:, (2 + c) * 128 : (3 + c) * 128]
+
+
+def unpack_kernel(in_ref, grad_ref, step_ref):
+    for c in (0, 1):
+        grad_ref[c * SHARDS : (c + 1) * SHARDS, :] = in_ref[:, c, :]
+        step_ref[c * SHARDS : (c + 1) * SHARDS, :] = in_ref[:, 2 + c, :]
 
 
 def attend_kernel(q_ref, kv0, kv1, kv2, kv3, kv4, out_ref):
@@ -175,26 +203,31 @@
     return pltpu.with_memory_space_constraint(x, pltpu.VMEM)
 
 
-def call_before(skip, packed, tables):
-    return pl.pallas_call(
-        before_kernel,
-        out_shape=(
-            pltpu.VMEM((4, HALF, 256), jnp.float32),
-            pltpu.VMEM((2, SHARDS, 128), jnp.float32),
-            pltpu.VMEM((2, SHARDS, 128), jnp.float32),
-        ),
-        in_specs=[SMEM] + [VMEM] * 7,
-        out_specs=(VMEM,) * 3,
+def call_pack(parts, *inputs):
+    return pl.pallas_call(
+        pack_kernel,
+        out_shape=pltpu.VMEM((SHARDS, 8, 128), jnp.float32),
+        in_specs=[VMEM] * 4,
+        out_specs=VMEM,
+    )(near(parts), *[near(x) for x in inputs])
+
+
+def call_student(skip, packed, tables):
+    return pl.pallas_call(
+        student_kernel,
+        out_shape=pltpu.VMEM((SHARDS, 4, 128), jnp.float32),
+        in_specs=[SMEM] + [VMEM] * 11,
+        out_specs=VMEM,
     )(skip, near(packed), *tables)
 
 
-def call_after(skip, target, spectra, pre, gate, tables):
-    return pl.pallas_call(
-        after_kernel,
-        out_shape=pltpu.VMEM((SHARDS, 4, 128), jnp.float32),
-        in_specs=[SMEM] + [VMEM] * 10,
-        out_specs=VMEM,
-    )(skip, near(target), near(spectra), near(pre), near(gate), *tables)
+def call_unpack(out):
+    return pl.pallas_call(
+        unpack_kernel,
+        out_shape=(jax.ShapeDtypeStruct((128, 128), jnp.float32),) * 2,
+        in_specs=[VMEM],
+        out_specs=(VMEM,) * 2,
+    )(near(out))
 
 
 def call_attend(queries, blocks):
@@ -228,33 +261,22 @@
     tables = [near(jnp.asarray(t)) for t in transform_tables()]
     rows = [[y * ROW + p for p in range(ROW)] for y in range(SHARDS // ROW)]
 
-    packed = jnp.concatenate(
-        [
-            part.astype(jnp.float32).reshape(SHARDS, 2, 128)
-            for part in (conv_input, gate_input, filter_taps)
-        ],
-        axis=1,
-    )
-    packed = lax.all_to_all(packed, "seq", 0, 0)
     own = jnp.stack([key_heads[:, 0], value_heads[:, 0]])
     blocks = [
         lax.ppermute(own, "seq", [(i, i + ROW * k) for i in range(SHARDS - ROW * k)])
         for k in range(BACK, 0, -1)
     ] + [own]
-    packed, queries = lax.optimization_barrier((packed, jnp.transpose(query_heads, (1, 0, 2))))
-    queries = lax.all_gather(queries, "seq", axis_index_groups=rows)
-    spectra, pre, gate = call_before(skip_gain, packed, tables)
-
+    queries = lax.all_gather(jnp.transpose(query_heads, (1, 0, 2)), "seq", axis_index_groups=rows)
     proj = distill_proj.reshape(256, 1024).T
     parts = call_attend(queries, blocks)
     parts = lax.all_to_all(parts, "seq", 0, 0, axis_index_groups=rows)
     target = call_merge(parts, proj)
     target = lax.all_to_all(target, ("role", "head"), 0, 0)
-    target = jnp.sum(target.astype(jnp.float32), axis=0).reshape(SHARDS, 2, 128)
-    target = lax.all_to_all(target, "seq", 0, 0)
-    out = call_after(skip_gain, target, spectra, pre, gate, tables)
+    packed = call_pack(target, conv_input, gate_input, filter_taps)
+    packed = lax.all_to_all(packed, "seq", 0, 0)
+    out = call_student(skip_gain, packed, tables)
     out = lax.all_to_all(out, "seq", 0, 0)
-    return out[:, :2].reshape(128, 128), out[:, 2:].reshape(128, 128)
+    return call_unpack(out)
 
 
 def solution(mesh):

time: 115 us -> 107 us (0.930)
  blocking collectives: 46.8 us -> 67.6 us
  starting transfers between devices: 36.5 us -> 18.9 us
  waiting for transfers between devices: 17.9 us -> 9.63 us
  other arithmetic: 2.27 us -> 0.81 us
  local copies, waits for them, and re-layouts: 1.76 us -> 0.31 us
    all_to_all x0 -> x1, blocking collectives: none -> 19.4 us  [body(): packed = lax.all_to_all(packed, 'seq', 0, 0)]
    all_to_all x2 -> x0, starting transfers between devices: 18.7 us -> none  [the longest x1 11.8 us: body(): packed = lax.all_to_all(packed, 'seq', 0, 0)]
    all_to_all x2 -> x0, waiting for transfers between devices: 8.26 us -> none  [the longest x1 7.83 us: body(): target = lax.all_to_all(target, 'seq', 0, 0)]
    pallas_call x2 -> x3, Pallas kernels: 4.44 us -> 3.69 us  [the longest x1 2.8 us: call_student(): pl.pallas_call(student_kernel, out_shape=pltpu.VMEM((SHARDS, 4, 128), jnp...]
  transfers between devices with their start and end apart: 7 -> 5, of which waited for: 3 -> 1; matrix products, arithmetic and copies ran while one was open for 0% -> 0% of each run, Pallas kernels for 2% -> 0%
where the time goes in v3:
time: 107 us; the launch traced here: 106 us
  blocking collectives  67.6 us (63%)
  starting transfers between devices  18.9 us (18%)
  waiting for transfers between devices  9.63 us (9%)
  Pallas kernels  7.88 us (7%)
    all_to_all x1, blocking collectives, body(): packed = lax.all_to_all(packed, 'seq', 0, 0)  19.4 us
    all_to_all x1, blocking collectives, body(): target = lax.all_to_all(target, ('role', 'head'), 0, 0)  17.7 us
    all_to_all x1, blocking collectives, body(): out = lax.all_to_all(out, 'seq', 0, 0)  15.7 us
    ppermute x4, starting transfers between devices, body(): lax.ppermute(own, 'seq', [(i, i + ROW * k) for i in range(SHARDS - ROW *...  14.9 us
    all_gather x1, blocking collectives, body(): lax.all_gather(jnp.transpose(query_heads, (1, 0, 2)), 'seq', axis_index_g...  14.8 us
    all_to_all x1, waiting for transfers between devices, body(): parts = lax.all_to_all(parts, 'seq', 0, 0, axis_index_groups=rows)  9.62 us
    all_to_all x1, starting transfers between devices, body(): parts = lax.all_to_all(parts, 'seq', 0, 0, axis_index_groups=rows)  3.97 us
    pallas_call x1, Pallas kernels, call_attend(): pl.pallas_call(attend_kernel, out_shape=pltpu.VMEM((ROW, 272, 128), jnp.b...  3.32 us
  transfers between devices with their start and end apart: 5, of which 1 were waited for; matrix products, arithmetic and copies ran while one was open for 0% of the time, Pallas kernels for 0%

profile of v3, /device:TPU:1, one launch (start us, length us, event | category | flops | bytes accessed | tf_op | source)
XLA Modules:
  0.0 106.1 jit_solution(2631086318110881492)
XLA Ops:
  0.6 0.8 pad_maximum_fusion.kv4
  1.5 4.0 %collective-permute-start.3 = (bf16[2,128,128]{2,1,0:T(8,128)(2,1)S(1)}, bf16[2,128,128]{2,1,0:T(8,128)(2,1)S(1)}, u32[]{:S(2)}, u32[]{:S(2)}) collective-permute-start(bf16[2,128,128]{2,1,0:T(8,128)(2,1)S(1)} %pad_maximum_fusion.kv4), channel_id=1, source_target_pairs={{0,32},{4,36},{8,40},{12,44},{16,48},{20,52},{24,56},{28,60},{32,6... | collective-permute-start | bytes 196616 | tf_op jit(solution)/shard_map/ppermute | solution.py:266
  5.5 4.2 %collective-permute-start.2 = (bf16[2,128,128]{2,1,0:T(8,128)(2,1)S(1)}, bf16[2,128,128]{2,1,0:T(8,128)(2,1)S(1)}, u32[]{:S(2)}, u32[]{:S(2)}) collective-permute-start(bf16[2,128,128]{2,1,0:T(8,128)(2,1)S(1)} %pad_maximum_fusion.kv4), channel_id=1, source_target_pairs={{0,64},{4,68},{8,72},{12,76},{16,80},{20,84},{24,88},{28,92},{32,9... | collective-permute-start | bytes 196616 | tf_op jit(solution)/shard_map/ppermute | solution.py:266
  9.7 4.6 %collective-permute-start.1 = (bf16[2,128,128]{2,1,0:T(8,128)(2,1)S(1)}, bf16[2,128,128]{2,1,0:T(8,128)(2,1)S(1)}, u32[]{:S(2)}, u32[]{:S(2)}) collective-permute-start(bf16[2,128,128]{2,1,0:T(8,128)(2,1)S(1)} %pad_maximum_fusion.kv4), channel_id=1, source_target_pairs={{0,96},{4,100},{8,104},{12,108},{16,112},{20,116},{24,120},{28,124... | collective-permute-start | bytes 196616 | tf_op jit(solution)/shard_map/ppermute | solution.py:266
  14.4 2.0 %collective-permute-start = (bf16[2,128,128]{2,1,0:T(8,128)(2,1)S(1)}, bf16[2,128,128]{2,1,0:T(8,128)(2,1)S(1)}, u32[]{:S(2)}, u32[]{:S(2)}) collective-permute-start(bf16[2,128,128]{2,1,0:T(8,128)(2,1)S(1)} %pad_maximum_fusion.kv4), channel_id=1, source_target_pairs={{0,128},{4,132},{8,136},{12,140},{16,144},{20,148},{24,152},{28,15... | collective-permute-start | bytes 196616 | tf_op jit(solution)/shard_map/ppermute | solution.py:266
  16.4 14.8 %all-gather = bf16[16,128,128]{2,1,0:T(8,128)(2,1)S(1)} all-gather(bf16[2,128,128]{2,1,0:T(8,128)(2,1)S(1)} %bitcast.11), channel_id=2, replica_groups={{0,4,8,12,16,20,24,28},{32,36,40,44,48,52,56,60},{64,68,72,76,80,84,88,..., dimensions={0}, use_global_device_ids=true | all-gather | bytes 589824 | tf_op jit(solution)/shard_map/all_gather | solution.py:269
  31.3 3.3 %shard_map.185 = bf16[8,272,128]{2,1,0:T(8,128)(2,1)} custom-call(bf16[8,2,128,128]{3,2,1,0:T(8,128)(2,1)S(1)} %bitcast.8, bf16[2,128,128]{2,1,0:T(8,128)(2,1)S(1)} %collective-permute-done.kv0, bf16[2,128,128]{2,1,0:T(8,128)(2,1)S(1)} %collective-permute-done.1.kv1, bf16[2,128,128]{2,1,0:T(8,128)(2,1)S(1)} %collective-permute-done.2.kv2, ...), custom_call_target="tpu_custom_call" | custom-call | tf_op jit(solution)/shard_map/pallas_call | solution.py:234
  34.6 4.0 %all-to-all-start = ((bf16[8,272,128]{2,1,0:T(8,128)(2,1)}), bf16[8,272,128]{2,1,0:T(8,128)(2,1)S(1)}, u32[]{:S(2)}, u32[]{:S(2)}) async-start(bf16[8,272,128]{2,1,0:T(8,128)(2,1)} %shard_map.185), calls=%async_computation | async-start | bytes 1114112 | tf_op jit(solution)/shard_map/all_to_all | solution.py:272
  38.6 0.2 copy.24
  38.8 9.6 %all-to-all-done.parts_ref = bf16[8,272,128]{2,1,0:T(8,128)(2,1)S(1)} async-done(((bf16[8,272,128]{2,1,0:T(8,128)(2,1)}), bf16[8,272,128]{2,1,0:T(8,128)(2,1)S(1)}, u32[]{:S(2)}, u32[]{:S(2)}) %all-to-all-start) | async-done | bytes 557088 | tf_op jit(solution)/shard_map/all_to_all | solution.py:272
  48.4 0.9 shard_map.186
  49.3 17.7 %all_to_all.20.parts_ref = bf16[8,128,128]{2,1,0:T(8,128)(2,1)S(1)} all-to-all(bf16[8,128,128]{2,1,0:T(8,128)(2,1)S(1)} %shard_map.186), channel_id=1, replica_groups=mesh['role'=2,'seq'=64,'head'=4] {'role','head'}, dimensions={0} | all-to-all | bytes 524288 | tf_op jit(solution)/shard_map/all_to_all | solution.py:274
  67.0 0.0 copy-start.5
  67.1 0.0 copy-start.6
  67.1 0.0 copy-start.7
  67.1 0.0 copy-start.8
  67.1 0.0 copy-start.11
  67.1 0.0 copy-start.12
  67.1 0.2 shard_map.187
  67.3 0.0 copy-start
  67.4 19.4 %all_to_all.21.in_ref = f32[64,8,128]{2,1,0:T(8,128)S(1)} all-to-all(f32[64,8,128]{2,1,0:T(8,128)S(1)} %shard_map.187), channel_id=1, replica_groups=mesh['role'=2,'seq'=64,'head'=4] {'seq'}, dimensions={0} | all-to-all | bytes 524288 | tf_op jit(solution)/shard_map/all_to_all | solution.py:276
  86.9 2.8 %shard_map.188 = f32[64,4,128]{2,1,0:T(4,128)S(1)} custom-call(f32[128]{0:T(128)} %skip_ref.1, f32[64,8,128]{2,1,0:T(8,128)S(1)} %all_to_all.21.in_ref, f32[72,128]{1,0:T(8,128)S(1)} %copy-done.8, f32[72,128]{1,0:T(8,128)S(1)} %copy-done.7, bf16[144,64]{1,0:T(8,128)(2,1)S(1)} %copy-done.6, bf16[144,64]{1,0:T(8,128)(2,1)S(1)} %copy-done.5, ...), custom_call_target="tpu_custom_call" | custom-call | tf_op jit(solution)/shard_map/pallas_call | solution.py:216
  89.7 15.7 %all_to_all.22.in_ref = f32[64,4,128]{2,1,0:T(4,128)S(1)} all-to-all(f32[64,4,128]{2,1,0:T(4,128)S(1)} %shard_map.188), channel_id=1, replica_groups=mesh['role'=2,'seq'=64,'head'=4] {'seq'}, dimensions={0} | all-to-all | bytes 262144 | tf_op jit(solution)/shard_map/all_to_all | solution.py:278
  105.3 0.7 shard_map.189
  (28 shorter events, 0.1 us)
Async XLA Ops:
  0.6 15.8 %copy-start.14 = (bf16[128,2,128]{2,1,0:T(2,128)(2,1)S(1)}, bf16[128,2,128]{2,1,0:T(2,128)(2,1)}, u32[]{:S(2)}) copy-start(bf16[128,2,128]{2,1,0:T(2,128)(2,1)} %param.18) | copy-start | bytes 196612
  1.5 29.8 %collective-permute-start.3 = (bf16[2,128,128]{2,1,0:T(8,128)(2,1)S(1)}, bf16[2,128,128]{2,1,0:T(8,128)(2,1)S(1)}, u32[]{:S(2)}, u32[]{:S(2)}) collective-permute-start(bf16[2,128,128]{2,1,0:T(8,128)(2,1)S(1)} %pad_maximum_fusion.kv4), channel_id=1, source_target_pairs={{0,32},{4,36},{8,40},{12,44},{16,48},{20,52},{24,56},{28,60},{32,6... | collective-permute-start | bytes 196616 | tf_op jit(solution)/shard_map/ppermute | solution.py:266
  5.5 25.8 %collective-permute-start.2 = (bf16[2,128,128]{2,1,0:T(8,128)(2,1)S(1)}, bf16[2,128,128]{2,1,0:T(8,128)(2,1)S(1)}, u32[]{:S(2)}, u32[]{:S(2)}) collective-permute-start(bf16[2,128,128]{2,1,0:T(8,128)(2,1)S(1)} %pad_maximum_fusion.kv4), channel_id=1, source_target_pairs={{0,64},{4,68},{8,72},{12,76},{16,80},{20,84},{24,88},{28,92},{32,9... | collective-permute-start | bytes 196616 | tf_op jit(solution)/shard_map/ppermute | solution.py:266
  9.7 21.5 %collective-permute-start.1 = (bf16[2,128,128]{2,1,0:T(8,128)(2,1)S(1)}, bf16[2,128,128]{2,1,0:T(8,128)(2,1)S(1)}, u32[]{:S(2)}, u32[]{:S(2)}) collective-permute-start(bf16[2,128,128]{2,1,0:T(8,128)(2,1)S(1)} %pad_maximum_fusion.kv4), channel_id=1, source_target_pairs={{0,96},{4,100},{8,104},{12,108},{16,112},{20,116},{24,120},{28,124... | collective-permute-start | bytes 196616 | tf_op jit(solution)/shard_map/ppermute | solution.py:266
  14.4 16.9 %collective-permute-start = (bf16[2,128,128]{2,1,0:T(8,128)(2,1)S(1)}, bf16[2,128,128]{2,1,0:T(8,128)(2,1)S(1)}, u32[]{:S(2)}, u32[]{:S(2)}) collective-permute-start(bf16[2,128,128]{2,1,0:T(8,128)(2,1)S(1)} %pad_maximum_fusion.kv4), channel_id=1, source_target_pairs={{0,128},{4,132},{8,136},{12,140},{16,144},{20,148},{24,152},{28,15... | collective-permute-start | bytes 196616 | tf_op jit(solution)/shard_map/ppermute | solution.py:266
  34.6 4.0 %copy-start.13 = (bf16[2,128,1024]{2,1,0:T(8,128)(2,1)S(1)}, bf16[2,128,1024]{2,1,0:T(8,128)(2,1)}, u32[]{:S(2)}) copy-start(bf16[2,128,1024]{2,1,0:T(8,128)(2,1)} %param.21) | copy-start | bytes 1572868
  34.6 13.8 %all-to-all-start = ((bf16[8,272,128]{2,1,0:T(8,128)(2,1)}), bf16[8,272,128]{2,1,0:T(8,128)(2,1)S(1)}, u32[]{:S(2)}, u32[]{:S(2)}) async-start(bf16[8,272,128]{2,1,0:T(8,128)(2,1)} %shard_map.185), calls=%async_computation | async-start | bytes 1114112 | tf_op jit(solution)/shard_map/all_to_all | solution.py:272
  49.3 17.8 %copy-start.4 = (f32[128,128]{1,0:T(8,128)S(1)}, f32[128,128]{1,0:T(8,128)}, u32[]{:S(2)}) copy-start(f32[128,128]{1,0:T(8,128)} %taps_ref.1) | copy-start | bytes 196612
  49.3 17.8 %copy-start.9 = (bf16[128,128]{1,0:T(8,128)(2,1)S(1)}, bf16[128,128]{1,0:T(8,128)(2,1)}, u32[]{:S(2)}) copy-start(bf16[128,128]{1,0:T(8,128)(2,1)} %input_ref.1) | copy-start | bytes 98308
  49.3 17.8 %copy-start.10 = (bf16[128,128]{1,0:T(8,128)(2,1)S(1)}, bf16[128,128]{1,0:T(8,128)(2,1)}, u32[]{:S(2)}) copy-start(bf16[128,128]{1,0:T(8,128)(2,1)} %gate_ref.1) | copy-start | bytes 98308
  67.0 19.7 %copy-start.5 = (bf16[144,64]{1,0:T(8,128)(2,1)S(1)}, bf16[144,64]{1,0:T(8,128)(2,1)}, u32[]{:S(2)}) copy-start(bf16[144,64]{1,0:T(8,128)(2,1)} %constant.23.clone.f1) | copy-start | bytes 55300
  67.1 19.7 %copy-start.6 = (bf16[144,64]{1,0:T(8,128)(2,1)S(1)}, bf16[144,64]{1,0:T(8,128)(2,1)}, u32[]{:S(2)}) copy-start(bf16[144,64]{1,0:T(8,128)(2,1)} %constant.22.clone.f0) | copy-start | bytes 55300
  67.1 19.7 %copy-start.7 = (f32[72,128]{1,0:T(8,128)S(1)}, f32[72,128]{1,0:T(8,128)}, u32[]{:S(2)}) copy-start(f32[72,128]{1,0:T(8,128)} %constant.21.clone.ts) | copy-start | bytes 110596
  67.1 19.7 %copy-start.8 = (f32[72,128]{1,0:T(8,128)S(1)}, f32[72,128]{1,0:T(8,128)}, u32[]{:S(2)}) copy-start(f32[72,128]{1,0:T(8,128)} %constant.20.clone.tc) | copy-start | bytes 110596
  67.1 19.7 %copy-start.11 = (bf16[64,144]{1,0:T(8,128)(2,1)S(1)}, bf16[64,144]{1,0:T(8,128)(2,1)}, u32[]{:S(2)}) copy-start(bf16[64,144]{1,0:T(8,128)(2,1)} %constant.25.clone.l1) | copy-start | bytes 55300
  67.1 19.7 %copy-start.12 = (bf16[64,144]{1,0:T(8,128)(2,1)S(1)}, bf16[64,144]{1,0:T(8,128)(2,1)}, u32[]{:S(2)}) copy-start(bf16[64,144]{1,0:T(8,128)(2,1)} %constant.24.clone.l0) | copy-start | bytes 55300
  67.3 19.5 %copy-start = (bf16[256,256]{1,0:T(8,128)(2,1)S(1)}, bf16[256,256]{1,0:T(8,128)(2,1)}, u32[]{:S(2)}) copy-start(bf16[256,256]{1,0:T(8,128)(2,1)} %constant.29.clone.b1) | copy-start | bytes 393220
  67.3 19.5 %copy-start.1 = (bf16[256,256]{1,0:T(8,128)(2,1)S(1)}, bf16[256,256]{1,0:T(8,128)(2,1)}, u32[]{:S(2)}) copy-start(bf16[256,256]{1,0:T(8,128)(2,1)} %constant.28.clone.b0) | copy-start | bytes 393220
  67.3 19.5 %copy-start.2 = (bf16[256,256]{1,0:T(8,128)(2,1)S(1)}, bf16[256,256]{1,0:T(8,128)(2,1)}, u32[]{:S(2)}) copy-start(bf16[256,256]{1,0:T(8,128)(2,1)} %constant.27.clone.w1) | copy-start | bytes 393220
  67.3 19.5 %copy-start.3 = (bf16[256,256]{1,0:T(8,128)(2,1)S(1)}, bf16[256,256]{1,0:T(8,128)(2,1)}, u32[]{:S(2)}) copy-start(bf16[256,256]{1,0:T(8,128)(2,1)} %constant.26.clone.w0) | copy-start | bytes 393220

commit v4 on v3

--- a/solution.py
+++ b/solution.py
@@ -129,13 +129,14 @@
         step_ref[c * SHARDS : (c + 1) * SHARDS, :] = in_ref[:, 2 + c, :]
 
 
-def attend_kernel(q_ref, kv0, kv1, kv2, kv3, kv4, out_ref):
+def attend_kernel(q_ref, kv_ref, out_ref):
     rank = lax.axis_index("seq")
     row, mine = rank // ROW, rank % ROW
     scale = 128 ** -0.5
-    keys = jnp.concatenate([ref[0] for ref in (kv4, kv0, kv1, kv2, kv3)], 0)
+    order = [row] + [jnp.maximum(row - BACK + r, 0) for r in range(BACK)]
+    keys = jnp.concatenate([kv_ref[n, 0] for n in order], 0)
     ones = jnp.ones((5 * SHARD, 128), jnp.bfloat16)
-    values = jnp.concatenate([jnp.concatenate([ref[1] for ref in (kv4, kv0, kv1, kv2, kv3)], 0), ones], 1)
+    values = jnp.concatenate([jnp.concatenate([kv_ref[n, 1] for n in order], 0), ones], 1)
     lag = lax.broadcasted_iota(jnp.int32, (SHARD, SHARD), 0) - lax.broadcasted_iota(jnp.int32, (SHARD, SHARD), 1)
     diagonal = lag == 0
     zero = jnp.zeros((SHARD, SHARD), jnp.float32)
@@ -230,13 +231,13 @@
     )(near(out))
 
 
-def call_attend(queries, blocks):
+def call_attend(queries, pairs):
     return pl.pallas_call(
         attend_kernel,
         out_shape=pltpu.VMEM((ROW, 272, 128), jnp.bfloat16),
-        in_specs=[VMEM] * 6,
-        out_specs=VMEM,
-    )(near(queries), *[near(b) for b in blocks])
+        in_specs=[VMEM] * 2,
+        out_specs=VMEM,
+    )(near(queries), near(pairs))
 
 
 def call_merge(parts, proj):
@@ -261,14 +262,13 @@
     tables = [near(jnp.asarray(t)) for t in transform_tables()]
     rows = [[y * ROW + p for p in range(ROW)] for y in range(SHARDS // ROW)]
 
+    columns = [[y * ROW + p for y in range(SHARDS // ROW)] for p in range(ROW)]
     own = jnp.stack([key_heads[:, 0], value_heads[:, 0]])
-    blocks = [
-        lax.ppermute(own, "seq", [(i, i + ROW * k) for i in range(SHARDS - ROW * k)])
-        for k in range(BACK, 0, -1)
-    ] + [own]
+    pairs = jnp.broadcast_to(own, (SHARDS // ROW,) + own.shape)
+    pairs = lax.all_to_all(pairs, "seq", 0, 0, axis_index_groups=columns)
     queries = lax.all_gather(jnp.transpose(query_heads, (1, 0, 2)), "seq", axis_index_groups=rows)
     proj = distill_proj.reshape(256, 1024).T
-    parts = call_attend(queries, blocks)
+    parts = call_attend(queries, pairs)
     parts = lax.all_to_all(parts, "seq", 0, 0, axis_index_groups=rows)
     target = call_merge(parts, proj)
     target = lax.all_to_all(target, ("role", "head"), 0, 0)

time: 107 us -> 105 us (0.981)
  starting transfers between devices: 18.9 us -> 15 us
  blocking collectives: 67.6 us -> 68.7 us
    ppermute x4 -> x0, starting transfers between devices: 14.9 us -> none  [body(): lax.ppermute(own, 'seq', [(i, i + ROW * k) for i in range(SHARDS - ROW *...]
    all_to_all x0 -> x1, starting transfers between devices: none -> 7.78 us  [body(): pairs = lax.all_to_all(pairs, 'seq', 0, 0, axis_index_groups=columns)]
    all_to_all x1, starting transfers between devices: 3.97 us -> 7.17 us  [body(): parts = lax.all_to_all(parts, 'seq', 0, 0, axis_index_groups=rows)]
  transfers between devices with their start and end apart: 5 -> 2, of which waited for: 1 -> 1; matrix products, arithmetic and copies ran while one was open for 0% -> 0% of each run, Pallas kernels for 0% -> 0%
where the time goes in v4:
time: 105 us; the launch traced here: 104 us
  blocking collectives  68.7 us (65%)
  starting transfers between devices  15 us (14%)
  waiting for transfers between devices  9.63 us (9%)
  Pallas kernels  7.9 us (8%)
  local copies, waits for them, and re-layouts  1.22 us (1%)
    all_to_all x1, blocking collectives, body(): packed = lax.all_to_all(packed, 'seq', 0, 0)  19.6 us
    all_to_all x1, blocking collectives, body(): target = lax.all_to_all(target, ('role', 'head'), 0, 0)  17.7 us
    all_gather x1, blocking collectives, body(): lax.all_gather(jnp.transpose(query_heads, (1, 0, 2)), 'seq', axis_index_g...  15.7 us
    all_to_all x1, blocking collectives, body(): out = lax.all_to_all(out, 'seq', 0, 0)  15.6 us
    all_to_all x1, waiting for transfers between devices, body(): parts = lax.all_to_all(parts, 'seq', 0, 0, axis_index_groups=rows)  9.62 us
    all_to_all x1, starting transfers between devices, body(): pairs = lax.all_to_all(pairs, 'seq', 0, 0, axis_index_groups=columns)  7.78 us
    all_to_all x1, starting transfers between devices, body(): parts = lax.all_to_all(parts, 'seq', 0, 0, axis_index_groups=rows)  7.17 us
    pallas_call x1, Pallas kernels, call_attend(): pl.pallas_call(attend_kernel, out_shape=pltpu.VMEM((ROW, 272, 128), jnp.b...  3.35 us
  transfers between devices with their start and end apart: 2, of which 1 were waited for; matrix products, arithmetic and copies ran while one was open for 0% of the time, Pallas kernels for 0%

profile of v4, /device:TPU:1, one launch (start us, length us, event | category | flops | bytes accessed | tf_op | source)
XLA Modules:
  0.0 104.0 jit_solution(10040277030201406890)
XLA Ops:
  0.6 0.8 pad_maximum_fusion
  1.4 0.9 broadcast_in_dim.3
  2.3 7.8 %all-to-all-start = ((bf16[8,2,128,128]{3,2,1,0:T(8,128)(2,1)}), bf16[8,2,128,128]{3,2,1,0:T(8,128)(2,1)S(1)}, u32[]{:S(2)}, u32[]{:S(2)}) async-start(bf16[8,2,128,128]{3,2,1,0:T(8,128)(2,1)} %broadcast_in_dim.3), calls=%async_computation | async-start | bytes 1048576 | tf_op jit(solution)/shard_map/all_to_all | solution.py:268
  10.1 15.7 %all-gather = bf16[16,128,128]{2,1,0:T(8,128)(2,1)S(1)} all-gather(bf16[2,128,128]{2,1,0:T(8,128)(2,1)S(1)} %bitcast.11), channel_id=2, replica_groups={{0,4,8,12,16,20,24,28},{32,36,40,44,48,52,56,60},{64,68,72,76,80,84,88,..., dimensions={0}, use_global_device_ids=true | all-gather | bytes 589824 | tf_op jit(solution)/shard_map/all_gather | solution.py:269
  25.8 3.3 %shard_map.185 = bf16[8,272,128]{2,1,0:T(8,128)(2,1)} custom-call(bf16[8,2,128,128]{3,2,1,0:T(8,128)(2,1)S(1)} %bitcast.8, bf16[8,2,128,128]{3,2,1,0:T(8,128)(2,1)S(1)} %all-to-all-done.kv_ref), custom_call_target="tpu_custom_call" | custom-call | tf_op jit(solution)/shard_map/pallas_call | solution.py:235
  29.2 7.2 %all-to-all-start.1 = ((bf16[8,272,128]{2,1,0:T(8,128)(2,1)}), bf16[8,272,128]{2,1,0:T(8,128)(2,1)S(1)}, u32[]{:S(2)}, u32[]{:S(2)}) async-start(bf16[8,272,128]{2,1,0:T(8,128)(2,1)} %shard_map.185), calls=%async_computation.1 | async-start | bytes 1114112 | tf_op jit(solution)/shard_map/all_to_all | solution.py:272
  36.3 0.2 copy.24
  36.5 9.6 %all-to-all-done.1.parts_ref = bf16[8,272,128]{2,1,0:T(8,128)(2,1)S(1)} async-done(((bf16[8,272,128]{2,1,0:T(8,128)(2,1)}), bf16[8,272,128]{2,1,0:T(8,128)(2,1)S(1)}, u32[]{:S(2)}, u32[]{:S(2)}) %all-to-all-start.1) | async-done | bytes 557088 | tf_op jit(solution)/shard_map/all_to_all | solution.py:272
  46.2 0.9 shard_map.186
  47.1 17.7 %all_to_all.25.parts_ref = bf16[8,128,128]{2,1,0:T(8,128)(2,1)S(1)} all-to-all(bf16[8,128,128]{2,1,0:T(8,128)(2,1)S(1)} %shard_map.186), channel_id=1, replica_groups=mesh['role'=2,'seq'=64,'head'=4] {'role','head'}, dimensions={0} | all-to-all | bytes 524288 | tf_op jit(solution)/shard_map/all_to_all | solution.py:274
  64.8 0.0 copy-start.5
  64.8 0.0 copy-start.6
  64.8 0.0 copy-start.7
  64.9 0.0 copy-start.8
  64.9 0.0 copy-start.11
  64.9 0.0 copy-start.12
  64.9 0.2 shard_map.187
  65.1 0.0 copy-start
  65.1 0.0 copy-start.1
  65.1 0.0 copy-start.2
  65.1 19.6 %all_to_all.26.in_ref = f32[64,8,128]{2,1,0:T(8,128)S(1)} all-to-all(f32[64,8,128]{2,1,0:T(8,128)S(1)} %shard_map.187), channel_id=1, replica_groups=mesh['role'=2,'seq'=64,'head'=4] {'seq'}, dimensions={0} | all-to-all | bytes 524288 | tf_op jit(solution)/shard_map/all_to_all | solution.py:276
  84.8 2.8 %shard_map.188 = f32[64,4,128]{2,1,0:T(4,128)S(1)} custom-call(f32[128]{0:T(128)} %skip_ref.1, f32[64,8,128]{2,1,0:T(8,128)S(1)} %all_to_all.26.in_ref, f32[72,128]{1,0:T(8,128)S(1)} %copy-done.8, f32[72,128]{1,0:T(8,128)S(1)} %copy-done.7, bf16[144,64]{1,0:T(8,128)(2,1)S(1)} %copy-done.6, bf16[144,64]{1,0:T(8,128)(2,1)S(1)} %copy-done.5, ...), custom_call_target="tpu_custom_call" | custom-call | tf_op jit(solution)/shard_map/pallas_call | solution.py:217
  87.7 15.6 %all_to_all.27.in_ref = f32[64,4,128]{2,1,0:T(4,128)S(1)} all-to-all(f32[64,4,128]{2,1,0:T(4,128)S(1)} %shard_map.188), channel_id=1, replica_groups=mesh['role'=2,'seq'=64,'head'=4] {'seq'}, dimensions={0} | all-to-all | bytes 262144 | tf_op jit(solution)/shard_map/all_to_all | solution.py:278
  103.3 0.7 shard_map.189
  (23 shorter events, 0.1 us)
Async XLA Ops:
  2.3 7.8 %copy-start.14 = (bf16[128,2,128]{2,1,0:T(2,128)(2,1)S(1)}, bf16[128,2,128]{2,1,0:T(2,128)(2,1)}, u32[]{:S(2)}) copy-start(bf16[128,2,128]{2,1,0:T(2,128)(2,1)} %param.18) | copy-start | bytes 196612
  2.3 23.5 %all-to-all-start = ((bf16[8,2,128,128]{3,2,1,0:T(8,128)(2,1)}), bf16[8,2,128,128]{3,2,1,0:T(8,128)(2,1)S(1)}, u32[]{:S(2)}, u32[]{:S(2)}) async-start(bf16[8,2,128,128]{3,2,1,0:T(8,128)(2,1)} %broadcast_in_dim.3), calls=%async_computation | async-start | bytes 1048576 | tf_op jit(solution)/shard_map/all_to_all | solution.py:268
  29.2 7.2 %copy-start.13 = (bf16[2,128,1024]{2,1,0:T(8,128)(2,1)S(1)}, bf16[2,128,1024]{2,1,0:T(8,128)(2,1)}, u32[]{:S(2)}) copy-start(bf16[2,128,1024]{2,1,0:T(8,128)(2,1)} %param.21) | copy-start | bytes 1572868
  29.2 17.0 %all-to-all-start.1 = ((bf16[8,272,128]{2,1,0:T(8,128)(2,1)}), bf16[8,272,128]{2,1,0:T(8,128)(2,1)S(1)}, u32[]{:S(2)}, u32[]{:S(2)}) async-start(bf16[8,272,128]{2,1,0:T(8,128)(2,1)} %shard_map.185), calls=%async_computation.1 | async-start | bytes 1114112 | tf_op jit(solution)/shard_map/all_to_all | solution.py:272
  47.0 17.8 %copy-start.4 = (f32[128,128]{1,0:T(8,128)S(1)}, f32[128,128]{1,0:T(8,128)}, u32[]{:S(2)}) copy-start(f32[128,128]{1,0:T(8,128)} %taps_ref.1) | copy-start | bytes 196612
  47.0 17.8 %copy-start.9 = (bf16[128,128]{1,0:T(8,128)(2,1)S(1)}, bf16[128,128]{1,0:T(8,128)(2,1)}, u32[]{:S(2)}) copy-start(bf16[128,128]{1,0:T(8,128)(2,1)} %input_ref.1) | copy-start | bytes 98308
  47.1 17.8 %copy-start.10 = (bf16[128,128]{1,0:T(8,128)(2,1)S(1)}, bf16[128,128]{1,0:T(8,128)(2,1)}, u32[]{:S(2)}) copy-start(bf16[128,128]{1,0:T(8,128)(2,1)} %gate_ref.1) | copy-start | bytes 98308
  64.8 19.9 %copy-start.5 = (bf16[144,64]{1,0:T(8,128)(2,1)S(1)}, bf16[144,64]{1,0:T(8,128)(2,1)}, u32[]{:S(2)}) copy-start(bf16[144,64]{1,0:T(8,128)(2,1)} %constant.23.clone.f1) | copy-start | bytes 55300
  64.8 19.9 %copy-start.6 = (bf16[144,64]{1,0:T(8,128)(2,1)S(1)}, bf16[144,64]{1,0:T(8,128)(2,1)}, u32[]{:S(2)}) copy-start(bf16[144,64]{1,0:T(8,128)(2,1)} %constant.22.clone.f0) | copy-start | bytes 55300
  64.8 19.9 %copy-start.7 = (f32[72,128]{1,0:T(8,128)S(1)}, f32[72,128]{1,0:T(8,128)}, u32[]{:S(2)}) copy-start(f32[72,128]{1,0:T(8,128)} %constant.21.clone.ts) | copy-start | bytes 110596
  64.9 19.9 %copy-start.8 = (f32[72,128]{1,0:T(8,128)S(1)}, f32[72,128]{1,0:T(8,128)}, u32[]{:S(2)}) copy-start(f32[72,128]{1,0:T(8,128)} %constant.20.clone.tc) | copy-start | bytes 110596
  64.9 19.9 %copy-start.11 = (bf16[64,144]{1,0:T(8,128)(2,1)S(1)}, bf16[64,144]{1,0:T(8,128)(2,1)}, u32[]{:S(2)}) copy-start(bf16[64,144]{1,0:T(8,128)(2,1)} %constant.25.clone.l1) | copy-start | bytes 55300
  64.9 19.9 %copy-start.12 = (bf16[64,144]{1,0:T(8,128)(2,1)S(1)}, bf16[64,144]{1,0:T(8,128)(2,1)}, u32[]{:S(2)}) copy-start(bf16[64,144]{1,0:T(8,128)(2,1)} %constant.24.clone.l0) | copy-start | bytes 55300
  65.1 19.7 %copy-start = (bf16[256,256]{1,0:T(8,128)(2,1)S(1)}, bf16[256,256]{1,0:T(8,128)(2,1)}, u32[]{:S(2)}) copy-start(bf16[256,256]{1,0:T(8,128)(2,1)} %constant.29.clone.b1) | copy-start | bytes 393220
  65.1 19.7 %copy-start.1 = (bf16[256,256]{1,0:T(8,128)(2,1)S(1)}, bf16[256,256]{1,0:T(8,128)(2,1)}, u32[]{:S(2)}) copy-start(bf16[256,256]{1,0:T(8,128)(2,1)} %constant.28.clone.b0) | copy-start | bytes 393220
  65.1 19.7 %copy-start.2 = (bf16[256,256]{1,0:T(8,128)(2,1)S(1)}, bf16[256,256]{1,0:T(8,128)(2,1)}, u32[]{:S(2)}) copy-start(bf16[256,256]{1,0:T(8,128)(2,1)} %constant.27.clone.w1) | copy-start | bytes 393220
  65.1 19.7 %copy-start.3 = (bf16[256,256]{1,0:T(8,128)(2,1)S(1)}, bf16[256,256]{1,0:T(8,128)(2,1)}, u32[]{:S(2)}) copy-start(bf16[256,256]{1,0:T(8,128)(2,1)} %constant.26.clone.w0) | copy-start | bytes 393220

commit v5 on v4

--- a/solution.py
+++ b/solution.py
@@ -89,21 +89,29 @@
     return jnp.concatenate([ar * br + ai * bi, ar * bi - ai * br], 1)
 
 
-def pack_kernel(parts_ref, input_ref, gate_ref, taps_ref, out_ref):
+def repeat_kernel(key_ref, value_ref, out_ref):
+    for n in range(SHARDS // ROW):
+        out_ref[n, 0] = key_ref[...]
+        out_ref[n, 1] = value_ref[...]
+
+
+def pack_kernel(parts_ref, input_ref, gate_ref, taps_ref, out_ref, wide_ref):
     target = parts_ref[0].astype(jnp.float32)
     for n in range(1, 8):
         target += parts_ref[n].astype(jnp.float32)
     arrays = (target, input_ref[...], gate_ref[...], taps_ref[...])
     for n, array in enumerate(arrays):
         array = array.astype(jnp.float32)
-        out_ref[:, 2 * n, :] = array[:SHARDS]
-        out_ref[:, 2 * n + 1, :] = array[SHARDS:]
-
-
-def student_kernel(skip_ref, in_ref, tc, ts, f0, f1, l0, l1, w0, w1, b0, b1, out_ref):
+        wide_ref[:, 2 * n, :] = array[:SHARDS]
+        wide_ref[:, 2 * n + 1, :] = array[SHARDS:]
+    out_ref[...] = wide_ref[...].astype(jnp.bfloat16)
+
+
+def student_kernel(skip_ref, in_ref, tc, ts, f0, f1, l0, l1, w0, w1, b0, b1, out_ref, wide_in, wide_out):
+    wide_in[...] = in_ref[...].astype(jnp.float32)
     rank = lax.axis_index("seq")
     skip = [skip_ref[rank], skip_ref[rank + SHARDS]]
-    target, signal, gate, taps = [[in_ref[:, 2 * n + c, :] for c in (0, 1)] for n in range(4)]
+    target, signal, gate, taps = [[wide_in[:, 2 * n + c, :] for c in (0, 1)] for n in range(4)]
     turn = tc[...], ts[...]
     ahead = (f0[...], f1[...]), *turn, (w0[...], w1[...])
     behind = (l0[...], l1[...]), *turn, (b0[...], b1[...])
@@ -119,14 +127,16 @@
     signals = to_signals(mixed, *behind)
     scale = (SHARDS * SHARD) ** -0.5
     for c in (0, 1):
-        out_ref[:, c, :] = skip[c] * back[c] + signals[:, c * 128 : (c + 1) * 128]
-        out_ref[:, 2 + c, :] = scale * signals[:, (2 + c) * 128 : (3 + c) * 128]
-
-
-def unpack_kernel(in_ref, grad_ref, step_ref):
+        wide_out[:, c, :] = skip[c] * back[c] + signals[:, c * 128 : (c + 1) * 128]
+        wide_out[:, 2 + c, :] = scale * signals[:, (2 + c) * 128 : (3 + c) * 128]
+    out_ref[...] = wide_out[...].astype(jnp.bfloat16)
+
+
+def unpack_kernel(in_ref, grad_ref, step_ref, wide_ref):
+    wide_ref[...] = in_ref[...].astype(jnp.float32)
     for c in (0, 1):
-        grad_ref[c * SHARDS : (c + 1) * SHARDS, :] = in_ref[:, c, :]
-        step_ref[c * SHARDS : (c + 1) * SHARDS, :] = in_ref[:, 2 + c, :]
+        grad_ref[c * SHARDS : (c + 1) * SHARDS, :] = wide_ref[:, c, :]
+        step_ref[c * SHARDS : (c + 1) * SHARDS, :] = wide_ref[:, 2 + c, :]
 
 
 def attend_kernel(q_ref, kv_ref, out_ref):
@@ -204,21 +214,32 @@
     return pltpu.with_memory_space_constraint(x, pltpu.VMEM)
 
 
+def call_repeat(key, value):
+    return pl.pallas_call(
+        repeat_kernel,
+        out_shape=pltpu.VMEM((SHARDS // ROW, 2, SHARD, 128), jnp.bfloat16),
+        in_specs=[VMEM] * 2,
+        out_specs=VMEM,
+    )(key, value)
+
+
 def call_pack(parts, *inputs):
     return pl.pallas_call(
         pack_kernel,
-        out_shape=pltpu.VMEM((SHARDS, 8, 128), jnp.float32),
+        out_shape=pltpu.VMEM((SHARDS, 8, 128), jnp.bfloat16),
         in_specs=[VMEM] * 4,
         out_specs=VMEM,
+        scratch_shapes=[pltpu.VMEM((SHARDS, 8, 128), jnp.float32)],
     )(near(parts), *[near(x) for x in inputs])
 
 
 def call_student(skip, packed, tables):
     return pl.pallas_call(
         student_kernel,
-        out_shape=pltpu.VMEM((SHARDS, 4, 128), jnp.float32),
+        out_shape=pltpu.VMEM((SHARDS, 4, 128), jnp.bfloat16),
         in_specs=[SMEM] + [VMEM] * 11,
         out_specs=VMEM,
+        scratch_shapes=[pltpu.VMEM((SHARDS, 8, 128), jnp.float32), pltpu.VMEM((SHARDS, 4, 128), jnp.float32)],
     )(skip, near(packed), *tables)
 
 
@@ -228,6 +249,7 @@
         out_shape=(jax.ShapeDtypeStruct((128, 128), jnp.float32),) * 2,
         in_specs=[VMEM],
         out_specs=(VMEM,) * 2,
+        scratch_shapes=[pltpu.VMEM((SHARDS, 4, 128), jnp.float32)],
     )(near(out))
 
 
@@ -263,8 +285,7 @@
     rows = [[y * ROW + p for p in range(ROW)] for y in range(SHARDS // ROW)]
 
     columns = [[y * ROW + p for y in range(SHARDS // ROW)] for p in range(ROW)]
-    own = jnp.stack([key_heads[:, 0], value_heads[:, 0]])
-    pairs = jnp.broadcast_to(own, (SHARDS // ROW,) + own.shape)
+    pairs = call_repeat(key_heads[:, 0], value_heads[:, 0])
     pairs = lax.all_to_all(pairs, "seq", 0, 0, axis_index_groups=columns)
     queries = lax.all_gather(jnp.transpose(query_heads, (1, 0, 2)), "seq", axis_index_groups=rows)
     proj = distill_proj.reshape(256, 1024).T

time: 105 us -> 101 us (0.962)
  blocking collectives: 68.7 us -> 64.9 us
  Pallas kernels: 7.9 us -> 9.62 us
    all_to_all x1, blocking collectives: 19.6 us -> 17.6 us  [body(): packed = lax.all_to_all(packed, 'seq', 0, 0)]
    all_to_all x1, blocking collectives: 15.6 us -> 13.9 us  [body(): out = lax.all_to_all(out, 'seq', 0, 0)]
    pallas_call x1 -> x2, Pallas kernels: 0.17 us -> 1.85 us  [the longest x1 1.65 us: call_repeat(): pl.pallas_call(repeat_kernel, out_shape=pltpu.VMEM((SHARDS // ROW, 2, SHA...]
where the time goes in v5:
time: 101 us; the launch traced here: 100 us
  blocking collectives  64.9 us (64%)
  starting transfers between devices  14.9 us (15%)
  waiting for transfers between devices  9.63 us (10%)
  Pallas kernels  9.62 us (10%)
    all_to_all x1, blocking collectives, body(): target = lax.all_to_all(target, ('role', 'head'), 0, 0)  17.7 us
    all_to_all x1, blocking collectives, body(): packed = lax.all_to_all(packed, 'seq', 0, 0)  17.6 us
    all_gather x1, blocking collectives, body(): lax.all_gather(jnp.transpose(query_heads, (1, 0, 2)), 'seq', axis_index_g...  15.7 us
    all_to_all x1, blocking collectives, body(): out = lax.all_to_all(out, 'seq', 0, 0)  13.9 us
    all_to_all x1, waiting for transfers between devices, body(): parts = lax.all_to_all(parts, 'seq', 0, 0, axis_index_groups=rows)  9.62 us
    all_to_all x1, starting transfers between devices, body(): pairs = lax.all_to_all(pairs, 'seq', 0, 0, axis_index_groups=columns)  7.78 us
    all_to_all x1, starting transfers between devices, body(): parts = lax.all_to_all(parts, 'seq', 0, 0, axis_index_groups=rows)  7.17 us
    pallas_call x1, Pallas kernels, call_attend(): pl.pallas_call(attend_kernel, out_shape=pltpu.VMEM((ROW, 272, 128), jnp.b...  3.35 us
  transfers between devices with their start and end apart: 2, of which 1 were waited for; matrix products, arithmetic and copies ran while one was open for 0% of the time, Pallas kernels for 0%

profile of v5, /device:TPU:1, one launch (start us, length us, event | category | flops | bytes accessed | tf_op | source)
XLA Modules:
  0.0 100.3 jit_solution(2896353549544278381)
XLA Ops:
  0.6 1.7 %shard_map.185 = bf16[8,2,128,128]{3,2,1,0:T(8,128)(2,1)} custom-call(bf16[128,128]{1,0:T(8,128)(2,1)} %bitcast.12, bf16[128,128]{1,0:T(8,128)(2,1)} %bitcast.13), custom_call_target="tpu_custom_call" | custom-call | tf_op jit(solution)/shard_map/pallas_call | solution.py:218
  2.3 7.8 %all-to-all-start = ((bf16[8,2,128,128]{3,2,1,0:T(8,128)(2,1)}), bf16[8,2,128,128]{3,2,1,0:T(8,128)(2,1)S(1)}, u32[]{:S(2)}, u32[]{:S(2)}) async-start(bf16[8,2,128,128]{3,2,1,0:T(8,128)(2,1)} %shard_map.185), calls=%async_computation | async-start | bytes 1048576 | tf_op jit(solution)/shard_map/all_to_all | solution.py:289
  10.1 15.7 %all-gather = bf16[16,128,128]{2,1,0:T(8,128)(2,1)S(1)} all-gather(bf16[2,128,128]{2,1,0:T(8,128)(2,1)S(1)} %bitcast.11), channel_id=2, replica_groups={{0,4,8,12,16,20,24,28},{32,36,40,44,48,52,56,60},{64,68,72,76,80,84,88,..., dimensions={0}, use_global_device_ids=true | all-gather | bytes 589824 | tf_op jit(solution)/shard_map/all_gather | solution.py:290
  25.8 3.3 %shard_map.186 = bf16[8,272,128]{2,1,0:T(8,128)(2,1)} custom-call(bf16[8,2,128,128]{3,2,1,0:T(8,128)(2,1)S(1)} %bitcast.8, bf16[8,2,128,128]{3,2,1,0:T(8,128)(2,1)S(1)} %all-to-all-done.kv_ref), custom_call_target="tpu_custom_call" | custom-call | tf_op jit(solution)/shard_map/pallas_call | solution.py:257
  29.1 7.2 %all-to-all-start.1 = ((bf16[8,272,128]{2,1,0:T(8,128)(2,1)}), bf16[8,272,128]{2,1,0:T(8,128)(2,1)S(1)}, u32[]{:S(2)}, u32[]{:S(2)}) async-start(bf16[8,272,128]{2,1,0:T(8,128)(2,1)} %shard_map.186), calls=%async_computation.1 | async-start | bytes 1114112 | tf_op jit(solution)/shard_map/all_to_all | solution.py:293
  36.3 0.2 copy.24
  36.5 9.6 %all-to-all-done.1.parts_ref = bf16[8,272,128]{2,1,0:T(8,128)(2,1)S(1)} async-done(((bf16[8,272,128]{2,1,0:T(8,128)(2,1)}), bf16[8,272,128]{2,1,0:T(8,128)(2,1)S(1)}, u32[]{:S(2)}, u32[]{:S(2)}) %all-to-all-start.1) | async-done | bytes 557088 | tf_op jit(solution)/shard_map/all_to_all | solution.py:293
  46.1 0.9 shard_map.187
  47.0 17.7 %all_to_all.25.parts_ref = bf16[8,128,128]{2,1,0:T(8,128)(2,1)S(1)} all-to-all(bf16[8,128,128]{2,1,0:T(8,128)(2,1)S(1)} %shard_map.187), channel_id=1, replica_groups=mesh['role'=2,'seq'=64,'head'=4] {'role','head'}, dimensions={0} | all-to-all | bytes 524288 | tf_op jit(solution)/shard_map/all_to_all | solution.py:295
  64.8 0.0 copy-start.2
  64.8 0.0 copy-start.3
  64.8 0.0 copy-start.5
  64.8 0.0 copy-start.6
  64.8 0.0 copy-start.7
  64.8 0.0 copy-start.8
  64.9 0.0 copy-start.11
  64.9 0.0 copy-start.12
  64.9 0.2 shard_map.188
  65.1 0.0 copy-start
  65.1 0.0 copy-start.1
  65.1 17.6 %all_to_all.26.in_ref = bf16[64,8,128]{2,1,0:T(8,128)(2,1)S(1)} all-to-all(bf16[64,8,128]{2,1,0:T(8,128)(2,1)S(1)} %shard_map.188), channel_id=1, replica_groups=mesh['role'=2,'seq'=64,'head'=4] {'seq'}, dimensions={0} | all-to-all | bytes 262144 | tf_op jit(solution)/shard_map/all_to_all | solution.py:297
  82.8 2.8 %shard_map.189 = bf16[64,4,128]{2,1,0:T(4,128)(2,1)S(1)} custom-call(f32[128]{0:T(128)} %skip_ref.1, bf16[64,8,128]{2,1,0:T(8,128)(2,1)S(1)} %all_to_all.26.in_ref, f32[72,128]{1,0:T(8,128)S(1)} %copy-done.8, f32[72,128]{1,0:T(8,128)S(1)} %copy-done.7, bf16[144,64]{1,0:T(8,128)(2,1)S(1)} %copy-done.6, bf16[144,64]{1,0:T(8,128)(2,1)S(1)} %copy-done.5, ...), custom_call_target="tpu_custom_call" | custom-call | tf_op jit(solution)/shard_map/pallas_call | solution.py:237
  85.6 13.9 %all_to_all.27.in_ref = bf16[64,4,128]{2,1,0:T(4,128)(2,1)S(1)} all-to-all(bf16[64,4,128]{2,1,0:T(4,128)(2,1)S(1)} %shard_map.189), channel_id=1, replica_groups=mesh['role'=2,'seq'=64,'head'=4] {'seq'}, dimensions={0} | all-to-all | bytes 131072 | tf_op jit(solution)/shard_map/all_to_all | solution.py:299
  99.5 0.7 shard_map.190
  (22 shorter events, 0.1 us)
Async XLA Ops:
  2.3 7.8 %copy-start.14 = (bf16[128,2,128]{2,1,0:T(2,128)(2,1)S(1)}, bf16[128,2,128]{2,1,0:T(2,128)(2,1)}, u32[]{:S(2)}) copy-start(bf16[128,2,128]{2,1,0:T(2,128)(2,1)} %param.18) | copy-start | bytes 196612
  2.3 23.5 %all-to-all-start = ((bf16[8,2,128,128]{3,2,1,0:T(8,128)(2,1)}), bf16[8,2,128,128]{3,2,1,0:T(8,128)(2,1)S(1)}, u32[]{:S(2)}, u32[]{:S(2)}) async-start(bf16[8,2,128,128]{3,2,1,0:T(8,128)(2,1)} %shard_map.185), calls=%async_computation | async-start | bytes 1048576 | tf_op jit(solution)/shard_map/all_to_all | solution.py:289
  29.1 7.2 %copy-start.13 = (bf16[2,128,1024]{2,1,0:T(8,128)(2,1)S(1)}, bf16[2,128,1024]{2,1,0:T(8,128)(2,1)}, u32[]{:S(2)}) copy-start(bf16[2,128,1024]{2,1,0:T(8,128)(2,1)} %param.21) | copy-start | bytes 1572868
  29.1 17.0 %all-to-all-start.1 = ((bf16[8,272,128]{2,1,0:T(8,128)(2,1)}), bf16[8,272,128]{2,1,0:T(8,128)(2,1)S(1)}, u32[]{:S(2)}, u32[]{:S(2)}) async-start(bf16[8,272,128]{2,1,0:T(8,128)(2,1)} %shard_map.186), calls=%async_computation.1 | async-start | bytes 1114112 | tf_op jit(solution)/shard_map/all_to_all | solution.py:293
  47.0 17.8 %copy-start.4 = (f32[128,128]{1,0:T(8,128)S(1)}, f32[128,128]{1,0:T(8,128)}, u32[]{:S(2)}) copy-start(f32[128,128]{1,0:T(8,128)} %taps_ref.1) | copy-start | bytes 196612
  47.0 17.8 %copy-start.9 = (bf16[128,128]{1,0:T(8,128)(2,1)S(1)}, bf16[128,128]{1,0:T(8,128)(2,1)}, u32[]{:S(2)}) copy-start(bf16[128,128]{1,0:T(8,128)(2,1)} %input_ref.1) | copy-start | bytes 98308
  47.0 17.8 %copy-start.10 = (bf16[128,128]{1,0:T(8,128)(2,1)S(1)}, bf16[128,128]{1,0:T(8,128)(2,1)}, u32[]{:S(2)}) copy-start(bf16[128,128]{1,0:T(8,128)(2,1)} %gate_ref.1) | copy-start | bytes 98308
  64.8 17.9 %copy-start.2 = (bf16[256,256]{1,0:T(8,128)(2,1)S(1)}, bf16[256,256]{1,0:T(8,128)(2,1)}, u32[]{:S(2)}) copy-start(bf16[256,256]{1,0:T(8,128)(2,1)} %constant.27.clone.w1) | copy-start | bytes 393220
  64.8 17.9 %copy-start.3 = (bf16[256,256]{1,0:T(8,128)(2,1)S(1)}, bf16[256,256]{1,0:T(8,128)(2,1)}, u32[]{:S(2)}) copy-start(bf16[256,256]{1,0:T(8,128)(2,1)} %constant.26.clone.w0) | copy-start | bytes 393220
  64.8 17.9 %copy-start.5 = (bf16[144,64]{1,0:T(8,128)(2,1)S(1)}, bf16[144,64]{1,0:T(8,128)(2,1)}, u32[]{:S(2)}) copy-start(bf16[144,64]{1,0:T(8,128)(2,1)} %constant.23.clone.f1) | copy-start | bytes 55300
  64.8 17.9 %copy-start.6 = (bf16[144,64]{1,0:T(8,128)(2,1)S(1)}, bf16[144,64]{1,0:T(8,128)(2,1)}, u32[]{:S(2)}) copy-start(bf16[144,64]{1,0:T(8,128)(2,1)} %constant.22.clone.f0) | copy-start | bytes 55300
  64.8 17.9 %copy-start.7 = (f32[72,128]{1,0:T(8,128)S(1)}, f32[72,128]{1,0:T(8,128)}, u32[]{:S(2)}) copy-start(f32[72,128]{1,0:T(8,128)} %constant.21.clone.ts) | copy-start | bytes 110596
  64.8 17.9 %copy-start.8 = (f32[72,128]{1,0:T(8,128)S(1)}, f32[72,128]{1,0:T(8,128)}, u32[]{:S(2)}) copy-start(f32[72,128]{1,0:T(8,128)} %constant.20.clone.tc) | copy-start | bytes 110596
  64.9 17.9 %copy-start.11 = (bf16[64,144]{1,0:T(8,128)(2,1)S(1)}, bf16[64,144]{1,0:T(8,128)(2,1)}, u32[]{:S(2)}) copy-start(bf16[64,144]{1,0:T(8,128)(2,1)} %constant.25.clone.l1) | copy-start | bytes 55300
  64.9 17.9 %copy-start.12 = (bf16[64,144]{1,0:T(8,128)(2,1)S(1)}, bf16[64,144]{1,0:T(8,128)(2,1)}, u32[]{:S(2)}) copy-start(bf16[64,144]{1,0:T(8,128)(2,1)} %constant.24.clone.l0) | copy-start | bytes 55300
  65.1 17.7 %copy-start = (bf16[256,256]{1,0:T(8,128)(2,1)S(1)}, bf16[256,256]{1,0:T(8,128)(2,1)}, u32[]{:S(2)}) copy-start(bf16[256,256]{1,0:T(8,128)(2,1)} %constant.29.clone.b1) | copy-start | bytes 393220
  65.1 17.7 %copy-start.1 = (bf16[256,256]{1,0:T(8,128)(2,1)S(1)}, bf16[256,256]{1,0:T(8,128)(2,1)}, u32[]{:S(2)}) copy-start(bf16[256,256]{1,0:T(8,128)(2,1)} %constant.28.clone.b0) | copy-start | bytes 393220

commit v6 on v5

--- a/solution.py
+++ b/solution.py
@@ -10,6 +10,7 @@
 WINDOW = 4096
 SHARD = 128
 ROW = 8
+GROUP = 4
 BACK = WINDOW // (ROW * SHARD)
 SHARDS = 64
 HALF = 72
@@ -139,31 +140,42 @@
         step_ref[c * SHARDS : (c + 1) * SHARDS, :] = wide_ref[:, 2 + c, :]
 
 
-def attend_kernel(q_ref, kv_ref, out_ref):
+def attend_kernel(q_ref, own_ref, sibling_ref, out_ref):
     rank = lax.axis_index("seq")
-    row, mine = rank // ROW, rank % ROW
+    row, mine, core = rank // ROW, rank % ROW // 2, rank % 2
     scale = 128 ** -0.5
     order = [row] + [jnp.maximum(row - BACK + r, 0) for r in range(BACK)]
-    keys = jnp.concatenate([kv_ref[n, 0] for n in order], 0)
-    ones = jnp.ones((5 * SHARD, 128), jnp.bfloat16)
-    values = jnp.concatenate([jnp.concatenate([kv_ref[n, 1] for n in order], 0), ones], 1)
+    sources = (own_ref, sibling_ref)
+    keys = jnp.concatenate([ref[n, 0] for ref in sources for n in order], 0)
+    ones = jnp.ones((10 * SHARD, 128), jnp.bfloat16)
+    values = jnp.concatenate([jnp.concatenate([ref[n, 1] for ref in sources for n in order], 0), ones], 1)
     lag = lax.broadcasted_iota(jnp.int32, (SHARD, SHARD), 0) - lax.broadcasted_iota(jnp.int32, (SHARD, SHARD), 1)
     diagonal = lag == 0
     zero = jnp.zeros((SHARD, SHARD), jnp.float32)
-    for theirs in range(ROW):
-        newest = lag >= (mine - theirs) * SHARD
+    for theirs in range(GROUP):
+        ahead = 2 * (mine - theirs) * SHARD
+        newest = [lag >= ahead, lag >= ahead + (1 - 2 * core) * SHARD]
         stats = []
         for h in (0, 1):
             scores = lax.dot_general(
                 q_ref[theirs, h], keys, (((1,), (1,)), ((), ())), preferred_element_type=jnp.float32
             )
-            parts = [scores[:, n * SHARD : (n + 1) * SHARD] for n in range(5)]
-            blocks = [jnp.where(newest, parts[0], jnp.where(row >= BACK, parts[1], NEG))]
-            blocks += [jnp.where(row >= BACK - r, parts[1 + r], NEG) for r in (1, 2, 3)]
-            top = jnp.maximum(jnp.maximum(blocks[0], blocks[1]), jnp.maximum(blocks[2], blocks[3]))
+            parts = [scores[:, n * SHARD : (n + 1) * SHARD] for n in range(10)]
+            blocks = []
+            for source in (0, 1):
+                part = parts[5 * source : 5 * source + 5]
+                blocks.append(jnp.where(newest[source], part[0], jnp.where(row >= BACK, part[1], NEG)))
+                blocks += [jnp.where(row >= BACK - r, part[1 + r], NEG) for r in (1, 2, 3)]
+            top = blocks[0]
+            for block in blocks[1:]:
+                top = jnp.maximum(top, block)
             top = jnp.maximum(jnp.max(top, axis=1, keepdims=True), 0.5 * NEG)
             weights = [jnp.exp((b - top) * scale) for b in blocks]
-            spread = [jnp.where(newest, weights[0], zero), jnp.where(newest, zero, weights[0])] + weights[1:]
+            spread = []
+            for source in (0, 1):
+                part = weights[4 * source : 4 * source + 4]
+                spread += [jnp.where(newest[source], part[0], zero), jnp.where(newest[source], zero, part[0])]
+                spread += part[1:]
             spread = jnp.concatenate([w.astype(jnp.bfloat16) for w in spread], 1)
             sums = jnp.dot(spread, values, preferred_element_type=jnp.float32)
             total = sums[:, 128:]
@@ -183,20 +195,20 @@
     shares = []
     for h in (0, 1):
         sums = []
-        for p in range(ROW):
+        for p in range(GROUP):
             stats = parts_ref[p, 256:272, :].astype(jnp.float32)
             sums.append(stats[3 * h : 3 * h + 1] + stats[3 * h + 1 : 3 * h + 2] + stats[3 * h + 2 : 3 * h + 3])
         sums = jnp.concatenate(sums, 0)
         share = jnp.exp(sums - jnp.max(sums, axis=0, keepdims=True))
         shares.append(share / jnp.sum(share, axis=0, keepdims=True))
-    shares.append(jnp.zeros((112, 128), jnp.float32))
+    shares.append(jnp.zeros((128 - 2 * GROUP, 128), jnp.float32))
     shares = jnp.concatenate(shares, 0).T
     heads = []
     for h in (0, 1):
         merged = None
-        for p in range(ROW):
+        for p in range(GROUP):
             part = parts_ref[p, h * 128 : (h + 1) * 128, :].astype(jnp.float32)
-            part = shares[:, h * ROW + p : h * ROW + p + 1] * part
+            part = shares[:, h * GROUP + p : h * GROUP + p + 1] * part
             merged = part if merged is None else merged + part
         heads.append(merged.astype(jnp.bfloat16))
     attended = jnp.concatenate(heads, 1)
@@ -253,13 +265,13 @@
     )(near(out))
 
 
-def call_attend(queries, pairs):
+def call_attend(queries, own, sibling):
     return pl.pallas_call(
         attend_kernel,
-        out_shape=pltpu.VMEM((ROW, 272, 128), jnp.bfloat16),
-        in_specs=[VMEM] * 2,
-        out_specs=VMEM,
-    )(near(queries), near(pairs))
+        out_shape=pltpu.VMEM((GROUP, 272, 128), jnp.bfloat16),
+        in_specs=[VMEM] * 3,
+        out_specs=VMEM,
+    )(near(queries), near(own), near(sibling))
 
 
 def call_merge(parts, proj):
@@ -282,15 +294,17 @@
     skip_gain,
 ):
     tables = [near(jnp.asarray(t)) for t in transform_tables()]
-    rows = [[y * ROW + p for p in range(ROW)] for y in range(SHARDS // ROW)]
-
-    columns = [[y * ROW + p for y in range(SHARDS // ROW)] for p in range(ROW)]
+    lines = range(SHARDS // ROW)
+    groups = [[y * ROW + 2 * x + core for x in range(GROUP)] for y in lines for core in (0, 1)]
+    columns = [[y * ROW + p for y in lines] for p in range(ROW)]
     pairs = call_repeat(key_heads[:, 0], value_heads[:, 0])
-    pairs = lax.all_to_all(pairs, "seq", 0, 0, axis_index_groups=columns)
-    queries = lax.all_gather(jnp.transpose(query_heads, (1, 0, 2)), "seq", axis_index_groups=rows)
+    own = lax.all_to_all(pairs, "seq", 0, 0, axis_index_groups=columns)
+    queries = lax.all_gather(jnp.transpose(query_heads, (1, 0, 2)), "seq", axis_index_groups=groups)
+    own, queries = lax.optimization_barrier((own, queries))
+    sibling = lax.ppermute(own, "seq", [(i, i ^ 1) for i in range(SHARDS)])
     proj = distill_proj.reshape(256, 1024).T
-    parts = call_attend(queries, pairs)
-    parts = lax.all_to_all(parts, "seq", 0, 0, axis_index_groups=rows)
+    parts = call_attend(queries, own, sibling)
+    parts = lax.all_to_all(parts, "seq", 0, 0, axis_index_groups=groups)
     target = call_merge(parts, proj)
     target = lax.all_to_all(target, ("role", "head"), 0, 0)
     packed = call_pack(target, conv_input, gate_input, filter_taps)

time: 101 us -> 98.9 us (0.979)
  blocking collectives: 64.9 us -> 59.4 us
  starting transfers between devices: 14.9 us -> 17.5 us
  waiting for transfers between devices: 9.63 us -> 11.4 us
    ppermute x0 -> x1, starting transfers between devices: none -> 5.59 us  [body(): sibling = lax.ppermute(own, 'seq', [(i, i ^ 1) for i in range(SHARDS)])]
    all_gather x1, blocking collectives: 15.7 us -> 10.6 us  [body(): lax.all_gather(jnp.transpose(query_heads, (1, 0, 2)), 'seq', axis_index_g...]
    all_to_all x2, starting transfers between devices: 14.9 us -> 11.9 us  [the longest x1 7.78 us: body(): own = lax.all_to_all(pairs, 'seq', 0, 0, axis_index_groups=columns)]
    ppermute x0 -> x1, waiting for transfers between devices: none -> 1.51 us  [body(): sibling = lax.ppermute(own, 'seq', [(i, i ^ 1) for i in range(SHARDS)])]
  transfers between devices with their start and end apart: 2 -> 3, of which waited for: 1 -> 3; matrix products, arithmetic and copies ran while one was open for 0% -> 0% of each run, Pallas kernels for 0% -> 0%
where the time goes in v6:
time: 98.9 us; the launch traced here: 98.4 us
  blocking collectives  59.4 us (60%)
  starting transfers between devices  17.5 us (18%)
  waiting for transfers between devices  11.4 us (12%)
  Pallas kernels  8.87 us (9%)
    all_to_all x1, blocking collectives, body(): target = lax.all_to_all(target, ('role', 'head'), 0, 0)  17.8 us
    all_to_all x1, blocking collectives, body(): packed = lax.all_to_all(packed, 'seq', 0, 0)  17.2 us
    all_to_all x1, blocking collectives, body(): out = lax.all_to_all(out, 'seq', 0, 0)  13.8 us
    all_gather x1, blocking collectives, body(): lax.all_gather(jnp.transpose(query_heads, (1, 0, 2)), 'seq', axis_index_g...  10.6 us
    all_to_all x1, starting transfers between devices, body(): own = lax.all_to_all(pairs, 'seq', 0, 0, axis_index_groups=columns)  7.78 us
    all_to_all x1, waiting for transfers between devices, body(): parts = lax.all_to_all(parts, 'seq', 0, 0, axis_index_groups=groups)  5.77 us
    ppermute x1, starting transfers between devices, body(): sibling = lax.ppermute(own, 'seq', [(i, i ^ 1) for i in range(SHARDS)])  5.59 us
    all_to_all x1, starting transfers between devices, body(): parts = lax.all_to_all(parts, 'seq', 0, 0, axis_index_groups=groups)  4.14 us
  transfers between devices with their start and end apart: 3, of which 3 were waited for; matrix products, arithmetic and copies ran while one was open for 0% of the time, Pallas kernels for 0%

profile of v6, /device:TPU:1, one launch (start us, length us, event | category | flops | bytes accessed | tf_op | source)
XLA Modules:
  0.0 98.4 jit_solution(4020298042406106235)
XLA Ops:
  0.6 1.6 %shard_map.185 = bf16[8,2,128,128]{3,2,1,0:T(8,128)(2,1)} custom-call(bf16[128,128]{1,0:T(8,128)(2,1)} %bitcast.12, bf16[128,128]{1,0:T(8,128)(2,1)} %bitcast.13), custom_call_target="tpu_custom_call" | custom-call | tf_op jit(solution)/shard_map/pallas_call | solution.py:230
  2.3 7.8 %all-to-all-start = ((bf16[8,2,128,128]{3,2,1,0:T(8,128)(2,1)}), bf16[8,2,128,128]{3,2,1,0:T(8,128)(2,1)S(1)}, u32[]{:S(2)}, u32[]{:S(2)}) async-start(bf16[8,2,128,128]{3,2,1,0:T(8,128)(2,1)} %shard_map.185), calls=%async_computation | async-start | bytes 1048576 | tf_op jit(solution)/shard_map/all_to_all | solution.py:301
  10.1 10.6 %all-gather = bf16[8,128,128]{2,1,0:T(8,128)(2,1)S(1)} all-gather(bf16[2,128,128]{2,1,0:T(8,128)(2,1)S(1)} %bitcast.11), channel_id=2, replica_groups={{0,8,16,24},{4,12,20,28},{32,40,48,56},{36,44,52,60},{64,72,80,88},{68,..., dimensions={0}, use_global_device_ids=true | all-gather | bytes 327680 | tf_op jit(solution)/shard_map/all_gather | solution.py:302
  20.7 4.1 %all-to-all-done.own_ref = bf16[8,2,128,128]{3,2,1,0:T(8,128)(2,1)S(1)} async-done(((bf16[8,2,128,128]{3,2,1,0:T(8,128)(2,1)}), bf16[8,2,128,128]{3,2,1,0:T(8,128)(2,1)S(1)}, u32[]{:S(2)}, u32[]{:S(2)}) %all-to-all-start) | async-done | bytes 524320 | tf_op jit(solution)/shard_map/all_to_all | solution.py:301
  24.8 5.6 %collective-permute-start = (bf16[8,2,128,128]{3,2,1,0:T(8,128)(2,1)S(1)}, bf16[8,2,128,128]{3,2,1,0:T(8,128)(2,1)S(1)}, u32[]{:S(2)}, u32[]{:S(2)}) collective-permute-start(bf16[8,2,128,128]{3,2,1,0:T(8,128)(2,1)S(1)} %all-to-all-done.own_ref), channel_id=1, source_target_pairs={{0,4},{4,0},{8,12},{12,8},{16,20},{20,16},{24,28},{28,24},{32,36},... | collective-permute-start | bytes 1572872 | tf_op jit(solution)/shard_map/ppermute | solution.py:304
  30.4 1.5 %collective-permute-done.sibling_ref = bf16[8,2,128,128]{3,2,1,0:T(8,128)(2,1)S(1)} collective-permute-done((bf16[8,2,128,128]{3,2,1,0:T(8,128)(2,1)S(1)}, bf16[8,2,128,128]{3,2,1,0:T(8,128)(2,1)S(1)}, u32[]{:S(2)}, u32[]{:S(2)}) %collective-permute-start) | collective-permute-done | bytes 524320 | tf_op jit(solution)/shard_map/ppermute | solution.py:304
  31.9 2.8 %shard_map.186 = bf16[4,272,128]{2,1,0:T(8,128)(2,1)} custom-call(bf16[4,2,128,128]{3,2,1,0:T(8,128)(2,1)S(1)} %bitcast.9, bf16[8,2,128,128]{3,2,1,0:T(8,128)(2,1)S(1)} %all-to-all-done.own_ref, bf16[8,2,128,128]{3,2,1,0:T(8,128)(2,1)S(1)} %collective-permute-done.sibling_ref), custom_call_target="tpu_custom_call" | custom-call | tf_op jit(solution)/shard_map/pallas_call | solution.py:269
  34.7 4.1 %all-to-all-start.1 = ((bf16[4,272,128]{2,1,0:T(8,128)(2,1)}), bf16[4,272,128]{2,1,0:T(8,128)(2,1)S(1)}, u32[]{:S(2)}, u32[]{:S(2)}) async-start(bf16[4,272,128]{2,1,0:T(8,128)(2,1)} %shard_map.186), calls=%async_computation.1 | async-start | bytes 557056 | tf_op jit(solution)/shard_map/all_to_all | solution.py:307
  38.9 0.2 copy.24
  39.1 5.8 %all-to-all-done.1.parts_ref = bf16[4,272,128]{2,1,0:T(8,128)(2,1)S(1)} async-done(((bf16[4,272,128]{2,1,0:T(8,128)(2,1)}), bf16[4,272,128]{2,1,0:T(8,128)(2,1)S(1)}, u32[]{:S(2)}, u32[]{:S(2)}) %all-to-all-start.1) | async-done | bytes 278560 | tf_op jit(solution)/shard_map/all_to_all | solution.py:307
  44.8 0.7 shard_map.187
  45.6 17.8 %all_to_all.25.parts_ref = bf16[8,128,128]{2,1,0:T(8,128)(2,1)S(1)} all-to-all(bf16[8,128,128]{2,1,0:T(8,128)(2,1)S(1)} %shard_map.187), channel_id=1, replica_groups=mesh['role'=2,'seq'=64,'head'=4] {'role','head'}, dimensions={0} | all-to-all | bytes 524288 | tf_op jit(solution)/shard_map/all_to_all | solution.py:309
  63.4 0.0 copy-start.2
  63.4 0.0 copy-start.3
  63.4 0.0 copy-start.5
  63.4 0.0 copy-start.6
  63.4 0.0 copy-start.8
  63.4 0.0 copy-start.11
  63.5 0.0 copy-start.12
  63.5 0.2 shard_map.188
  63.7 17.2 %all_to_all.26.in_ref = bf16[64,8,128]{2,1,0:T(8,128)(2,1)S(1)} all-to-all(bf16[64,8,128]{2,1,0:T(8,128)(2,1)S(1)} %shard_map.188), channel_id=1, replica_groups=mesh['role'=2,'seq'=64,'head'=4] {'seq'}, dimensions={0} | all-to-all | bytes 262144 | tf_op jit(solution)/shard_map/all_to_all | solution.py:311
  81.0 2.8 %shard_map.189 = bf16[64,4,128]{2,1,0:T(4,128)(2,1)S(1)} custom-call(f32[128]{0:T(128)} %skip_ref.1, bf16[64,8,128]{2,1,0:T(8,128)(2,1)S(1)} %all_to_all.26.in_ref, f32[72,128]{1,0:T(8,128)S(1)} %copy-done.5, f32[72,128]{1,0:T(8,128)S(1)} %copy-done.6, bf16[144,64]{1,0:T(8,128)(2,1)S(1)} %copy-done.7, bf16[144,64]{1,0:T(8,128)(2,1)S(1)} %copy-done.8, ...), custom_call_target="tpu_custom_call" | custom-call | tf_op jit(solution)/shard_map/pallas_call | solution.py:249
  83.8 13.8 %all_to_all.27.in_ref = bf16[64,4,128]{2,1,0:T(4,128)(2,1)S(1)} all-to-all(bf16[64,4,128]{2,1,0:T(4,128)(2,1)S(1)} %shard_map.189), channel_id=1, replica_groups=mesh['role'=2,'seq'=64,'head'=4] {'seq'}, dimensions={0} | all-to-all | bytes 131072 | tf_op jit(solution)/shard_map/all_to_all | solution.py:313
  97.7 0.7 shard_map.190
  (24 shorter events, 0.1 us)
Async XLA Ops:
  2.3 7.8 %copy-start.14 = (bf16[128,2,128]{2,1,0:T(2,128)(2,1)S(1)}, bf16[128,2,128]{2,1,0:T(2,128)(2,1)}, u32[]{:S(2)}) copy-start(bf16[128,2,128]{2,1,0:T(2,128)(2,1)} %param.18) | copy-start | bytes 196612
  2.3 22.5 %all-to-all-start = ((bf16[8,2,128,128]{3,2,1,0:T(8,128)(2,1)}), bf16[8,2,128,128]{3,2,1,0:T(8,128)(2,1)S(1)}, u32[]{:S(2)}, u32[]{:S(2)}) async-start(bf16[8,2,128,128]{3,2,1,0:T(8,128)(2,1)} %shard_map.185), calls=%async_computation | async-start | bytes 1048576 | tf_op jit(solution)/shard_map/all_to_all | solution.py:301
  24.8 7.1 %collective-permute-start = (bf16[8,2,128,128]{3,2,1,0:T(8,128)(2,1)S(1)}, bf16[8,2,128,128]{3,2,1,0:T(8,128)(2,1)S(1)}, u32[]{:S(2)}, u32[]{:S(2)}) collective-permute-start(bf16[8,2,128,128]{3,2,1,0:T(8,128)(2,1)S(1)} %all-to-all-done.own_ref), channel_id=1, source_target_pairs={{0,4},{4,0},{8,12},{12,8},{16,20},{20,16},{24,28},{28,24},{32,36},... | collective-permute-start | bytes 1572872 | tf_op jit(solution)/shard_map/ppermute | solution.py:304
  34.7 4.1 %copy-start.13 = (bf16[2,128,1024]{2,1,0:T(8,128)(2,1)S(1)}, bf16[2,128,1024]{2,1,0:T(8,128)(2,1)}, u32[]{:S(2)}) copy-start(bf16[2,128,1024]{2,1,0:T(8,128)(2,1)} %param.21) | copy-start | bytes 1572868
  34.7 10.1 %all-to-all-start.1 = ((bf16[4,272,128]{2,1,0:T(8,128)(2,1)}), bf16[4,272,128]{2,1,0:T(8,128)(2,1)S(1)}, u32[]{:S(2)}, u32[]{:S(2)}) async-start(bf16[4,272,128]{2,1,0:T(8,128)(2,1)} %shard_map.186), calls=%async_computation.1 | async-start | bytes 557056 | tf_op jit(solution)/shard_map/all_to_all | solution.py:307
  45.5 17.8 %copy-start.4 = (f32[128,128]{1,0:T(8,128)S(1)}, f32[128,128]{1,0:T(8,128)}, u32[]{:S(2)}) copy-start(f32[128,128]{1,0:T(8,128)} %taps_ref.1) | copy-start | bytes 196612
  45.5 17.8 %copy-start.9 = (bf16[128,128]{1,0:T(8,128)(2,1)S(1)}, bf16[128,128]{1,0:T(8,128)(2,1)}, u32[]{:S(2)}) copy-start(bf16[128,128]{1,0:T(8,128)(2,1)} %input_ref.1) | copy-start | bytes 98308
  45.5 17.8 %copy-start.10 = (bf16[128,128]{1,0:T(8,128)(2,1)S(1)}, bf16[128,128]{1,0:T(8,128)(2,1)}, u32[]{:S(2)}) copy-start(bf16[128,128]{1,0:T(8,128)(2,1)} %gate_ref.1) | copy-start | bytes 98308
  63.4 17.6 %copy-start.2 = (bf16[256,256]{1,0:T(8,128)(2,1)S(1)}, bf16[256,256]{1,0:T(8,128)(2,1)}, u32[]{:S(2)}) copy-start(bf16[256,256]{1,0:T(8,128)(2,1)} %constant.28.clone.b0) | copy-start | bytes 393220
  63.4 17.5 %copy-start.3 = (bf16[256,256]{1,0:T(8,128)(2,1)S(1)}, bf16[256,256]{1,0:T(8,128)(2,1)}, u32[]{:S(2)}) copy-start(bf16[256,256]{1,0:T(8,128)(2,1)} %constant.29.clone.b1) | copy-start | bytes 393220
  63.4 17.5 %copy-start.5 = (f32[72,128]{1,0:T(8,128)S(1)}, f32[72,128]{1,0:T(8,128)}, u32[]{:S(2)}) copy-start(f32[72,128]{1,0:T(8,128)} %constant.20.clone.tc) | copy-start | bytes 110596
  63.4 17.5 %copy-start.6 = (f32[72,128]{1,0:T(8,128)S(1)}, f32[72,128]{1,0:T(8,128)}, u32[]{:S(2)}) copy-start(f32[72,128]{1,0:T(8,128)} %constant.21.clone.ts) | copy-start | bytes 110596
  63.4 17.5 %copy-start.7 = (bf16[144,64]{1,0:T(8,128)(2,1)S(1)}, bf16[144,64]{1,0:T(8,128)(2,1)}, u32[]{:S(2)}) copy-start(bf16[144,64]{1,0:T(8,128)(2,1)} %constant.22.clone.f0) | copy-start | bytes 55300
  63.4 17.5 %copy-start.8 = (bf16[144,64]{1,0:T(8,128)(2,1)S(1)}, bf16[144,64]{1,0:T(8,128)(2,1)}, u32[]{:S(2)}) copy-start(bf16[144,64]{1,0:T(8,128)(2,1)} %constant.23.clone.f1) | copy-start | bytes 55300
  63.4 17.5 %copy-start.11 = (bf16[64,144]{1,0:T(8,128)(2,1)S(1)}, bf16[64,144]{1,0:T(8,128)(2,1)}, u32[]{:S(2)}) copy-start(bf16[64,144]{1,0:T(8,128)(2,1)} %constant.24.clone.l0) | copy-start | bytes 55300
  63.5 17.5 %copy-start.12 = (bf16[64,144]{1,0:T(8,128)(2,1)S(1)}, bf16[64,144]{1,0:T(8,128)(2,1)}, u32[]{:S(2)}) copy-start(bf16[64,144]{1,0:T(8,128)(2,1)} %constant.25.clone.l1) | copy-start | bytes 55300
  63.7 17.3 %copy-start = (bf16[256,256]{1,0:T(8,128)(2,1)S(1)}, bf16[256,256]{1,0:T(8,128)(2,1)}, u32[]{:S(2)}) copy-start(bf16[256,256]{1,0:T(8,128)(2,1)} %constant.26.clone.w0) | copy-start | bytes 393220
  63.7 17.3 %copy-start.1 = (bf16[256,256]{1,0:T(8,128)(2,1)S(1)}, bf16[256,256]{1,0:T(8,128)(2,1)}, u32[]{:S(2)}) copy-start(bf16[256,256]{1,0:T(8,128)(2,1)} %constant.27.clone.w1) | copy-start | bytes 393220

commit v7 on v6

--- a/solution.py
+++ b/solution.py
@@ -90,10 +90,15 @@
     return jnp.concatenate([ar * br + ai * bi, ar * bi - ai * br], 1)
 
 
-def repeat_kernel(key_ref, value_ref, out_ref):
+def repeat_kernel(key_ref, value_ref, out_ref, done):
+    copies = []
     for n in range(SHARDS // ROW):
-        out_ref[n, 0] = key_ref[...]
-        out_ref[n, 1] = value_ref[...]
+        for m, ref in enumerate((key_ref, value_ref)):
+            copies.append(pltpu.make_async_copy(ref, out_ref.at[n, m], done.at[n, m]))
+    for copy in copies:
+        copy.start()
+    for copy in copies:
+        copy.wait()
 
 
 def pack_kernel(parts_ref, input_ref, gate_ref, taps_ref, out_ref, wide_ref):
@@ -227,11 +232,13 @@
 
 
 def call_repeat(key, value):
+    anywhere = pl.BlockSpec(memory_space=pl.ANY)
     return pl.pallas_call(
         repeat_kernel,
-        out_shape=pltpu.VMEM((SHARDS // ROW, 2, SHARD, 128), jnp.bfloat16),
-        in_specs=[VMEM] * 2,
-        out_specs=VMEM,
+        out_shape=jax.ShapeDtypeStruct((SHARDS // ROW, 2, SHARD, 128), jnp.bfloat16),
+        in_specs=[anywhere] * 2,
+        out_specs=anywhere,
+        scratch_shapes=[pltpu.SemaphoreType.DMA((SHARDS // ROW, 2))],
     )(key, value)
 
 
@@ -300,9 +307,9 @@
     pairs = call_repeat(key_heads[:, 0], value_heads[:, 0])
     own = lax.all_to_all(pairs, "seq", 0, 0, axis_index_groups=columns)
     queries = lax.all_gather(jnp.transpose(query_heads, (1, 0, 2)), "seq", axis_index_groups=groups)
-    own, queries = lax.optimization_barrier((own, queries))
+    proj = distill_proj.reshape(256, 1024).T
+    own, queries, proj = lax.optimization_barrier((own, queries, proj))
     sibling = lax.ppermute(own, "seq", [(i, i ^ 1) for i in range(SHARDS)])
-    proj = distill_proj.reshape(256, 1024).T
     parts = call_attend(queries, own, sibling)
     parts = lax.all_to_all(parts, "seq", 0, 0, axis_index_groups=groups)
     target = call_merge(parts, proj)

time: 98.9 us -> 114 us (1.15)
  Pallas kernels: 8.87 us -> 23.6 us
  blocking collectives: 59.4 us -> 70.3 us
  waiting for transfers between devices: 11.4 us -> 5.43 us
  starting transfers between devices: 17.5 us -> 13.4 us
    pallas_call x1, Pallas kernels: 1.64 us -> 17.1 us  [call_repeat(): pl.pallas_call(repeat_kernel, out_shape=jax.ShapeDtypeStruct((SHARDS // R...]
    all_to_all x0 -> x1, blocking collectives: none -> 10.1 us  [body(): parts = lax.all_to_all(parts, 'seq', 0, 0, axis_index_groups=groups)]
    all_to_all x1 -> x0, waiting for transfers between devices: 5.77 us -> none  [body(): parts = lax.all_to_all(parts, 'seq', 0, 0, axis_index_groups=groups)]
    all_to_all x1 -> x0, starting transfers between devices: 4.14 us -> none  [body(): parts = lax.all_to_all(parts, 'seq', 0, 0, axis_index_groups=groups)]
  transfers between devices with their start and end apart: 3 -> 2, of which waited for: 3 -> 2; matrix products, arithmetic and copies ran while one was open for 0% -> 0% of each run, Pallas kernels for 0% -> 0%
where the time goes in v7:
time: 114 us
  blocking collectives  70.3 us (62%)
  Pallas kernels  23.6 us (21%)
  starting transfers between devices  13.4 us (12%)
  waiting for transfers between devices  5.43 us (5%)
    all_to_all x1, blocking collectives, body(): packed = lax.all_to_all(packed, 'seq', 0, 0)  18.1 us
    all_to_all x1, blocking collectives, body(): target = lax.all_to_all(target, ('role', 'head'), 0, 0)  17.7 us
    pallas_call x1, Pallas kernels, call_repeat(): pl.pallas_call(repeat_kernel, out_shape=jax.ShapeDtypeStruct((SHARDS // R...  17.1 us
    all_to_all x1, blocking collectives, body(): out = lax.all_to_all(out, 'seq', 0, 0)  13.8 us
    all_gather x1, blocking collectives, body(): lax.all_gather(jnp.transpose(query_heads, (1, 0, 2)), 'seq', axis_index_g...  10.6 us
    all_to_all x1, blocking collectives, body(): parts = lax.all_to_all(parts, 'seq', 0, 0, axis_index_groups=groups)  10.1 us
    all_to_all x1, starting transfers between devices, body(): own = lax.all_to_all(pairs, 'seq', 0, 0, axis_index_groups=columns)  7.79 us
    ppermute x1, starting transfers between devices, body(): sibling = lax.ppermute(own, 'seq', [(i, i ^ 1) for i in range(SHARDS)])  5.59 us
  transfers between devices with their start and end apart: 2, of which 2 were waited for; matrix products, arithmetic and copies ran while one was open for 0% of the time, Pallas kernels for 0%

profile of v7, /device:TPU:1, one launch (start us, length us, event | category | flops | bytes accessed | tf_op | source)
XLA Modules:
  0.0 114.0 jit_solution(9723511049965843161)
XLA Ops:
  0.6 17.1 %shard_map.185 = bf16[8,2,128,128]{3,2,1,0:T(8,128)(2,1)} custom-call(bf16[128,128]{1,0:T(8,128)(2,1)} %bitcast.12, bf16[128,128]{1,0:T(8,128)(2,1)} %bitcast.13), custom_call_target="tpu_custom_call" | custom-call | tf_op jit(solution)/shard_map/pallas_call | solution.py:236
  17.8 7.8 %all-to-all-start = ((bf16[8,2,128,128]{3,2,1,0:T(8,128)(2,1)}), bf16[8,2,128,128]{3,2,1,0:T(8,128)(2,1)S(1)}, u32[]{:S(2)}, u32[]{:S(2)}) async-start(bf16[8,2,128,128]{3,2,1,0:T(8,128)(2,1)} %shard_map.185), calls=%async_computation | async-start | bytes 1048576 | tf_op jit(solution)/shard_map/all_to_all | solution.py:308
  25.6 0.2 copy.24
  25.8 10.6 %all-gather = bf16[8,128,128]{2,1,0:T(8,128)(2,1)S(1)} all-gather(bf16[2,128,128]{2,1,0:T(8,128)(2,1)S(1)} %bitcast.11), channel_id=2, replica_groups={{0,8,16,24},{4,12,20,28},{32,40,48,56},{36,44,52,60},{64,72,80,88},{68,..., dimensions={0}, use_global_device_ids=true | all-gather | bytes 327680 | tf_op jit(solution)/shard_map/all_gather | solution.py:309
  36.4 3.9 %all-to-all-done.own_ref = bf16[8,2,128,128]{3,2,1,0:T(8,128)(2,1)S(1)} async-done(((bf16[8,2,128,128]{3,2,1,0:T(8,128)(2,1)}), bf16[8,2,128,128]{3,2,1,0:T(8,128)(2,1)S(1)}, u32[]{:S(2)}, u32[]{:S(2)}) %all-to-all-start) | async-done | bytes 524320 | tf_op jit(solution)/shard_map/all_to_all | solution.py:308
  40.3 5.6 %collective-permute-start = (bf16[8,2,128,128]{3,2,1,0:T(8,128)(2,1)S(1)}, bf16[8,2,128,128]{3,2,1,0:T(8,128)(2,1)S(1)}, u32[]{:S(2)}, u32[]{:S(2)}) collective-permute-start(bf16[8,2,128,128]{3,2,1,0:T(8,128)(2,1)S(1)} %all-to-all-done.own_ref), channel_id=1, source_target_pairs={{0,4},{4,0},{8,12},{12,8},{16,20},{20,16},{24,28},{28,24},{32,36},... | collective-permute-start | bytes 1572872 | tf_op jit(solution)/shard_map/ppermute | solution.py:312
  45.9 1.5 %collective-permute-done.sibling_ref = bf16[8,2,128,128]{3,2,1,0:T(8,128)(2,1)S(1)} collective-permute-done((bf16[8,2,128,128]{3,2,1,0:T(8,128)(2,1)S(1)}, bf16[8,2,128,128]{3,2,1,0:T(8,128)(2,1)S(1)}, u32[]{:S(2)}, u32[]{:S(2)}) %collective-permute-start) | collective-permute-done | bytes 524320 | tf_op jit(solution)/shard_map/ppermute | solution.py:312
  47.5 2.1 %shard_map.186 = bf16[4,272,128]{2,1,0:T(8,128)(2,1)S(1)} custom-call(bf16[4,2,128,128]{3,2,1,0:T(8,128)(2,1)S(1)} %bitcast.9, bf16[8,2,128,128]{3,2,1,0:T(8,128)(2,1)S(1)} %all-to-all-done.own_ref, bf16[8,2,128,128]{3,2,1,0:T(8,128)(2,1)S(1)} %collective-permute-done.sibling_ref), custom_call_target="tpu_custom_call" | custom-call | tf_op jit(solution)/shard_map/pallas_call | solution.py:276
  49.5 10.1 %all_to_all.25.parts_ref = bf16[4,272,128]{2,1,0:T(8,128)(2,1)S(1)} all-to-all(bf16[4,272,128]{2,1,0:T(8,128)(2,1)S(1)} %shard_map.186), channel_id=1, replica_groups={{0,8,16,24},{4,12,20,28},{32,40,48,56},{36,44,52,60},{64,72,80,88},{68,..., dimensions={0} | all-to-all | bytes 557056 | tf_op jit(solution)/shard_map/all_to_all | solution.py:314
  59.6 0.7 shard_map.187
  60.3 17.7 %all_to_all.26.parts_ref = bf16[8,128,128]{2,1,0:T(8,128)(2,1)S(1)} all-to-all(bf16[8,128,128]{2,1,0:T(8,128)(2,1)S(1)} %shard_map.187), channel_id=1, replica_groups=mesh['role'=2,'seq'=64,'head'=4] {'role','head'}, dimensions={0} | all-to-all | bytes 524288 | tf_op jit(solution)/shard_map/all_to_all | solution.py:316
  78.1 0.0 copy-start.2
  78.1 0.0 copy-start.3
  78.1 0.0 copy-start.5
  78.1 0.0 copy-start.7
  78.2 0.0 copy-start.8
  78.2 0.0 copy-start.11
  78.2 0.0 copy-start.12
  78.2 0.2 shard_map.188
  78.4 0.0 copy-start
  78.4 18.1 %all_to_all.27.in_ref = bf16[64,8,128]{2,1,0:T(8,128)(2,1)S(1)} all-to-all(bf16[64,8,128]{2,1,0:T(8,128)(2,1)S(1)} %shard_map.188), channel_id=1, replica_groups=mesh['role'=2,'seq'=64,'head'=4] {'seq'}, dimensions={0} | all-to-all | bytes 262144 | tf_op jit(solution)/shard_map/all_to_all | solution.py:318
  96.6 2.8 %shard_map.189 = bf16[64,4,128]{2,1,0:T(4,128)(2,1)S(1)} custom-call(f32[128]{0:T(128)} %skip_ref.1, bf16[64,8,128]{2,1,0:T(8,128)(2,1)S(1)} %all_to_all.27.in_ref, f32[72,128]{1,0:T(8,128)S(1)} %copy-done.8, f32[72,128]{1,0:T(8,128)S(1)} %copy-done.7, bf16[144,64]{1,0:T(8,128)(2,1)S(1)} %copy-done.6, bf16[144,64]{1,0:T(8,128)(2,1)S(1)} %copy-done.5, ...), custom_call_target="tpu_custom_call" | custom-call | tf_op jit(solution)/shard_map/pallas_call | solution.py:256
  99.5 13.8 %all_to_all.28.in_ref = bf16[64,4,128]{2,1,0:T(4,128)(2,1)S(1)} all-to-all(bf16[64,4,128]{2,1,0:T(4,128)(2,1)S(1)} %shard_map.189), channel_id=1, replica_groups=mesh['role'=2,'seq'=64,'head'=4] {'seq'}, dimensions={0} | all-to-all | bytes 131072 | tf_op jit(solution)/shard_map/all_to_all | solution.py:320
  113.2 0.7 shard_map.190
  (23 shorter events, 0.1 us)
Async XLA Ops:
  17.8 7.8 %copy-start.14 = (bf16[128,2,128]{2,1,0:T(2,128)(2,1)S(1)}, bf16[128,2,128]{2,1,0:T(2,128)(2,1)}, u32[]{:S(2)}) copy-start(bf16[128,2,128]{2,1,0:T(2,128)(2,1)} %param.18) | copy-start | bytes 196612
  17.8 7.8 %copy-start.13 = (bf16[2,128,1024]{2,1,0:T(8,128)(2,1)S(1)}, bf16[2,128,1024]{2,1,0:T(8,128)(2,1)}, u32[]{:S(2)}) copy-start(bf16[2,128,1024]{2,1,0:T(8,128)(2,1)} %param.21) | copy-start | bytes 1572868
  17.8 22.5 %all-to-all-start = ((bf16[8,2,128,128]{3,2,1,0:T(8,128)(2,1)}), bf16[8,2,128,128]{3,2,1,0:T(8,128)(2,1)S(1)}, u32[]{:S(2)}, u32[]{:S(2)}) async-start(bf16[8,2,128,128]{3,2,1,0:T(8,128)(2,1)} %shard_map.185), calls=%async_computation | async-start | bytes 1048576 | tf_op jit(solution)/shard_map/all_to_all | solution.py:308
  40.3 7.1 %collective-permute-start = (bf16[8,2,128,128]{3,2,1,0:T(8,128)(2,1)S(1)}, bf16[8,2,128,128]{3,2,1,0:T(8,128)(2,1)S(1)}, u32[]{:S(2)}, u32[]{:S(2)}) collective-permute-start(bf16[8,2,128,128]{3,2,1,0:T(8,128)(2,1)S(1)} %all-to-all-done.own_ref), channel_id=1, source_target_pairs={{0,4},{4,0},{8,12},{12,8},{16,20},{20,16},{24,28},{28,24},{32,36},... | collective-permute-start | bytes 1572872 | tf_op jit(solution)/shard_map/ppermute | solution.py:312
  60.3 17.8 %copy-start.4 = (f32[128,128]{1,0:T(8,128)S(1)}, f32[128,128]{1,0:T(8,128)}, u32[]{:S(2)}) copy-start(f32[128,128]{1,0:T(8,128)} %taps_ref.1) | copy-start | bytes 196612
  60.3 17.8 %copy-start.9 = (bf16[128,128]{1,0:T(8,128)(2,1)S(1)}, bf16[128,128]{1,0:T(8,128)(2,1)}, u32[]{:S(2)}) copy-start(bf16[128,128]{1,0:T(8,128)(2,1)} %input_ref.1) | copy-start | bytes 98308
  60.3 17.8 %copy-start.10 = (bf16[128,128]{1,0:T(8,128)(2,1)S(1)}, bf16[128,128]{1,0:T(8,128)(2,1)}, u32[]{:S(2)}) copy-start(bf16[128,128]{1,0:T(8,128)(2,1)} %gate_ref.1) | copy-start | bytes 98308
  78.1 18.4 %copy-start.2 = (bf16[256,256]{1,0:T(8,128)(2,1)S(1)}, bf16[256,256]{1,0:T(8,128)(2,1)}, u32[]{:S(2)}) copy-start(bf16[256,256]{1,0:T(8,128)(2,1)} %constant.27.clone.w1) | copy-start | bytes 393220
  78.1 18.4 %copy-start.3 = (bf16[256,256]{1,0:T(8,128)(2,1)S(1)}, bf16[256,256]{1,0:T(8,128)(2,1)}, u32[]{:S(2)}) copy-start(bf16[256,256]{1,0:T(8,128)(2,1)} %constant.26.clone.w0) | copy-start | bytes 393220
  78.1 18.4 %copy-start.5 = (bf16[144,64]{1,0:T(8,128)(2,1)S(1)}, bf16[144,64]{1,0:T(8,128)(2,1)}, u32[]{:S(2)}) copy-start(bf16[144,64]{1,0:T(8,128)(2,1)} %constant.23.clone.f1) | copy-start | bytes 55300
  78.1 18.4 %copy-start.6 = (bf16[144,64]{1,0:T(8,128)(2,1)S(1)}, bf16[144,64]{1,0:T(8,128)(2,1)}, u32[]{:S(2)}) copy-start(bf16[144,64]{1,0:T(8,128)(2,1)} %constant.22.clone.f0) | copy-start | bytes 55300
  78.1 18.4 %copy-start.7 = (f32[72,128]{1,0:T(8,128)S(1)}, f32[72,128]{1,0:T(8,128)}, u32[]{:S(2)}) copy-start(f32[72,128]{1,0:T(8,128)} %constant.21.clone.ts) | copy-start | bytes 110596
  78.2 18.4 %copy-start.8 = (f32[72,128]{1,0:T(8,128)S(1)}, f32[72,128]{1,0:T(8,128)}, u32[]{:S(2)}) copy-start(f32[72,128]{1,0:T(8,128)} %constant.20.clone.tc) | copy-start | bytes 110596
  78.2 18.4 %copy-start.11 = (bf16[64,144]{1,0:T(8,128)(2,1)S(1)}, bf16[64,144]{1,0:T(8,128)(2,1)}, u32[]{:S(2)}) copy-start(bf16[64,144]{1,0:T(8,128)(2,1)} %constant.25.clone.l1) | copy-start | bytes 55300
  78.2 18.4 %copy-start.12 = (bf16[64,144]{1,0:T(8,128)(2,1)S(1)}, bf16[64,144]{1,0:T(8,128)(2,1)}, u32[]{:S(2)}) copy-start(bf16[64,144]{1,0:T(8,128)(2,1)} %constant.24.clone.l0) | copy-start | bytes 55300
  78.4 18.2 %copy-start = (bf16[256,256]{1,0:T(8,128)(2,1)S(1)}, bf16[256,256]{1,0:T(8,128)(2,1)}, u32[]{:S(2)}) copy-start(bf16[256,256]{1,0:T(8,128)(2,1)} %constant.29.clone.b1) | copy-start | bytes 393220
  78.4 18.2 %copy-start.1 = (bf16[256,256]{1,0:T(8,128)(2,1)S(1)}, bf16[256,256]{1,0:T(8,128)(2,1)}, u32[]{:S(2)}) copy-start(bf16[256,256]{1,0:T(8,128)(2,1)} %constant.28.clone.b0) | copy-start | bytes 393220

commit v8 on v7

--- a/solution.py
+++ b/solution.py
@@ -34,29 +34,25 @@
     forward = np.block([[cosine, -sine], [sine, cosine]])
     backward = np.block([[cosine, sine], [-sine, cosine]])
     tables = [np.asarray(t, np.float32) for t in (np.cos(turn), np.sin(turn))]
-    for table in (first, last, forward, backward):
+    for table, axis in ((first, 1), (last, 1), (forward, 0), (backward, 0)):
         high = np.asarray(table, ml_dtypes.bfloat16)
-        tables += [high, np.asarray(table - high.astype(np.float64), ml_dtypes.bfloat16)]
+        low = np.asarray(table - high.astype(np.float64), ml_dtypes.bfloat16)
+        tables.append(np.concatenate([high, high, low], axis))
     return tables
 
 
-def halves(x):
+def triple(x, axis):
     high = x.astype(jnp.bfloat16)
-    return high, (x - high.astype(jnp.float32)).astype(jnp.bfloat16)
-
-
-def dot32(a, b):
-    return jnp.dot(a, b, preferred_element_type=jnp.float32)
+    low = (x - high.astype(jnp.float32)).astype(jnp.bfloat16)
+    return jnp.concatenate([high, low, high], axis)
 
 
 def table_times(table, x):
-    high, low = halves(x)
-    return dot32(table[0], high) + (dot32(table[0], low) + dot32(table[1], high))
+    return jnp.dot(table, triple(x, 0), preferred_element_type=jnp.float32)
 
 
 def times_table(x, table):
-    high, low = halves(x)
-    return dot32(high, table[0]) + (dot32(low, table[0]) + dot32(high, table[1]))
+    return jnp.dot(triple(x, 1), table, preferred_element_type=jnp.float32)
 
 
 def to_spectra(signals, first, turn_cos, turn_sin, forward):
@@ -90,13 +86,17 @@
     return jnp.concatenate([ar * br + ai * bi, ar * bi - ai * br], 1)
 
 
-def repeat_kernel(key_ref, value_ref, out_ref, done):
+def repeat_kernel(key_ref, value_ref, out_ref, held, arrived, done):
+    loads = []
+    for m, ref in enumerate((key_ref, value_ref)):
+        loads.append(pltpu.make_async_copy(ref, held.at[m], arrived.at[m]))
+        loads[m].start()
     copies = []
-    for n in range(SHARDS // ROW):
-        for m, ref in enumerate((key_ref, value_ref)):
-            copies.append(pltpu.make_async_copy(ref, out_ref.at[n, m], done.at[n, m]))
-    for copy in copies:
-        copy.start()
+    for m in (0, 1):
+        loads[m].wait()
+        for n in range(SHARDS // ROW):
+            copies.append(pltpu.make_async_copy(held.at[m], out_ref.at[n, m], done.at[n, m]))
+            copies[-1].start()
     for copy in copies:
         copy.wait()
 
@@ -113,14 +113,14 @@
     out_ref[...] = wide_ref[...].astype(jnp.bfloat16)
 
 
-def student_kernel(skip_ref, in_ref, tc, ts, f0, f1, l0, l1, w0, w1, b0, b1, out_ref, wide_in, wide_out):
+def student_kernel(skip_ref, in_ref, tc, ts, first, last, forward, backward, out_ref, wide_in, wide_out):
     wide_in[...] = in_ref[...].astype(jnp.float32)
     rank = lax.axis_index("seq")
     skip = [skip_ref[rank], skip_ref[rank + SHARDS]]
     target, signal, gate, taps = [[wide_in[:, 2 * n + c, :] for c in (0, 1)] for n in range(4)]
     turn = tc[...], ts[...]
-    ahead = (f0[...], f1[...]), *turn, (w0[...], w1[...])
-    behind = (l0[...], l1[...]), *turn, (b0[...], b1[...])
+    ahead = first[...], *turn, forward[...]
+    behind = last[...], *turn, backward[...]
     spectra = to_spectra(signal + taps, *ahead)
     conv = to_signals([product(spectra[c], spectra[2 + c]) for c in (0, 1)], *behind)
     back = []
@@ -238,7 +238,11 @@
         out_shape=jax.ShapeDtypeStruct((SHARDS // ROW, 2, SHARD, 128), jnp.bfloat16),
         in_specs=[anywhere] * 2,
         out_specs=anywhere,
-        scratch_shapes=[pltpu.SemaphoreType.DMA((SHARDS // ROW, 2))],
+        scratch_shapes=[
+            pltpu.VMEM((2, SHARD, 128), jnp.bfloat16),
+            pltpu.SemaphoreType.DMA((2,)),
+            pltpu.SemaphoreType.DMA((SHARDS // ROW, 2)),
+        ],
     )(key, value)
 
 
@@ -256,7 +260,7 @@
     return pl.pallas_call(
         student_kernel,
         out_shape=pltpu.VMEM((SHARDS, 4, 128), jnp.bfloat16),
-        in_specs=[SMEM] + [VMEM] * 11,
+        in_specs=[SMEM] + [VMEM] * 7,
         out_specs=VMEM,
         scratch_shapes=[pltpu.VMEM((SHARDS, 8, 128), jnp.float32), pltpu.VMEM((SHARDS, 4, 128), jnp.float32)],
     )(skip, near(packed), *tables)

time: 114 us -> 98.6 us (0.86)
  Pallas kernels: 23.6 us -> 7.99 us
    pallas_call x1, Pallas kernels: 17.1 us -> 1.72 us  [call_repeat(): pl.pallas_call(repeat_kernel, out_shape=jax.ShapeDtypeStruct((SHARDS // R...]
where the time goes in v8:
time: 98.6 us; the launch traced here: 98.1 us
  blocking collectives  70.2 us (71%)
  starting transfers between devices  13.4 us (14%)
  Pallas kernels  7.99 us (8%)
  waiting for transfers between devices  5.43 us (6%)
    all_to_all x1, blocking collectives, body(): packed = lax.all_to_all(packed, 'seq', 0, 0)  18 us
    all_to_all x1, blocking collectives, body(): target = lax.all_to_all(target, ('role', 'head'), 0, 0)  17.7 us
    all_to_all x1, blocking collectives, body(): out = lax.all_to_all(out, 'seq', 0, 0)  13.8 us
    all_gather x1, blocking collectives, body(): lax.all_gather(jnp.transpose(query_heads, (1, 0, 2)), 'seq', axis_index_g...  10.6 us
    all_to_all x1, blocking collectives, body(): parts = lax.all_to_all(parts, 'seq', 0, 0, axis_index_groups=groups)  10.1 us
    all_to_all x1, starting transfers between devices, body(): own = lax.all_to_all(pairs, 'seq', 0, 0, axis_index_groups=columns)  7.79 us
    ppermute x1, starting transfers between devices, body(): sibling = lax.ppermute(own, 'seq', [(i, i ^ 1) for i in range(SHARDS)])  5.59 us
    all_to_all x1, waiting for transfers between devices, body(): own = lax.all_to_all(pairs, 'seq', 0, 0, axis_index_groups=columns)  3.91 us
  transfers between devices with their start and end apart: 2, of which 2 were waited for; matrix products, arithmetic and copies ran while one was open for 0% of the time, Pallas kernels for 0%

profile of v8, /device:TPU:1, one launch (start us, length us, event | category | flops | bytes accessed | tf_op | source)
XLA Modules:
  0.0 98.1 jit_solution(16205924520862434130)
XLA Ops:
  0.6 1.7 %shard_map.149 = bf16[8,2,128,128]{3,2,1,0:T(8,128)(2,1)} custom-call(bf16[128,128]{1,0:T(8,128)(2,1)} %bitcast.12, bf16[128,128]{1,0:T(8,128)(2,1)} %bitcast.13), custom_call_target="tpu_custom_call" | custom-call | tf_op jit(solution)/shard_map/pallas_call | solution.py:236
  2.4 0.0 copy-start.10
  2.4 0.0 copy-start.9
  2.4 7.8 %all-to-all-start = ((bf16[8,2,128,128]{3,2,1,0:T(8,128)(2,1)}), bf16[8,2,128,128]{3,2,1,0:T(8,128)(2,1)S(1)}, u32[]{:S(2)}, u32[]{:S(2)}) async-start(bf16[8,2,128,128]{3,2,1,0:T(8,128)(2,1)} %shard_map.149), calls=%async_computation | async-start | bytes 1048576 | tf_op jit(solution)/shard_map/all_to_all | solution.py:312
  10.2 0.2 copy.20
  10.4 10.6 %all-gather = bf16[8,128,128]{2,1,0:T(8,128)(2,1)S(1)} all-gather(bf16[2,128,128]{2,1,0:T(8,128)(2,1)S(1)} %bitcast.11), channel_id=2, replica_groups={{0,8,16,24},{4,12,20,28},{32,40,48,56},{36,44,52,60},{64,72,80,88},{68,..., dimensions={0}, use_global_device_ids=true | all-gather | bytes 327680 | tf_op jit(solution)/shard_map/all_gather | solution.py:313
  21.0 3.9 %all-to-all-done.own_ref = bf16[8,2,128,128]{3,2,1,0:T(8,128)(2,1)S(1)} async-done(((bf16[8,2,128,128]{3,2,1,0:T(8,128)(2,1)}), bf16[8,2,128,128]{3,2,1,0:T(8,128)(2,1)S(1)}, u32[]{:S(2)}, u32[]{:S(2)}) %all-to-all-start) | async-done | bytes 524320 | tf_op jit(solution)/shard_map/all_to_all | solution.py:312
  24.9 5.6 %collective-permute-start = (bf16[8,2,128,128]{3,2,1,0:T(8,128)(2,1)S(1)}, bf16[8,2,128,128]{3,2,1,0:T(8,128)(2,1)S(1)}, u32[]{:S(2)}, u32[]{:S(2)}) collective-permute-start(bf16[8,2,128,128]{3,2,1,0:T(8,128)(2,1)S(1)} %all-to-all-done.own_ref), channel_id=1, source_target_pairs={{0,4},{4,0},{8,12},{12,8},{16,20},{20,16},{24,28},{28,24},{32,36},... | collective-permute-start | bytes 1572872 | tf_op jit(solution)/shard_map/ppermute | solution.py:316
  30.5 1.5 %collective-permute-done.sibling_ref = bf16[8,2,128,128]{3,2,1,0:T(8,128)(2,1)S(1)} collective-permute-done((bf16[8,2,128,128]{3,2,1,0:T(8,128)(2,1)S(1)}, bf16[8,2,128,128]{3,2,1,0:T(8,128)(2,1)S(1)}, u32[]{:S(2)}, u32[]{:S(2)}) %collective-permute-start) | collective-permute-done | bytes 524320 | tf_op jit(solution)/shard_map/ppermute | solution.py:316
  32.0 2.1 %shard_map.150 = bf16[4,272,128]{2,1,0:T(8,128)(2,1)S(1)} custom-call(bf16[4,2,128,128]{3,2,1,0:T(8,128)(2,1)S(1)} %bitcast.9, bf16[8,2,128,128]{3,2,1,0:T(8,128)(2,1)S(1)} %all-to-all-done.own_ref, bf16[8,2,128,128]{3,2,1,0:T(8,128)(2,1)S(1)} %collective-permute-done.sibling_ref), custom_call_target="tpu_custom_call" | custom-call | tf_op jit(solution)/shard_map/pallas_call | solution.py:280
  34.1 10.1 %all_to_all.25.parts_ref = bf16[4,272,128]{2,1,0:T(8,128)(2,1)S(1)} all-to-all(bf16[4,272,128]{2,1,0:T(8,128)(2,1)S(1)} %shard_map.150), channel_id=1, replica_groups={{0,8,16,24},{4,12,20,28},{32,40,48,56},{36,44,52,60},{64,72,80,88},{68,..., dimensions={0} | all-to-all | bytes 557056 | tf_op jit(solution)/shard_map/all_to_all | solution.py:318
  44.2 0.7 shard_map.151
  44.9 0.0 copy-start.2
  45.0 0.0 copy-start.3
  45.0 0.0 copy-start.5
  45.0 0.0 copy-start.6
  45.0 17.7 %all_to_all.26.parts_ref = bf16[8,128,128]{2,1,0:T(8,128)(2,1)S(1)} all-to-all(bf16[8,128,128]{2,1,0:T(8,128)(2,1)S(1)} %shard_map.151), channel_id=1, replica_groups=mesh['role'=2,'seq'=64,'head'=4] {'role','head'}, dimensions={0} | all-to-all | bytes 524288 | tf_op jit(solution)/shard_map/all_to_all | solution.py:320
  62.7 0.0 copy-start
  62.8 0.0 copy-start.1
  62.8 0.2 shard_map.152
  63.0 18.0 %all_to_all.27.in_ref = bf16[64,8,128]{2,1,0:T(8,128)(2,1)S(1)} all-to-all(bf16[64,8,128]{2,1,0:T(8,128)(2,1)S(1)} %shard_map.152), channel_id=1, replica_groups=mesh['role'=2,'seq'=64,'head'=4] {'seq'}, dimensions={0} | all-to-all | bytes 262144 | tf_op jit(solution)/shard_map/all_to_all | solution.py:322
  81.0 2.6 %shard_map.153 = bf16[64,4,128]{2,1,0:T(4,128)(2,1)S(1)} custom-call(f32[128]{0:T(128)} %skip_ref.1, bf16[64,8,128]{2,1,0:T(8,128)(2,1)S(1)} %all_to_all.27.in_ref, f32[72,128]{1,0:T(8,128)S(1)} %copy-done.6, f32[72,128]{1,0:T(8,128)S(1)} %copy-done.5, bf16[144,192]{1,0:T(8,128)(2,1)S(1)} %copy-done.2, bf16[64,432]{1,0:T(8,128)(2,1)S(1)} %copy-done.3, ...), custom_call_target="tpu_custom_call" | custom-call | tf_op jit(solution)/shard_map/pallas_call | solution.py:260
  83.6 13.8 %all_to_all.28.in_ref = bf16[64,4,128]{2,1,0:T(4,128)(2,1)S(1)} all-to-all(bf16[64,4,128]{2,1,0:T(4,128)(2,1)S(1)} %shard_map.153), channel_id=1, replica_groups=mesh['role'=2,'seq'=64,'head'=4] {'seq'}, dimensions={0} | all-to-all | bytes 131072 | tf_op jit(solution)/shard_map/all_to_all | solution.py:324
  97.4 0.7 shard_map.154
  (15 shorter events, 0.0 us)
Async XLA Ops:
  2.4 7.8 %copy-start.10 = (bf16[128,2,128]{2,1,0:T(2,128)(2,1)S(1)}, bf16[128,2,128]{2,1,0:T(2,128)(2,1)}, u32[]{:S(2)}) copy-start(bf16[128,2,128]{2,1,0:T(2,128)(2,1)} %param.14) | copy-start | bytes 196612
  2.4 7.8 %copy-start.9 = (bf16[2,128,1024]{2,1,0:T(8,128)(2,1)S(1)}, bf16[2,128,1024]{2,1,0:T(8,128)(2,1)}, u32[]{:S(2)}) copy-start(bf16[2,128,1024]{2,1,0:T(8,128)(2,1)} %param.17) | copy-start | bytes 1572868
  2.4 22.5 %all-to-all-start = ((bf16[8,2,128,128]{3,2,1,0:T(8,128)(2,1)}), bf16[8,2,128,128]{3,2,1,0:T(8,128)(2,1)S(1)}, u32[]{:S(2)}, u32[]{:S(2)}) async-start(bf16[8,2,128,128]{3,2,1,0:T(8,128)(2,1)} %shard_map.149), calls=%async_computation | async-start | bytes 1048576 | tf_op jit(solution)/shard_map/all_to_all | solution.py:312
  24.9 7.1 %collective-permute-start = (bf16[8,2,128,128]{3,2,1,0:T(8,128)(2,1)S(1)}, bf16[8,2,128,128]{3,2,1,0:T(8,128)(2,1)S(1)}, u32[]{:S(2)}, u32[]{:S(2)}) collective-permute-start(bf16[8,2,128,128]{3,2,1,0:T(8,128)(2,1)S(1)} %all-to-all-done.own_ref), channel_id=1, source_target_pairs={{0,4},{4,0},{8,12},{12,8},{16,20},{20,16},{24,28},{28,24},{32,36},... | collective-permute-start | bytes 1572872 | tf_op jit(solution)/shard_map/ppermute | solution.py:316
  44.9 17.8 %copy-start.4 = (f32[128,128]{1,0:T(8,128)S(1)}, f32[128,128]{1,0:T(8,128)}, u32[]{:S(2)}) copy-start(f32[128,128]{1,0:T(8,128)} %taps_ref.1) | copy-start | bytes 196612
  44.9 17.8 %copy-start.7 = (bf16[128,128]{1,0:T(8,128)(2,1)S(1)}, bf16[128,128]{1,0:T(8,128)(2,1)}, u32[]{:S(2)}) copy-start(bf16[128,128]{1,0:T(8,128)(2,1)} %input_ref.1) | copy-start | bytes 98308
  44.9 17.8 %copy-start.8 = (bf16[128,128]{1,0:T(8,128)(2,1)S(1)}, bf16[128,128]{1,0:T(8,128)(2,1)}, u32[]{:S(2)}) copy-start(bf16[128,128]{1,0:T(8,128)(2,1)} %gate_ref.1) | copy-start | bytes 98308
  44.9 36.0 %copy-start.2 = (bf16[144,192]{1,0:T(8,128)(2,1)S(1)}, bf16[144,192]{1,0:T(8,128)(2,1)}, u32[]{:S(2)}) copy-start(bf16[144,192]{1,0:T(8,128)(2,1)} %constant.14.clone.first) | copy-start | bytes 165892
  45.0 36.0 %copy-start.3 = (bf16[64,432]{1,0:T(8,128)(2,1)S(1)}, bf16[64,432]{1,0:T(8,128)(2,1)}, u32[]{:S(2)}) copy-start(bf16[64,432]{1,0:T(8,128)(2,1)} %constant.15.clone.last) | copy-start | bytes 165892
  45.0 36.0 %copy-start.5 = (f32[72,128]{1,0:T(8,128)S(1)}, f32[72,128]{1,0:T(8,128)}, u32[]{:S(2)}) copy-start(f32[72,128]{1,0:T(8,128)} %constant.13.clone.ts) | copy-start | bytes 110596
  45.0 36.0 %copy-start.6 = (f32[72,128]{1,0:T(8,128)S(1)}, f32[72,128]{1,0:T(8,128)}, u32[]{:S(2)}) copy-start(f32[72,128]{1,0:T(8,128)} %constant.12.clone.tc) | copy-start | bytes 110596
  62.7 18.2 %copy-start = (bf16[768,256]{1,0:T(8,128)(2,1)S(1)}, bf16[768,256]{1,0:T(8,128)(2,1)}, u32[]{:S(2)}) copy-start(bf16[768,256]{1,0:T(8,128)(2,1)} %constant.17.clone.backward) | copy-start | bytes 1179652
  62.8 18.2 %copy-start.1 = (bf16[768,256]{1,0:T(8,128)(2,1)S(1)}, bf16[768,256]{1,0:T(8,128)(2,1)}, u32[]{:S(2)}) copy-start(bf16[768,256]{1,0:T(8,128)(2,1)} %constant.16.clone.forward) | copy-start | bytes 1179652

commit v9 on v8

--- a/solution.py
+++ b/solution.py
@@ -86,19 +86,9 @@
     return jnp.concatenate([ar * br + ai * bi, ar * bi - ai * br], 1)
 
 
-def repeat_kernel(key_ref, value_ref, out_ref, held, arrived, done):
-    loads = []
-    for m, ref in enumerate((key_ref, value_ref)):
-        loads.append(pltpu.make_async_copy(ref, held.at[m], arrived.at[m]))
-        loads[m].start()
-    copies = []
-    for m in (0, 1):
-        loads[m].wait()
-        for n in range(SHARDS // ROW):
-            copies.append(pltpu.make_async_copy(held.at[m], out_ref.at[n, m], done.at[n, m]))
-            copies[-1].start()
-    for copy in copies:
-        copy.wait()
+def join_kernel(*refs):
+    for n in range(BACK + 1):
+        refs[-1][n] = refs[n][...]
 
 
 def pack_kernel(parts_ref, input_ref, gate_ref, taps_ref, out_ref, wide_ref):
@@ -149,11 +139,11 @@
     rank = lax.axis_index("seq")
     row, mine, core = rank // ROW, rank % ROW // 2, rank % 2
     scale = 128 ** -0.5
-    order = [row] + [jnp.maximum(row - BACK + r, 0) for r in range(BACK)]
     sources = (own_ref, sibling_ref)
-    keys = jnp.concatenate([ref[n, 0] for ref in sources for n in order], 0)
+    keys = jnp.concatenate([ref[n, 0] for ref in sources for n in range(BACK + 1)], 0)
     ones = jnp.ones((10 * SHARD, 128), jnp.bfloat16)
-    values = jnp.concatenate([jnp.concatenate([ref[n, 1] for ref in sources for n in order], 0), ones], 1)
+    values = [ref[n, 1] for ref in sources for n in range(BACK + 1)]
+    values = jnp.concatenate([jnp.concatenate(values, 0), ones], 1)
     lag = lax.broadcasted_iota(jnp.int32, (SHARD, SHARD), 0) - lax.broadcasted_iota(jnp.int32, (SHARD, SHARD), 1)
     diagonal = lag == 0
     zero = jnp.zeros((SHARD, SHARD), jnp.float32)
@@ -231,19 +221,13 @@
     return pltpu.with_memory_space_constraint(x, pltpu.VMEM)
 
 
-def call_repeat(key, value):
-    anywhere = pl.BlockSpec(memory_space=pl.ANY)
-    return pl.pallas_call(
-        repeat_kernel,
-        out_shape=jax.ShapeDtypeStruct((SHARDS // ROW, 2, SHARD, 128), jnp.bfloat16),
-        in_specs=[anywhere] * 2,
-        out_specs=anywhere,
-        scratch_shapes=[
-            pltpu.VMEM((2, SHARD, 128), jnp.bfloat16),
-            pltpu.SemaphoreType.DMA((2,)),
-            pltpu.SemaphoreType.DMA((SHARDS // ROW, 2)),
-        ],
-    )(key, value)
+def call_join(blocks):
+    return pl.pallas_call(
+        join_kernel,
+        out_shape=pltpu.VMEM((BACK + 1, 2, SHARD, 128), jnp.bfloat16),
+        in_specs=[VMEM] * (BACK + 1),
+        out_specs=VMEM,
+    )(*[near(block) for block in blocks])
 
 
 def call_pack(parts, *inputs):
@@ -307,12 +291,18 @@
     tables = [near(jnp.asarray(t)) for t in transform_tables()]
     lines = range(SHARDS // ROW)
     groups = [[y * ROW + 2 * x + core for x in range(GROUP)] for y in lines for core in (0, 1)]
-    columns = [[y * ROW + p for y in lines] for p in range(ROW)]
-    pairs = call_repeat(key_heads[:, 0], value_heads[:, 0])
-    own = lax.all_to_all(pairs, "seq", 0, 0, axis_index_groups=columns)
-    queries = lax.all_gather(jnp.transpose(query_heads, (1, 0, 2)), "seq", axis_index_groups=groups)
+    queries = jnp.transpose(query_heads, (1, 0, 2))
+    queries = lax.all_to_all(
+        jnp.broadcast_to(queries, (GROUP,) + queries.shape), "seq", 0, 0, axis_index_groups=groups
+    )
+    block = jnp.stack([key_heads[:, 0], value_heads[:, 0]])
+    blocks = [
+        lax.ppermute(block, "seq", [(i, i + ROW * k) for i in range(SHARDS - ROW * k)])
+        for k in range(1, BACK + 1)
+    ]
     proj = distill_proj.reshape(256, 1024).T
-    own, queries, proj = lax.optimization_barrier((own, queries, proj))
+    own = call_join([block] + blocks[::-1])
+    queries, proj, own = lax.optimization_barrier((queries, proj, own))
     sibling = lax.ppermute(own, "seq", [(i, i ^ 1) for i in range(SHARDS)])
     parts = call_attend(queries, own, sibling)
     parts = lax.all_to_all(parts, "seq", 0, 0, axis_index_groups=groups)

time: 98.6 us -> 102 us (1.034)
  starting transfers between devices: 13.4 us -> 22.8 us
  blocking collectives: 70.2 us -> 66.5 us
  waiting for transfers between devices: 5.43 us -> 2.89 us
  Pallas kernels: 7.99 us -> 6.29 us
  local copies, waits for them, and re-layouts: 0.29 us -> 1.87 us
    ppermute x0 -> x4, starting transfers between devices: none -> 14.1 us  [body(): lax.ppermute(block, 'seq', [(i, i + ROW * k) for i in range(SHARDS - ROW...]
    all_gather x1 -> x0, blocking collectives: 10.6 us -> none  [body(): lax.all_gather(jnp.transpose(query_heads, (1, 0, 2)), 'seq', axis_index_g...]
    all_to_all x1, blocking collectives: 18 us -> 24.3 us  [body(): packed = lax.all_to_all(packed, 'seq', 0, 0)]
    all_to_all x1, waiting for transfers between devices: 3.91 us -> 0.01 us  [body(): lax.all_to_all(jnp.broadcast_to(queries, (GROUP,) + queries.shape), 'seq'...]
    all_to_all x1, starting transfers between devices: 7.79 us -> 4.97 us  [body(): lax.all_to_all(jnp.broadcast_to(queries, (GROUP,) + queries.shape), 'seq'...]
    ppermute x1, starting transfers between devices: 5.59 us -> 3.7 us  [body(): sibling = lax.ppermute(own, 'seq', [(i, i ^ 1) for i in range(SHARDS)])]
    pallas_call x1, Pallas kernels: 1.72 us -> 0.02 us  [call_join(): pl.pallas_call(join_kernel, out_shape=pltpu.VMEM((BACK + 1, 2, SHARD, 128...]
    ppermute x0 -> x4, waiting for transfers between devices: none -> 1.65 us  [body(): lax.ppermute(block, 'seq', [(i, i + ROW * k) for i in range(SHARDS - ROW...]
  transfers between devices with their start and end apart: 2 -> 6, of which waited for: 2 -> 2; matrix products, arithmetic and copies ran while one was open for 0% -> 0% of each run, Pallas kernels for 0% -> 0%
where the time goes in v9:
time: 102 us; the launch traced here: 101 us
  blocking collectives  66.5 us (65%)
  starting transfers between devices  22.8 us (22%)
  Pallas kernels  6.29 us (6%)
  waiting for transfers between devices  2.89 us (3%)
  local copies, waits for them, and re-layouts  1.87 us (2%)
    all_to_all x1, blocking collectives, body(): packed = lax.all_to_all(packed, 'seq', 0, 0)  24.3 us
    all_to_all x1, blocking collectives, body(): target = lax.all_to_all(target, ('role', 'head'), 0, 0)  17.8 us
    ppermute x4, starting transfers between devices, body(): lax.ppermute(block, 'seq', [(i, i + ROW * k) for i in range(SHARDS - ROW...  14.1 us
    all_to_all x1, blocking collectives, body(): out = lax.all_to_all(out, 'seq', 0, 0)  13.9 us
    all_to_all x1, blocking collectives, body(): parts = lax.all_to_all(parts, 'seq', 0, 0, axis_index_groups=groups)  10.6 us
    all_to_all x1, starting transfers between devices, body(): lax.all_to_all(jnp.broadcast_to(queries, (GROUP,) + queries.shape), 'seq'...  4.97 us
    ppermute x1, starting transfers between devices, body(): sibling = lax.ppermute(own, 'seq', [(i, i ^ 1) for i in range(SHARDS)])  3.7 us
    pallas_call x1, Pallas kernels, call_student(): pl.pallas_call(student_kernel, out_shape=pltpu.VMEM((SHARDS, 4, 128), jnp...  2.59 us
  transfers between devices with their start and end apart: 6, of which 2 were waited for; matrix products, arithmetic and copies ran while one was open for 0% of the time, Pallas kernels for 0%

profile of v9, /device:TPU:1, one launch (start us, length us, event | category | flops | bytes accessed | tf_op | source)
XLA Modules:
  0.0 101.2 jit_solution(14180196274856691872)
XLA Ops:
  0.6 0.9 copy.16
  1.5 0.7 broadcast_in_dim.3
  2.2 5.0 %all-to-all-start = ((bf16[4,2,128,128]{3,2,1,0:T(8,128)(2,1)}), bf16[4,2,128,128]{3,2,1,0:T(8,128)(2,1)S(1)}, u32[]{:S(2)}, u32[]{:S(2)}) async-start(bf16[4,2,128,128]{3,2,1,0:T(8,128)(2,1)} %broadcast_in_dim.3), calls=%async_computation | async-start | bytes 524288 | tf_op jit(solution)/shard_map/all_to_all | solution.py:295
  7.2 3.2 %collective-permute-start.3 = (bf16[2,128,128]{2,1,0:T(8,128)(2,1)S(1)}, bf16[2,128,128]{2,1,0:T(8,128)(2,1)S(1)}, u32[]{:S(2)}, u32[]{:S(2)}) collective-permute-start(bf16[2,128,128]{2,1,0:T(8,128)(2,1)S(1)} %pad_maximum_fusion.refs_0_), channel_id=1, source_target_pairs={{0,32},{4,36},{8,40},{12,44},{16,48},{20,52},{24,56},{28,60},{32,6... | collective-permute-start | bytes 196616 | tf_op jit(solution)/shard_map/ppermute | solution.py:300
  10.4 4.2 %collective-permute-start.2 = (bf16[2,128,128]{2,1,0:T(8,128)(2,1)S(1)}, bf16[2,128,128]{2,1,0:T(8,128)(2,1)S(1)}, u32[]{:S(2)}, u32[]{:S(2)}) collective-permute-start(bf16[2,128,128]{2,1,0:T(8,128)(2,1)S(1)} %pad_maximum_fusion.refs_0_), channel_id=1, source_target_pairs={{0,64},{4,68},{8,72},{12,76},{16,80},{20,84},{24,88},{28,92},{32,9... | collective-permute-start | bytes 196616 | tf_op jit(solution)/shard_map/ppermute | solution.py:300
  14.7 4.6 %collective-permute-start.1 = (bf16[2,128,128]{2,1,0:T(8,128)(2,1)S(1)}, bf16[2,128,128]{2,1,0:T(8,128)(2,1)S(1)}, u32[]{:S(2)}, u32[]{:S(2)}) collective-permute-start(bf16[2,128,128]{2,1,0:T(8,128)(2,1)S(1)} %pad_maximum_fusion.refs_0_), channel_id=1, source_target_pairs={{0,96},{4,100},{8,104},{12,108},{16,112},{20,116},{24,120},{28,124... | collective-permute-start | bytes 196616 | tf_op jit(solution)/shard_map/ppermute | solution.py:300
  19.3 2.0 %collective-permute-start = (bf16[2,128,128]{2,1,0:T(8,128)(2,1)S(1)}, bf16[2,128,128]{2,1,0:T(8,128)(2,1)S(1)}, u32[]{:S(2)}, u32[]{:S(2)}) collective-permute-start(bf16[2,128,128]{2,1,0:T(8,128)(2,1)S(1)} %pad_maximum_fusion.refs_0_), channel_id=1, source_target_pairs={{0,128},{4,132},{8,136},{12,140},{16,144},{20,148},{24,152},{28,15... | collective-permute-start | bytes 196616 | tf_op jit(solution)/shard_map/ppermute | solution.py:300
  21.4 0.2 copy.18
  21.6 1.6 %collective-permute-done.refs_1_ = bf16[2,128,128]{2,1,0:T(8,128)(2,1)S(1)} collective-permute-done((bf16[2,128,128]{2,1,0:T(8,128)(2,1)S(1)}, bf16[2,128,128]{2,1,0:T(8,128)(2,1)S(1)}, u32[]{:S(2)}, u32[]{:S(2)}) %collective-permute-start) | collective-permute-done | bytes 65568 | tf_op jit(solution)/shard_map/ppermute | solution.py:300
  23.3 3.7 %collective-permute-start.4 = (bf16[5,2,128,128]{3,2,1,0:T(8,128)(2,1)S(1)}, bf16[5,2,128,128]{3,2,1,0:T(8,128)(2,1)S(1)}, u32[]{:S(2)}, u32[]{:S(2)}) collective-permute-start(bf16[5,2,128,128]{3,2,1,0:T(8,128)(2,1)S(1)} %shard_map.149.own_ref), channel_id=1, source_target_pairs={{0,4},{4,0},{8,12},{12,8},{16,20},{20,16},{24,28},{28,24},{32,36},... | collective-permute-start | bytes 983048 | tf_op jit(solution)/shard_map/ppermute | solution.py:306
  27.0 1.2 %collective-permute-done.4.sibling_ref = bf16[5,2,128,128]{3,2,1,0:T(8,128)(2,1)S(1)} collective-permute-done((bf16[5,2,128,128]{3,2,1,0:T(8,128)(2,1)S(1)}, bf16[5,2,128,128]{3,2,1,0:T(8,128)(2,1)S(1)}, u32[]{:S(2)}, u32[]{:S(2)}) %collective-permute-start.4) | collective-permute-done | bytes 327712 | tf_op jit(solution)/shard_map/ppermute | solution.py:306
  28.2 2.1 %shard_map.150 = bf16[4,272,128]{2,1,0:T(8,128)(2,1)S(1)} custom-call(bf16[4,2,128,128]{3,2,1,0:T(8,128)(2,1)S(1)} %all-to-all-done.q_ref, bf16[5,2,128,128]{3,2,1,0:T(8,128)(2,1)S(1)} %shard_map.149.own_ref, bf16[5,2,128,128]{3,2,1,0:T(8,128)(2,1)S(1)} %collective-permute-done.4.sibling_ref), custom_call_target="tpu_custom_call" | custom-call | tf_op jit(solution)/shard_map/pallas_call | solution.py:264
  30.3 10.6 %all_to_all.25.parts_ref = bf16[4,272,128]{2,1,0:T(8,128)(2,1)S(1)} all-to-all(bf16[4,272,128]{2,1,0:T(8,128)(2,1)S(1)} %shard_map.150), channel_id=1, replica_groups={{0,8,16,24},{4,12,20,28},{32,40,48,56},{36,44,52,60},{64,72,80,88},{68,..., dimensions={0} | all-to-all | bytes 557056 | tf_op jit(solution)/shard_map/all_to_all | solution.py:308
  40.9 0.7 shard_map.151
  41.6 0.0 copy-start.2
  41.6 0.0 copy-start.3
  41.7 0.0 copy-start.6
  41.7 17.8 %all_to_all.26.parts_ref = bf16[8,128,128]{2,1,0:T(8,128)(2,1)S(1)} all-to-all(bf16[8,128,128]{2,1,0:T(8,128)(2,1)S(1)} %shard_map.151), channel_id=1, replica_groups=mesh['role'=2,'seq'=64,'head'=4] {'role','head'}, dimensions={0} | all-to-all | bytes 524288 | tf_op jit(solution)/shard_map/all_to_all | solution.py:310
  59.4 0.0 copy-start
  59.5 0.2 shard_map.152
  59.7 24.3 %all_to_all.27.in_ref = bf16[64,8,128]{2,1,0:T(8,128)(2,1)S(1)} all-to-all(bf16[64,8,128]{2,1,0:T(8,128)(2,1)S(1)} %shard_map.152), channel_id=1, replica_groups=mesh['role'=2,'seq'=64,'head'=4] {'seq'}, dimensions={0} | all-to-all | bytes 262144 | tf_op jit(solution)/shard_map/all_to_all | solution.py:312
  84.0 2.6 %shard_map.153 = bf16[64,4,128]{2,1,0:T(4,128)(2,1)S(1)} custom-call(f32[128]{0:T(128)} %skip_ref.1, bf16[64,8,128]{2,1,0:T(8,128)(2,1)S(1)} %all_to_all.27.in_ref, f32[72,128]{1,0:T(8,128)S(1)} %copy-done.6, f32[72,128]{1,0:T(8,128)S(1)} %copy-done.5, bf16[144,192]{1,0:T(8,128)(2,1)S(1)} %copy-done.2, bf16[64,432]{1,0:T(8,128)(2,1)S(1)} %copy-done.3, ...), custom_call_target="tpu_custom_call" | custom-call | tf_op jit(solution)/shard_map/pallas_call | solution.py:244
  86.6 13.9 %all_to_all.28.in_ref = bf16[64,4,128]{2,1,0:T(4,128)(2,1)S(1)} all-to-all(bf16[64,4,128]{2,1,0:T(4,128)(2,1)S(1)} %shard_map.153), channel_id=1, replica_groups=mesh['role'=2,'seq'=64,'head'=4] {'seq'}, dimensions={0} | all-to-all | bytes 131072 | tf_op jit(solution)/shard_map/all_to_all | solution.py:314
  100.5 0.7 shard_map.154
  (26 shorter events, 0.1 us)
Async XLA Ops:
  1.5 19.9 %copy-start.9 = (bf16[2,128,1024]{2,1,0:T(8,128)(2,1)S(1)}, bf16[2,128,1024]{2,1,0:T(8,128)(2,1)}, u32[]{:S(2)}) copy-start(bf16[2,128,1024]{2,1,0:T(8,128)(2,1)} %param.17) | copy-start | bytes 1572868
  2.2 5.0 %copy-start.10 = (bf16[128,1,128]{2,0,1:T(8,128)(2,1)S(1)}, bf16[128,1,128]{2,0,1:T(8,128)(2,1)}, u32[]{:S(2)}) copy-start(bf16[128,1,128]{2,0,1:T(8,128)(2,1)} %param.16) | copy-start | bytes 98308
  2.2 5.0 %copy-start.11 = (bf16[128,1,128]{2,0,1:T(8,128)(2,1)S(1)}, bf16[128,1,128]{2,0,1:T(8,128)(2,1)}, u32[]{:S(2)}) copy-start(bf16[128,1,128]{2,0,1:T(8,128)(2,1)} %param.15) | copy-start | bytes 98308
  2.2 21.0 %all-to-all-start = ((bf16[4,2,128,128]{3,2,1,0:T(8,128)(2,1)}), bf16[4,2,128,128]{3,2,1,0:T(8,128)(2,1)S(1)}, u32[]{:S(2)}, u32[]{:S(2)}) async-start(bf16[4,2,128,128]{3,2,1,0:T(8,128)(2,1)} %broadcast_in_dim.3), calls=%async_computation | async-start | bytes 524288 | tf_op jit(solution)/shard_map/all_to_all | solution.py:295
  7.2 14.3 %collective-permute-start.3 = (bf16[2,128,128]{2,1,0:T(8,128)(2,1)S(1)}, bf16[2,128,128]{2,1,0:T(8,128)(2,1)S(1)}, u32[]{:S(2)}, u32[]{:S(2)}) collective-permute-start(bf16[2,128,128]{2,1,0:T(8,128)(2,1)S(1)} %pad_maximum_fusion.refs_0_), channel_id=1, source_target_pairs={{0,32},{4,36},{8,40},{12,44},{16,48},{20,52},{24,56},{28,60},{32,6... | collective-permute-start | bytes 196616 | tf_op jit(solution)/shard_map/ppermute | solution.py:300
  10.4 11.1 %collective-permute-start.2 = (bf16[2,128,128]{2,1,0:T(8,128)(2,1)S(1)}, bf16[2,128,128]{2,1,0:T(8,128)(2,1)S(1)}, u32[]{:S(2)}, u32[]{:S(2)}) collective-permute-start(bf16[2,128,128]{2,1,0:T(8,128)(2,1)S(1)} %pad_maximum_fusion.refs_0_), channel_id=1, source_target_pairs={{0,64},{4,68},{8,72},{12,76},{16,80},{20,84},{24,88},{28,92},{32,9... | collective-permute-start | bytes 196616 | tf_op jit(solution)/shard_map/ppermute | solution.py:300
  14.7 6.9 %collective-permute-start.1 = (bf16[2,128,128]{2,1,0:T(8,128)(2,1)S(1)}, bf16[2,128,128]{2,1,0:T(8,128)(2,1)S(1)}, u32[]{:S(2)}, u32[]{:S(2)}) collective-permute-start(bf16[2,128,128]{2,1,0:T(8,128)(2,1)S(1)} %pad_maximum_fusion.refs_0_), channel_id=1, source_target_pairs={{0,96},{4,100},{8,104},{12,108},{16,112},{20,116},{24,120},{28,124... | collective-permute-start | bytes 196616 | tf_op jit(solution)/shard_map/ppermute | solution.py:300
  19.3 3.9 %collective-permute-start = (bf16[2,128,128]{2,1,0:T(8,128)(2,1)S(1)}, bf16[2,128,128]{2,1,0:T(8,128)(2,1)S(1)}, u32[]{:S(2)}, u32[]{:S(2)}) collective-permute-start(bf16[2,128,128]{2,1,0:T(8,128)(2,1)S(1)} %pad_maximum_fusion.refs_0_), channel_id=1, source_target_pairs={{0,128},{4,132},{8,136},{12,140},{16,144},{20,148},{24,152},{28,15... | collective-permute-start | bytes 196616 | tf_op jit(solution)/shard_map/ppermute | solution.py:300
  23.3 4.9 %collective-permute-start.4 = (bf16[5,2,128,128]{3,2,1,0:T(8,128)(2,1)S(1)}, bf16[5,2,128,128]{3,2,1,0:T(8,128)(2,1)S(1)}, u32[]{:S(2)}, u32[]{:S(2)}) collective-permute-start(bf16[5,2,128,128]{3,2,1,0:T(8,128)(2,1)S(1)} %shard_map.149.own_ref), channel_id=1, source_target_pairs={{0,4},{4,0},{8,12},{12,8},{16,20},{20,16},{24,28},{28,24},{32,36},... | collective-permute-start | bytes 983048 | tf_op jit(solution)/shard_map/ppermute | solution.py:306
  41.6 17.8 %copy-start.4 = (f32[128,128]{1,0:T(8,128)S(1)}, f32[128,128]{1,0:T(8,128)}, u32[]{:S(2)}) copy-start(f32[128,128]{1,0:T(8,128)} %taps_ref.1) | copy-start | bytes 196612
  41.6 17.8 %copy-start.7 = (bf16[128,128]{1,0:T(8,128)(2,1)S(1)}, bf16[128,128]{1,0:T(8,128)(2,1)}, u32[]{:S(2)}) copy-start(bf16[128,128]{1,0:T(8,128)(2,1)} %input_ref.1) | copy-start | bytes 98308
  41.6 17.8 %copy-start.8 = (bf16[128,128]{1,0:T(8,128)(2,1)S(1)}, bf16[128,128]{1,0:T(8,128)(2,1)}, u32[]{:S(2)}) copy-start(bf16[128,128]{1,0:T(8,128)(2,1)} %gate_ref.1) | copy-start | bytes 98308
  41.6 42.3 %copy-start.2 = (bf16[144,192]{1,0:T(8,128)(2,1)S(1)}, bf16[144,192]{1,0:T(8,128)(2,1)}, u32[]{:S(2)}) copy-start(bf16[144,192]{1,0:T(8,128)(2,1)} %constant.14.clone.first) | copy-start | bytes 165892
  41.6 42.3 %copy-start.3 = (bf16[64,432]{1,0:T(8,128)(2,1)S(1)}, bf16[64,432]{1,0:T(8,128)(2,1)}, u32[]{:S(2)}) copy-start(bf16[64,432]{1,0:T(8,128)(2,1)} %constant.15.clone.last) | copy-start | bytes 165892
  41.6 42.3 %copy-start.5 = (f32[72,128]{1,0:T(8,128)S(1)}, f32[72,128]{1,0:T(8,128)}, u32[]{:S(2)}) copy-start(f32[72,128]{1,0:T(8,128)} %constant.13.clone.ts) | copy-start | bytes 110596
  41.7 42.3 %copy-start.6 = (f32[72,128]{1,0:T(8,128)S(1)}, f32[72,128]{1,0:T(8,128)}, u32[]{:S(2)}) copy-start(f32[72,128]{1,0:T(8,128)} %constant.12.clone.tc) | copy-start | bytes 110596
  59.4 24.6 %copy-start = (bf16[768,256]{1,0:T(8,128)(2,1)S(1)}, bf16[768,256]{1,0:T(8,128)(2,1)}, u32[]{:S(2)}) copy-start(bf16[768,256]{1,0:T(8,128)(2,1)} %constant.17.clone.backward) | copy-start | bytes 1179652
  59.4 24.6 %copy-start.1 = (bf16[768,256]{1,0:T(8,128)(2,1)S(1)}, bf16[768,256]{1,0:T(8,128)(2,1)}, u32[]{:S(2)}) copy-start(bf16[768,256]{1,0:T(8,128)(2,1)} %constant.16.clone.forward) | copy-start | bytes 1179652

commit v10 on v8

--- a/solution.py
+++ b/solution.py
@@ -105,7 +105,7 @@
     target = parts_ref[0].astype(jnp.float32)
     for n in range(1, 8):
         target += parts_ref[n].astype(jnp.float32)
-    arrays = (target, input_ref[...], gate_ref[...], taps_ref[...])
+    arrays = (target.T, input_ref[...], gate_ref[...], taps_ref[...])
     for n, array in enumerate(arrays):
         array = array.astype(jnp.float32)
         wide_ref[:, 2 * n, :] = array[:SHARDS]
@@ -154,16 +154,21 @@
     keys = jnp.concatenate([ref[n, 0] for ref in sources for n in order], 0)
     ones = jnp.ones((10 * SHARD, 128), jnp.bfloat16)
     values = jnp.concatenate([jnp.concatenate([ref[n, 1] for ref in sources for n in order], 0), ones], 1)
-    lag = lax.broadcasted_iota(jnp.int32, (SHARD, SHARD), 0) - lax.broadcasted_iota(jnp.int32, (SHARD, SHARD), 1)
-    diagonal = lag == 0
+    rows = lax.broadcasted_iota(jnp.int32, (SHARD, SHARD), 0)
+    columns = lax.broadcasted_iota(jnp.int32, (SHARD, SHARD), 1)
+    diagonal = rows == columns
     zero = jnp.zeros((SHARD, SHARD), jnp.float32)
     for theirs in range(GROUP):
         ahead = 2 * (mine - theirs) * SHARD
-        newest = [lag >= ahead, lag >= ahead + (1 - 2 * core) * SHARD]
         stats = []
-        for h in (0, 1):
+        for half in (0, 1):
+            lag = half * (SHARD // 2) + rows // 2 - columns
+            newest = [lag >= ahead, lag >= ahead + (1 - 2 * core) * SHARD]
             scores = lax.dot_general(
-                q_ref[theirs, h], keys, (((1,), (1,)), ((), ())), preferred_element_type=jnp.float32
+                q_ref[theirs, half * SHARD : (half + 1) * SHARD, :],
+                keys,
+                (((1,), (1,)), ((), ())),
+                preferred_element_type=jnp.float32,
             )
             parts = [scores[:, n * SHARD : (n + 1) * SHARD] for n in range(10)]
             blocks = []
@@ -185,7 +190,7 @@
             sums = jnp.dot(spread, values, preferred_element_type=jnp.float32)
             total = sums[:, 128:]
             safe = jnp.maximum(total, 1e-30)
-            out_ref[theirs, h * 128 : (h + 1) * 128, :] = (sums[:, :128] / safe).astype(jnp.bfloat16)
+            out_ref[theirs, half * SHARD : (half + 1) * SHARD, :] = (sums[:, :128] / safe).astype(jnp.bfloat16)
             log_sum = jnp.where(total > 0.0, top * scale + jnp.log(safe), NEG)
             log_sum = jnp.sum(jnp.where(diagonal, log_sum, 0.0), axis=0, keepdims=True)
             high = log_sum.astype(jnp.bfloat16).astype(jnp.float32)
@@ -196,31 +201,29 @@
         out_ref[theirs, 256:272, :] = jnp.concatenate(stats, 0).astype(jnp.bfloat16)
 
 
-def merge_kernel(parts_ref, proj_ref, out_ref):
+def merge_kernel(parts_ref, proj_ref, out_ref, merged_ref):
     shares = []
-    for h in (0, 1):
+    for half in (0, 1):
         sums = []
         for p in range(GROUP):
             stats = parts_ref[p, 256:272, :].astype(jnp.float32)
-            sums.append(stats[3 * h : 3 * h + 1] + stats[3 * h + 1 : 3 * h + 2] + stats[3 * h + 2 : 3 * h + 3])
+            sums.append(jnp.sum(stats[3 * half : 3 * half + 3], axis=0, keepdims=True))
         sums = jnp.concatenate(sums, 0)
         share = jnp.exp(sums - jnp.max(sums, axis=0, keepdims=True))
         shares.append(share / jnp.sum(share, axis=0, keepdims=True))
     shares.append(jnp.zeros((128 - 2 * GROUP, 128), jnp.float32))
     shares = jnp.concatenate(shares, 0).T
-    heads = []
-    for h in (0, 1):
+    for half in (0, 1):
         merged = None
         for p in range(GROUP):
-            part = parts_ref[p, h * 128 : (h + 1) * 128, :].astype(jnp.float32)
-            part = shares[:, h * GROUP + p : h * GROUP + p + 1] * part
+            part = parts_ref[p, half * SHARD : (half + 1) * SHARD, :].astype(jnp.float32)
+            part = shares[:, half * GROUP + p : half * GROUP + p + 1] * part
             merged = part if merged is None else merged + part
-        heads.append(merged.astype(jnp.bfloat16))
-    attended = jnp.concatenate(heads, 1)
-    target = lax.dot_general(
-        proj_ref[...], attended, (((1,), (1,)), ((), ())), preferred_element_type=jnp.float32
-    )
-    out_ref[...] = target.reshape(8, 128, 128).astype(jnp.bfloat16)
+        merged_ref[half * SHARD : (half + 1) * SHARD, :] = merged
+    attended = jnp.concatenate([merged_ref[pl.ds(h, SHARD, stride=2), :] for h in (0, 1)], 1)
+    target = jnp.dot(attended.astype(jnp.bfloat16), proj_ref[...], preferred_element_type=jnp.float32)
+    for n in range(8):
+        out_ref[n] = target[:, n * 128 : (n + 1) * 128].astype(jnp.bfloat16)
 
 
 VMEM = pl.BlockSpec(memory_space=pltpu.VMEM)
@@ -291,6 +294,7 @@
         out_shape=pltpu.VMEM((8, 128, 128), jnp.bfloat16),
         in_specs=[VMEM] * 2,
         out_specs=VMEM,
+        scratch_shapes=[pltpu.VMEM((2 * SHARD, 128), jnp.float32)],
     )(near(parts), near(proj))
 
 
@@ -310,13 +314,12 @@
     columns = [[y * ROW + p for y in lines] for p in range(ROW)]
     pairs = call_repeat(key_heads[:, 0], value_heads[:, 0])
     own = lax.all_to_all(pairs, "seq", 0, 0, axis_index_groups=columns)
-    queries = lax.all_gather(jnp.transpose(query_heads, (1, 0, 2)), "seq", axis_index_groups=groups)
-    proj = distill_proj.reshape(256, 1024).T
-    own, queries, proj = lax.optimization_barrier((own, queries, proj))
+    queries = lax.all_gather(query_heads.reshape(2 * SHARD, 128), "seq", axis_index_groups=groups)
+    own, queries = lax.optimization_barrier((own, queries))
     sibling = lax.ppermute(own, "seq", [(i, i ^ 1) for i in range(SHARDS)])
     parts = call_attend(queries, own, sibling)
     parts = lax.all_to_all(parts, "seq", 0, 0, axis_index_groups=groups)
-    target = call_merge(parts, proj)
+    target = call_merge(parts, distill_proj.reshape(256, 1024))
     target = lax.all_to_all(target, ("role", "head"), 0, 0)
     packed = call_pack(target, conv_input, gate_input, filter_taps)
     packed = lax.all_to_all(packed, "seq", 0, 0)

time: 98.6 us -> 98.6 us (level)
  no operation moved by 1% of the time
where the time goes in v10:
time: 98.6 us; the launch traced here: 98.1 us
  blocking collectives  70.3 us (71%)
  starting transfers between devices  13.4 us (14%)
  Pallas kernels  7.86 us (8%)
  waiting for transfers between devices  5.67 us (6%)
    all_to_all x1, blocking collectives, body(): packed = lax.all_to_all(packed, 'seq', 0, 0)  18 us
    all_to_all x1, blocking collectives, body(): target = lax.all_to_all(target, ('role', 'head'), 0, 0)  17.8 us
    all_to_all x1, blocking collectives, body(): out = lax.all_to_all(out, 'seq', 0, 0)  13.8 us
    all_gather x1, blocking collectives, body(): lax.all_gather(query_heads.reshape(2 * SHARD, 128), 'seq', axis_index_gro...  10.6 us
    all_to_all x1, blocking collectives, body(): parts = lax.all_to_all(parts, 'seq', 0, 0, axis_index_groups=groups)  10.2 us
    all_to_all x1, starting transfers between devices, body(): own = lax.all_to_all(pairs, 'seq', 0, 0, axis_index_groups=columns)  7.79 us
    ppermute x1, starting transfers between devices, body(): sibling = lax.ppermute(own, 'seq', [(i, i ^ 1) for i in range(SHARDS)])  5.59 us
    all_to_all x1, waiting for transfers between devices, body(): own = lax.all_to_all(pairs, 'seq', 0, 0, axis_index_groups=columns)  4.15 us
  transfers between devices with their start and end apart: 2, of which 2 were waited for; matrix products, arithmetic and copies ran while one was open for 0% of the time, Pallas kernels for 0%

profile of v10, /device:TPU:1, one launch (start us, length us, event | category | flops | bytes accessed | tf_op | source)
XLA Modules:
  0.0 98.1 jit_solution(15162916486834080631)
XLA Ops:
  0.6 1.7 %shard_map.149 = bf16[8,2,128,128]{3,2,1,0:T(8,128)(2,1)} custom-call(bf16[128,128]{1,0:T(8,128)(2,1)} %bitcast.6, bf16[128,128]{1,0:T(8,128)(2,1)} %bitcast.7), custom_call_target="tpu_custom_call" | custom-call | tf_op jit(solution)/shard_map/pallas_call | solution.py:239
  2.4 0.0 copy-start.10
  2.4 7.8 %all-to-all-start = ((bf16[8,2,128,128]{3,2,1,0:T(8,128)(2,1)}), bf16[8,2,128,128]{3,2,1,0:T(8,128)(2,1)S(1)}, u32[]{:S(2)}, u32[]{:S(2)}) async-start(bf16[8,2,128,128]{3,2,1,0:T(8,128)(2,1)} %shard_map.149), calls=%async_computation | async-start | bytes 1048576 | tf_op jit(solution)/shard_map/all_to_all | solution.py:316
  10.2 10.6 %all_gather.3.q_ref = bf16[4,256,128]{2,1,0:T(8,128)(2,1)S(1)} all-gather(bf16[1,256,128]{2,1,0:T(8,128)(2,1)S(1)} %bitcast.5), channel_id=1, replica_groups={{0,8,16,24},{4,12,20,28},{32,40,48,56},{36,44,52,60},{64,72,80,88},{68,..., dimensions={0}, use_global_device_ids=true | all-gather | bytes 327680 | tf_op jit(solution)/shard_map/all_gather | solution.py:317
  20.8 4.2 %all-to-all-done.own_ref = bf16[8,2,128,128]{3,2,1,0:T(8,128)(2,1)S(1)} async-done(((bf16[8,2,128,128]{3,2,1,0:T(8,128)(2,1)}), bf16[8,2,128,128]{3,2,1,0:T(8,128)(2,1)S(1)}, u32[]{:S(2)}, u32[]{:S(2)}) %all-to-all-start) | async-done | bytes 524320 | tf_op jit(solution)/shard_map/all_to_all | solution.py:316
  24.9 5.6 %collective-permute-start = (bf16[8,2,128,128]{3,2,1,0:T(8,128)(2,1)S(1)}, bf16[8,2,128,128]{3,2,1,0:T(8,128)(2,1)S(1)}, u32[]{:S(2)}, u32[]{:S(2)}) collective-permute-start(bf16[8,2,128,128]{3,2,1,0:T(8,128)(2,1)S(1)} %all-to-all-done.own_ref), channel_id=1, source_target_pairs={{0,4},{4,0},{8,12},{12,8},{16,20},{20,16},{24,28},{28,24},{32,36},... | collective-permute-start | bytes 1572872 | tf_op jit(solution)/shard_map/ppermute | solution.py:319
  30.5 1.5 %collective-permute-done.sibling_ref = bf16[8,2,128,128]{3,2,1,0:T(8,128)(2,1)S(1)} collective-permute-done((bf16[8,2,128,128]{3,2,1,0:T(8,128)(2,1)S(1)}, bf16[8,2,128,128]{3,2,1,0:T(8,128)(2,1)S(1)}, u32[]{:S(2)}, u32[]{:S(2)}) %collective-permute-start) | collective-permute-done | bytes 524320 | tf_op jit(solution)/shard_map/ppermute | solution.py:319
  32.0 2.0 %shard_map.150 = bf16[4,272,128]{2,1,0:T(8,128)(2,1)S(1)} custom-call(bf16[4,256,128]{2,1,0:T(8,128)(2,1)S(1)} %all_gather.3.q_ref, bf16[8,2,128,128]{3,2,1,0:T(8,128)(2,1)S(1)} %all-to-all-done.own_ref, bf16[8,2,128,128]{3,2,1,0:T(8,128)(2,1)S(1)} %collective-permute-done.sibling_ref), custom_call_target="tpu_custom_call" | custom-call | tf_op jit(solution)/shard_map/pallas_call | solution.py:283
  34.1 0.0 copy-start
  34.1 10.2 %all_to_all.25.parts_ref = bf16[4,272,128]{2,1,0:T(8,128)(2,1)S(1)} all-to-all(bf16[4,272,128]{2,1,0:T(8,128)(2,1)S(1)} %shard_map.150), channel_id=1, replica_groups={{0,8,16,24},{4,12,20,28},{32,40,48,56},{36,44,52,60},{64,72,80,88},{68,..., dimensions={0} | all-to-all | bytes 557056 | tf_op jit(solution)/shard_map/all_to_all | solution.py:321
  44.3 0.6 shard_map.151
  44.9 0.0 copy-start.9
  44.9 0.0 copy-start.3
  44.9 0.0 copy-start.4
  45.0 0.0 copy-start.6
  45.0 0.0 copy-start.7
  45.0 17.8 %all_to_all.26.parts_ref = bf16[8,128,128]{2,1,0:T(8,128)(2,1)S(1)} all-to-all(bf16[8,128,128]{2,1,0:T(8,128)(2,1)S(1)} %shard_map.151), channel_id=1, replica_groups=mesh['role'=2,'seq'=64,'head'=4] {'role','head'}, dimensions={0} | all-to-all | bytes 524288 | tf_op jit(solution)/shard_map/all_to_all | solution.py:323
  62.8 0.0 copy-start.1
  62.8 0.0 copy-start.2
  62.8 0.2 shard_map.152
  63.0 18.0 %all_to_all.27.in_ref = bf16[64,8,128]{2,1,0:T(8,128)(2,1)S(1)} all-to-all(bf16[64,8,128]{2,1,0:T(8,128)(2,1)S(1)} %shard_map.152), channel_id=1, replica_groups=mesh['role'=2,'seq'=64,'head'=4] {'seq'}, dimensions={0} | all-to-all | bytes 262144 | tf_op jit(solution)/shard_map/all_to_all | solution.py:325
  81.0 2.6 %shard_map.153 = bf16[64,4,128]{2,1,0:T(4,128)(2,1)S(1)} custom-call(f32[128]{0:T(128)} %skip_ref.1, bf16[64,8,128]{2,1,0:T(8,128)(2,1)S(1)} %all_to_all.27.in_ref, f32[72,128]{1,0:T(8,128)S(1)} %copy-done.7, f32[72,128]{1,0:T(8,128)S(1)} %copy-done.6, bf16[144,192]{1,0:T(8,128)(2,1)S(1)} %copy-done.3, bf16[64,432]{1,0:T(8,128)(2,1)S(1)} %copy-done.4, ...), custom_call_target="tpu_custom_call" | custom-call | tf_op jit(solution)/shard_map/pallas_call | solution.py:263
  83.6 13.8 %all_to_all.28.in_ref = bf16[64,4,128]{2,1,0:T(4,128)(2,1)S(1)} all-to-all(bf16[64,4,128]{2,1,0:T(4,128)(2,1)S(1)} %shard_map.153), channel_id=1, replica_groups=mesh['role'=2,'seq'=64,'head'=4] {'seq'}, dimensions={0} | all-to-all | bytes 131072 | tf_op jit(solution)/shard_map/all_to_all | solution.py:327
  97.4 0.7 shard_map.154
  (13 shorter events, 0.0 us)
Async XLA Ops:
  2.4 7.8 %copy-start.10 = (bf16[128,2,128]{2,1,0:T(2,128)(2,1)S(1)}, bf16[128,2,128]{2,1,0:T(2,128)(2,1)}, u32[]{:S(2)}) copy-start(bf16[128,2,128]{2,1,0:T(2,128)(2,1)} %param.14) | copy-start | bytes 196612
  2.4 22.5 %all-to-all-start = ((bf16[8,2,128,128]{3,2,1,0:T(8,128)(2,1)}), bf16[8,2,128,128]{3,2,1,0:T(8,128)(2,1)S(1)}, u32[]{:S(2)}, u32[]{:S(2)}) async-start(bf16[8,2,128,128]{3,2,1,0:T(8,128)(2,1)} %shard_map.149), calls=%async_computation | async-start | bytes 1048576 | tf_op jit(solution)/shard_map/all_to_all | solution.py:316
  24.9 7.1 %collective-permute-start = (bf16[8,2,128,128]{3,2,1,0:T(8,128)(2,1)S(1)}, bf16[8,2,128,128]{3,2,1,0:T(8,128)(2,1)S(1)}, u32[]{:S(2)}, u32[]{:S(2)}) collective-permute-start(bf16[8,2,128,128]{3,2,1,0:T(8,128)(2,1)S(1)} %all-to-all-done.own_ref), channel_id=1, source_target_pairs={{0,4},{4,0},{8,12},{12,8},{16,20},{20,16},{24,28},{28,24},{32,36},... | collective-permute-start | bytes 1572872 | tf_op jit(solution)/shard_map/ppermute | solution.py:319
  34.1 10.2 %copy-start = (bf16[2,128,1024]{2,1,0:T(8,128)(2,1)S(1)}, bf16[2,128,1024]{2,1,0:T(8,128)(2,1)}, u32[]{:S(2)}) copy-start(bf16[2,128,1024]{2,1,0:T(8,128)(2,1)} %param.17) | copy-start | bytes 1572868
  44.9 17.8 %copy-start.5 = (f32[128,128]{1,0:T(8,128)S(1)}, f32[128,128]{1,0:T(8,128)}, u32[]{:S(2)}) copy-start(f32[128,128]{1,0:T(8,128)} %taps_ref.1) | copy-start | bytes 196612
  44.9 17.8 %copy-start.8 = (bf16[128,128]{1,0:T(8,128)(2,1)S(1)}, bf16[128,128]{1,0:T(8,128)(2,1)}, u32[]{:S(2)}) copy-start(bf16[128,128]{1,0:T(8,128)(2,1)} %input_ref.1) | copy-start | bytes 98308
  44.9 17.8 %copy-start.9 = (bf16[128,128]{1,0:T(8,128)(2,1)S(1)}, bf16[128,128]{1,0:T(8,128)(2,1)}, u32[]{:S(2)}) copy-start(bf16[128,128]{1,0:T(8,128)(2,1)} %gate_ref.1) | copy-start | bytes 98308
  44.9 36.0 %copy-start.3 = (bf16[144,192]{1,0:T(8,128)(2,1)S(1)}, bf16[144,192]{1,0:T(8,128)(2,1)}, u32[]{:S(2)}) copy-start(bf16[144,192]{1,0:T(8,128)(2,1)} %constant.14.clone.first) | copy-start | bytes 165892
  44.9 36.0 %copy-start.4 = (bf16[64,432]{1,0:T(8,128)(2,1)S(1)}, bf16[64,432]{1,0:T(8,128)(2,1)}, u32[]{:S(2)}) copy-start(bf16[64,432]{1,0:T(8,128)(2,1)} %constant.15.clone.last) | copy-start | bytes 165892
  45.0 36.0 %copy-start.6 = (f32[72,128]{1,0:T(8,128)S(1)}, f32[72,128]{1,0:T(8,128)}, u32[]{:S(2)}) copy-start(f32[72,128]{1,0:T(8,128)} %constant.13.clone.ts) | copy-start | bytes 110596
  45.0 36.0 %copy-start.7 = (f32[72,128]{1,0:T(8,128)S(1)}, f32[72,128]{1,0:T(8,128)}, u32[]{:S(2)}) copy-start(f32[72,128]{1,0:T(8,128)} %constant.12.clone.tc) | copy-start | bytes 110596
  62.8 18.2 %copy-start.1 = (bf16[768,256]{1,0:T(8,128)(2,1)S(1)}, bf16[768,256]{1,0:T(8,128)(2,1)}, u32[]{:S(2)}) copy-start(bf16[768,256]{1,0:T(8,128)(2,1)} %constant.17.clone.backward) | copy-start | bytes 1179652
  62.8 18.2 %copy-start.2 = (bf16[768,256]{1,0:T(8,128)(2,1)S(1)}, bf16[768,256]{1,0:T(8,128)(2,1)}, u32[]{:S(2)}) copy-start(bf16[768,256]{1,0:T(8,128)(2,1)} %constant.16.clone.forward) | copy-start | bytes 1179652

commit v11 on v10

--- a/solution.py
+++ b/solution.py
@@ -15,6 +15,7 @@
 SHARDS = 64
 HALF = 72
 NEG = -1e30
+LOG2E = 1.4426950408889634
 
 
 def transform_tables():
@@ -149,49 +150,57 @@
     rank = lax.axis_index("seq")
     row, mine, core = rank // ROW, rank % ROW // 2, rank % 2
     scale = 128 ** -0.5
-    order = [row] + [jnp.maximum(row - BACK + r, 0) for r in range(BACK)]
-    sources = (own_ref, sibling_ref)
-    keys = jnp.concatenate([ref[n, 0] for ref in sources for n in order], 0)
-    ones = jnp.ones((10 * SHARD, 128), jnp.bfloat16)
-    values = jnp.concatenate([jnp.concatenate([ref[n, 1] for ref in sources for n in order], 0), ones], 1)
+    oldest = jnp.maximum(row - BACK, 0)
+    full = [(ref, jnp.maximum(row - BACK + r, 0)) for ref in (own_ref, sibling_ref) for r in (1, 2, 3)]
+    full_live = [row >= BACK - r for r in (1, 2, 3)] * 2
+    full_keys = jnp.concatenate([ref[n, 0] for ref, n in full], 0)
+    full_values = jnp.concatenate([ref[n, 1] for ref, n in full], 0)
     rows = lax.broadcasted_iota(jnp.int32, (SHARD, SHARD), 0)
     columns = lax.broadcasted_iota(jnp.int32, (SHARD, SHARD), 1)
     diagonal = rows == columns
     zero = jnp.zeros((SHARD, SHARD), jnp.float32)
-    for theirs in range(GROUP):
-        ahead = 2 * (mine - theirs) * SHARD
-        stats = []
+    for step in range(GROUP):
+        theirs = (mine + step) % GROUP
+        newer = core == 1 if step == 0 else theirs > mine
+        edge = jnp.where(newer, row, oldest)
+        edges = [(sibling_ref, edge)]
+        edges = ([(own_ref, row), (own_ref, oldest)] if step == 0 else [(own_ref, edge)]) + edges
+        live = jnp.logical_or(newer, row >= BACK)
+        keys = jnp.concatenate([ref[n, 0] for ref, n in edges] + [full_keys], 0)
+        values = jnp.concatenate([ref[n, 1] for ref, n in edges] + [full_values], 0)
+        values = jnp.concatenate([values, jnp.ones(values.shape, jnp.bfloat16)], 1)
+        scores = lax.dot_general(
+            q_ref[theirs], keys, (((1,), (1,)), ((), ())), preferred_element_type=jnp.float32
+        )
+        spreads, tops = [], []
         for half in (0, 1):
-            lag = half * (SHARD // 2) + rows // 2 - columns
-            newest = [lag >= ahead, lag >= ahead + (1 - 2 * core) * SHARD]
-            scores = lax.dot_general(
-                q_ref[theirs, half * SHARD : (half + 1) * SHARD, :],
-                keys,
-                (((1,), (1,)), ((), ())),
-                preferred_element_type=jnp.float32,
-            )
-            parts = [scores[:, n * SHARD : (n + 1) * SHARD] for n in range(10)]
-            blocks = []
-            for source in (0, 1):
-                part = parts[5 * source : 5 * source + 5]
-                blocks.append(jnp.where(newest[source], part[0], jnp.where(row >= BACK, part[1], NEG)))
-                blocks += [jnp.where(row >= BACK - r, part[1 + r], NEG) for r in (1, 2, 3)]
+            parts = scores[half * SHARD : (half + 1) * SHARD]
+            parts = [parts[:, n * SHARD : (n + 1) * SHARD] for n in range(len(edges) + 6)]
+            if step == 0:
+                newest = half * (SHARD // 2) + rows // 2 >= columns
+                blocks = [jnp.where(newest, parts[0], jnp.where(row >= BACK, parts[1], NEG))]
+            else:
+                blocks = [jnp.where(live, parts[0], NEG)]
+            blocks.append(jnp.where(live, parts[len(edges) - 1], NEG))
+            blocks += [jnp.where(ok, part, NEG) for ok, part in zip(full_live, parts[len(edges) :])]
             top = blocks[0]
             for block in blocks[1:]:
                 top = jnp.maximum(top, block)
             top = jnp.maximum(jnp.max(top, axis=1, keepdims=True), 0.5 * NEG)
-            weights = [jnp.exp((b - top) * scale) for b in blocks]
-            spread = []
-            for source in (0, 1):
-                part = weights[4 * source : 4 * source + 4]
-                spread += [jnp.where(newest[source], part[0], zero), jnp.where(newest[source], zero, part[0])]
-                spread += part[1:]
-            spread = jnp.concatenate([w.astype(jnp.bfloat16) for w in spread], 1)
-            sums = jnp.dot(spread, values, preferred_element_type=jnp.float32)
-            total = sums[:, 128:]
-            safe = jnp.maximum(total, 1e-30)
-            out_ref[theirs, half * SHARD : (half + 1) * SHARD, :] = (sums[:, :128] / safe).astype(jnp.bfloat16)
-            log_sum = jnp.where(total > 0.0, top * scale + jnp.log(safe), NEG)
+            tops.append(top)
+            shift = top * (scale * LOG2E)
+            weights = [jnp.exp2(b * (scale * LOG2E) - shift) for b in blocks]
+            if step == 0:
+                weights = [jnp.where(newest, weights[0], zero), jnp.where(newest, zero, weights[0])] + weights[1:]
+            spreads.append(jnp.concatenate([w.astype(jnp.bfloat16) for w in weights], 1))
+        sums = jnp.dot(jnp.concatenate(spreads, 0), values, preferred_element_type=jnp.float32)
+        total = sums[:, 128:]
+        safe = jnp.maximum(total, 1e-30)
+        out_ref[theirs, :256, :] = (sums[:, :128] / safe).astype(jnp.bfloat16)
+        log_sums = jnp.where(total > 0.0, jnp.concatenate(tops, 0) * scale + jnp.log(safe), NEG)
+        stats = []
+        for half in (0, 1):
+            log_sum = log_sums[half * SHARD : (half + 1) * SHARD]
             log_sum = jnp.sum(jnp.where(diagonal, log_sum, 0.0), axis=0, keepdims=True)
             high = log_sum.astype(jnp.bfloat16).astype(jnp.float32)
             rest = log_sum - high

time: 98.6 us -> 98.6 us (level)
  no operation moved by 1% of the time
where the time goes in v11:
time: 98.6 us; the launch traced here: 98.1 us
  blocking collectives  70.3 us (71%)
  starting transfers between devices  13.4 us (14%)
  Pallas kernels  7.81 us (8%)
  waiting for transfers between devices  5.67 us (6%)
    all_to_all x1, blocking collectives, body(): packed = lax.all_to_all(packed, 'seq', 0, 0)  18 us
    all_to_all x1, blocking collectives, body(): target = lax.all_to_all(target, ('role', 'head'), 0, 0)  17.8 us
    all_to_all x1, blocking collectives, body(): out = lax.all_to_all(out, 'seq', 0, 0)  13.8 us
    all_gather x1, blocking collectives, body(): lax.all_gather(query_heads.reshape(2 * SHARD, 128), 'seq', axis_index_gro...  10.6 us
    all_to_all x1, blocking collectives, body(): parts = lax.all_to_all(parts, 'seq', 0, 0, axis_index_groups=groups)  10.2 us
    all_to_all x1, starting transfers between devices, body(): own = lax.all_to_all(pairs, 'seq', 0, 0, axis_index_groups=columns)  7.79 us
    ppermute x1, starting transfers between devices, body(): sibling = lax.ppermute(own, 'seq', [(i, i ^ 1) for i in range(SHARDS)])  5.59 us
    all_to_all x1, waiting for transfers between devices, body(): own = lax.all_to_all(pairs, 'seq', 0, 0, axis_index_groups=columns)  4.15 us
  transfers between devices with their start and end apart: 2, of which 2 were waited for; matrix products, arithmetic and copies ran while one was open for 0% of the time, Pallas kernels for 0%

profile of v11, /device:TPU:1, one launch (start us, length us, event | category | flops | bytes accessed | tf_op | source)
XLA Modules:
  0.0 98.1 jit_solution(6468397134090653244)
XLA Ops:
  0.6 1.7 %shard_map.149 = bf16[8,2,128,128]{3,2,1,0:T(8,128)(2,1)} custom-call(bf16[128,128]{1,0:T(8,128)(2,1)} %bitcast.6, bf16[128,128]{1,0:T(8,128)(2,1)} %bitcast.7), custom_call_target="tpu_custom_call" | custom-call | tf_op jit(solution)/shard_map/pallas_call | solution.py:248
  2.4 0.0 copy-start.10
  2.4 7.8 %all-to-all-start = ((bf16[8,2,128,128]{3,2,1,0:T(8,128)(2,1)}), bf16[8,2,128,128]{3,2,1,0:T(8,128)(2,1)S(1)}, u32[]{:S(2)}, u32[]{:S(2)}) async-start(bf16[8,2,128,128]{3,2,1,0:T(8,128)(2,1)} %shard_map.149), calls=%async_computation | async-start | bytes 1048576 | tf_op jit(solution)/shard_map/all_to_all | solution.py:325
  10.2 10.6 %all_gather.3.q_ref = bf16[4,256,128]{2,1,0:T(8,128)(2,1)S(1)} all-gather(bf16[1,256,128]{2,1,0:T(8,128)(2,1)S(1)} %bitcast.5), channel_id=1, replica_groups={{0,8,16,24},{4,12,20,28},{32,40,48,56},{36,44,52,60},{64,72,80,88},{68,..., dimensions={0}, use_global_device_ids=true | all-gather | bytes 327680 | tf_op jit(solution)/shard_map/all_gather | solution.py:326
  20.8 4.2 %all-to-all-done.own_ref = bf16[8,2,128,128]{3,2,1,0:T(8,128)(2,1)S(1)} async-done(((bf16[8,2,128,128]{3,2,1,0:T(8,128)(2,1)}), bf16[8,2,128,128]{3,2,1,0:T(8,128)(2,1)S(1)}, u32[]{:S(2)}, u32[]{:S(2)}) %all-to-all-start) | async-done | bytes 524320 | tf_op jit(solution)/shard_map/all_to_all | solution.py:325
  24.9 5.6 %collective-permute-start = (bf16[8,2,128,128]{3,2,1,0:T(8,128)(2,1)S(1)}, bf16[8,2,128,128]{3,2,1,0:T(8,128)(2,1)S(1)}, u32[]{:S(2)}, u32[]{:S(2)}) collective-permute-start(bf16[8,2,128,128]{3,2,1,0:T(8,128)(2,1)S(1)} %all-to-all-done.own_ref), channel_id=1, source_target_pairs={{0,4},{4,0},{8,12},{12,8},{16,20},{20,16},{24,28},{28,24},{32,36},... | collective-permute-start | bytes 1572872 | tf_op jit(solution)/shard_map/ppermute | solution.py:328
  30.5 1.5 %collective-permute-done.sibling_ref = bf16[8,2,128,128]{3,2,1,0:T(8,128)(2,1)S(1)} collective-permute-done((bf16[8,2,128,128]{3,2,1,0:T(8,128)(2,1)S(1)}, bf16[8,2,128,128]{3,2,1,0:T(8,128)(2,1)S(1)}, u32[]{:S(2)}, u32[]{:S(2)}) %collective-permute-start) | collective-permute-done | bytes 524320 | tf_op jit(solution)/shard_map/ppermute | solution.py:328
  32.0 2.0 %shard_map.150 = bf16[4,272,128]{2,1,0:T(8,128)(2,1)S(1)} custom-call(bf16[4,256,128]{2,1,0:T(8,128)(2,1)S(1)} %all_gather.3.q_ref, bf16[8,2,128,128]{3,2,1,0:T(8,128)(2,1)S(1)} %all-to-all-done.own_ref, bf16[8,2,128,128]{3,2,1,0:T(8,128)(2,1)S(1)} %collective-permute-done.sibling_ref), custom_call_target="tpu_custom_call" | custom-call | tf_op jit(solution)/shard_map/pallas_call | solution.py:292
  34.0 0.0 copy-start
  34.0 10.2 %all_to_all.25.parts_ref = bf16[4,272,128]{2,1,0:T(8,128)(2,1)S(1)} all-to-all(bf16[4,272,128]{2,1,0:T(8,128)(2,1)S(1)} %shard_map.150), channel_id=1, replica_groups={{0,8,16,24},{4,12,20,28},{32,40,48,56},{36,44,52,60},{64,72,80,88},{68,..., dimensions={0} | all-to-all | bytes 557056 | tf_op jit(solution)/shard_map/all_to_all | solution.py:330
  44.3 0.6 shard_map.151
  44.8 0.0 copy-start.5
  44.9 0.0 copy-start.3
  44.9 0.0 copy-start.4
  44.9 0.0 copy-start.6
  44.9 0.0 copy-start.7
  44.9 17.8 %all_to_all.26.parts_ref = bf16[8,128,128]{2,1,0:T(8,128)(2,1)S(1)} all-to-all(bf16[8,128,128]{2,1,0:T(8,128)(2,1)S(1)} %shard_map.151), channel_id=1, replica_groups=mesh['role'=2,'seq'=64,'head'=4] {'role','head'}, dimensions={0} | all-to-all | bytes 524288 | tf_op jit(solution)/shard_map/all_to_all | solution.py:332
  62.7 0.0 copy-start.1
  62.7 0.0 copy-start.2
  62.7 0.2 shard_map.152
  62.9 18.0 %all_to_all.27.in_ref = bf16[64,8,128]{2,1,0:T(8,128)(2,1)S(1)} all-to-all(bf16[64,8,128]{2,1,0:T(8,128)(2,1)S(1)} %shard_map.152), channel_id=1, replica_groups=mesh['role'=2,'seq'=64,'head'=4] {'seq'}, dimensions={0} | all-to-all | bytes 262144 | tf_op jit(solution)/shard_map/all_to_all | solution.py:334
  80.9 2.6 %shard_map.153 = bf16[64,4,128]{2,1,0:T(4,128)(2,1)S(1)} custom-call(f32[128]{0:T(128)} %skip_ref.1, bf16[64,8,128]{2,1,0:T(8,128)(2,1)S(1)} %all_to_all.27.in_ref, f32[72,128]{1,0:T(8,128)S(1)} %copy-done.7, f32[72,128]{1,0:T(8,128)S(1)} %copy-done.6, bf16[144,192]{1,0:T(8,128)(2,1)S(1)} %copy-done.3, bf16[64,432]{1,0:T(8,128)(2,1)S(1)} %copy-done.4, ...), custom_call_target="tpu_custom_call" | custom-call | tf_op jit(solution)/shard_map/pallas_call | solution.py:272
  83.5 13.8 %all_to_all.28.in_ref = bf16[64,4,128]{2,1,0:T(4,128)(2,1)S(1)} all-to-all(bf16[64,4,128]{2,1,0:T(4,128)(2,1)S(1)} %shard_map.153), channel_id=1, replica_groups=mesh['role'=2,'seq'=64,'head'=4] {'seq'}, dimensions={0} | all-to-all | bytes 131072 | tf_op jit(solution)/shard_map/all_to_all | solution.py:336
  97.3 0.7 shard_map.154
  (13 shorter events, 0.0 us)
Async XLA Ops:
  2.4 7.8 %copy-start.10 = (bf16[128,2,128]{2,1,0:T(2,128)(2,1)S(1)}, bf16[128,2,128]{2,1,0:T(2,128)(2,1)}, u32[]{:S(2)}) copy-start(bf16[128,2,128]{2,1,0:T(2,128)(2,1)} %param.14) | copy-start | bytes 196612
  2.4 22.5 %all-to-all-start = ((bf16[8,2,128,128]{3,2,1,0:T(8,128)(2,1)}), bf16[8,2,128,128]{3,2,1,0:T(8,128)(2,1)S(1)}, u32[]{:S(2)}, u32[]{:S(2)}) async-start(bf16[8,2,128,128]{3,2,1,0:T(8,128)(2,1)} %shard_map.149), calls=%async_computation | async-start | bytes 1048576 | tf_op jit(solution)/shard_map/all_to_all | solution.py:325
  24.9 7.1 %collective-permute-start = (bf16[8,2,128,128]{3,2,1,0:T(8,128)(2,1)S(1)}, bf16[8,2,128,128]{3,2,1,0:T(8,128)(2,1)S(1)}, u32[]{:S(2)}, u32[]{:S(2)}) collective-permute-start(bf16[8,2,128,128]{3,2,1,0:T(8,128)(2,1)S(1)} %all-to-all-done.own_ref), channel_id=1, source_target_pairs={{0,4},{4,0},{8,12},{12,8},{16,20},{20,16},{24,28},{28,24},{32,36},... | collective-permute-start | bytes 1572872 | tf_op jit(solution)/shard_map/ppermute | solution.py:328
  34.0 10.2 %copy-start = (bf16[2,128,1024]{2,1,0:T(8,128)(2,1)S(1)}, bf16[2,128,1024]{2,1,0:T(8,128)(2,1)}, u32[]{:S(2)}) copy-start(bf16[2,128,1024]{2,1,0:T(8,128)(2,1)} %param.17) | copy-start | bytes 1572868
  44.8 17.8 %copy-start.5 = (f32[128,128]{1,0:T(8,128)S(1)}, f32[128,128]{1,0:T(8,128)}, u32[]{:S(2)}) copy-start(f32[128,128]{1,0:T(8,128)} %taps_ref.1) | copy-start | bytes 196612
  44.8 17.8 %copy-start.8 = (bf16[128,128]{1,0:T(8,128)(2,1)S(1)}, bf16[128,128]{1,0:T(8,128)(2,1)}, u32[]{:S(2)}) copy-start(bf16[128,128]{1,0:T(8,128)(2,1)} %input_ref.1) | copy-start | bytes 98308
  44.9 17.8 %copy-start.9 = (bf16[128,128]{1,0:T(8,128)(2,1)S(1)}, bf16[128,128]{1,0:T(8,128)(2,1)}, u32[]{:S(2)}) copy-start(bf16[128,128]{1,0:T(8,128)(2,1)} %gate_ref.1) | copy-start | bytes 98308
  44.9 36.0 %copy-start.3 = (bf16[144,192]{1,0:T(8,128)(2,1)S(1)}, bf16[144,192]{1,0:T(8,128)(2,1)}, u32[]{:S(2)}) copy-start(bf16[144,192]{1,0:T(8,128)(2,1)} %constant.14.clone.first) | copy-start | bytes 165892
  44.9 36.0 %copy-start.4 = (bf16[64,432]{1,0:T(8,128)(2,1)S(1)}, bf16[64,432]{1,0:T(8,128)(2,1)}, u32[]{:S(2)}) copy-start(bf16[64,432]{1,0:T(8,128)(2,1)} %constant.15.clone.last) | copy-start | bytes 165892
  44.9 36.0 %copy-start.6 = (f32[72,128]{1,0:T(8,128)S(1)}, f32[72,128]{1,0:T(8,128)}, u32[]{:S(2)}) copy-start(f32[72,128]{1,0:T(8,128)} %constant.13.clone.ts) | copy-start | bytes 110596
  44.9 36.0 %copy-start.7 = (f32[72,128]{1,0:T(8,128)S(1)}, f32[72,128]{1,0:T(8,128)}, u32[]{:S(2)}) copy-start(f32[72,128]{1,0:T(8,128)} %constant.12.clone.tc) | copy-start | bytes 110596
  62.7 18.2 %copy-start.1 = (bf16[768,256]{1,0:T(8,128)(2,1)S(1)}, bf16[768,256]{1,0:T(8,128)(2,1)}, u32[]{:S(2)}) copy-start(bf16[768,256]{1,0:T(8,128)(2,1)} %constant.17.clone.backward) | copy-start | bytes 1179652
  62.7 18.2 %copy-start.2 = (bf16[768,256]{1,0:T(8,128)(2,1)S(1)}, bf16[768,256]{1,0:T(8,128)(2,1)}, u32[]{:S(2)}) copy-start(bf16[768,256]{1,0:T(8,128)(2,1)} %constant.16.clone.forward) | copy-start | bytes 1179652

commit v12 on v11

--- a/solution.py
+++ b/solution.py
@@ -10,7 +10,6 @@
 WINDOW = 4096
 SHARD = 128
 ROW = 8
-GROUP = 4
 BACK = WINDOW // (ROW * SHARD)
 SHARDS = 64
 HALF = 72
@@ -146,28 +145,26 @@
         step_ref[c * SHARDS : (c + 1) * SHARDS, :] = wide_ref[:, 2 + c, :]
 
 
-def attend_kernel(q_ref, own_ref, sibling_ref, out_ref):
+def attend_kernel(q_ref, kv_ref, out_ref):
     rank = lax.axis_index("seq")
-    row, mine, core = rank // ROW, rank % ROW // 2, rank % 2
+    row, mine = rank // ROW, rank % ROW
     scale = 128 ** -0.5
     oldest = jnp.maximum(row - BACK, 0)
-    full = [(ref, jnp.maximum(row - BACK + r, 0)) for ref in (own_ref, sibling_ref) for r in (1, 2, 3)]
-    full_live = [row >= BACK - r for r in (1, 2, 3)] * 2
-    full_keys = jnp.concatenate([ref[n, 0] for ref, n in full], 0)
-    full_values = jnp.concatenate([ref[n, 1] for ref, n in full], 0)
+    full = [jnp.maximum(row - BACK + r, 0) for r in (1, 2, 3)]
+    full_live = [row >= BACK - r for r in (1, 2, 3)]
+    full_keys = jnp.concatenate([kv_ref[n, 0] for n in full], 0)
+    full_values = jnp.concatenate([kv_ref[n, 1] for n in full], 0)
     rows = lax.broadcasted_iota(jnp.int32, (SHARD, SHARD), 0)
     columns = lax.broadcasted_iota(jnp.int32, (SHARD, SHARD), 1)
     diagonal = rows == columns
     zero = jnp.zeros((SHARD, SHARD), jnp.float32)
-    for step in range(GROUP):
-        theirs = (mine + step) % GROUP
-        newer = core == 1 if step == 0 else theirs > mine
-        edge = jnp.where(newer, row, oldest)
-        edges = [(sibling_ref, edge)]
-        edges = ([(own_ref, row), (own_ref, oldest)] if step == 0 else [(own_ref, edge)]) + edges
+    for step in range(ROW):
+        theirs = (mine + step) % ROW
+        newer = theirs > mine
+        edges = [row, oldest] if step == 0 else [jnp.where(newer, row, oldest)]
         live = jnp.logical_or(newer, row >= BACK)
-        keys = jnp.concatenate([ref[n, 0] for ref, n in edges] + [full_keys], 0)
-        values = jnp.concatenate([ref[n, 1] for ref, n in edges] + [full_values], 0)
+        keys = jnp.concatenate([kv_ref[n, 0] for n in edges] + [full_keys], 0)
+        values = jnp.concatenate([kv_ref[n, 1] for n in edges] + [full_values], 0)
         values = jnp.concatenate([values, jnp.ones(values.shape, jnp.bfloat16)], 1)
         scores = lax.dot_general(
             q_ref[theirs], keys, (((1,), (1,)), ((), ())), preferred_element_type=jnp.float32
@@ -175,13 +172,12 @@
         spreads, tops = [], []
         for half in (0, 1):
             parts = scores[half * SHARD : (half + 1) * SHARD]
-            parts = [parts[:, n * SHARD : (n + 1) * SHARD] for n in range(len(edges) + 6)]
+            parts = [parts[:, n * SHARD : (n + 1) * SHARD] for n in range(len(edges) + 3)]
             if step == 0:
                 newest = half * (SHARD // 2) + rows // 2 >= columns
                 blocks = [jnp.where(newest, parts[0], jnp.where(row >= BACK, parts[1], NEG))]
             else:
                 blocks = [jnp.where(live, parts[0], NEG)]
-            blocks.append(jnp.where(live, parts[len(edges) - 1], NEG))
             blocks += [jnp.where(ok, part, NEG) for ok, part in zip(full_live, parts[len(edges) :])]
             top = blocks[0]
             for block in blocks[1:]:
@@ -214,19 +210,19 @@
     shares = []
     for half in (0, 1):
         sums = []
-        for p in range(GROUP):
+        for p in range(ROW):
             stats = parts_ref[p, 256:272, :].astype(jnp.float32)
             sums.append(jnp.sum(stats[3 * half : 3 * half + 3], axis=0, keepdims=True))
         sums = jnp.concatenate(sums, 0)
         share = jnp.exp(sums - jnp.max(sums, axis=0, keepdims=True))
         shares.append(share / jnp.sum(share, axis=0, keepdims=True))
-    shares.append(jnp.zeros((128 - 2 * GROUP, 128), jnp.float32))
+    shares.append(jnp.zeros((128 - 2 * ROW, 128), jnp.float32))
     shares = jnp.concatenate(shares, 0).T
     for half in (0, 1):
         merged = None
-        for p in range(GROUP):
+        for p in range(ROW):
             part = parts_ref[p, half * SHARD : (half + 1) * SHARD, :].astype(jnp.float32)
-            part = shares[:, half * GROUP + p : half * GROUP + p + 1] * part
+            part = shares[:, half * ROW + p : half * ROW + p + 1] * part
             merged = part if merged is None else merged + part
         merged_ref[half * SHARD : (half + 1) * SHARD, :] = merged
     attended = jnp.concatenate([merged_ref[pl.ds(h, SHARD, stride=2), :] for h in (0, 1)], 1)
@@ -288,13 +284,13 @@
     )(near(out))
 
 
-def call_attend(queries, own, sibling):
+def call_attend(queries, pairs):
     return pl.pallas_call(
         attend_kernel,
-        out_shape=pltpu.VMEM((GROUP, 272, 128), jnp.bfloat16),
-        in_specs=[VMEM] * 3,
+        out_shape=pltpu.VMEM((ROW, 272, 128), jnp.bfloat16),
+        in_specs=[VMEM] * 2,
         out_specs=VMEM,
-    )(near(queries), near(own), near(sibling))
+    )(near(queries), near(pairs))
 
 
 def call_merge(parts, proj):
@@ -319,15 +315,13 @@
 ):
     tables = [near(jnp.asarray(t)) for t in transform_tables()]
     lines = range(SHARDS // ROW)
-    groups = [[y * ROW + 2 * x + core for x in range(GROUP)] for y in lines for core in (0, 1)]
+    rows = [[y * ROW + p for p in range(ROW)] for y in lines]
     columns = [[y * ROW + p for y in lines] for p in range(ROW)]
     pairs = call_repeat(key_heads[:, 0], value_heads[:, 0])
-    own = lax.all_to_all(pairs, "seq", 0, 0, axis_index_groups=columns)
-    queries = lax.all_gather(query_heads.reshape(2 * SHARD, 128), "seq", axis_index_groups=groups)
-    own, queries = lax.optimization_barrier((own, queries))
-    sibling = lax.ppermute(own, "seq", [(i, i ^ 1) for i in range(SHARDS)])
-    parts = call_attend(queries, own, sibling)
-    parts = lax.all_to_all(parts, "seq", 0, 0, axis_index_groups=groups)
+    pairs = lax.all_to_all(pairs, "seq", 0, 0, axis_index_groups=columns)
+    queries = lax.all_gather(query_heads.reshape(2 * SHARD, 128), "seq", axis_index_groups=rows)
+    parts = call_attend(queries, pairs)
+    parts = lax.all_to_all(parts, "seq", 0, 0, axis_index_groups=rows)
     target = call_merge(parts, distill_proj.reshape(256, 1024))
     target = lax.all_to_all(target, ("role", "head"), 0, 0)
     packed = call_pack(target, conv_input, gate_input, filter_taps)

time: 98.6 us -> 99.1 us (level)
  blocking collectives: 70.3 us -> 81.7 us
  waiting for transfers between devices: 5.67 us -> 0.01 us
  starting transfers between devices: 13.4 us -> 7.79 us
    all_to_all x1, blocking collectives: 10.2 us -> 17.2 us  [body(): parts = lax.all_to_all(parts, 'seq', 0, 0, axis_index_groups=rows)]
    ppermute x1 -> x0, starting transfers between devices: 5.59 us -> none  [body(): sibling = lax.ppermute(own, 'seq', [(i, i ^ 1) for i in range(SHARDS)])]
    all_gather x1, blocking collectives: 10.6 us -> 15.7 us  [body(): lax.all_gather(query_heads.reshape(2 * SHARD, 128), 'seq', axis_index_gro...]
    all_to_all x1, waiting for transfers between devices: 4.15 us -> 0.01 us  [body(): pairs = lax.all_to_all(pairs, 'seq', 0, 0, axis_index_groups=columns)]
    ppermute x1 -> x0, waiting for transfers between devices: 1.51 us -> none  [body(): sibling = lax.ppermute(own, 'seq', [(i, i ^ 1) for i in range(SHARDS)])]
  transfers between devices with their start and end apart: 2 -> 1, of which waited for: 2 -> 0; matrix products, arithmetic and copies ran while one was open for 0% -> 0% of each run, Pallas kernels for 0% -> 0%
where the time goes in v12:
time: 99.1 us; the launch traced here: 98.6 us
  blocking collectives  81.7 us (82%)
  Pallas kernels  8.23 us (8%)
  starting transfers between devices  7.79 us (8%)
    all_to_all x1, blocking collectives, body(): target = lax.all_to_all(target, ('role', 'head'), 0, 0)  17.7 us
    all_to_all x1, blocking collectives, body(): packed = lax.all_to_all(packed, 'seq', 0, 0)  17.2 us
    all_to_all x1, blocking collectives, body(): parts = lax.all_to_all(parts, 'seq', 0, 0, axis_index_groups=rows)  17.2 us
    all_gather x1, blocking collectives, body(): lax.all_gather(query_heads.reshape(2 * SHARD, 128), 'seq', axis_index_gro...  15.7 us
    all_to_all x1, blocking collectives, body(): out = lax.all_to_all(out, 'seq', 0, 0)  13.9 us
    all_to_all x1, starting transfers between devices, body(): pairs = lax.all_to_all(pairs, 'seq', 0, 0, axis_index_groups=columns)  7.79 us
    pallas_call x1, Pallas kernels, call_student(): pl.pallas_call(student_kernel, out_shape=pltpu.VMEM((SHARDS, 4, 128), jnp...  2.59 us
    pallas_call x1, Pallas kernels, call_attend(): pl.pallas_call(attend_kernel, out_shape=pltpu.VMEM((ROW, 272, 128), jnp.b...  2.23 us
  transfers between devices with their start and end apart: 1, of which 0 were waited for; matrix products, arithmetic and copies ran while one was open for 0% of the time, Pallas kernels for 0%

profile of v12, /device:TPU:1, one launch (start us, length us, event | category | flops | bytes accessed | tf_op | source)
XLA Modules:
  0.0 98.6 jit_solution(7117735139155046193)
XLA Ops:
  0.6 1.7 %shard_map.149 = bf16[8,2,128,128]{3,2,1,0:T(8,128)(2,1)} custom-call(bf16[128,128]{1,0:T(8,128)(2,1)} %bitcast.6, bf16[128,128]{1,0:T(8,128)(2,1)} %bitcast.7), custom_call_target="tpu_custom_call" | custom-call | tf_op jit(solution)/shard_map/pallas_call | solution.py:244
  2.4 0.0 copy-start.10
  2.4 7.8 %all-to-all-start = ((bf16[8,2,128,128]{3,2,1,0:T(8,128)(2,1)}), bf16[8,2,128,128]{3,2,1,0:T(8,128)(2,1)S(1)}, u32[]{:S(2)}, u32[]{:S(2)}) async-start(bf16[8,2,128,128]{3,2,1,0:T(8,128)(2,1)} %shard_map.149), calls=%async_computation | async-start | bytes 1048576 | tf_op jit(solution)/shard_map/all_to_all | solution.py:321
  10.2 15.7 %all_gather.3.q_ref = bf16[8,256,128]{2,1,0:T(8,128)(2,1)S(1)} all-gather(bf16[1,256,128]{2,1,0:T(8,128)(2,1)S(1)} %bitcast.5), channel_id=1, replica_groups={{0,4,8,12,16,20,24,28},{32,36,40,44,48,52,56,60},{64,68,72,76,80,84,88,..., dimensions={0}, use_global_device_ids=true | all-gather | bytes 589824 | tf_op jit(solution)/shard_map/all_gather | solution.py:322
  25.9 0.0 all-to-all-done.kv_ref
  25.9 2.2 %shard_map.150 = bf16[8,272,128]{2,1,0:T(8,128)(2,1)S(1)} custom-call(bf16[8,256,128]{2,1,0:T(8,128)(2,1)S(1)} %all_gather.3.q_ref, bf16[8,2,128,128]{3,2,1,0:T(8,128)(2,1)S(1)} %all-to-all-done.kv_ref), custom_call_target="tpu_custom_call" | custom-call | tf_op jit(solution)/shard_map/pallas_call | solution.py:288
  28.1 0.0 copy-start
  28.1 17.2 %all_to_all.25.parts_ref = bf16[8,272,128]{2,1,0:T(8,128)(2,1)S(1)} all-to-all(bf16[8,272,128]{2,1,0:T(8,128)(2,1)S(1)} %shard_map.150), channel_id=1, replica_groups={{0,4,8,12,16,20,24,28},{32,36,40,44,48,52,56,60},{64,68,72,76,80,84,88,..., dimensions={0} | all-to-all | bytes 1114112 | tf_op jit(solution)/shard_map/all_to_all | solution.py:324
  45.3 0.8 shard_map.151
  46.0 0.0 copy-start.5
  46.0 0.0 copy-start.8
  46.1 0.0 copy-start.9
  46.1 0.0 copy-start.3
  46.1 0.0 copy-start.4
  46.1 0.0 copy-start.6
  46.1 0.0 copy-start.7
  46.1 17.7 %all_to_all.26.parts_ref = bf16[8,128,128]{2,1,0:T(8,128)(2,1)S(1)} all-to-all(bf16[8,128,128]{2,1,0:T(8,128)(2,1)S(1)} %shard_map.151), channel_id=1, replica_groups=mesh['role'=2,'seq'=64,'head'=4] {'role','head'}, dimensions={0} | all-to-all | bytes 524288 | tf_op jit(solution)/shard_map/all_to_all | solution.py:326
  63.9 0.0 copy-start.1
  63.9 0.0 copy-start.2
  63.9 0.2 shard_map.152
  64.1 17.2 %all_to_all.27.in_ref = bf16[64,8,128]{2,1,0:T(8,128)(2,1)S(1)} all-to-all(bf16[64,8,128]{2,1,0:T(8,128)(2,1)S(1)} %shard_map.152), channel_id=1, replica_groups=mesh['role'=2,'seq'=64,'head'=4] {'seq'}, dimensions={0} | all-to-all | bytes 262144 | tf_op jit(solution)/shard_map/all_to_all | solution.py:328
  81.4 2.6 %shard_map.153 = bf16[64,4,128]{2,1,0:T(4,128)(2,1)S(1)} custom-call(f32[128]{0:T(128)} %skip_ref.1, bf16[64,8,128]{2,1,0:T(8,128)(2,1)S(1)} %all_to_all.27.in_ref, f32[72,128]{1,0:T(8,128)S(1)} %copy-done.7, f32[72,128]{1,0:T(8,128)S(1)} %copy-done.6, bf16[144,192]{1,0:T(8,128)(2,1)S(1)} %copy-done.3, bf16[64,432]{1,0:T(8,128)(2,1)S(1)} %copy-done.4, ...), custom_call_target="tpu_custom_call" | custom-call | tf_op jit(solution)/shard_map/pallas_call | solution.py:268
  84.0 13.9 %all_to_all.28.in_ref = bf16[64,4,128]{2,1,0:T(4,128)(2,1)S(1)} all-to-all(bf16[64,4,128]{2,1,0:T(4,128)(2,1)S(1)} %shard_map.153), channel_id=1, replica_groups=mesh['role'=2,'seq'=64,'head'=4] {'seq'}, dimensions={0} | all-to-all | bytes 131072 | tf_op jit(solution)/shard_map/all_to_all | solution.py:330
  97.9 0.7 shard_map.154
  (11 shorter events, 0.0 us)
Async XLA Ops:
  2.4 7.8 %copy-start.10 = (bf16[128,2,128]{2,1,0:T(2,128)(2,1)S(1)}, bf16[128,2,128]{2,1,0:T(2,128)(2,1)}, u32[]{:S(2)}) copy-start(bf16[128,2,128]{2,1,0:T(2,128)(2,1)} %param.14) | copy-start | bytes 196612
  2.4 23.5 %all-to-all-start = ((bf16[8,2,128,128]{3,2,1,0:T(8,128)(2,1)}), bf16[8,2,128,128]{3,2,1,0:T(8,128)(2,1)S(1)}, u32[]{:S(2)}, u32[]{:S(2)}) async-start(bf16[8,2,128,128]{3,2,1,0:T(8,128)(2,1)} %shard_map.149), calls=%async_computation | async-start | bytes 1048576 | tf_op jit(solution)/shard_map/all_to_all | solution.py:321
  28.1 17.2 %copy-start = (bf16[2,128,1024]{2,1,0:T(8,128)(2,1)S(1)}, bf16[2,128,1024]{2,1,0:T(8,128)(2,1)}, u32[]{:S(2)}) copy-start(bf16[2,128,1024]{2,1,0:T(8,128)(2,1)} %param.17) | copy-start | bytes 1572868
  46.0 17.8 %copy-start.5 = (f32[128,128]{1,0:T(8,128)S(1)}, f32[128,128]{1,0:T(8,128)}, u32[]{:S(2)}) copy-start(f32[128,128]{1,0:T(8,128)} %taps_ref.1) | copy-start | bytes 196612
  46.0 17.8 %copy-start.8 = (bf16[128,128]{1,0:T(8,128)(2,1)S(1)}, bf16[128,128]{1,0:T(8,128)(2,1)}, u32[]{:S(2)}) copy-start(bf16[128,128]{1,0:T(8,128)(2,1)} %input_ref.1) | copy-start | bytes 98308
  46.1 17.8 %copy-start.9 = (bf16[128,128]{1,0:T(8,128)(2,1)S(1)}, bf16[128,128]{1,0:T(8,128)(2,1)}, u32[]{:S(2)}) copy-start(bf16[128,128]{1,0:T(8,128)(2,1)} %gate_ref.1) | copy-start | bytes 98308
  46.1 35.3 %copy-start.3 = (bf16[144,192]{1,0:T(8,128)(2,1)S(1)}, bf16[144,192]{1,0:T(8,128)(2,1)}, u32[]{:S(2)}) copy-start(bf16[144,192]{1,0:T(8,128)(2,1)} %constant.14.clone.first) | copy-start | bytes 165892
  46.1 35.3 %copy-start.4 = (bf16[64,432]{1,0:T(8,128)(2,1)S(1)}, bf16[64,432]{1,0:T(8,128)(2,1)}, u32[]{:S(2)}) copy-start(bf16[64,432]{1,0:T(8,128)(2,1)} %constant.15.clone.last) | copy-start | bytes 165892
  46.1 35.2 %copy-start.6 = (f32[72,128]{1,0:T(8,128)S(1)}, f32[72,128]{1,0:T(8,128)}, u32[]{:S(2)}) copy-start(f32[72,128]{1,0:T(8,128)} %constant.13.clone.ts) | copy-start | bytes 110596
  46.1 35.2 %copy-start.7 = (f32[72,128]{1,0:T(8,128)S(1)}, f32[72,128]{1,0:T(8,128)}, u32[]{:S(2)}) copy-start(f32[72,128]{1,0:T(8,128)} %constant.12.clone.tc) | copy-start | bytes 110596
  63.9 17.5 %copy-start.1 = (bf16[768,256]{1,0:T(8,128)(2,1)S(1)}, bf16[768,256]{1,0:T(8,128)(2,1)}, u32[]{:S(2)}) copy-start(bf16[768,256]{1,0:T(8,128)(2,1)} %constant.17.clone.backward) | copy-start | bytes 1179652
  63.9 17.5 %copy-start.2 = (bf16[768,256]{1,0:T(8,128)(2,1)S(1)}, bf16[768,256]{1,0:T(8,128)(2,1)}, u32[]{:S(2)}) copy-start(bf16[768,256]{1,0:T(8,128)(2,1)} %constant.16.clone.forward) | copy-start | bytes 1179652

commit v13 on v11

--- a/solution.py
+++ b/solution.py
@@ -146,62 +146,82 @@
         step_ref[c * SHARDS : (c + 1) * SHARDS, :] = wide_ref[:, 2 + c, :]
 
 
-def attend_kernel(q_ref, own_ref, sibling_ref, out_ref):
+def attend_part(query, kv_ref, row, edges, live, diagonal, before):
+    scale = 128 ** -0.5
+    full = [jnp.maximum(row - BACK + r, 0) for r in (1, 2, 3)]
+    order = edges + full
+    keys = jnp.concatenate([kv_ref[n, 0] for n in order], 0)
+    values = jnp.concatenate([kv_ref[n, 1] for n in order], 0)
+    values = jnp.concatenate([values, jnp.ones(values.shape, jnp.bfloat16)], 1)
+    scores = lax.dot_general(query, keys, (((1,), (1,)), ((), ())), preferred_element_type=jnp.float32)
+    rows = lax.broadcasted_iota(jnp.int32, (SHARD, SHARD), 0)
+    columns = lax.broadcasted_iota(jnp.int32, (SHARD, SHARD), 1)
+    zero = jnp.zeros((SHARD, SHARD), jnp.float32)
+    spreads, tops = [], []
+    for half in (0, 1):
+        parts = scores[half * SHARD : (half + 1) * SHARD]
+        parts = [parts[:, n * SHARD : (n + 1) * SHARD] for n in range(len(order))]
+        if diagonal:
+            newest = half * (SHARD // 2) + rows // 2 >= columns
+            blocks = [jnp.where(newest, parts[0], jnp.where(row >= BACK, parts[1], NEG))]
+        else:
+            blocks = [jnp.where(live, parts[0], NEG)]
+        blocks += [jnp.where(row >= BACK - r, parts[len(edges) + r - 1], NEG) for r in (1, 2, 3)]
+        top = jnp.maximum(jnp.maximum(blocks[0], blocks[1]), jnp.maximum(blocks[2], blocks[3]))
+        top = jnp.max(top, axis=1, keepdims=True)
+        top = jnp.maximum(top, 0.5 * NEG if before is None else before[half * SHARD : (half + 1) * SHARD])
+        tops.append(top)
+        shift = top * (scale * LOG2E)
+        weights = [jnp.exp2(b * (scale * LOG2E) - shift) for b in blocks]
+        if diagonal:
+            weights = [jnp.where(newest, weights[0], zero), jnp.where(newest, zero, weights[0])] + weights[1:]
+        spreads.append(jnp.concatenate([w.astype(jnp.bfloat16) for w in weights], 1))
+    sums = jnp.dot(jnp.concatenate(spreads, 0), values, preferred_element_type=jnp.float32)
+    return jnp.concatenate(tops, 0), sums[:, :128], sums[:, 128:]
+
+
+def low_lanes():
+    return lax.broadcasted_iota(jnp.int32, (2 * SHARD, 128), 1) < 64
+
+
+def attend_own_kernel(q_ref, kv_ref, sums_ref, stats_ref):
+    rank = lax.axis_index("seq")
+    row, mine = rank // ROW, rank % ROW // 2
+    oldest = jnp.maximum(row - BACK, 0)
+    for step in range(GROUP):
+        theirs = (mine + step) % GROUP
+        newer = theirs > mine
+        edges = [row, oldest] if step == 0 else [jnp.where(newer, row, oldest)]
+        live = jnp.logical_or(newer, row >= BACK)
+        top, sums, total = attend_part(q_ref[theirs], kv_ref, row, edges, live, step == 0, None)
+        sums_ref[step] = sums
+        stats_ref[step] = jnp.where(low_lanes(), top, total)
+
+
+def attend_sibling_kernel(q_ref, kv_ref, sums_ref, stats_ref, out_ref):
     rank = lax.axis_index("seq")
     row, mine, core = rank // ROW, rank % ROW // 2, rank % 2
     scale = 128 ** -0.5
     oldest = jnp.maximum(row - BACK, 0)
-    full = [(ref, jnp.maximum(row - BACK + r, 0)) for ref in (own_ref, sibling_ref) for r in (1, 2, 3)]
-    full_live = [row >= BACK - r for r in (1, 2, 3)] * 2
-    full_keys = jnp.concatenate([ref[n, 0] for ref, n in full], 0)
-    full_values = jnp.concatenate([ref[n, 1] for ref, n in full], 0)
     rows = lax.broadcasted_iota(jnp.int32, (SHARD, SHARD), 0)
     columns = lax.broadcasted_iota(jnp.int32, (SHARD, SHARD), 1)
-    diagonal = rows == columns
-    zero = jnp.zeros((SHARD, SHARD), jnp.float32)
     for step in range(GROUP):
         theirs = (mine + step) % GROUP
         newer = core == 1 if step == 0 else theirs > mine
-        edge = jnp.where(newer, row, oldest)
-        edges = [(sibling_ref, edge)]
-        edges = ([(own_ref, row), (own_ref, oldest)] if step == 0 else [(own_ref, edge)]) + edges
         live = jnp.logical_or(newer, row >= BACK)
-        keys = jnp.concatenate([ref[n, 0] for ref, n in edges] + [full_keys], 0)
-        values = jnp.concatenate([ref[n, 1] for ref, n in edges] + [full_values], 0)
-        values = jnp.concatenate([values, jnp.ones(values.shape, jnp.bfloat16)], 1)
-        scores = lax.dot_general(
-            q_ref[theirs], keys, (((1,), (1,)), ((), ())), preferred_element_type=jnp.float32
-        )
-        spreads, tops = [], []
-        for half in (0, 1):
-            parts = scores[half * SHARD : (half + 1) * SHARD]
-            parts = [parts[:, n * SHARD : (n + 1) * SHARD] for n in range(len(edges) + 6)]
-            if step == 0:
-                newest = half * (SHARD // 2) + rows // 2 >= columns
-                blocks = [jnp.where(newest, parts[0], jnp.where(row >= BACK, parts[1], NEG))]
-            else:
-                blocks = [jnp.where(live, parts[0], NEG)]
-            blocks.append(jnp.where(live, parts[len(edges) - 1], NEG))
-            blocks += [jnp.where(ok, part, NEG) for ok, part in zip(full_live, parts[len(edges) :])]
-            top = blocks[0]
-            for block in blocks[1:]:
-                top = jnp.maximum(top, block)
-            top = jnp.maximum(jnp.max(top, axis=1, keepdims=True), 0.5 * NEG)
-            tops.append(top)
-            shift = top * (scale * LOG2E)
-            weights = [jnp.exp2(b * (scale * LOG2E) - shift) for b in blocks]
-            if step == 0:
-                weights = [jnp.where(newest, weights[0], zero), jnp.where(newest, zero, weights[0])] + weights[1:]
-            spreads.append(jnp.concatenate([w.astype(jnp.bfloat16) for w in weights], 1))
-        sums = jnp.dot(jnp.concatenate(spreads, 0), values, preferred_element_type=jnp.float32)
-        total = sums[:, 128:]
+        stats = stats_ref[step]
+        before, total_before = stats[:, :1], stats[:, 127:]
+        edges = [jnp.where(newer, row, oldest)]
+        top, sums, total = attend_part(q_ref[theirs], kv_ref, row, edges, live, False, before)
+        share = jnp.exp2((before - top) * (scale * LOG2E))
+        total = total + share * total_before
         safe = jnp.maximum(total, 1e-30)
-        out_ref[theirs, :256, :] = (sums[:, :128] / safe).astype(jnp.bfloat16)
-        log_sums = jnp.where(total > 0.0, jnp.concatenate(tops, 0) * scale + jnp.log(safe), NEG)
+        out_ref[theirs, :256, :] = ((sums + share * sums_ref[step]) / safe).astype(jnp.bfloat16)
+        log_sums = jnp.where(total > 0.0, top * scale + jnp.log(safe), NEG)
         stats = []
         for half in (0, 1):
             log_sum = log_sums[half * SHARD : (half + 1) * SHARD]
-            log_sum = jnp.sum(jnp.where(diagonal, log_sum, 0.0), axis=0, keepdims=True)
+            log_sum = jnp.sum(jnp.where(rows == columns, log_sum, 0.0), axis=0, keepdims=True)
             high = log_sum.astype(jnp.bfloat16).astype(jnp.float32)
             rest = log_sum - high
             middle = rest.astype(jnp.bfloat16).astype(jnp.float32)
@@ -289,12 +309,20 @@
 
 
 def call_attend(queries, own, sibling):
-    return pl.pallas_call(
-        attend_kernel,
+    queries = near(queries)
+    held = pltpu.VMEM((GROUP, 2 * SHARD, 128), jnp.float32)
+    sums, stats = pl.pallas_call(
+        attend_own_kernel,
+        out_shape=(held, held),
+        in_specs=[VMEM] * 2,
+        out_specs=(VMEM,) * 2,
+    )(queries, near(own))
+    return pl.pallas_call(
+        attend_sibling_kernel,
         out_shape=pltpu.VMEM((GROUP, 272, 128), jnp.bfloat16),
-        in_specs=[VMEM] * 3,
+        in_specs=[VMEM] * 4,
         out_specs=VMEM,
-    )(near(queries), near(own), near(sibling))
+    )(queries, near(sibling), near(sums), near(stats))
 
 
 def call_merge(parts, proj):

time: 98.6 us -> 98.3 us (level)
  waiting for transfers between devices: 5.67 us -> 4.4 us
    ppermute x1, waiting for transfers between devices: 1.51 us -> 0.25 us  [body(): sibling = lax.ppermute(own, 'seq', [(i, i ^ 1) for i in range(SHARDS)])]
    pallas_call x1 -> x2, Pallas kernels: 1.99 us -> 2.96 us  [the longest x1 1.7 us: call_attend(): pl.pallas_call(attend_sibling_kernel, out_shape=pltpu.VMEM((GROUP, 272, 1...]
  transfers between devices with their start and end apart: 2 -> 2, of which waited for: 2 -> 2; matrix products, arithmetic and copies ran while one was open for 0% -> 0% of each run, Pallas kernels for 0% -> 1%
where the time goes in v13:
time: 98.3 us; the launch traced here: 97.8 us
  blocking collectives  70.3 us (72%)
  starting transfers between devices  13.4 us (14%)
  Pallas kernels  8.77 us (9%)
  waiting for transfers between devices  4.4 us (4%)
    all_to_all x1, blocking collectives, body(): packed = lax.all_to_all(packed, 'seq', 0, 0)  18 us
    all_to_all x1, blocking collectives, body(): target = lax.all_to_all(target, ('role', 'head'), 0, 0)  17.8 us
    all_to_all x1, blocking collectives, body(): out = lax.all_to_all(out, 'seq', 0, 0)  13.8 us
    all_gather x1, blocking collectives, body(): lax.all_gather(query_heads.reshape(2 * SHARD, 128), 'seq', axis_index_gro...  10.6 us
    all_to_all x1, blocking collectives, body(): parts = lax.all_to_all(parts, 'seq', 0, 0, axis_index_groups=groups)  10.2 us
    all_to_all x1, starting transfers between devices, body(): own = lax.all_to_all(pairs, 'seq', 0, 0, axis_index_groups=columns)  7.79 us
    ppermute x1, starting transfers between devices, body(): sibling = lax.ppermute(own, 'seq', [(i, i ^ 1) for i in range(SHARDS)])  5.59 us
    all_to_all x1, waiting for transfers between devices, body(): own = lax.all_to_all(pairs, 'seq', 0, 0, axis_index_groups=columns)  4.15 us
  transfers between devices with their start and end apart: 2, of which 2 were waited for; matrix products, arithmetic and copies ran while one was open for 0% of the time, Pallas kernels for 1%

profile of v13, /device:TPU:1, one launch (start us, length us, event | category | flops | bytes accessed | tf_op | source)
XLA Modules:
  0.0 97.8 jit_solution(2106283319924181664)
XLA Ops:
  0.6 1.7 %shard_map.149 = bf16[8,2,128,128]{3,2,1,0:T(8,128)(2,1)} custom-call(bf16[128,128]{1,0:T(8,128)(2,1)} %bitcast.6, bf16[128,128]{1,0:T(8,128)(2,1)} %bitcast.7), custom_call_target="tpu_custom_call" | custom-call | tf_op jit(solution)/shard_map/pallas_call | solution.py:268
  2.4 7.8 %all-to-all-start = ((bf16[8,2,128,128]{3,2,1,0:T(8,128)(2,1)}), bf16[8,2,128,128]{3,2,1,0:T(8,128)(2,1)S(1)}, u32[]{:S(2)}, u32[]{:S(2)}) async-start(bf16[8,2,128,128]{3,2,1,0:T(8,128)(2,1)} %shard_map.149), calls=%async_computation | async-start | bytes 1048576 | tf_op jit(solution)/shard_map/all_to_all | solution.py:353
  10.2 10.6 %all_gather.3.q_ref = bf16[4,256,128]{2,1,0:T(8,128)(2,1)S(1)} all-gather(bf16[1,256,128]{2,1,0:T(8,128)(2,1)S(1)} %bitcast.5), channel_id=1, replica_groups={{0,8,16,24},{4,12,20,28},{32,40,48,56},{36,44,52,60},{64,72,80,88},{68,..., dimensions={0}, use_global_device_ids=true | all-gather | bytes 327680 | tf_op jit(solution)/shard_map/all_gather | solution.py:354
  20.8 4.2 %all-to-all-done.kv_ref = bf16[8,2,128,128]{3,2,1,0:T(8,128)(2,1)S(1)} async-done(((bf16[8,2,128,128]{3,2,1,0:T(8,128)(2,1)}), bf16[8,2,128,128]{3,2,1,0:T(8,128)(2,1)S(1)}, u32[]{:S(2)}, u32[]{:S(2)}) %all-to-all-start) | async-done | bytes 524320 | tf_op jit(solution)/shard_map/all_to_all | solution.py:353
  24.9 5.6 %collective-permute-start = (bf16[8,2,128,128]{3,2,1,0:T(8,128)(2,1)S(1)}, bf16[8,2,128,128]{3,2,1,0:T(8,128)(2,1)S(1)}, u32[]{:S(2)}, u32[]{:S(2)}) collective-permute-start(bf16[8,2,128,128]{3,2,1,0:T(8,128)(2,1)S(1)} %all-to-all-done.kv_ref), channel_id=1, source_target_pairs={{0,4},{4,0},{8,12},{12,8},{16,20},{20,16},{24,28},{28,24},{32,36},... | collective-permute-start | bytes 1572872 | tf_op jit(solution)/shard_map/ppermute | solution.py:356
  30.5 1.3 %shard_map.150 = (f32[4,256,128]{2,1,0:T(8,128)S(1)}, f32[4,256,128]{2,1,0:T(8,128)S(1)}) custom-call(bf16[4,256,128]{2,1,0:T(8,128)(2,1)S(1)} %all_gather.3.q_ref, bf16[8,2,128,128]{3,2,1,0:T(8,128)(2,1)S(1)} %all-to-all-done.kv_ref), custom_call_target="tpu_custom_call" | custom-call | tf_op jit(solution)/shard_map/pallas_call | solution.py:314
  31.8 0.3 collective-permute-done.kv_ref
  32.0 1.7 %shard_map.151 = bf16[4,272,128]{2,1,0:T(8,128)(2,1)S(1)} custom-call(bf16[4,256,128]{2,1,0:T(8,128)(2,1)S(1)} %all_gather.3.q_ref, bf16[8,2,128,128]{3,2,1,0:T(8,128)(2,1)S(1)} %collective-permute-done.kv_ref, f32[4,256,128]{2,1,0:T(8,128)S(1)} %get-tuple-element.8.sums_ref, f32[4,256,128]{2,1,0:T(8,128)S(1)} %get-tuple-element.9.stats_ref), custom_call_target="tpu_custom_call" | custom-call | tf_op jit(solution)/shard_map/pallas_call | solution.py:320
  33.7 0.0 copy-start
  33.7 10.2 %all_to_all.25.parts_ref = bf16[4,272,128]{2,1,0:T(8,128)(2,1)S(1)} all-to-all(bf16[4,272,128]{2,1,0:T(8,128)(2,1)S(1)} %shard_map.151), channel_id=1, replica_groups={{0,8,16,24},{4,12,20,28},{32,40,48,56},{36,44,52,60},{64,72,80,88},{68,..., dimensions={0} | all-to-all | bytes 557056 | tf_op jit(solution)/shard_map/all_to_all | solution.py:358
  44.0 0.6 shard_map.152
  44.5 0.0 copy-start.5
  44.6 0.0 copy-start.3
  44.6 0.0 copy-start.4
  44.6 0.0 copy-start.6
  44.6 0.0 copy-start.7
  44.6 17.8 %all_to_all.26.parts_ref = bf16[8,128,128]{2,1,0:T(8,128)(2,1)S(1)} all-to-all(bf16[8,128,128]{2,1,0:T(8,128)(2,1)S(1)} %shard_map.152), channel_id=1, replica_groups=mesh['role'=2,'seq'=64,'head'=4] {'role','head'}, dimensions={0} | all-to-all | bytes 524288 | tf_op jit(solution)/shard_map/all_to_all | solution.py:360
  62.4 0.0 copy-start.1
  62.4 0.0 copy-start.2
  62.4 0.2 shard_map.153
  62.6 18.0 %all_to_all.27.in_ref = bf16[64,8,128]{2,1,0:T(8,128)(2,1)S(1)} all-to-all(bf16[64,8,128]{2,1,0:T(8,128)(2,1)S(1)} %shard_map.153), channel_id=1, replica_groups=mesh['role'=2,'seq'=64,'head'=4] {'seq'}, dimensions={0} | all-to-all | bytes 262144 | tf_op jit(solution)/shard_map/all_to_all | solution.py:362
  80.6 2.6 %shard_map.154 = bf16[64,4,128]{2,1,0:T(4,128)(2,1)S(1)} custom-call(f32[128]{0:T(128)} %skip_ref.1, bf16[64,8,128]{2,1,0:T(8,128)(2,1)S(1)} %all_to_all.27.in_ref, f32[72,128]{1,0:T(8,128)S(1)} %copy-done.7, f32[72,128]{1,0:T(8,128)S(1)} %copy-done.6, bf16[144,192]{1,0:T(8,128)(2,1)S(1)} %copy-done.3, bf16[64,432]{1,0:T(8,128)(2,1)S(1)} %copy-done.4, ...), custom_call_target="tpu_custom_call" | custom-call | tf_op jit(solution)/shard_map/pallas_call | solution.py:292
  83.2 13.8 %all_to_all.28.in_ref = bf16[64,4,128]{2,1,0:T(4,128)(2,1)S(1)} all-to-all(bf16[64,4,128]{2,1,0:T(4,128)(2,1)S(1)} %shard_map.154), channel_id=1, replica_groups=mesh['role'=2,'seq'=64,'head'=4] {'seq'}, dimensions={0} | all-to-all | bytes 131072 | tf_op jit(solution)/shard_map/all_to_all | solution.py:364
  97.0 0.7 shard_map.155
  (14 shorter events, 0.0 us)
Async XLA Ops:
  2.4 7.8 %copy-start.10 = (bf16[128,2,128]{2,1,0:T(2,128)(2,1)S(1)}, bf16[128,2,128]{2,1,0:T(2,128)(2,1)}, u32[]{:S(2)}) copy-start(bf16[128,2,128]{2,1,0:T(2,128)(2,1)} %param.14) | copy-start | bytes 196612
  2.4 22.5 %all-to-all-start = ((bf16[8,2,128,128]{3,2,1,0:T(8,128)(2,1)}), bf16[8,2,128,128]{3,2,1,0:T(8,128)(2,1)S(1)}, u32[]{:S(2)}, u32[]{:S(2)}) async-start(bf16[8,2,128,128]{3,2,1,0:T(8,128)(2,1)} %shard_map.149), calls=%async_computation | async-start | bytes 1048576 | tf_op jit(solution)/shard_map/all_to_all | solution.py:353
  24.9 7.1 %collective-permute-start = (bf16[8,2,128,128]{3,2,1,0:T(8,128)(2,1)S(1)}, bf16[8,2,128,128]{3,2,1,0:T(8,128)(2,1)S(1)}, u32[]{:S(2)}, u32[]{:S(2)}) collective-permute-start(bf16[8,2,128,128]{3,2,1,0:T(8,128)(2,1)S(1)} %all-to-all-done.kv_ref), channel_id=1, source_target_pairs={{0,4},{4,0},{8,12},{12,8},{16,20},{20,16},{24,28},{28,24},{32,36},... | collective-permute-start | bytes 1572872 | tf_op jit(solution)/shard_map/ppermute | solution.py:356
  33.7 10.2 %copy-start = (bf16[2,128,1024]{2,1,0:T(8,128)(2,1)S(1)}, bf16[2,128,1024]{2,1,0:T(8,128)(2,1)}, u32[]{:S(2)}) copy-start(bf16[2,128,1024]{2,1,0:T(8,128)(2,1)} %param.17) | copy-start | bytes 1572868
  44.5 17.8 %copy-start.5 = (f32[128,128]{1,0:T(8,128)S(1)}, f32[128,128]{1,0:T(8,128)}, u32[]{:S(2)}) copy-start(f32[128,128]{1,0:T(8,128)} %taps_ref.1) | copy-start | bytes 196612
  44.6 17.8 %copy-start.8 = (bf16[128,128]{1,0:T(8,128)(2,1)S(1)}, bf16[128,128]{1,0:T(8,128)(2,1)}, u32[]{:S(2)}) copy-start(bf16[128,128]{1,0:T(8,128)(2,1)} %input_ref.1) | copy-start | bytes 98308
  44.6 17.8 %copy-start.9 = (bf16[128,128]{1,0:T(8,128)(2,1)S(1)}, bf16[128,128]{1,0:T(8,128)(2,1)}, u32[]{:S(2)}) copy-start(bf16[128,128]{1,0:T(8,128)(2,1)} %gate_ref.1) | copy-start | bytes 98308
  44.6 36.0 %copy-start.3 = (bf16[144,192]{1,0:T(8,128)(2,1)S(1)}, bf16[144,192]{1,0:T(8,128)(2,1)}, u32[]{:S(2)}) copy-start(bf16[144,192]{1,0:T(8,128)(2,1)} %constant.14.clone.first) | copy-start | bytes 165892
  44.6 36.0 %copy-start.4 = (bf16[64,432]{1,0:T(8,128)(2,1)S(1)}, bf16[64,432]{1,0:T(8,128)(2,1)}, u32[]{:S(2)}) copy-start(bf16[64,432]{1,0:T(8,128)(2,1)} %constant.15.clone.last) | copy-start | bytes 165892
  44.6 36.0 %copy-start.6 = (f32[72,128]{1,0:T(8,128)S(1)}, f32[72,128]{1,0:T(8,128)}, u32[]{:S(2)}) copy-start(f32[72,128]{1,0:T(8,128)} %constant.13.clone.ts) | copy-start | bytes 110596
  44.6 36.0 %copy-start.7 = (f32[72,128]{1,0:T(8,128)S(1)}, f32[72,128]{1,0:T(8,128)}, u32[]{:S(2)}) copy-start(f32[72,128]{1,0:T(8,128)} %constant.12.clone.tc) | copy-start | bytes 110596
  62.4 18.2 %copy-start.1 = (bf16[768,256]{1,0:T(8,128)(2,1)S(1)}, bf16[768,256]{1,0:T(8,128)(2,1)}, u32[]{:S(2)}) copy-start(bf16[768,256]{1,0:T(8,128)(2,1)} %constant.17.clone.backward) | copy-start | bytes 1179652
  62.4 18.2 %copy-start.2 = (bf16[768,256]{1,0:T(8,128)(2,1)S(1)}, bf16[768,256]{1,0:T(8,128)(2,1)}, u32[]{:S(2)}) copy-start(bf16[768,256]{1,0:T(8,128)(2,1)} %constant.16.clone.forward) | copy-start | bytes 1179652

commit v14 on v13

--- a/solution.py
+++ b/solution.py
@@ -38,14 +38,14 @@
     for table, axis in ((first, 1), (last, 1), (forward, 0), (backward, 0)):
         high = np.asarray(table, ml_dtypes.bfloat16)
         low = np.asarray(table - high.astype(np.float64), ml_dtypes.bfloat16)
-        tables.append(np.concatenate([high, high, low], axis))
+        tables.append(np.concatenate([high, low, high], axis))
     return tables
 
 
 def triple(x, axis):
     high = x.astype(jnp.bfloat16)
     low = (x - high.astype(jnp.float32)).astype(jnp.bfloat16)
-    return jnp.concatenate([high, low, high], axis)
+    return jnp.concatenate([high, high, low], axis)
 
 
 def table_times(table, x):
@@ -56,8 +56,14 @@
     return jnp.dot(triple(x, 1), table, preferred_element_type=jnp.float32)
 
 
-def to_spectra(signals, first, turn_cos, turn_sin, forward):
-    stacked = table_times(first, jnp.concatenate(signals, 1))
+def to_spectra(signals, first, turn_cos, turn_sin, forward, exact=False):
+    joined = jnp.concatenate(signals, 1)
+    if exact:
+        joined = joined.astype(jnp.bfloat16)
+        joined = jnp.concatenate([joined, joined], 0)
+        stacked = jnp.dot(first[:, : 2 * SHARDS], joined, preferred_element_type=jnp.float32)
+    else:
+        stacked = table_times(first, joined)
     rows = []
     for n in range(len(signals)):
         re = stacked[:HALF, n * 128 : (n + 1) * 128]
@@ -114,15 +120,15 @@
     out_ref[...] = wide_ref[...].astype(jnp.bfloat16)
 
 
-def student_kernel(skip_ref, in_ref, tc, ts, first, last, forward, backward, out_ref, wide_in, wide_out):
-    wide_in[...] = in_ref[...].astype(jnp.float32)
+def student_kernel(skip_ref, in_ref, tc, ts, first, last, forward, backward, out_ref, wide_out):
+    wide = in_ref[...].astype(jnp.float32)
     rank = lax.axis_index("seq")
     skip = [skip_ref[rank], skip_ref[rank + SHARDS]]
-    target, signal, gate, taps = [[wide_in[:, 2 * n + c, :] for c in (0, 1)] for n in range(4)]
+    target, signal, gate, taps = [[wide[:, 2 * n + c, :] for c in (0, 1)] for n in range(4)]
     turn = tc[...], ts[...]
     ahead = first[...], *turn, forward[...]
     behind = last[...], *turn, backward[...]
-    spectra = to_spectra(signal + taps, *ahead)
+    spectra = to_spectra(signal + taps, *ahead, exact=True)
     conv = to_signals([product(spectra[c], spectra[2 + c]) for c in (0, 1)], *behind)
     back = []
     for c in (0, 1):
@@ -139,11 +145,11 @@
     out_ref[...] = wide_out[...].astype(jnp.bfloat16)
 
 
-def unpack_kernel(in_ref, grad_ref, step_ref, wide_ref):
-    wide_ref[...] = in_ref[...].astype(jnp.float32)
+def unpack_kernel(in_ref, grad_ref, step_ref):
+    wide = in_ref[...].astype(jnp.float32)
     for c in (0, 1):
-        grad_ref[c * SHARDS : (c + 1) * SHARDS, :] = wide_ref[:, c, :]
-        step_ref[c * SHARDS : (c + 1) * SHARDS, :] = wide_ref[:, 2 + c, :]
+        grad_ref[c * SHARDS : (c + 1) * SHARDS, :] = wide[:, c, :]
+        step_ref[c * SHARDS : (c + 1) * SHARDS, :] = wide[:, 2 + c, :]
 
 
 def attend_part(query, kv_ref, row, edges, live, diagonal, before):
@@ -226,8 +232,8 @@
             rest = log_sum - high
             middle = rest.astype(jnp.bfloat16).astype(jnp.float32)
             stats += [high, middle, rest - middle]
-        stats.append(jnp.zeros((10, 128), jnp.float32))
-        out_ref[theirs, 256:272, :] = jnp.concatenate(stats, 0).astype(jnp.bfloat16)
+        stats.append(jnp.zeros((2, 128), jnp.float32))
+        out_ref[theirs, 256:264, :] = jnp.concatenate(stats, 0).astype(jnp.bfloat16)
 
 
 def merge_kernel(parts_ref, proj_ref, out_ref, merged_ref):
@@ -235,7 +241,7 @@
     for half in (0, 1):
         sums = []
         for p in range(GROUP):
-            stats = parts_ref[p, 256:272, :].astype(jnp.float32)
+            stats = parts_ref[p, 256:264, :].astype(jnp.float32)
             sums.append(jnp.sum(stats[3 * half : 3 * half + 3], axis=0, keepdims=True))
         sums = jnp.concatenate(sums, 0)
         share = jnp.exp(sums - jnp.max(sums, axis=0, keepdims=True))
@@ -294,7 +300,7 @@
         out_shape=pltpu.VMEM((SHARDS, 4, 128), jnp.bfloat16),
         in_specs=[SMEM] + [VMEM] * 7,
         out_specs=VMEM,
-        scratch_shapes=[pltpu.VMEM((SHARDS, 8, 128), jnp.float32), pltpu.VMEM((SHARDS, 4, 128), jnp.float32)],
+        scratch_shapes=[pltpu.VMEM((SHARDS, 4, 128), jnp.float32)],
     )(skip, near(packed), *tables)
 
 
@@ -304,7 +310,6 @@
         out_shape=(jax.ShapeDtypeStruct((128, 128), jnp.float32),) * 2,
         in_specs=[VMEM],
         out_specs=(VMEM,) * 2,
-        scratch_shapes=[pltpu.VMEM((SHARDS, 4, 128), jnp.float32)],
     )(near(out))
 
 
@@ -319,7 +324,7 @@
     )(queries, near(own))
     return pl.pallas_call(
         attend_sibling_kernel,
-        out_shape=pltpu.VMEM((GROUP, 272, 128), jnp.bfloat16),
+        out_shape=pltpu.VMEM((GROUP, 264, 128), jnp.bfloat16),
         in_specs=[VMEM] * 4,
         out_specs=VMEM,
     )(queries, near(sibling), near(sums), near(stats))

time: 98.3 us -> 97.5 us (level)
  no operation moved by 1% of the time
where the time goes in v14:
time: 97.5 us; the launch traced here: 96.9 us
  blocking collectives  69.6 us (71%)
  starting transfers between devices  13.4 us (14%)
  Pallas kernels  8.73 us (9%)
  waiting for transfers between devices  4.4 us (5%)
    all_to_all x1, blocking collectives, body(): target = lax.all_to_all(target, ('role', 'head'), 0, 0)  17.8 us
    all_to_all x1, blocking collectives, body(): packed = lax.all_to_all(packed, 'seq', 0, 0)  17.4 us
    all_to_all x1, blocking collectives, body(): out = lax.all_to_all(out, 'seq', 0, 0)  13.9 us
    all_gather x1, blocking collectives, body(): lax.all_gather(query_heads.reshape(2 * SHARD, 128), 'seq', axis_index_gro...  10.6 us
    all_to_all x1, blocking collectives, body(): parts = lax.all_to_all(parts, 'seq', 0, 0, axis_index_groups=groups)  9.84 us
    all_to_all x1, starting transfers between devices, body(): own = lax.all_to_all(pairs, 'seq', 0, 0, axis_index_groups=columns)  7.79 us
    ppermute x1, starting transfers between devices, body(): sibling = lax.ppermute(own, 'seq', [(i, i ^ 1) for i in range(SHARDS)])  5.59 us
    all_to_all x1, waiting for transfers between devices, body(): own = lax.all_to_all(pairs, 'seq', 0, 0, axis_index_groups=columns)  4.15 us
  transfers between devices with their start and end apart: 2, of which 2 were waited for; matrix products, arithmetic and copies ran while one was open for 0% of the time, Pallas kernels for 1%

profile of v14, /device:TPU:1, one launch (start us, length us, event | category | flops | bytes accessed | tf_op | source)
XLA Modules:
  0.0 96.9 jit_solution(2327653874657137285)
XLA Ops:
  0.6 1.7 %shard_map.149 = bf16[8,2,128,128]{3,2,1,0:T(8,128)(2,1)} custom-call(bf16[128,128]{1,0:T(8,128)(2,1)} %bitcast.6, bf16[128,128]{1,0:T(8,128)(2,1)} %bitcast.7), custom_call_target="tpu_custom_call" | custom-call | tf_op jit(solution)/shard_map/pallas_call | solution.py:274
  2.4 0.0 copy-start.10
  2.4 7.8 %all-to-all-start = ((bf16[8,2,128,128]{3,2,1,0:T(8,128)(2,1)}), bf16[8,2,128,128]{3,2,1,0:T(8,128)(2,1)S(1)}, u32[]{:S(2)}, u32[]{:S(2)}) async-start(bf16[8,2,128,128]{3,2,1,0:T(8,128)(2,1)} %shard_map.149), calls=%async_computation | async-start | bytes 1048576 | tf_op jit(solution)/shard_map/all_to_all | solution.py:358
  10.2 10.6 %all_gather.3.q_ref = bf16[4,256,128]{2,1,0:T(8,128)(2,1)S(1)} all-gather(bf16[1,256,128]{2,1,0:T(8,128)(2,1)S(1)} %bitcast.5), channel_id=1, replica_groups={{0,8,16,24},{4,12,20,28},{32,40,48,56},{36,44,52,60},{64,72,80,88},{68,..., dimensions={0}, use_global_device_ids=true | all-gather | bytes 327680 | tf_op jit(solution)/shard_map/all_gather | solution.py:359
  20.8 4.2 %all-to-all-done.kv_ref = bf16[8,2,128,128]{3,2,1,0:T(8,128)(2,1)S(1)} async-done(((bf16[8,2,128,128]{3,2,1,0:T(8,128)(2,1)}), bf16[8,2,128,128]{3,2,1,0:T(8,128)(2,1)S(1)}, u32[]{:S(2)}, u32[]{:S(2)}) %all-to-all-start) | async-done | bytes 524320 | tf_op jit(solution)/shard_map/all_to_all | solution.py:358
  24.9 5.6 %collective-permute-start = (bf16[8,2,128,128]{3,2,1,0:T(8,128)(2,1)S(1)}, bf16[8,2,128,128]{3,2,1,0:T(8,128)(2,1)S(1)}, u32[]{:S(2)}, u32[]{:S(2)}) collective-permute-start(bf16[8,2,128,128]{3,2,1,0:T(8,128)(2,1)S(1)} %all-to-all-done.kv_ref), channel_id=1, source_target_pairs={{0,4},{4,0},{8,12},{12,8},{16,20},{20,16},{24,28},{28,24},{32,36},... | collective-permute-start | bytes 1572872 | tf_op jit(solution)/shard_map/ppermute | solution.py:361
  30.5 1.3 %shard_map.150 = (f32[4,256,128]{2,1,0:T(8,128)S(1)}, f32[4,256,128]{2,1,0:T(8,128)S(1)}) custom-call(bf16[4,256,128]{2,1,0:T(8,128)(2,1)S(1)} %all_gather.3.q_ref, bf16[8,2,128,128]{3,2,1,0:T(8,128)(2,1)S(1)} %all-to-all-done.kv_ref), custom_call_target="tpu_custom_call" | custom-call | tf_op jit(solution)/shard_map/pallas_call | solution.py:319
  31.8 0.3 collective-permute-done.kv_ref
  32.0 1.7 %shard_map.151 = bf16[4,264,128]{2,1,0:T(8,128)(2,1)S(1)} custom-call(bf16[4,256,128]{2,1,0:T(8,128)(2,1)S(1)} %all_gather.3.q_ref, bf16[8,2,128,128]{3,2,1,0:T(8,128)(2,1)S(1)} %collective-permute-done.kv_ref, f32[4,256,128]{2,1,0:T(8,128)S(1)} %get-tuple-element.8.sums_ref, f32[4,256,128]{2,1,0:T(8,128)S(1)} %get-tuple-element.9.stats_ref), custom_call_target="tpu_custom_call" | custom-call | tf_op jit(solution)/shard_map/pallas_call | solution.py:325
  33.7 9.8 %all_to_all.25.parts_ref = bf16[4,264,128]{2,1,0:T(8,128)(2,1)S(1)} all-to-all(bf16[4,264,128]{2,1,0:T(8,128)(2,1)S(1)} %shard_map.151), channel_id=1, replica_groups={{0,8,16,24},{4,12,20,28},{32,40,48,56},{36,44,52,60},{64,72,80,88},{68,..., dimensions={0} | all-to-all | bytes 540672 | tf_op jit(solution)/shard_map/all_to_all | solution.py:363
  43.6 0.6 shard_map.152
  44.2 0.0 copy-start.9
  44.2 0.0 copy-start.3
  44.2 0.0 copy-start.4
  44.2 0.0 copy-start.6
  44.2 0.0 copy-start.7
  44.3 17.8 %all_to_all.26.parts_ref = bf16[8,128,128]{2,1,0:T(8,128)(2,1)S(1)} all-to-all(bf16[8,128,128]{2,1,0:T(8,128)(2,1)S(1)} %shard_map.152), channel_id=1, replica_groups=mesh['role'=2,'seq'=64,'head'=4] {'role','head'}, dimensions={0} | all-to-all | bytes 524288 | tf_op jit(solution)/shard_map/all_to_all | solution.py:365
  62.1 0.0 copy-start.1
  62.1 0.0 copy-start.2
  62.1 0.2 shard_map.153
  62.3 17.4 %all_to_all.27.in_ref = bf16[64,8,128]{2,1,0:T(8,128)(2,1)S(1)} all-to-all(bf16[64,8,128]{2,1,0:T(8,128)(2,1)S(1)} %shard_map.153), channel_id=1, replica_groups=mesh['role'=2,'seq'=64,'head'=4] {'seq'}, dimensions={0} | all-to-all | bytes 262144 | tf_op jit(solution)/shard_map/all_to_all | solution.py:367
  79.8 2.6 %shard_map.154 = bf16[64,4,128]{2,1,0:T(4,128)(2,1)S(1)} custom-call(f32[128]{0:T(128)} %skip_ref.1, bf16[64,8,128]{2,1,0:T(8,128)(2,1)S(1)} %all_to_all.27.in_ref, f32[72,128]{1,0:T(8,128)S(1)} %copy-done.7, f32[72,128]{1,0:T(8,128)S(1)} %copy-done.6, bf16[144,192]{1,0:T(8,128)(2,1)S(1)} %copy-done.3, bf16[64,432]{1,0:T(8,128)(2,1)S(1)} %copy-done.4, ...), custom_call_target="tpu_custom_call" | custom-call | tf_op jit(solution)/shard_map/pallas_call | solution.py:298
  82.3 13.9 %all_to_all.28.in_ref = bf16[64,4,128]{2,1,0:T(4,128)(2,1)S(1)} all-to-all(bf16[64,4,128]{2,1,0:T(4,128)(2,1)S(1)} %shard_map.154), channel_id=1, replica_groups=mesh['role'=2,'seq'=64,'head'=4] {'seq'}, dimensions={0} | all-to-all | bytes 131072 | tf_op jit(solution)/shard_map/all_to_all | solution.py:369
  96.2 0.7 shard_map.155
  (14 shorter events, 0.0 us)
Async XLA Ops:
  2.4 7.8 %copy-start.10 = (bf16[128,2,128]{2,1,0:T(2,128)(2,1)S(1)}, bf16[128,2,128]{2,1,0:T(2,128)(2,1)}, u32[]{:S(2)}) copy-start(bf16[128,2,128]{2,1,0:T(2,128)(2,1)} %param.14) | copy-start | bytes 196612
  2.4 22.5 %all-to-all-start = ((bf16[8,2,128,128]{3,2,1,0:T(8,128)(2,1)}), bf16[8,2,128,128]{3,2,1,0:T(8,128)(2,1)S(1)}, u32[]{:S(2)}, u32[]{:S(2)}) async-start(bf16[8,2,128,128]{3,2,1,0:T(8,128)(2,1)} %shard_map.149), calls=%async_computation | async-start | bytes 1048576 | tf_op jit(solution)/shard_map/all_to_all | solution.py:358
  24.9 7.1 %collective-permute-start = (bf16[8,2,128,128]{3,2,1,0:T(8,128)(2,1)S(1)}, bf16[8,2,128,128]{3,2,1,0:T(8,128)(2,1)S(1)}, u32[]{:S(2)}, u32[]{:S(2)}) collective-permute-start(bf16[8,2,128,128]{3,2,1,0:T(8,128)(2,1)S(1)} %all-to-all-done.kv_ref), channel_id=1, source_target_pairs={{0,4},{4,0},{8,12},{12,8},{16,20},{20,16},{24,28},{28,24},{32,36},... | collective-permute-start | bytes 1572872 | tf_op jit(solution)/shard_map/ppermute | solution.py:361
  33.7 9.9 %copy-start = (bf16[2,128,1024]{2,1,0:T(8,128)(2,1)S(1)}, bf16[2,128,1024]{2,1,0:T(8,128)(2,1)}, u32[]{:S(2)}) copy-start(bf16[2,128,1024]{2,1,0:T(8,128)(2,1)} %param.17) | copy-start | bytes 1572868
  44.2 17.9 %copy-start.5 = (f32[128,128]{1,0:T(8,128)S(1)}, f32[128,128]{1,0:T(8,128)}, u32[]{:S(2)}) copy-start(f32[128,128]{1,0:T(8,128)} %taps_ref.1) | copy-start | bytes 196612
  44.2 17.9 %copy-start.8 = (bf16[128,128]{1,0:T(8,128)(2,1)S(1)}, bf16[128,128]{1,0:T(8,128)(2,1)}, u32[]{:S(2)}) copy-start(bf16[128,128]{1,0:T(8,128)(2,1)} %input_ref.1) | copy-start | bytes 98308
  44.2 17.9 %copy-start.9 = (bf16[128,128]{1,0:T(8,128)(2,1)S(1)}, bf16[128,128]{1,0:T(8,128)(2,1)}, u32[]{:S(2)}) copy-start(bf16[128,128]{1,0:T(8,128)(2,1)} %gate_ref.1) | copy-start | bytes 98308
  44.2 35.5 %copy-start.3 = (bf16[144,192]{1,0:T(8,128)(2,1)S(1)}, bf16[144,192]{1,0:T(8,128)(2,1)}, u32[]{:S(2)}) copy-start(bf16[144,192]{1,0:T(8,128)(2,1)} %constant.14.clone.first) | copy-start | bytes 165892
  44.2 35.5 %copy-start.4 = (bf16[64,432]{1,0:T(8,128)(2,1)S(1)}, bf16[64,432]{1,0:T(8,128)(2,1)}, u32[]{:S(2)}) copy-start(bf16[64,432]{1,0:T(8,128)(2,1)} %constant.15.clone.last) | copy-start | bytes 165892
  44.2 35.5 %copy-start.6 = (f32[72,128]{1,0:T(8,128)S(1)}, f32[72,128]{1,0:T(8,128)}, u32[]{:S(2)}) copy-start(f32[72,128]{1,0:T(8,128)} %constant.13.clone.ts) | copy-start | bytes 110596
  44.2 35.5 %copy-start.7 = (f32[72,128]{1,0:T(8,128)S(1)}, f32[72,128]{1,0:T(8,128)}, u32[]{:S(2)}) copy-start(f32[72,128]{1,0:T(8,128)} %constant.12.clone.tc) | copy-start | bytes 110596
  62.1 17.7 %copy-start.1 = (bf16[768,256]{1,0:T(8,128)(2,1)S(1)}, bf16[768,256]{1,0:T(8,128)(2,1)}, u32[]{:S(2)}) copy-start(bf16[768,256]{1,0:T(8,128)(2,1)} %constant.17.clone.backward) | copy-start | bytes 1179652
  62.1 17.7 %copy-start.2 = (bf16[768,256]{1,0:T(8,128)(2,1)S(1)}, bf16[768,256]{1,0:T(8,128)(2,1)}, u32[]{:S(2)}) copy-start(bf16[768,256]{1,0:T(8,128)(2,1)} %constant.16.clone.forward) | copy-start | bytes 1179652

commit v15 on v14

--- a/solution.py
+++ b/solution.py
@@ -200,8 +200,8 @@
         edges = [row, oldest] if step == 0 else [jnp.where(newer, row, oldest)]
         live = jnp.logical_or(newer, row >= BACK)
         top, sums, total = attend_part(q_ref[theirs], kv_ref, row, edges, live, step == 0, None)
-        sums_ref[step] = sums
-        stats_ref[step] = jnp.where(low_lanes(), top, total)
+        sums_ref[theirs] = sums
+        stats_ref[theirs] = jnp.where(low_lanes(), top, total)
 
 
 def attend_sibling_kernel(q_ref, kv_ref, sums_ref, stats_ref, out_ref):
@@ -211,23 +211,45 @@
     oldest = jnp.maximum(row - BACK, 0)
     rows = lax.broadcasted_iota(jnp.int32, (SHARD, SHARD), 0)
     columns = lax.broadcasted_iota(jnp.int32, (SHARD, SHARD), 1)
-    for step in range(GROUP):
-        theirs = (mine + step) % GROUP
-        newer = core == 1 if step == 0 else theirs > mine
-        live = jnp.logical_or(newer, row >= BACK)
-        stats = stats_ref[step]
-        before, total_before = stats[:, :1], stats[:, 127:]
-        edges = [jnp.where(newer, row, oldest)]
-        top, sums, total = attend_part(q_ref[theirs], kv_ref, row, edges, live, False, before)
-        share = jnp.exp2((before - top) * (scale * LOG2E))
-        total = total + share * total_before
-        safe = jnp.maximum(total, 1e-30)
-        out_ref[theirs, :256, :] = ((sums + share * sums_ref[step]) / safe).astype(jnp.bfloat16)
-        log_sums = jnp.where(total > 0.0, top * scale + jnp.log(safe), NEG)
+    full = [jnp.maximum(row - BACK + r, 0) for r in (1, 2, 3)]
+    ones = jnp.ones((SHARD, 128), jnp.bfloat16)
+    keys = jnp.concatenate([kv_ref[n, 0] for n in full], 0)
+    values = jnp.concatenate([jnp.concatenate([kv_ref[n, 1], ones], 1) for n in full], 0)
+    contract = (((1,), (1,)), ((), ()))
+    queries = q_ref[...].reshape(GROUP * 2 * SHARD, 128)
+    scores = lax.dot_general(queries, keys, contract, preferred_element_type=jnp.float32)
+    tops, edge_sums, spreads = [], [], []
+    for theirs in range(GROUP):
+        newer = jnp.where(mine == theirs, core, (mine < theirs).astype(jnp.int32)) == 1
+        edge = jnp.where(newer, row, oldest)
+        block = lax.dot_general(q_ref[theirs], kv_ref[edge, 0], contract, preferred_element_type=jnp.float32)
+        blocks = [jnp.where(jnp.logical_or(newer, row >= BACK), block, NEG)]
+        part = scores[theirs * 2 * SHARD : (theirs + 1) * 2 * SHARD]
+        for r in (1, 2, 3):
+            blocks.append(jnp.where(row >= BACK - r, part[:, (r - 1) * SHARD : r * SHARD], NEG))
+        top = jnp.maximum(jnp.maximum(blocks[0], blocks[1]), jnp.maximum(blocks[2], blocks[3]))
+        top = jnp.maximum(jnp.max(top, axis=1, keepdims=True), stats_ref[theirs, :, :1])
+        tops.append(top)
+        shift = top * (scale * LOG2E)
+        weights = [jnp.exp2(b * (scale * LOG2E) - shift).astype(jnp.bfloat16) for b in blocks]
+        edge_values = jnp.concatenate([kv_ref[edge, 1], ones], 1)
+        edge_sums.append(jnp.dot(weights[0], edge_values, preferred_element_type=jnp.float32))
+        spreads.append(jnp.concatenate(weights[1:], 1))
+    all_sums = jnp.dot(jnp.concatenate(spreads, 0), values, preferred_element_type=jnp.float32)
+    for theirs in range(GROUP):
+        top = tops[theirs]
+        sums = all_sums[theirs * 2 * SHARD : (theirs + 1) * 2 * SHARD] + edge_sums[theirs]
+        share = jnp.exp2((stats_ref[theirs, :, :1] - top) * (scale * LOG2E))
+        total = sums[:, 128:] + share * stats_ref[theirs, :, 127:]
+        merged = sums[:, :128] + share * sums_ref[theirs]
+        out_ref[theirs, :256, :] = (merged / jnp.maximum(total, 1e-30)).astype(jnp.bfloat16)
         stats = []
         for half in (0, 1):
-            log_sum = log_sums[half * SHARD : (half + 1) * SHARD]
-            log_sum = jnp.sum(jnp.where(rows == columns, log_sum, 0.0), axis=0, keepdims=True)
+            part = slice(half * SHARD, (half + 1) * SHARD)
+            total_row = jnp.sum(jnp.where(rows == columns, total[part], 0.0), axis=0, keepdims=True)
+            top_row = jnp.sum(jnp.where(rows == columns, top[part], 0.0), axis=0, keepdims=True)
+            log_sum = top_row * scale + jnp.log(jnp.maximum(total_row, 1e-30))
+            log_sum = jnp.where(total_row > 0.0, log_sum, NEG)
             high = log_sum.astype(jnp.bfloat16).astype(jnp.float32)
             rest = log_sum - high
             middle = rest.astype(jnp.bfloat16).astype(jnp.float32)

time: 97.5 us -> 97.9 us (level)
  no operation moved by 1% of the time
where the time goes in v15:
time: 97.9 us; the launch traced here: 97.4 us
  blocking collectives  69.6 us (71%)
  starting transfers between devices  13.4 us (14%)
  Pallas kernels  9.22 us (9%)
  waiting for transfers between devices  4.4 us (4%)
    all_to_all x1, blocking collectives, body(): target = lax.all_to_all(target, ('role', 'head'), 0, 0)  17.8 us
    all_to_all x1, blocking collectives, body(): packed = lax.all_to_all(packed, 'seq', 0, 0)  17.4 us
    all_to_all x1, blocking collectives, body(): out = lax.all_to_all(out, 'seq', 0, 0)  13.9 us
    all_gather x1, blocking collectives, body(): lax.all_gather(query_heads.reshape(2 * SHARD, 128), 'seq', axis_index_gro...  10.6 us
    all_to_all x1, blocking collectives, body(): parts = lax.all_to_all(parts, 'seq', 0, 0, axis_index_groups=groups)  9.85 us
    all_to_all x1, starting transfers between devices, body(): own = lax.all_to_all(pairs, 'seq', 0, 0, axis_index_groups=columns)  7.79 us
    ppermute x1, starting transfers between devices, body(): sibling = lax.ppermute(own, 'seq', [(i, i ^ 1) for i in range(SHARDS)])  5.59 us
    all_to_all x1, waiting for transfers between devices, body(): own = lax.all_to_all(pairs, 'seq', 0, 0, axis_index_groups=columns)  4.15 us
  transfers between devices with their start and end apart: 2, of which 2 were waited for; matrix products, arithmetic and copies ran while one was open for 0% of the time, Pallas kernels for 1%

profile of v15, /device:TPU:1, one launch (start us, length us, event | category | flops | bytes accessed | tf_op | source)
XLA Modules:
  0.0 97.4 jit_solution(13486686383161706987)
XLA Ops:
  0.6 1.7 %shard_map.149 = bf16[8,2,128,128]{3,2,1,0:T(8,128)(2,1)} custom-call(bf16[128,128]{1,0:T(8,128)(2,1)} %bitcast.6, bf16[128,128]{1,0:T(8,128)(2,1)} %bitcast.7), custom_call_target="tpu_custom_call" | custom-call | tf_op jit(solution)/shard_map/pallas_call | solution.py:296
  2.4 7.8 %all-to-all-start = ((bf16[8,2,128,128]{3,2,1,0:T(8,128)(2,1)}), bf16[8,2,128,128]{3,2,1,0:T(8,128)(2,1)S(1)}, u32[]{:S(2)}, u32[]{:S(2)}) async-start(bf16[8,2,128,128]{3,2,1,0:T(8,128)(2,1)} %shard_map.149), calls=%async_computation | async-start | bytes 1048576 | tf_op jit(solution)/shard_map/all_to_all | solution.py:380
  10.2 10.6 %all_gather.3.q_ref = bf16[4,256,128]{2,1,0:T(8,128)(2,1)S(1)} all-gather(bf16[1,256,128]{2,1,0:T(8,128)(2,1)S(1)} %bitcast.5), channel_id=1, replica_groups={{0,8,16,24},{4,12,20,28},{32,40,48,56},{36,44,52,60},{64,72,80,88},{68,..., dimensions={0}, use_global_device_ids=true | all-gather | bytes 327680 | tf_op jit(solution)/shard_map/all_gather | solution.py:381
  20.8 4.2 %all-to-all-done.kv_ref = bf16[8,2,128,128]{3,2,1,0:T(8,128)(2,1)S(1)} async-done(((bf16[8,2,128,128]{3,2,1,0:T(8,128)(2,1)}), bf16[8,2,128,128]{3,2,1,0:T(8,128)(2,1)S(1)}, u32[]{:S(2)}, u32[]{:S(2)}) %all-to-all-start) | async-done | bytes 524320 | tf_op jit(solution)/shard_map/all_to_all | solution.py:380
  24.9 5.6 %collective-permute-start = (bf16[8,2,128,128]{3,2,1,0:T(8,128)(2,1)S(1)}, bf16[8,2,128,128]{3,2,1,0:T(8,128)(2,1)S(1)}, u32[]{:S(2)}, u32[]{:S(2)}) collective-permute-start(bf16[8,2,128,128]{3,2,1,0:T(8,128)(2,1)S(1)} %all-to-all-done.kv_ref), channel_id=1, source_target_pairs={{0,4},{4,0},{8,12},{12,8},{16,20},{20,16},{24,28},{28,24},{32,36},... | collective-permute-start | bytes 1572872 | tf_op jit(solution)/shard_map/ppermute | solution.py:383
  30.5 1.3 %shard_map.150 = (f32[4,256,128]{2,1,0:T(8,128)S(1)}, f32[4,256,128]{2,1,0:T(8,128)S(1)}) custom-call(bf16[4,256,128]{2,1,0:T(8,128)(2,1)S(1)} %all_gather.3.q_ref, bf16[8,2,128,128]{3,2,1,0:T(8,128)(2,1)S(1)} %all-to-all-done.kv_ref), custom_call_target="tpu_custom_call" | custom-call | tf_op jit(solution)/shard_map/pallas_call | solution.py:341
  31.8 0.3 collective-permute-done.kv_ref
  32.0 2.2 %shard_map.151 = bf16[4,264,128]{2,1,0:T(8,128)(2,1)S(1)} custom-call(bf16[4,256,128]{2,1,0:T(8,128)(2,1)S(1)} %all_gather.3.q_ref, bf16[8,2,128,128]{3,2,1,0:T(8,128)(2,1)S(1)} %collective-permute-done.kv_ref, f32[4,256,128]{2,1,0:T(8,128)S(1)} %get-tuple-element.8.sums_ref, f32[4,256,128]{2,1,0:T(8,128)S(1)} %get-tuple-element.9.stats_ref), custom_call_target="tpu_custom_call" | custom-call | tf_op jit(solution)/shard_map/pallas_call | solution.py:347
  34.2 9.8 %all_to_all.25.parts_ref = bf16[4,264,128]{2,1,0:T(8,128)(2,1)S(1)} all-to-all(bf16[4,264,128]{2,1,0:T(8,128)(2,1)S(1)} %shard_map.151), channel_id=1, replica_groups={{0,8,16,24},{4,12,20,28},{32,40,48,56},{36,44,52,60},{64,72,80,88},{68,..., dimensions={0} | all-to-all | bytes 540672 | tf_op jit(solution)/shard_map/all_to_all | solution.py:385
  44.1 0.6 shard_map.152
  44.7 0.0 copy-start.8
  44.7 0.0 copy-start.9
  44.7 0.0 copy-start.3
  44.7 0.0 copy-start.4
  44.7 0.0 copy-start.6
  44.7 0.0 copy-start.7
  44.8 17.8 %all_to_all.26.parts_ref = bf16[8,128,128]{2,1,0:T(8,128)(2,1)S(1)} all-to-all(bf16[8,128,128]{2,1,0:T(8,128)(2,1)S(1)} %shard_map.152), channel_id=1, replica_groups=mesh['role'=2,'seq'=64,'head'=4] {'role','head'}, dimensions={0} | all-to-all | bytes 524288 | tf_op jit(solution)/shard_map/all_to_all | solution.py:387
  62.6 0.0 copy-start.1
  62.6 0.0 copy-start.2
  62.6 0.2 shard_map.153
  62.8 17.4 %all_to_all.27.in_ref = bf16[64,8,128]{2,1,0:T(8,128)(2,1)S(1)} all-to-all(bf16[64,8,128]{2,1,0:T(8,128)(2,1)S(1)} %shard_map.153), channel_id=1, replica_groups=mesh['role'=2,'seq'=64,'head'=4] {'seq'}, dimensions={0} | all-to-all | bytes 262144 | tf_op jit(solution)/shard_map/all_to_all | solution.py:389
  80.3 2.6 %shard_map.154 = bf16[64,4,128]{2,1,0:T(4,128)(2,1)S(1)} custom-call(f32[128]{0:T(128)} %skip_ref.1, bf16[64,8,128]{2,1,0:T(8,128)(2,1)S(1)} %all_to_all.27.in_ref, f32[72,128]{1,0:T(8,128)S(1)} %copy-done.7, f32[72,128]{1,0:T(8,128)S(1)} %copy-done.6, bf16[144,192]{1,0:T(8,128)(2,1)S(1)} %copy-done.3, bf16[64,432]{1,0:T(8,128)(2,1)S(1)} %copy-done.4, ...), custom_call_target="tpu_custom_call" | custom-call | tf_op jit(solution)/shard_map/pallas_call | solution.py:320
  82.8 13.9 %all_to_all.28.in_ref = bf16[64,4,128]{2,1,0:T(4,128)(2,1)S(1)} all-to-all(bf16[64,4,128]{2,1,0:T(4,128)(2,1)S(1)} %shard_map.154), channel_id=1, replica_groups=mesh['role'=2,'seq'=64,'head'=4] {'seq'}, dimensions={0} | all-to-all | bytes 131072 | tf_op jit(solution)/shard_map/all_to_all | solution.py:391
  96.7 0.7 shard_map.155
  (14 shorter events, 0.0 us)
Async XLA Ops:
  2.4 7.8 %copy-start.10 = (bf16[128,2,128]{2,1,0:T(2,128)(2,1)S(1)}, bf16[128,2,128]{2,1,0:T(2,128)(2,1)}, u32[]{:S(2)}) copy-start(bf16[128,2,128]{2,1,0:T(2,128)(2,1)} %param.14) | copy-start | bytes 196612
  2.4 22.5 %all-to-all-start = ((bf16[8,2,128,128]{3,2,1,0:T(8,128)(2,1)}), bf16[8,2,128,128]{3,2,1,0:T(8,128)(2,1)S(1)}, u32[]{:S(2)}, u32[]{:S(2)}) async-start(bf16[8,2,128,128]{3,2,1,0:T(8,128)(2,1)} %shard_map.149), calls=%async_computation | async-start | bytes 1048576 | tf_op jit(solution)/shard_map/all_to_all | solution.py:380
  24.9 7.1 %collective-permute-start = (bf16[8,2,128,128]{3,2,1,0:T(8,128)(2,1)S(1)}, bf16[8,2,128,128]{3,2,1,0:T(8,128)(2,1)S(1)}, u32[]{:S(2)}, u32[]{:S(2)}) collective-permute-start(bf16[8,2,128,128]{3,2,1,0:T(8,128)(2,1)S(1)} %all-to-all-done.kv_ref), channel_id=1, source_target_pairs={{0,4},{4,0},{8,12},{12,8},{16,20},{20,16},{24,28},{28,24},{32,36},... | collective-permute-start | bytes 1572872 | tf_op jit(solution)/shard_map/ppermute | solution.py:383
  34.2 9.9 %copy-start = (bf16[2,128,1024]{2,1,0:T(8,128)(2,1)S(1)}, bf16[2,128,1024]{2,1,0:T(8,128)(2,1)}, u32[]{:S(2)}) copy-start(bf16[2,128,1024]{2,1,0:T(8,128)(2,1)} %param.17) | copy-start | bytes 1572868
  44.7 17.9 %copy-start.5 = (f32[128,128]{1,0:T(8,128)S(1)}, f32[128,128]{1,0:T(8,128)}, u32[]{:S(2)}) copy-start(f32[128,128]{1,0:T(8,128)} %taps_ref.1) | copy-start | bytes 196612
  44.7 17.9 %copy-start.8 = (bf16[128,128]{1,0:T(8,128)(2,1)S(1)}, bf16[128,128]{1,0:T(8,128)(2,1)}, u32[]{:S(2)}) copy-start(bf16[128,128]{1,0:T(8,128)(2,1)} %input_ref.1) | copy-start | bytes 98308
  44.7 17.9 %copy-start.9 = (bf16[128,128]{1,0:T(8,128)(2,1)S(1)}, bf16[128,128]{1,0:T(8,128)(2,1)}, u32[]{:S(2)}) copy-start(bf16[128,128]{1,0:T(8,128)(2,1)} %gate_ref.1) | copy-start | bytes 98308
  44.7 35.5 %copy-start.3 = (bf16[144,192]{1,0:T(8,128)(2,1)S(1)}, bf16[144,192]{1,0:T(8,128)(2,1)}, u32[]{:S(2)}) copy-start(bf16[144,192]{1,0:T(8,128)(2,1)} %constant.14.clone.first) | copy-start | bytes 165892
  44.7 35.5 %copy-start.4 = (bf16[64,432]{1,0:T(8,128)(2,1)S(1)}, bf16[64,432]{1,0:T(8,128)(2,1)}, u32[]{:S(2)}) copy-start(bf16[64,432]{1,0:T(8,128)(2,1)} %constant.15.clone.last) | copy-start | bytes 165892
  44.7 35.5 %copy-start.6 = (f32[72,128]{1,0:T(8,128)S(1)}, f32[72,128]{1,0:T(8,128)}, u32[]{:S(2)}) copy-start(f32[72,128]{1,0:T(8,128)} %constant.13.clone.ts) | copy-start | bytes 110596
  44.7 35.5 %copy-start.7 = (f32[72,128]{1,0:T(8,128)S(1)}, f32[72,128]{1,0:T(8,128)}, u32[]{:S(2)}) copy-start(f32[72,128]{1,0:T(8,128)} %constant.12.clone.tc) | copy-start | bytes 110596
  62.6 17.7 %copy-start.1 = (bf16[768,256]{1,0:T(8,128)(2,1)S(1)}, bf16[768,256]{1,0:T(8,128)(2,1)}, u32[]{:S(2)}) copy-start(bf16[768,256]{1,0:T(8,128)(2,1)} %constant.17.clone.backward) | copy-start | bytes 1179652
  62.6 17.7 %copy-start.2 = (bf16[768,256]{1,0:T(8,128)(2,1)S(1)}, bf16[768,256]{1,0:T(8,128)(2,1)}, u32[]{:S(2)}) copy-start(bf16[768,256]{1,0:T(8,128)(2,1)} %constant.16.clone.forward) | copy-start | bytes 1179652

commit v16 on v14

--- a/solution.py
+++ b/solution.py
@@ -211,9 +211,11 @@
     oldest = jnp.maximum(row - BACK, 0)
     rows = lax.broadcasted_iota(jnp.int32, (SHARD, SHARD), 0)
     columns = lax.broadcasted_iota(jnp.int32, (SHARD, SHARD), 1)
-    for step in range(GROUP):
+
+    @pl.loop(0, GROUP)
+    def _(step):
         theirs = (mine + step) % GROUP
-        newer = core == 1 if step == 0 else theirs > mine
+        newer = jnp.where(step == 0, core, (theirs > mine).astype(jnp.int32)) == 1
         live = jnp.logical_or(newer, row >= BACK)
         stats = stats_ref[step]
         before, total_before = stats[:, :1], stats[:, 127:]

time: 97.5 us -> 98.7 us (1.012)
  Pallas kernels: 8.73 us -> 9.98 us
    pallas_call x1, Pallas kernels: 1.7 us -> 2.94 us  [call_attend(): pl.pallas_call(attend_sibling_kernel, out_shape=pltpu.VMEM((GROUP, 264, 1...]
where the time goes in v16:
time: 98.7 us; the launch traced here: 98.2 us
  blocking collectives  69.5 us (70%)
  starting transfers between devices  13.4 us (14%)
  Pallas kernels  9.98 us (10%)
  waiting for transfers between devices  4.4 us (4%)
    all_to_all x1, blocking collectives, body(): target = lax.all_to_all(target, ('role', 'head'), 0, 0)  17.8 us
    all_to_all x1, blocking collectives, body(): packed = lax.all_to_all(packed, 'seq', 0, 0)  17.4 us
    all_to_all x1, blocking collectives, body(): out = lax.all_to_all(out, 'seq', 0, 0)  13.9 us
    all_gather x1, blocking collectives, body(): lax.all_gather(query_heads.reshape(2 * SHARD, 128), 'seq', axis_index_gro...  10.6 us
    all_to_all x1, blocking collectives, body(): parts = lax.all_to_all(parts, 'seq', 0, 0, axis_index_groups=groups)  9.84 us
    all_to_all x1, starting transfers between devices, body(): own = lax.all_to_all(pairs, 'seq', 0, 0, axis_index_groups=columns)  7.79 us
    ppermute x1, starting transfers between devices, body(): sibling = lax.ppermute(own, 'seq', [(i, i ^ 1) for i in range(SHARDS)])  5.59 us
    all_to_all x1, waiting for transfers between devices, body(): own = lax.all_to_all(pairs, 'seq', 0, 0, axis_index_groups=columns)  4.15 us
  transfers between devices with their start and end apart: 2, of which 2 were waited for; matrix products, arithmetic and copies ran while one was open for 0% of the time, Pallas kernels for 1%

profile of v16, /device:TPU:1, one launch (start us, length us, event | category | flops | bytes accessed | tf_op | source)
XLA Modules:
  0.0 98.2 jit_solution(9271452122042104599)
XLA Ops:
  0.6 1.7 %shard_map.149 = bf16[8,2,128,128]{3,2,1,0:T(8,128)(2,1)} custom-call(bf16[128,128]{1,0:T(8,128)(2,1)} %bitcast.6, bf16[128,128]{1,0:T(8,128)(2,1)} %bitcast.7), custom_call_target="tpu_custom_call" | custom-call | tf_op jit(solution)/shard_map/pallas_call | solution.py:276
  2.4 7.8 %all-to-all-start = ((bf16[8,2,128,128]{3,2,1,0:T(8,128)(2,1)}), bf16[8,2,128,128]{3,2,1,0:T(8,128)(2,1)S(1)}, u32[]{:S(2)}, u32[]{:S(2)}) async-start(bf16[8,2,128,128]{3,2,1,0:T(8,128)(2,1)} %shard_map.149), calls=%async_computation | async-start | bytes 1048576 | tf_op jit(solution)/shard_map/all_to_all | solution.py:360
  10.2 10.6 %all_gather.3.q_ref = bf16[4,256,128]{2,1,0:T(8,128)(2,1)S(1)} all-gather(bf16[1,256,128]{2,1,0:T(8,128)(2,1)S(1)} %bitcast.5), channel_id=1, replica_groups={{0,8,16,24},{4,12,20,28},{32,40,48,56},{36,44,52,60},{64,72,80,88},{68,..., dimensions={0}, use_global_device_ids=true | all-gather | bytes 327680 | tf_op jit(solution)/shard_map/all_gather | solution.py:361
  20.8 4.2 %all-to-all-done.kv_ref = bf16[8,2,128,128]{3,2,1,0:T(8,128)(2,1)S(1)} async-done(((bf16[8,2,128,128]{3,2,1,0:T(8,128)(2,1)}), bf16[8,2,128,128]{3,2,1,0:T(8,128)(2,1)S(1)}, u32[]{:S(2)}, u32[]{:S(2)}) %all-to-all-start) | async-done | bytes 524320 | tf_op jit(solution)/shard_map/all_to_all | solution.py:360
  24.9 5.6 %collective-permute-start = (bf16[8,2,128,128]{3,2,1,0:T(8,128)(2,1)S(1)}, bf16[8,2,128,128]{3,2,1,0:T(8,128)(2,1)S(1)}, u32[]{:S(2)}, u32[]{:S(2)}) collective-permute-start(bf16[8,2,128,128]{3,2,1,0:T(8,128)(2,1)S(1)} %all-to-all-done.kv_ref), channel_id=1, source_target_pairs={{0,4},{4,0},{8,12},{12,8},{16,20},{20,16},{24,28},{28,24},{32,36},... | collective-permute-start | bytes 1572872 | tf_op jit(solution)/shard_map/ppermute | solution.py:363
  30.5 1.3 %shard_map.150 = (f32[4,256,128]{2,1,0:T(8,128)S(1)}, f32[4,256,128]{2,1,0:T(8,128)S(1)}) custom-call(bf16[4,256,128]{2,1,0:T(8,128)(2,1)S(1)} %all_gather.3.q_ref, bf16[8,2,128,128]{3,2,1,0:T(8,128)(2,1)S(1)} %all-to-all-done.kv_ref), custom_call_target="tpu_custom_call" | custom-call | tf_op jit(solution)/shard_map/pallas_call | solution.py:321
  31.8 0.3 collective-permute-done.kv_ref
  32.0 2.9 %shard_map.151 = bf16[4,264,128]{2,1,0:T(8,128)(2,1)S(1)} custom-call(bf16[4,256,128]{2,1,0:T(8,128)(2,1)S(1)} %all_gather.3.q_ref, bf16[8,2,128,128]{3,2,1,0:T(8,128)(2,1)S(1)} %collective-permute-done.kv_ref, f32[4,256,128]{2,1,0:T(8,128)S(1)} %get-tuple-element.8.sums_ref, f32[4,256,128]{2,1,0:T(8,128)S(1)} %get-tuple-element.9.stats_ref), custom_call_target="tpu_custom_call" | custom-call | tf_op jit(solution)/shard_map/pallas_call | solution.py:327
  35.0 0.0 copy-start
  35.0 9.8 %all_to_all.25.parts_ref = bf16[4,264,128]{2,1,0:T(8,128)(2,1)S(1)} all-to-all(bf16[4,264,128]{2,1,0:T(8,128)(2,1)S(1)} %shard_map.151), channel_id=1, replica_groups={{0,8,16,24},{4,12,20,28},{32,40,48,56},{36,44,52,60},{64,72,80,88},{68,..., dimensions={0} | all-to-all | bytes 540672 | tf_op jit(solution)/shard_map/all_to_all | solution.py:365
  44.8 0.6 shard_map.152
  45.4 0.0 copy-start.5
  45.5 0.0 copy-start.3
  45.5 0.0 copy-start.4
  45.5 0.0 copy-start.6
  45.5 0.0 copy-start.7
  45.5 17.8 %all_to_all.26.parts_ref = bf16[8,128,128]{2,1,0:T(8,128)(2,1)S(1)} all-to-all(bf16[8,128,128]{2,1,0:T(8,128)(2,1)S(1)} %shard_map.152), channel_id=1, replica_groups=mesh['role'=2,'seq'=64,'head'=4] {'role','head'}, dimensions={0} | all-to-all | bytes 524288 | tf_op jit(solution)/shard_map/all_to_all | solution.py:367
  63.3 0.0 copy-start.1
  63.3 0.0 copy-start.2
  63.3 0.2 shard_map.153
  63.6 17.4 %all_to_all.27.in_ref = bf16[64,8,128]{2,1,0:T(8,128)(2,1)S(1)} all-to-all(bf16[64,8,128]{2,1,0:T(8,128)(2,1)S(1)} %shard_map.153), channel_id=1, replica_groups=mesh['role'=2,'seq'=64,'head'=4] {'seq'}, dimensions={0} | all-to-all | bytes 262144 | tf_op jit(solution)/shard_map/all_to_all | solution.py:369
  81.0 2.6 %shard_map.154 = bf16[64,4,128]{2,1,0:T(4,128)(2,1)S(1)} custom-call(f32[128]{0:T(128)} %skip_ref.1, bf16[64,8,128]{2,1,0:T(8,128)(2,1)S(1)} %all_to_all.27.in_ref, f32[72,128]{1,0:T(8,128)S(1)} %copy-done.7, f32[72,128]{1,0:T(8,128)S(1)} %copy-done.6, bf16[144,192]{1,0:T(8,128)(2,1)S(1)} %copy-done.3, bf16[64,432]{1,0:T(8,128)(2,1)S(1)} %copy-done.4, ...), custom_call_target="tpu_custom_call" | custom-call | tf_op jit(solution)/shard_map/pallas_call | solution.py:300
  83.6 13.9 %all_to_all.28.in_ref = bf16[64,4,128]{2,1,0:T(4,128)(2,1)S(1)} all-to-all(bf16[64,4,128]{2,1,0:T(4,128)(2,1)S(1)} %shard_map.154), channel_id=1, replica_groups=mesh['role'=2,'seq'=64,'head'=4] {'seq'}, dimensions={0} | all-to-all | bytes 131072 | tf_op jit(solution)/shard_map/all_to_all | solution.py:371
  97.5 0.7 shard_map.155
  (14 shorter events, 0.0 us)
Async XLA Ops:
  2.4 7.8 %copy-start.10 = (bf16[128,2,128]{2,1,0:T(2,128)(2,1)S(1)}, bf16[128,2,128]{2,1,0:T(2,128)(2,1)}, u32[]{:S(2)}) copy-start(bf16[128,2,128]{2,1,0:T(2,128)(2,1)} %param.14) | copy-start | bytes 196612
  2.4 22.5 %all-to-all-start = ((bf16[8,2,128,128]{3,2,1,0:T(8,128)(2,1)}), bf16[8,2,128,128]{3,2,1,0:T(8,128)(2,1)S(1)}, u32[]{:S(2)}, u32[]{:S(2)}) async-start(bf16[8,2,128,128]{3,2,1,0:T(8,128)(2,1)} %shard_map.149), calls=%async_computation | async-start | bytes 1048576 | tf_op jit(solution)/shard_map/all_to_all | solution.py:360
  24.9 7.1 %collective-permute-start = (bf16[8,2,128,128]{3,2,1,0:T(8,128)(2,1)S(1)}, bf16[8,2,128,128]{3,2,1,0:T(8,128)(2,1)S(1)}, u32[]{:S(2)}, u32[]{:S(2)}) collective-permute-start(bf16[8,2,128,128]{3,2,1,0:T(8,128)(2,1)S(1)} %all-to-all-done.kv_ref), channel_id=1, source_target_pairs={{0,4},{4,0},{8,12},{12,8},{16,20},{20,16},{24,28},{28,24},{32,36},... | collective-permute-start | bytes 1572872 | tf_op jit(solution)/shard_map/ppermute | solution.py:363
  35.0 9.9 %copy-start = (bf16[2,128,1024]{2,1,0:T(8,128)(2,1)S(1)}, bf16[2,128,1024]{2,1,0:T(8,128)(2,1)}, u32[]{:S(2)}) copy-start(bf16[2,128,1024]{2,1,0:T(8,128)(2,1)} %param.17) | copy-start | bytes 1572868
  45.4 17.9 %copy-start.5 = (f32[128,128]{1,0:T(8,128)S(1)}, f32[128,128]{1,0:T(8,128)}, u32[]{:S(2)}) copy-start(f32[128,128]{1,0:T(8,128)} %taps_ref.1) | copy-start | bytes 196612
  45.4 17.9 %copy-start.8 = (bf16[128,128]{1,0:T(8,128)(2,1)S(1)}, bf16[128,128]{1,0:T(8,128)(2,1)}, u32[]{:S(2)}) copy-start(bf16[128,128]{1,0:T(8,128)(2,1)} %input_ref.1) | copy-start | bytes 98308
  45.4 17.9 %copy-start.9 = (bf16[128,128]{1,0:T(8,128)(2,1)S(1)}, bf16[128,128]{1,0:T(8,128)(2,1)}, u32[]{:S(2)}) copy-start(bf16[128,128]{1,0:T(8,128)(2,1)} %gate_ref.1) | copy-start | bytes 98308
  45.5 35.5 %copy-start.3 = (bf16[144,192]{1,0:T(8,128)(2,1)S(1)}, bf16[144,192]{1,0:T(8,128)(2,1)}, u32[]{:S(2)}) copy-start(bf16[144,192]{1,0:T(8,128)(2,1)} %constant.14.clone.first) | copy-start | bytes 165892
  45.5 35.5 %copy-start.4 = (bf16[64,432]{1,0:T(8,128)(2,1)S(1)}, bf16[64,432]{1,0:T(8,128)(2,1)}, u32[]{:S(2)}) copy-start(bf16[64,432]{1,0:T(8,128)(2,1)} %constant.15.clone.last) | copy-start | bytes 165892
  45.5 35.5 %copy-start.6 = (f32[72,128]{1,0:T(8,128)S(1)}, f32[72,128]{1,0:T(8,128)}, u32[]{:S(2)}) copy-start(f32[72,128]{1,0:T(8,128)} %constant.13.clone.ts) | copy-start | bytes 110596
  45.5 35.5 %copy-start.7 = (f32[72,128]{1,0:T(8,128)S(1)}, f32[72,128]{1,0:T(8,128)}, u32[]{:S(2)}) copy-start(f32[72,128]{1,0:T(8,128)} %constant.12.clone.tc) | copy-start | bytes 110596
  63.3 17.7 %copy-start.1 = (bf16[768,256]{1,0:T(8,128)(2,1)S(1)}, bf16[768,256]{1,0:T(8,128)(2,1)}, u32[]{:S(2)}) copy-start(bf16[768,256]{1,0:T(8,128)(2,1)} %constant.17.clone.backward) | copy-start | bytes 1179652
  63.3 17.7 %copy-start.2 = (bf16[768,256]{1,0:T(8,128)(2,1)S(1)}, bf16[768,256]{1,0:T(8,128)(2,1)}, u32[]{:S(2)}) copy-start(bf16[768,256]{1,0:T(8,128)(2,1)} %constant.16.clone.forward) | copy-start | bytes 1179652

commit v17 on v14

--- a/solution.py
+++ b/solution.py
@@ -223,11 +223,13 @@
         total = total + share * total_before
         safe = jnp.maximum(total, 1e-30)
         out_ref[theirs, :256, :] = ((sums + share * sums_ref[step]) / safe).astype(jnp.bfloat16)
-        log_sums = jnp.where(total > 0.0, top * scale + jnp.log(safe), NEG)
         stats = []
         for half in (0, 1):
-            log_sum = log_sums[half * SHARD : (half + 1) * SHARD]
-            log_sum = jnp.sum(jnp.where(rows == columns, log_sum, 0.0), axis=0, keepdims=True)
+            part = slice(half * SHARD, (half + 1) * SHARD)
+            total_row = jnp.sum(jnp.where(rows == columns, total[part], 0.0), axis=0, keepdims=True)
+            top_row = jnp.sum(jnp.where(rows == columns, top[part], 0.0), axis=0, keepdims=True)
+            log_sum = top_row * scale + jnp.log(jnp.maximum(total_row, 1e-30))
+            log_sum = jnp.where(total_row > 0.0, log_sum, NEG)
             high = log_sum.astype(jnp.bfloat16).astype(jnp.float32)
             rest = log_sum - high
             middle = rest.astype(jnp.bfloat16).astype(jnp.float32)

time: 97.5 us -> 97.4 us (level)
  no operation moved by 1% of the time
where the time goes in v17:
time: 97.4 us; the launch traced here: 96.9 us
  blocking collectives  69.6 us (71%)
  starting transfers between devices  13.4 us (14%)
  Pallas kernels  8.71 us (9%)
  waiting for transfers between devices  4.4 us (5%)
    all_to_all x1, blocking collectives, body(): target = lax.all_to_all(target, ('role', 'head'), 0, 0)  17.8 us
    all_to_all x1, blocking collectives, body(): packed = lax.all_to_all(packed, 'seq', 0, 0)  17.4 us
    all_to_all x1, blocking collectives, body(): out = lax.all_to_all(out, 'seq', 0, 0)  13.9 us
    all_gather x1, blocking collectives, body(): lax.all_gather(query_heads.reshape(2 * SHARD, 128), 'seq', axis_index_gro...  10.6 us
    all_to_all x1, blocking collectives, body(): parts = lax.all_to_all(parts, 'seq', 0, 0, axis_index_groups=groups)  9.85 us
    all_to_all x1, starting transfers between devices, body(): own = lax.all_to_all(pairs, 'seq', 0, 0, axis_index_groups=columns)  7.79 us
    ppermute x1, starting transfers between devices, body(): sibling = lax.ppermute(own, 'seq', [(i, i ^ 1) for i in range(SHARDS)])  5.59 us
    all_to_all x1, waiting for transfers between devices, body(): own = lax.all_to_all(pairs, 'seq', 0, 0, axis_index_groups=columns)  4.15 us
  transfers between devices with their start and end apart: 2, of which 2 were waited for; matrix products, arithmetic and copies ran while one was open for 0% of the time, Pallas kernels for 1%

profile of v17, /device:TPU:1, one launch (start us, length us, event | category | flops | bytes accessed | tf_op | source)
XLA Modules:
  0.0 96.9 jit_solution(795198436291383358)
XLA Ops:
  0.6 1.7 %shard_map.149 = bf16[8,2,128,128]{3,2,1,0:T(8,128)(2,1)} custom-call(bf16[128,128]{1,0:T(8,128)(2,1)} %bitcast.6, bf16[128,128]{1,0:T(8,128)(2,1)} %bitcast.7), custom_call_target="tpu_custom_call" | custom-call | tf_op jit(solution)/shard_map/pallas_call | solution.py:276
  2.4 7.8 %all-to-all-start = ((bf16[8,2,128,128]{3,2,1,0:T(8,128)(2,1)}), bf16[8,2,128,128]{3,2,1,0:T(8,128)(2,1)S(1)}, u32[]{:S(2)}, u32[]{:S(2)}) async-start(bf16[8,2,128,128]{3,2,1,0:T(8,128)(2,1)} %shard_map.149), calls=%async_computation | async-start | bytes 1048576 | tf_op jit(solution)/shard_map/all_to_all | solution.py:360
  10.2 10.6 %all_gather.3.q_ref = bf16[4,256,128]{2,1,0:T(8,128)(2,1)S(1)} all-gather(bf16[1,256,128]{2,1,0:T(8,128)(2,1)S(1)} %bitcast.5), channel_id=1, replica_groups={{0,8,16,24},{4,12,20,28},{32,40,48,56},{36,44,52,60},{64,72,80,88},{68,..., dimensions={0}, use_global_device_ids=true | all-gather | bytes 327680 | tf_op jit(solution)/shard_map/all_gather | solution.py:361
  20.8 4.2 %all-to-all-done.kv_ref = bf16[8,2,128,128]{3,2,1,0:T(8,128)(2,1)S(1)} async-done(((bf16[8,2,128,128]{3,2,1,0:T(8,128)(2,1)}), bf16[8,2,128,128]{3,2,1,0:T(8,128)(2,1)S(1)}, u32[]{:S(2)}, u32[]{:S(2)}) %all-to-all-start) | async-done | bytes 524320 | tf_op jit(solution)/shard_map/all_to_all | solution.py:360
  24.9 5.6 %collective-permute-start = (bf16[8,2,128,128]{3,2,1,0:T(8,128)(2,1)S(1)}, bf16[8,2,128,128]{3,2,1,0:T(8,128)(2,1)S(1)}, u32[]{:S(2)}, u32[]{:S(2)}) collective-permute-start(bf16[8,2,128,128]{3,2,1,0:T(8,128)(2,1)S(1)} %all-to-all-done.kv_ref), channel_id=1, source_target_pairs={{0,4},{4,0},{8,12},{12,8},{16,20},{20,16},{24,28},{28,24},{32,36},... | collective-permute-start | bytes 1572872 | tf_op jit(solution)/shard_map/ppermute | solution.py:363
  30.5 1.3 %shard_map.150 = (f32[4,256,128]{2,1,0:T(8,128)S(1)}, f32[4,256,128]{2,1,0:T(8,128)S(1)}) custom-call(bf16[4,256,128]{2,1,0:T(8,128)(2,1)S(1)} %all_gather.3.q_ref, bf16[8,2,128,128]{3,2,1,0:T(8,128)(2,1)S(1)} %all-to-all-done.kv_ref), custom_call_target="tpu_custom_call" | custom-call | tf_op jit(solution)/shard_map/pallas_call | solution.py:321
  31.8 0.3 collective-permute-done.kv_ref
  32.0 1.7 %shard_map.151 = bf16[4,264,128]{2,1,0:T(8,128)(2,1)S(1)} custom-call(bf16[4,256,128]{2,1,0:T(8,128)(2,1)S(1)} %all_gather.3.q_ref, bf16[8,2,128,128]{3,2,1,0:T(8,128)(2,1)S(1)} %collective-permute-done.kv_ref, f32[4,256,128]{2,1,0:T(8,128)S(1)} %get-tuple-element.8.sums_ref, f32[4,256,128]{2,1,0:T(8,128)S(1)} %get-tuple-element.9.stats_ref), custom_call_target="tpu_custom_call" | custom-call | tf_op jit(solution)/shard_map/pallas_call | solution.py:327
  33.7 9.8 %all_to_all.25.parts_ref = bf16[4,264,128]{2,1,0:T(8,128)(2,1)S(1)} all-to-all(bf16[4,264,128]{2,1,0:T(8,128)(2,1)S(1)} %shard_map.151), channel_id=1, replica_groups={{0,8,16,24},{4,12,20,28},{32,40,48,56},{36,44,52,60},{64,72,80,88},{68,..., dimensions={0} | all-to-all | bytes 540672 | tf_op jit(solution)/shard_map/all_to_all | solution.py:365
  43.6 0.6 shard_map.152
  44.2 0.0 copy-start.8
  44.2 0.0 copy-start.9
  44.2 0.0 copy-start.3
  44.2 0.0 copy-start.4
  44.2 0.0 copy-start.6
  44.2 0.0 copy-start.7
  44.2 17.8 %all_to_all.26.parts_ref = bf16[8,128,128]{2,1,0:T(8,128)(2,1)S(1)} all-to-all(bf16[8,128,128]{2,1,0:T(8,128)(2,1)S(1)} %shard_map.152), channel_id=1, replica_groups=mesh['role'=2,'seq'=64,'head'=4] {'role','head'}, dimensions={0} | all-to-all | bytes 524288 | tf_op jit(solution)/shard_map/all_to_all | solution.py:367
  62.1 0.0 copy-start.1
  62.1 0.0 copy-start.2
  62.1 0.2 shard_map.153
  62.3 17.4 %all_to_all.27.in_ref = bf16[64,8,128]{2,1,0:T(8,128)(2,1)S(1)} all-to-all(bf16[64,8,128]{2,1,0:T(8,128)(2,1)S(1)} %shard_map.153), channel_id=1, replica_groups=mesh['role'=2,'seq'=64,'head'=4] {'seq'}, dimensions={0} | all-to-all | bytes 262144 | tf_op jit(solution)/shard_map/all_to_all | solution.py:369
  79.7 2.6 %shard_map.154 = bf16[64,4,128]{2,1,0:T(4,128)(2,1)S(1)} custom-call(f32[128]{0:T(128)} %skip_ref.1, bf16[64,8,128]{2,1,0:T(8,128)(2,1)S(1)} %all_to_all.27.in_ref, f32[72,128]{1,0:T(8,128)S(1)} %copy-done.7, f32[72,128]{1,0:T(8,128)S(1)} %copy-done.6, bf16[144,192]{1,0:T(8,128)(2,1)S(1)} %copy-done.3, bf16[64,432]{1,0:T(8,128)(2,1)S(1)} %copy-done.4, ...), custom_call_target="tpu_custom_call" | custom-call | tf_op jit(solution)/shard_map/pallas_call | solution.py:300
  82.3 13.9 %all_to_all.28.in_ref = bf16[64,4,128]{2,1,0:T(4,128)(2,1)S(1)} all-to-all(bf16[64,4,128]{2,1,0:T(4,128)(2,1)S(1)} %shard_map.154), channel_id=1, replica_groups=mesh['role'=2,'seq'=64,'head'=4] {'seq'}, dimensions={0} | all-to-all | bytes 131072 | tf_op jit(solution)/shard_map/all_to_all | solution.py:371
  96.2 0.7 shard_map.155
  (14 shorter events, 0.0 us)
Async XLA Ops:
  2.4 7.8 %copy-start.10 = (bf16[128,2,128]{2,1,0:T(2,128)(2,1)S(1)}, bf16[128,2,128]{2,1,0:T(2,128)(2,1)}, u32[]{:S(2)}) copy-start(bf16[128,2,128]{2,1,0:T(2,128)(2,1)} %param.14) | copy-start | bytes 196612
  2.4 22.5 %all-to-all-start = ((bf16[8,2,128,128]{3,2,1,0:T(8,128)(2,1)}), bf16[8,2,128,128]{3,2,1,0:T(8,128)(2,1)S(1)}, u32[]{:S(2)}, u32[]{:S(2)}) async-start(bf16[8,2,128,128]{3,2,1,0:T(8,128)(2,1)} %shard_map.149), calls=%async_computation | async-start | bytes 1048576 | tf_op jit(solution)/shard_map/all_to_all | solution.py:360
  24.9 7.1 %collective-permute-start = (bf16[8,2,128,128]{3,2,1,0:T(8,128)(2,1)S(1)}, bf16[8,2,128,128]{3,2,1,0:T(8,128)(2,1)S(1)}, u32[]{:S(2)}, u32[]{:S(2)}) collective-permute-start(bf16[8,2,128,128]{3,2,1,0:T(8,128)(2,1)S(1)} %all-to-all-done.kv_ref), channel_id=1, source_target_pairs={{0,4},{4,0},{8,12},{12,8},{16,20},{20,16},{24,28},{28,24},{32,36},... | collective-permute-start | bytes 1572872 | tf_op jit(solution)/shard_map/ppermute | solution.py:363
  33.7 9.9 %copy-start = (bf16[2,128,1024]{2,1,0:T(8,128)(2,1)S(1)}, bf16[2,128,1024]{2,1,0:T(8,128)(2,1)}, u32[]{:S(2)}) copy-start(bf16[2,128,1024]{2,1,0:T(8,128)(2,1)} %param.17) | copy-start | bytes 1572868
  44.2 17.9 %copy-start.5 = (f32[128,128]{1,0:T(8,128)S(1)}, f32[128,128]{1,0:T(8,128)}, u32[]{:S(2)}) copy-start(f32[128,128]{1,0:T(8,128)} %taps_ref.1) | copy-start | bytes 196612
  44.2 17.9 %copy-start.8 = (bf16[128,128]{1,0:T(8,128)(2,1)S(1)}, bf16[128,128]{1,0:T(8,128)(2,1)}, u32[]{:S(2)}) copy-start(bf16[128,128]{1,0:T(8,128)(2,1)} %input_ref.1) | copy-start | bytes 98308
  44.2 17.9 %copy-start.9 = (bf16[128,128]{1,0:T(8,128)(2,1)S(1)}, bf16[128,128]{1,0:T(8,128)(2,1)}, u32[]{:S(2)}) copy-start(bf16[128,128]{1,0:T(8,128)(2,1)} %gate_ref.1) | copy-start | bytes 98308
  44.2 35.5 %copy-start.3 = (bf16[144,192]{1,0:T(8,128)(2,1)S(1)}, bf16[144,192]{1,0:T(8,128)(2,1)}, u32[]{:S(2)}) copy-start(bf16[144,192]{1,0:T(8,128)(2,1)} %constant.14.clone.first) | copy-start | bytes 165892
  44.2 35.5 %copy-start.4 = (bf16[64,432]{1,0:T(8,128)(2,1)S(1)}, bf16[64,432]{1,0:T(8,128)(2,1)}, u32[]{:S(2)}) copy-start(bf16[64,432]{1,0:T(8,128)(2,1)} %constant.15.clone.last) | copy-start | bytes 165892
  44.2 35.5 %copy-start.6 = (f32[72,128]{1,0:T(8,128)S(1)}, f32[72,128]{1,0:T(8,128)}, u32[]{:S(2)}) copy-start(f32[72,128]{1,0:T(8,128)} %constant.13.clone.ts) | copy-start | bytes 110596
  44.2 35.5 %copy-start.7 = (f32[72,128]{1,0:T(8,128)S(1)}, f32[72,128]{1,0:T(8,128)}, u32[]{:S(2)}) copy-start(f32[72,128]{1,0:T(8,128)} %constant.12.clone.tc) | copy-start | bytes 110596
  62.1 17.7 %copy-start.1 = (bf16[768,256]{1,0:T(8,128)(2,1)S(1)}, bf16[768,256]{1,0:T(8,128)(2,1)}, u32[]{:S(2)}) copy-start(bf16[768,256]{1,0:T(8,128)(2,1)} %constant.17.clone.backward) | copy-start | bytes 1179652
  62.1 17.7 %copy-start.2 = (bf16[768,256]{1,0:T(8,128)(2,1)S(1)}, bf16[768,256]{1,0:T(8,128)(2,1)}, u32[]{:S(2)}) copy-start(bf16[768,256]{1,0:T(8,128)(2,1)} %constant.16.clone.forward) | copy-start | bytes 1179652
